TPU v7x, 32 devices: a whole 2x2x4 slice. The times are simulated.
32 devices in a mesh: fsdp: 4 (over z), cp: 2 (over x), tp: 4 (over y, core).
Axes of the slice: x: 2, y: 2, z: 4, core: 2. Of those that a mesh axis runs over, the one named last changes fastest.
Arguments:
- tokens: bfloat16 [8, 1024, 2304], P('fsdp', ('cp', 'tp')), may hold values from -6 to 6
- seq_lengths: int32 [8], P('fsdp'), may hold values from 256 to 1024, as said below
- attention_gain: bfloat16 [2304], replicated, may hold values from 0.5 to 1.5
- query_weight: bfloat16 [2304, 2304], P(('fsdp', 'cp'), 'tp'), may hold values from -0.1875 to 0.1875
- key_weight: bfloat16 [2304, 2304], P(('fsdp', 'cp'), 'tp'), may hold values from -0.1875 to 0.1875
- value_weight: bfloat16 [2304, 2304], P(('fsdp', 'cp'), 'tp'), may hold values from -0.125 to 0.125
- out_weight: bfloat16 [2304, 2304], P('tp', ('fsdp', 'cp')), may hold values from -3 to 3
- feedforward_gain: bfloat16 [2304], replicated, may hold values from 0.5 to 1.5
- gate_weight: bfloat16 [2304, 5760], P(('fsdp', 'cp'), 'tp'), may hold values from -0.125 to 0.125
- up_weight: bfloat16 [2304, 5760], P(('fsdp', 'cp'), 'tp'), may hold values from -0.125 to 0.125
- down_weight: bfloat16 [5760, 2304], P('tp', ('fsdp', 'cp')), may hold values from -0.4375 to 0.4375
- cotangent: bfloat16 [8, 1024, 2304], P('fsdp', ('cp', 'tp')), may hold values from -6 to 6
Outputs:
- output: bfloat16 [8, 1024, 2304], P('fsdp', ('cp', 'tp'))
- grad_tokens: bfloat16 [8, 1024, 2304], P('fsdp', ('cp', 'tp'))
- grad_query_weight: float32 [2304, 2304], P(('fsdp', 'cp'), 'tp')
- grad_key_weight: float32 [2304, 2304], P(('fsdp', 'cp'), 'tp')
- grad_value_weight: float32 [2304, 2304], P(('fsdp', 'cp'), 'tp')
- grad_out_weight: float32 [2304, 2304], P('tp', ('fsdp', 'cp'))
- grad_attention_gain: float32 [2304], replicated
- grad_gate_weight: float32 [2304, 5760], P(('fsdp', 'cp'), 'tp')
- grad_up_weight: float32 [2304, 5760], P(('fsdp', 'cp'), 'tp')
- grad_down_weight: float32 [5760, 2304], P('tp', ('fsdp', 'cp'))
- grad_feedforward_gain: float32 [2304], replicated
Inputs may be any that keep to these rules, and one draw needn't show every extreme that they name: `seq_lengths`: real tokens of each sequence; positions from this count on are padding. In every draw one sequence has exactly 1024 and another exactly 256.
All inputs are finite; a program needn't handle non-finite values.
Results may differ from a plain program's by a relative error of at most 0.015.
Values may be sent and summed in bfloat16 or wider, within the bound.
A program may use at most 320 MiB of HBM per device.

v0:
```python
import math

import jax
import jax.numpy as jnp
from jax import lax
from jax.sharding import PartitionSpec as P

HD = 64


EPSILON = 1e-05
BRANCH = 1.4 / math.sqrt(40.0)


def passed_along(value, axis, steps):
    count = lax.axis_size(axis)
    first, last = (max(0, -steps), min(count, count - steps))
    return lax.ppermute(value, axis, [(source, source + steps) for source in range(first, last)])


def normalize(values):
    return values * lax.rsqrt(jnp.mean(values * values, axis=-1, keepdims=True) + EPSILON)


def scaled_norm(values, gain_values):
    return normalize(values) * gain_values


def angles(places):
    frequency = jnp.power(10000.0, -2.0 * jnp.arange(HD // 2, dtype=jnp.float32) / HD)
    phase_angle = places[:, None] * frequency[None, :]
    return (jnp.cos(phase_angle)[:, None, :], jnp.sin(phase_angle)[:, None, :])


def rotate(values, cosine_table, sine_table):
    half_dim = values.shape[-1] // 2
    first = values[..., :half_dim]
    second = values[..., half_dim:]
    return jnp.concatenate(
        [first * cosine_table - second * sine_table, second * cosine_table + first * sine_table],
        axis=-1,
    )


def softmax_rows(scores):
    row_top = jnp.max(scores, axis=-1, keepdims=True)
    exponent = jnp.exp(scores - row_top)
    return exponent / jnp.sum(exponent, axis=-1, keepdims=True)


def silu_product(gate_pre, up_pre):
    return gate_pre / (1.0 + jnp.exp(-gate_pre)) * up_pre


def matmul(left, right):
    return jnp.dot(left, right, preferred_element_type=jnp.float32)


def rows_inner(left, right):
    return lax.dot_general(
        left, right, (((0,), (0,)), ((), ())), preferred_element_type=jnp.float32
    )


def cols_inner(left, right):
    return lax.dot_general(
        left, right, (((1,), (1,)), ((), ())), preferred_element_type=jnp.float32
    )


def owner_shares(gradients):
    return (
        lax.psum_scatter(gradients[0], ("fsdp", "cp"), scatter_dimension=0, tiled=True),
        lax.psum_scatter(gradients[1], ("fsdp", "cp"), scatter_dimension=0, tiled=True),
        lax.psum_scatter(gradients[2], ("fsdp", "cp"), scatter_dimension=0, tiled=True),
        lax.psum_scatter(gradients[3], ("fsdp", "cp"), scatter_dimension=1, tiled=True),
        lax.psum_scatter(gradients[4], ("fsdp", "cp"), scatter_dimension=0, tiled=True),
        lax.psum_scatter(gradients[5], ("fsdp", "cp"), scatter_dimension=0, tiled=True),
        lax.psum_scatter(gradients[6], ("fsdp", "cp"), scatter_dimension=1, tiled=True),
    )


def on_device(
    tokens,
    seq_lengths,
    attention_gain,
    query_weight,
    key_weight,
    value_weight,
    out_weight,
    feedforward_gain,
    gate_weight,
    up_weight,
    down_weight,
    cotangent,
):
    gathered = (
        lax.all_gather(query_weight, ("fsdp", "cp"), axis=0, tiled=True),
        lax.all_gather(key_weight, ("fsdp", "cp"), axis=0, tiled=True),
        lax.all_gather(value_weight, ("fsdp", "cp"), axis=0, tiled=True),
        lax.all_gather(out_weight, ("fsdp", "cp"), axis=1, tiled=True),
        lax.all_gather(gate_weight, ("fsdp", "cp"), axis=0, tiled=True),
        lax.all_gather(up_weight, ("fsdp", "cp"), axis=0, tiled=True),
        lax.all_gather(down_weight, ("fsdp", "cp"), axis=1, tiled=True),
    )
    full_query, full_key, full_value, full_out, full_gate, full_up, full_down = gathered
    local_rows = tokens.shape[1]
    half_rows = local_rows * lax.axis_size("tp")
    head_count = full_query.shape[1] // HD
    score_scale = 1.0 / math.sqrt(HD)
    own_places = lax.axis_index("cp") * half_rows + jnp.arange(half_rows, dtype=jnp.int32)
    key_places = jnp.concatenate([own_places - half_rows, own_places])
    cosine_table, sine_table = angles(own_places.astype(jnp.float32))
    gain_one = attention_gain.astype(jnp.float32)
    gain_two = feedforward_gain.astype(jnp.float32)
    gain_one_total = jnp.zeros(gain_one.shape, jnp.float32)
    gain_two_total = jnp.zeros(gain_two.shape, jnp.float32)
    totals = None
    outputs = []
    input_grads = []

    def turn_heads(values):
        return rotate(values, cosine_table, sine_table)

    for batch_slot in range(tokens.shape[0]):
        inputs = tokens[batch_slot].astype(jnp.float32)
        upstream = cotangent[batch_slot].astype(jnp.float32)
        length = seq_lengths[batch_slot]
        allowed = (
            (key_places[None, :] <= own_places[:, None])
            & (key_places[None, :] >= 0)
            & (key_places[None, :] < length)
        )
        norm_one, norm_one_back = jax.vjp(scaled_norm, inputs, gain_one)
        normed_one = lax.all_gather(norm_one.astype(jnp.bfloat16), "tp", axis=0, tiled=True)
        query_raw = matmul(normed_one, full_query).reshape(half_rows, head_count, HD)
        queries = turn_heads(query_raw).astype(jnp.bfloat16)
        own_keys = turn_heads(
            matmul(normed_one, full_key).reshape(half_rows, head_count, HD)
        ).astype(jnp.bfloat16)
        own_values = (
            matmul(normed_one, full_value).astype(jnp.bfloat16).reshape(half_rows, head_count, HD)
        )
        prior_keys, prior_values = passed_along((own_keys, own_values), "cp", 1)
        all_keys = jnp.concatenate([prior_keys, own_keys], axis=0)
        all_values = jnp.concatenate([prior_values, own_values], axis=0)

        def scores_now():
            raw_scores = (
                jnp.einsum("qhd,khd->hqk", queries, all_keys, preferred_element_type=jnp.float32)
                * score_scale
            )
            return jnp.where(allowed[None], raw_scores, -1e30)

        probabilities = softmax_rows(scores_now())
        context = jnp.einsum(
            "hqk,khd->qhd",
            probabilities.astype(jnp.bfloat16),
            all_values,
            preferred_element_type=jnp.float32,
        )
        context = context.astype(jnp.bfloat16).reshape(half_rows, head_count * HD)
        attention_local = lax.psum_scatter(
            matmul(context, full_out), "tp", scatter_dimension=0, tiled=True
        )
        middle = inputs + BRANCH * attention_local
        norm_two, norm_two_back = jax.vjp(scaled_norm, middle, gain_two)
        normed_two = lax.all_gather(norm_two.astype(jnp.bfloat16), "tp", axis=0, tiled=True)
        gate_pre = matmul(normed_two, full_gate)
        up_pre = matmul(normed_two, full_up)
        hidden_exact, silu_back = jax.vjp(silu_product, gate_pre, up_pre)
        hidden = hidden_exact.astype(jnp.bfloat16)
        feedforward_local = lax.psum_scatter(
            matmul(hidden, full_down), "tp", scatter_dimension=0, tiled=True
        )
        outputs.append((middle + BRANCH * feedforward_local).astype(jnp.bfloat16))
        grad_branch = lax.all_gather(
            (BRANCH * upstream).astype(jnp.bfloat16), "tp", axis=0, tiled=True
        )
        grad_down = rows_inner(hidden, grad_branch)
        grad_hidden = cols_inner(grad_branch, full_down)
        grad_gate_exact, grad_up_exact = silu_back(grad_hidden)
        grad_gate_pre = grad_gate_exact.astype(jnp.bfloat16)
        grad_up_pre = grad_up_exact.astype(jnp.bfloat16)
        grad_gate = rows_inner(normed_two, grad_gate_pre)
        grad_up = rows_inner(normed_two, grad_up_pre)
        grad_normed_two = cols_inner(grad_gate_pre, full_gate) + cols_inner(grad_up_pre, full_up)
        grad_norm_two = lax.psum_scatter(grad_normed_two, "tp", scatter_dimension=0, tiled=True)
        grad_middle_norm, grad_gain_two = norm_two_back(grad_norm_two)
        grad_middle = upstream + grad_middle_norm
        grad_attention = lax.all_gather(
            (BRANCH * grad_middle).astype(jnp.bfloat16), "tp", axis=0, tiled=True
        )
        grad_out = rows_inner(context, grad_attention)
        grad_context = (
            cols_inner(grad_attention, full_out)
            .astype(jnp.bfloat16)
            .reshape(half_rows, head_count, HD)
        )
        probabilities_again, softmax_back = jax.vjp(softmax_rows, scores_now())
        grad_probabilities = jnp.einsum(
            "qhd,khd->hqk", grad_context, all_values, preferred_element_type=jnp.float32
        )
        grad_all_values = jnp.einsum(
            "hqk,qhd->khd",
            probabilities_again.astype(jnp.bfloat16),
            grad_context,
            preferred_element_type=jnp.float32,
        )
        grad_scores = jnp.where(allowed[None], softmax_back(grad_probabilities)[0], 0.0).astype(
            jnp.bfloat16
        )
        grad_query_turned = (
            jnp.einsum("hqk,khd->qhd", grad_scores, all_keys, preferred_element_type=jnp.float32)
            * score_scale
        )
        grad_all_keys = (
            jnp.einsum("hqk,qhd->khd", grad_scores, queries, preferred_element_type=jnp.float32)
            * score_scale
        )
        returned_keys, returned_values = passed_along(
            (grad_all_keys[:half_rows], grad_all_values[:half_rows]), "cp", -1
        )
        grad_key_turned = grad_all_keys[half_rows:] + returned_keys
        grad_values = (
            (grad_all_values[half_rows:] + returned_values)
            .astype(jnp.bfloat16)
            .reshape(half_rows, head_count * HD)
        )
        unused_turn, turn_back = jax.vjp(turn_heads, query_raw)
        grad_queries = (
            turn_back(grad_query_turned)[0].astype(jnp.bfloat16).reshape(half_rows, head_count * HD)
        )
        grad_keys = (
            turn_back(grad_key_turned)[0].astype(jnp.bfloat16).reshape(half_rows, head_count * HD)
        )
        grad_query = rows_inner(normed_one, grad_queries)
        grad_key = rows_inner(normed_one, grad_keys)
        grad_value = rows_inner(normed_one, grad_values)
        grad_normed_one = (
            cols_inner(grad_queries, full_query)
            + cols_inner(grad_keys, full_key)
            + cols_inner(grad_values, full_value)
        )
        grad_norm_one = lax.psum_scatter(grad_normed_one, "tp", scatter_dimension=0, tiled=True)
        grad_inputs_norm, grad_gain_one = norm_one_back(grad_norm_one)
        input_grads.append((grad_middle + grad_inputs_norm).astype(jnp.bfloat16))
        gain_one_total = gain_one_total + grad_gain_one
        gain_two_total = gain_two_total + grad_gain_two
        step_grads = (grad_query, grad_key, grad_value, grad_out, grad_gate, grad_up, grad_down)
        step_grads = owner_shares(step_grads)
        if totals is None:
            totals = step_grads
        else:
            totals = tuple((earlier + later for earlier, later in zip(totals, step_grads)))
    gain_sums = lax.psum((gain_one_total, gain_two_total), ("fsdp", "cp", "tp"))
    return (
        jnp.stack(outputs),
        jnp.stack(input_grads),
        totals[0],
        totals[1],
        totals[2],
        totals[3],
        gain_sums[0],
        totals[4],
        totals[5],
        totals[6],
        gain_sums[1],
    )


def solution(mesh):
    in_specs = (
        P("fsdp", ("cp", "tp"), None),
        P("fsdp"),
        P(),
        P(("fsdp", "cp"), "tp"),
        P(("fsdp", "cp"), "tp"),
        P(("fsdp", "cp"), "tp"),
        P("tp", ("fsdp", "cp")),
        P(),
        P(("fsdp", "cp"), "tp"),
        P(("fsdp", "cp"), "tp"),
        P("tp", ("fsdp", "cp")),
        P("fsdp", ("cp", "tp"), None),
    )
    out_specs = (
        P("fsdp", ("cp", "tp"), None),
        P("fsdp", ("cp", "tp"), None),
        P(("fsdp", "cp"), "tp"),
        P(("fsdp", "cp"), "tp"),
        P(("fsdp", "cp"), "tp"),
        P("tp", ("fsdp", "cp")),
        P(),
        P(("fsdp", "cp"), "tp"),
        P(("fsdp", "cp"), "tp"),
        P("tp", ("fsdp", "cp")),
        P(),
    )
    return jax.shard_map(
        on_device, mesh=mesh, in_specs=in_specs, out_specs=out_specs, check_vma=False
    )
```

profile of v0, /device:TPU:0, one launch (start us, length us, event | category | flops | bytes accessed | tf_op | source)
XLA Modules:
  0.0 2551.6 jit_solution(5882309123810619268)
XLA Ops:
  40.2 60.6 %all-gather.22.cloned.1.call-done = bf16[2304,576]{1,0:T(8,128)(2,1)} async-done(((bf16[288,576]{1,0:T(8,128)(2,1)}), bf16[2304,576]{1,0:T(8,128)(2,1)}) %all-gather.22.cloned.1.call-update) | async-done | bytes 2654224 | tf_op jit(solution)/shard_map/all_gather | solution.py:99
  104.9 55.1 %all-gather.20.cloned.1.call-done = bf16[2304,576]{1,0:T(8,128)(2,1)} async-done(((bf16[288,576]{1,0:T(8,128)(2,1)}), bf16[2304,576]{1,0:T(8,128)(2,1)}) %all-gather.20.cloned.1.call-update) | async-done | bytes 2654224 | tf_op jit(solution)/shard_map/all_gather | solution.py:98
  164.4 20.3 all-gather.16.cloned.1.call-done
  198.6 48.4 %all-gather.18.cloned.1.call-done = bf16[2304,576]{1,0:T(8,128)(2,1)} async-done(((bf16[288,576]{1,0:T(8,128)(2,1)}), bf16[2304,576]{1,0:T(8,128)(2,1)}) %all-gather.18.cloned.1.call-update) | async-done | bytes 2654224 | tf_op jit(solution)/shard_map/all_gather | solution.py:100
  285.5 23.3 all-gather.24.cloned.1.call-done
  368.3 47.7 %reduce-scatter.20.cloned.1.call-done = f32[128,2304]{1,0:T(8,128)} async-done(((f32[512,2304]{1,0:T(8,128)}), f32[128,2304]{1,0:T(8,128)}) %reduce-scatter.20.cloned.1.call-update) | async-done | bytes 1179664 | tf_op jit(solution)/shard_map/reduce_scatter | solution.py:163
  423.8 103.2 %all-gather.30.cloned.1.call-done = bf16[2304,1440]{1,0:T(8,128)(2,1)} async-done(((bf16[288,1440]{1,0:T(8,128)(2,1)}), bf16[2304,1440]{1,0:T(8,128)(2,1)}) %all-gather.30.cloned.1.call-update) | async-done | bytes 6635536 | tf_op jit(solution)/shard_map/all_gather | solution.py:103
  527.0 24.3 all-gather.26.cloned.1.call-done
  560.3 102.0 %all-gather.28.cloned.1.call-done = bf16[2304,1440]{1,0:T(8,128)(2,1)} async-done(((bf16[288,1440]{1,0:T(8,128)(2,1)}), bf16[2304,1440]{1,0:T(8,128)(2,1)}) %all-gather.28.cloned.1.call-update) | async-done | bytes 6635536 | tf_op jit(solution)/shard_map/all_gather | solution.py:102
  686.6 111.0 %all-gather.32.cloned.1.call-done = bf16[1440,2304]{0,1:T(8,128)(2,1)} async-done(((bf16[1440,288]{0,1:T(8,128)(2,1)}), bf16[1440,2304]{0,1:T(8,128)(2,1)}) %all-gather.32.cloned.1.call-update) | async-done | bytes 6635536 | tf_op jit(solution)/shard_map/all_gather | solution.py:104
  823.2 45.5 %reduce-scatter.24.cloned.1.call-done = f32[128,2304]{1,0:T(8,128)} async-done(((f32[512,2304]{1,0:T(8,128)}), f32[128,2304]{1,0:T(8,128)}) %reduce-scatter.24.cloned.1.call-update) | async-done | bytes 1179664 | tf_op jit(solution)/shard_map/reduce_scatter | solution.py:188
  872.8 23.2 all-gather.36.cloned.1.call-done
  961.6 36.6 %reduce-scatter.28.cloned.1.call-done = f32[128,2304]{1,0:T(8,128)} async-done(((f32[512,2304]{1,0:T(8,128)}), f32[128,2304]{1,0:T(8,128)}) %reduce-scatter.28.cloned.1.call-update) | async-done | bytes 1179664 | tf_op jit(solution)/shard_map/reduce_scatter | solution.py:188
  1001.6 46.9 %reduce-scatter.22.cloned.1.call-done = f32[128,2304]{1,0:T(8,128)} async-done(((f32[512,2304]{1,0:T(8,128)}), f32[128,2304]{1,0:T(8,128)}) %reduce-scatter.22.cloned.1.call-update) | async-done | bytes 1179664 | tf_op jit(solution)/shard_map/reduce_scatter | solution.py:173
  1054.3 22.4 all-gather.44.cloned.1.call-done
  1242.8 26.9 %collective-permute-done.5 = f32[512,9,64]{0,2,1:T(8,128)S(1)} collective-permute-done((f32[512,9,64]{0,2,1:T(8,128)S(1)}, f32[512,9,64]{0,2,1:T(8,128)S(1)}, u32[]{:S(2)}, u32[]{:S(2)}) %collective-permute-start.5) | collective-permute-done | bytes 1179680 | tf_op jit(solution)/shard_map/ppermute | solution.py:18
  1374.2 41.4 %all-reduce.8 = (f32[2304]{0:T(1024)}, f32[2304]{0:T(1024)}) all-reduce(f32[2304]{0:T(1024)S(1)} %add.263, f32[2304]{0:T(1024)S(1)} %add.267), channel_id=1, replica_groups=mesh['fsdp'=4,'cp'=2,'tp'=4] {'fsdp','cp','tp'}, use_global_device_ids=true, to_apply=%region_36.37 | all-reduce | flops 4608 | bytes 36864 | tf_op jit(solution)/shard_map/psum | solution.py:256
  1425.2 73.5 %reduce-scatter.38.cloned.1.call-done = f32[576,288]{0,1:T(8,128)} async-done(((f32[576,2304]{0,1:T(8,128)}), f32[576,288]{0,1:T(8,128)}) %reduce-scatter.38.cloned.1.call-update) | async-done | bytes 663568 | tf_op jit(solution)/shard_map/reduce_scatter | solution.py:76
  1498.7 115.9 %reduce-scatter.36.cloned.1.call-done = f32[288,576]{1,0:T(8,128)} async-done(((f32[2304,576]{1,0:T(8,128)}), f32[288,576]{1,0:T(8,128)}) %reduce-scatter.36.cloned.1.call-update) | async-done | bytes 663568 | tf_op jit(solution)/shard_map/reduce_scatter | solution.py:75
  1614.6 115.8 %reduce-scatter.34.cloned.1.call-done = f32[288,576]{1,0:T(8,128)} async-done(((f32[2304,576]{1,0:T(8,128)}), f32[288,576]{1,0:T(8,128)}) %reduce-scatter.34.cloned.1.call-update) | async-done | bytes 663568 | tf_op jit(solution)/shard_map/reduce_scatter | solution.py:74
  1730.4 115.7 %reduce-scatter.32.cloned.1.call-done = f32[288,576]{1,0:T(8,128)} async-done(((f32[2304,576]{1,0:T(8,128)}), f32[288,576]{1,0:T(8,128)}) %reduce-scatter.32.cloned.1.call-update) | async-done | bytes 663568 | tf_op jit(solution)/shard_map/reduce_scatter | solution.py:73
  1846.1 233.3 %reduce-scatter.44.cloned.1.call-done = f32[1440,288]{0,1:T(8,128)} async-done(((f32[1440,2304]{0,1:T(8,128)}), f32[1440,288]{0,1:T(8,128)}) %reduce-scatter.44.cloned.1.call-update) | async-done | bytes 1658896 | tf_op jit(solution)/shard_map/reduce_scatter | solution.py:79
  2079.4 232.6 %reduce-scatter.42.cloned.1.call-done = f32[288,1440]{1,0:T(8,128)} async-done(((f32[2304,1440]{1,0:T(8,128)}), f32[288,1440]{1,0:T(8,128)}) %reduce-scatter.42.cloned.1.call-update) | async-done | bytes 1658896 | tf_op jit(solution)/shard_map/reduce_scatter | solution.py:78
  2311.9 232.4 %reduce-scatter.40.cloned.1.call-done = f32[288,1440]{1,0:T(8,128)} async-done(((f32[2304,1440]{1,0:T(8,128)}), f32[288,1440]{1,0:T(8,128)}) %reduce-scatter.40.cloned.1.call-update) | async-done | bytes 1658896 | tf_op jit(solution)/shard_map/reduce_scatter | solution.py:77
  (442 shorter events, 577.3 us)
Async XLA Ops:
  14.0 146.0 %all-gather.20.cloned.1.call-start = ((), (), s32[]{:S(2)}) async-start(), calls=%async_computation.17 | async-start | bytes 3317760 | tf_op jit(solution)/shard_map/all_gather | solution.py:98
  14.8 170.0 %all-gather.16.cloned.1.call-start = ((), (), s32[]{:S(2)}) async-start(), calls=%async_computation.15 | async-start | bytes 2949120 | tf_op jit(solution)/shard_map/all_gather | solution.py:135
  15.3 231.7 %all-gather.18.cloned.1.call-start = ((), (), s32[]{:S(2)}) async-start(), calls=%async_computation.16 | async-start | bytes 3317760 | tf_op jit(solution)/shard_map/all_gather | solution.py:100
  15.9 292.9 %all-gather.24.cloned.1.call-start = ((), (), s32[]{:S(2)}) async-start(), calls=%async_computation.19 | async-start | bytes 3317760 | tf_op jit(solution)/shard_map/all_gather | solution.py:101
  16.5 351.8 %reduce-scatter.16.cloned.1.call-start = ((), (), s32[]{:S(2)}) async-start(), calls=%async_computation.20 | async-start | bytes 5898240 | tf_op jit(solution)/shard_map/reduce_scatter | solution.py:163
  367.4 159.6 %all-gather.30.cloned.1.call-start = ((), (), s32[]{:S(2)}) async-start(), calls=%async_computation.23 | async-start | bytes 7962624 | tf_op jit(solution)/shard_map/all_gather | solution.py:103
  368.2 183.1 %all-gather.26.cloned.1.call-start = ((), (), s32[]{:S(2)}) async-start(), calls=%async_computation.21 | async-start | bytes 2949120 | tf_op jit(solution)/shard_map/all_gather | solution.py:168
  420.8 241.5 %all-gather.28.cloned.1.call-start = ((), (), s32[]{:S(2)}) async-start(), calls=%async_computation.22 | async-start | bytes 7962624 | tf_op jit(solution)/shard_map/all_gather | solution.py:102
  421.5 265.1 %all-gather.38.cloned.1.call-start = ((), (), s32[]{:S(2)}) async-start(), calls=%async_computation.30 | async-start | bytes 2949120 | tf_op jit(solution)/shard_map/all_gather | solution.py:177
  422.8 374.8 %all-gather.32.cloned.1.call-start = ((), (), s32[]{:S(2)}) async-start(), calls=%async_computation.24 | async-start | bytes 7962624 | tf_op jit(solution)/shard_map/all_gather | solution.py:104
  423.5 445.1 %reduce-scatter.24.cloned.1.call-start = ((), (), s32[]{:S(2)}) async-start(), calls=%async_computation.31 | async-start | bytes 5898240 | tf_op jit(solution)/shard_map/reduce_scatter | solution.py:188
  872.3 125.8 %reduce-scatter.28.cloned.1.call-start = ((), (), s32[]{:S(2)}) async-start(), calls=%async_computation.35 | async-start | bytes 5898240 | tf_op jit(solution)/shard_map/reduce_scatter | solution.py:188
  960.3 116.3 %all-gather.44.cloned.1.call-start = ((), (), s32[]{:S(2)}) async-start(), calls=%async_computation.36 | async-start | bytes 2949120 | tf_op jit(solution)/shard_map/all_gather | solution.py:191
  1054.0 317.1 %reduce-scatter.30.cloned.1.call-start = ((), (), s32[]{:S(2)}) async-start(), calls=%async_computation.37 | async-start | bytes 5898240 | tf_op jit(solution)/shard_map/reduce_scatter | solution.py:245
  1087.5 135.2 %collective-permute-start.7 = (f32[512,9,64]{0,2,1:T(8,128)}, f32[512,9,64]{0,2,1:T(8,128)}, u32[]{:S(2)}, u32[]{:S(2)}) collective-permute-start(f32[512,9,64]{0,2,1:T(8,128)} %slice.103), channel_id=1, source_target_pairs={{4,0},{5,1},{6,2},{7,3},{12,8},{13,9},{14,10},{15,11},{20,16},{21,... | collective-permute-start | bytes 3538952 | tf_op jit(solution)/shard_map/ppermute | solution.py:18
  1233.7 137.4 %reduce-scatter.26.cloned.1.call-start = ((), (), s32[]{:S(2)}) async-start(), calls=%async_computation.33 | async-start | bytes 5898240 | tf_op jit(solution)/shard_map/reduce_scatter | solution.py:245
  1278.5 141.2 %reduce-scatter.18.cloned.1.call-start = ((), (), s32[]{:S(2)}) async-start(), calls=%async_computation.25 | async-start | bytes 5898240 | tf_op jit(solution)/shard_map/reduce_scatter | solution.py:173
  1288.6 210.1 %reduce-scatter.38.cloned.1.call-start = ((), (), s32[]{:S(2)}) async-start(), calls=%async_computation.41 | async-start | bytes 6635520 | tf_op jit(solution)/shard_map/reduce_scatter | solution.py:76
  1298.5 316.1 %reduce-scatter.36.cloned.1.call-start = ((), (), s32[]{:S(2)}) async-start(), calls=%async_computation.40 | async-start | bytes 6635520 | tf_op jit(solution)/shard_map/reduce_scatter | solution.py:75
  1306.9 423.5 %reduce-scatter.34.cloned.1.call-start = ((), (), s32[]{:S(2)}) async-start(), calls=%async_computation.39 | async-start | bytes 6635520 | tf_op jit(solution)/shard_map/reduce_scatter | solution.py:74
  1316.2 529.9 %reduce-scatter.32.cloned.1.call-start = ((), (), s32[]{:S(2)}) async-start(), calls=%async_computation.38 | async-start | bytes 6635520 | tf_op jit(solution)/shard_map/reduce_scatter | solution.py:73
  1325.5 753.8 %reduce-scatter.44.cloned.1.call-start = ((), (), s32[]{:S(2)}) async-start(), calls=%async_computation.44 | async-start | bytes 15925248 | tf_op jit(solution)/shard_map/reduce_scatter | solution.py:79
  1341.8 970.2 %reduce-scatter.42.cloned.1.call-start = ((), (), s32[]{:S(2)}) async-start(), calls=%async_computation.43 | async-start | bytes 15925248 | tf_op jit(solution)/shard_map/reduce_scatter | solution.py:78
  1356.4 1187.9 %reduce-scatter.40.cloned.1.call-start = ((), (), s32[]{:S(2)}) async-start(), calls=%async_computation.42 | async-start | bytes 15925248 | tf_op jit(solution)/shard_map/reduce_scatter | solution.py:77
  (136 other events, 4297.4 us)
Sparse Core Ops, SparseCore 0:
  13.4 26.7 all-gather.33
  42.4 58.3 all-gather.21
  103.0 56.9 all-gather.19
  186.8 60.2 all-gather.17
  249.1 59.7 all-gather.23
  315.3 46.4 reduce-scatter.15
  367.5 48.3 reduce-scatter.19
  418.2 108.7 all-gather.29
  553.5 108.7 all-gather.27
  688.8 108.7 all-gather.31
  822.6 46.0 reduce-scatter.23
  950.3 47.8 reduce-scatter.27
  1000.5 47.8 reduce-scatter.21
  1052.5 24.0 all-gather.43
  1233.9 46.9 reduce-scatter.29
  1283.4 47.8 reduce-scatter.25
  1334.0 47.8 reduce-scatter.17
  1385.9 112.6 reduce-scatter.37
  1502.9 111.6 reduce-scatter.35
  1618.7 111.6 reduce-scatter.33
  1734.4 111.6 reduce-scatter.31
  1850.3 229.0 reduce-scatter.43
  2083.6 228.3 reduce-scatter.41
  2316.0 228.2 reduce-scatter.39
  (6 shorter events, 139.1 us)
where the time goes:
time: 2560 us; the launch traced here: 2550 us
  waiting for transfers between devices  1980 us (77%)
  matrix products  355 us (14%)
  other arithmetic  112 us (4%)
  blocking collectives  41.4 us (2%)
    reduce_scatter x1, waiting for transfers between devices, owner_shares(): lax.psum_scatter(gradients[6], ('fsdp', 'cp'), scatter_dimension=1, tiled...  233 us
    reduce_scatter x1, waiting for transfers between devices, owner_shares(): lax.psum_scatter(gradients[5], ('fsdp', 'cp'), scatter_dimension=0, tiled...  233 us
    reduce_scatter x1, waiting for transfers between devices, owner_shares(): lax.psum_scatter(gradients[4], ('fsdp', 'cp'), scatter_dimension=0, tiled...  232 us
    reduce_scatter x1, waiting for transfers between devices, owner_shares(): lax.psum_scatter(gradients[2], ('fsdp', 'cp'), scatter_dimension=0, tiled...  116 us
    reduce_scatter x1, waiting for transfers between devices, owner_shares(): lax.psum_scatter(gradients[1], ('fsdp', 'cp'), scatter_dimension=0, tiled...  116 us
    reduce_scatter x1, waiting for transfers between devices, owner_shares(): lax.psum_scatter(gradients[0], ('fsdp', 'cp'), scatter_dimension=0, tiled...  116 us
    all_gather x1, waiting for transfers between devices, on_device(): lax.all_gather(down_weight, ('fsdp', 'cp'), axis=1, tiled=True)  111 us
    all_gather x1, waiting for transfers between devices, on_device(): lax.all_gather(up_weight, ('fsdp', 'cp'), axis=0, tiled=True)  103 us
  transfers between devices with their start and end apart: 38, of which 28 were waited for; matrix products, arithmetic and copies ran while one was open for 15% of the time, Pallas kernels for 0%

commit v1 on v0

v1 whole, which is shorter than its diff:
```python
import functools
import math

import jax
import jax.numpy as jnp
import numpy as np
from jax import lax
from jax.experimental import pallas as pl
from jax.experimental.pallas import tpu as pltpu
from jax.sharding import PartitionSpec as P

HD = 64
EPSILON = 1e-05
BRANCH = 1.4 / math.sqrt(40.0)
BF = jnp.bfloat16
F32 = jnp.float32
TILE = 128
QUERY_ROWS = 256


def turned(values, cosine, sine):
    lane = lax.broadcasted_iota(jnp.int32, values.shape, 1)
    partner = jnp.where(
        lane % HD < HD // 2,
        pltpu.roll(values, TILE - HD // 2, 1),
        pltpu.roll(values, HD // 2, 1),
    )
    return values * cosine + partner * sine


def row_blocks(seq, sets, local):
    lanes = seq // sets // local
    return [
        ((t * sets + h) * local, (h * lanes + t) * local)
        for t in range(lanes)
        for h in range(sets)
    ]


def key_mask(length, first, rows, columns):
    place = first + lax.broadcasted_iota(jnp.int32, (rows, columns), 0)
    return place < length


def scores_of(keys, queries, length, first_query):
    raw = lax.dot_general(keys, queries, (((1,), (1,)), ((), ())), preferred_element_type=F32)
    key_place = lax.broadcasted_iota(jnp.int32, raw.shape, 0)
    query_place = first_query + lax.broadcasted_iota(jnp.int32, raw.shape, 1)
    return jnp.where((key_place <= query_place) & (key_place < length), raw, -1e30)


def attention_kernel(
    blocks, length_ref, projected, cosine, sine, context, q_heads, k_heads, v_heads, level, kept
):
    heads, seq, _ = q_heads.shape
    local = seq // len(blocks)
    length = length_ref[0]
    for gathered, ordered in blocks:
        source, target = pl.ds(gathered, local), pl.ds(ordered, local)
        for tile in range(-(-3 * heads // 2)):
            width = min(TILE, 3 * heads * HD - tile * TILE)
            values = projected[source, tile * TILE : tile * TILE + width]
            if tile * 2 < 2 * heads:
                values = turned(values, cosine[target, :], sine[target, :])
            for which in range(width // HD):
                index = tile * 2 + which
                piece = values[:, which * HD : (which + 1) * HD]
                if index < heads:
                    q_heads[index, target, :] = (piece * (1.0 / math.sqrt(HD))).astype(BF)
                elif index < 2 * heads:
                    k_heads[index - heads, target, :] = piece.astype(BF)
                else:
                    v_heads[index - 2 * heads, target, :] = piece.astype(BF)

    def one_head(head, carry):
        for first in range(0, seq, QUERY_ROWS):
            most = first + QUERY_ROWS
            queries = q_heads[head, first:most, :]
            keys = k_heads[head, :most, :]
            values = v_heads[head, :most, :]
            scores = scores_of(keys, queries, length, first)
            top = jnp.max(scores, axis=0, keepdims=True)
            exponent = jnp.exp(scores - top)
            total = jnp.sum(exponent, axis=0, keepdims=True)
            probabilities = (exponent * (1.0 / total)).astype(BF)
            level[head, :, first:most] = top + jnp.log(total)
            mixed = lax.dot_general(
                values, probabilities, (((0,), (0,)), ((), ())), preferred_element_type=F32
            )
            kept[head, first:most, :] = mixed.T.astype(BF)
        return carry

    lax.fori_loop(0, heads, one_head, 0)
    for gathered, ordered in blocks:
        source, target = pl.ds(ordered, local), pl.ds(gathered, local)
        for head in range(0, heads, 2):
            parts = [kept[index, source, :] for index in range(head, min(head + 2, heads))]
            joined = parts[0] if len(parts) == 1 else jnp.concatenate(parts, axis=1)
            context[target, head * HD : head * HD + joined.shape[1]] = joined


def attention(blocks, heads, length, projected, cosine, sine):
    seq = projected.shape[0]
    per_head = jax.ShapeDtypeStruct((heads, seq, HD), BF)
    vmem = pl.BlockSpec(memory_space=pltpu.VMEM)
    return pl.pallas_call(
        functools.partial(attention_kernel, blocks),
        out_shape=(
            jax.ShapeDtypeStruct((seq, heads * HD), BF),
            per_head,
            per_head,
            per_head,
            jax.ShapeDtypeStruct((heads, 1, seq), F32),
        ),
        in_specs=[pl.BlockSpec(memory_space=pltpu.SMEM), vmem, vmem, vmem],
        out_specs=(vmem,) * 5,
        scratch_shapes=[pltpu.VMEM((heads, seq, HD), BF)],
        compiler_params=pltpu.CompilerParams(vmem_limit_bytes=48 << 20),
        cost_estimate=pl.CostEstimate(
            flops=4 * heads * seq * seq * HD, transcendentals=heads * seq * seq, bytes_accessed=20 << 20
        ),
    )(length, projected, cosine, sine)


def attention_back_kernel(
    blocks, length_ref, grad_context, q_heads, k_heads, v_heads, level, cosine, sine,
    grad_projected, g_heads, dq, dk, dv,
):
    heads, seq, _ = q_heads.shape
    local = seq // len(blocks)
    length = length_ref[0]
    for gathered, ordered in blocks:
        source, target = pl.ds(gathered, local), pl.ds(ordered, local)
        for head in range(heads):
            g_heads[head, target, :] = grad_context[source, head * HD : (head + 1) * HD]

    def one_head(head, carry):
        keys_turned = k_heads[head].T
        for first in reversed(range(0, seq, QUERY_ROWS)):
            most = first + QUERY_ROWS
            queries = q_heads[head, first:most, :]
            upstream = g_heads[head, first:most, :]
            keys = k_heads[head, :most, :]
            values = v_heads[head, :most, :]
            scores = scores_of(keys, queries, length, first)
            probabilities = jnp.exp(scores - level[head, :, first:most])
            grad_probabilities = lax.dot_general(
                values, upstream, (((1,), (1,)), ((), ())), preferred_element_type=F32
            )
            weighted = probabilities * grad_probabilities
            balance = jnp.sum(weighted, axis=0, keepdims=True)
            grad_scores = (weighted - probabilities * balance).astype(BF)
            grad_keys = jnp.dot(grad_scores, queries, preferred_element_type=F32)
            grad_values = jnp.dot(
                probabilities.astype(BF), upstream, preferred_element_type=F32
            )
            if most == seq:
                dk[head, :, :] = grad_keys
                dv[head, :, :] = grad_values
            else:
                dk[head, :most, :] += grad_keys
                dv[head, :most, :] += grad_values
            grad_queries = jnp.dot(
                keys_turned[:, :most], grad_scores, preferred_element_type=F32
            )
            dq[head, first:most, :] = grad_queries.T * (1.0 / math.sqrt(HD))
        return carry

    lax.fori_loop(0, heads, one_head, 0)
    sources = [dq] * heads + [dk] * heads + [dv] * heads
    for gathered, ordered in blocks:
        source, target = pl.ds(ordered, local), pl.ds(gathered, local)
        for tile in range(-(-3 * heads // 2)):
            indices = range(tile * 2, min(tile * 2 + 2, 3 * heads))
            parts = [sources[index][index % heads, source, :] for index in indices]
            joined = parts[0] if len(parts) == 1 else jnp.concatenate(parts, axis=1)
            if tile * 2 < 2 * heads:
                joined = turned(joined, cosine[source, :], -sine[source, :])
            grad_projected[target, tile * TILE : tile * TILE + joined.shape[1]] = joined.astype(BF)


def attention_back(blocks, heads, length, grad_context, q_heads, k_heads, v_heads, level, cosine, sine):
    seq = grad_context.shape[0]
    vmem = pl.BlockSpec(memory_space=pltpu.VMEM)
    return pl.pallas_call(
        functools.partial(attention_back_kernel, blocks),
        out_shape=jax.ShapeDtypeStruct((seq, 3 * heads * HD), BF),
        in_specs=[pl.BlockSpec(memory_space=pltpu.SMEM)] + [vmem] * 7,
        out_specs=vmem,
        scratch_shapes=[
            pltpu.VMEM((heads, seq, HD), BF),
            pltpu.VMEM((heads, seq, HD), F32),
            pltpu.VMEM((heads, seq, HD), F32),
            pltpu.VMEM((heads, seq, HD), F32),
        ],
        compiler_params=pltpu.CompilerParams(vmem_limit_bytes=56 << 20),
        cost_estimate=pl.CostEstimate(
            flops=10 * heads * seq * seq * HD, transcendentals=heads * seq * seq, bytes_accessed=20 << 20
        ),
    )(length, grad_context, q_heads, k_heads, v_heads, level, cosine, sine)


def tables(seq):
    frequency = jnp.power(10000.0, -2.0 * jnp.arange(HD // 2, dtype=F32) / HD)
    angle = jnp.arange(seq, dtype=F32)[:, None] * frequency[None, :]
    cosine, sine = jnp.cos(angle), jnp.sin(angle)
    return jnp.tile(cosine, (1, 4)), jnp.concatenate([-sine, sine, -sine, sine], axis=1)


MESH = pl.DeviceIdType.MESH


def greet(count):
    barrier = pltpu.get_barrier_semaphore()
    z, c, t = lax.axis_index("fsdp"), lax.axis_index("cp"), lax.axis_index("tp")

    def hello(**place):
        pl.semaphore_signal(barrier, inc=1, device_id=place, device_id_type=MESH)

    hello(cp=1 - c)
    hello(tp=t + 1 - 2 * (t % 2))
    hello(tp=(t + 2) % 4)
    pl.when(z > 0)(lambda: hello(fsdp=z - 1))
    pl.when(z < count - 1)(lambda: hello(fsdp=z + 1))
    peers = 3 + jnp.minimum(z, 1) + jnp.minimum(count - 1 - z, 1)
    pl.semaphore_wait(barrier, peers)


class Mail:
    def __init__(self, send, recv):
        self.send, self.recv, self.used, self.open = send, recv, 0, []

    def slot(self):
        self.used += 1
        return self.used - 1

    def copy(self, slot, source, target, **place):
        return pltpu.make_async_remote_copy(
            src_ref=source,
            dst_ref=target,
            send_sem=self.send.at[slot],
            recv_sem=self.recv.at[slot],
            device_id=place,
            device_id_type=MESH,
        )

    def start(self, slot, source, target, when=None, **place):
        made = self.copy(slot, source, target, **place)
        if when is None:
            made.start()
        else:
            pl.when(when)(made.start)
        self.open.append((made, when))

    def arrive(self, slot, target, when=None, **place):
        made = self.copy(slot, target, target, **place)
        if when is None:
            made.wait_recv()
        else:
            pl.when(when)(made.wait_recv)

    def finish(self):
        for made, when in self.open:
            if when is None:
                made.wait_send()
            else:
                pl.when(when)(made.wait_send)


class Line:
    def __init__(self, mail, count, own, at, low=None, high=None):
        self.mail, self.count, self.own, self.at = mail, count, own, at
        self.low, self.high = low, high
        self.z = lax.axis_index("fsdp")
        self.up = [mail.slot() for _ in range(count)]
        self.down = [mail.slot() for _ in range(count)]

    def has_low(self, hop):
        return self.z >= hop

    def has_high(self, hop):
        return self.z <= self.count - 1 - hop

    def send(self, hop):
        z, count, mail = self.z, self.count, self.mail
        low, high = jnp.maximum(z - hop + 1, 0), jnp.minimum(z + hop - 1, count - 1)
        from_low = from_high = self.own
        if hop > 1:
            ready = hop == 2 and self.low is not None
            from_low = self.low if ready else self.at(low)
            from_high = self.high if ready else self.at(high)
        mail.start(
            self.up[hop], from_low, self.at(low),
            when=(z >= hop - 1) & (z < count - 1), fsdp=jnp.minimum(z + 1, count - 1),
        )
        mail.start(
            self.down[hop], from_high, self.at(high),
            when=(z <= count - hop) & (z > 0), fsdp=jnp.maximum(z - 1, 0),
        )

    def arrive(self, hop):
        z, count = self.z, self.count
        self.mail.arrive(
            self.up[hop], self.at(jnp.maximum(z - hop, 0)), when=self.has_low(hop), fsdp=z
        )
        self.mail.arrive(
            self.down[hop], self.at(jnp.minimum(z + hop, count - 1)), when=self.has_high(hop), fsdp=z
        )


class Across:
    def __init__(self, line, own, mine_at, other_at):
        self.line, self.own, self.mine_at, self.other_at = line, own, mine_at, other_at
        self.c = lax.axis_index("cp")
        self.low = [line.mail.slot() for _ in range(line.count)]
        self.high = [line.mail.slot() for _ in range(line.count)]

    def send(self, hop):
        line, mail = self.line, self.line.mail
        z, count, other = line.z, line.count, 1 - self.c
        if hop == 0:
            mail.start(self.low[0], self.own, self.mine_at(z), cp=other)
            return
        low, high = jnp.maximum(z - hop, 0), jnp.minimum(z + hop, count - 1)
        mail.start(self.low[hop], self.mine_at(low), self.mine_at(low), when=line.has_low(hop), cp=other)
        mail.start(self.high[hop], self.mine_at(high), self.mine_at(high), when=line.has_high(hop), cp=other)

    def arrive(self, hop):
        line, mail = self.line, self.line.mail
        z, count, other = line.z, line.count, 1 - self.c
        if hop == 0:
            mail.arrive(self.low[0], self.other_at(z), cp=other)
            return
        low, high = jnp.maximum(z - hop, 0), jnp.minimum(z + hop, count - 1)
        mail.arrive(self.low[hop], self.other_at(low), when=line.has_low(hop), cp=other)
        mail.arrive(self.high[hop], self.other_at(high), when=line.has_high(hop), cp=other)


def first_gather_kernel(
    count, normed, qkv, turned_out, wide, normed_full, qkv_full, out_half, low, high,
    send, recv, local,
):
    z, c, t = lax.axis_index("fsdp"), lax.axis_index("cp"), lax.axis_index("tp")
    beside, yonder = t + 1 - 2 * (t % 2), (t + 2) % 4
    mail = Mail(send, recv)
    greet(count)
    kept = [
        pltpu.make_async_copy(qkv, qkv_full.at[z, c], local.at[0]),
        pltpu.make_async_copy(turned_out, out_half.at[z], local.at[1]),
        pltpu.make_async_copy(normed.at[c], normed_full.at[t, c], local.at[2]),
    ]
    for copy in kept:
        copy.start()

    heads = Line(mail, count, qkv, lambda j: qkv_full.at[j, c])
    heads_across = Across(
        heads, qkv, lambda j: qkv_full.at[j, c], lambda j: qkv_full.at[j, 1 - c]
    )
    outs = Line(mail, count, turned_out, lambda j: out_half.at[j])
    wide_up, wide_down = mail.slot(), mail.slot()
    rows_x = mail.slot()
    rows_y = [mail.slot() for _ in range(2)]
    rows_core = [mail.slot() for _ in range(4)]

    mail.start(rows_x, normed.at[1 - c], normed_full.at[t, c], cp=1 - c)
    heads.send(1)
    heads_across.send(0)
    mail.start(rows_y[0], normed.at[c], normed_full.at[t, c], tp=yonder)
    mail.start(rows_core[0], normed.at[c], normed_full.at[t, c], tp=beside)
    mail.arrive(rows_x, normed_full.at[t, 1 - c], cp=1 - c)
    mail.start(rows_y[1], normed_full.at[t, 1 - c], normed_full.at[t, 1 - c], tp=yonder)
    mail.start(rows_core[1], normed_full.at[t, 1 - c], normed_full.at[t, 1 - c], tp=beside)

    def rows_on(k, half):
        mail.arrive(rows_y[k], normed_full.at[yonder, half], tp=yonder)
        mail.start(
            rows_core[2 + k], normed_full.at[yonder, half], normed_full.at[yonder, half], tp=beside
        )

    for hop in range(1, count):
        heads.arrive(hop)
        if hop + 1 < count:
            heads.send(hop + 1)
        if hop > 1:
            outs.arrive(hop - 1)
        outs.send(hop)
        heads_across.send(hop)
        if hop == 1:
            rows_on(0, c)
            rows_on(1, 1 - c)
    mail.start(wide_up, wide, low, when=z < count - 1, fsdp=jnp.minimum(z + 1, count - 1))
    mail.start(wide_down, wide, high, when=z > 0, fsdp=jnp.maximum(z - 1, 0))
    if count > 1:
        outs.arrive(count - 1)
    for hop in range(count):
        heads_across.arrive(hop)
    mail.arrive(rows_core[0], normed_full.at[beside, c], tp=beside)
    mail.arrive(rows_core[1], normed_full.at[beside, 1 - c], tp=beside)
    far = (beside + 2) % 4
    mail.arrive(rows_core[2], normed_full.at[far, c], tp=beside)
    mail.arrive(rows_core[3], normed_full.at[far, 1 - c], tp=beside)
    mail.arrive(wide_up, low, when=z > 0, fsdp=z)
    mail.arrive(wide_down, high, when=z < count - 1, fsdp=z)
    for copy in kept:
        copy.wait()
    mail.finish()


def first_gather(count, normed, qkv, turned_out, wide):
    slots = 6 * count + 9
    anywhere = pl.BlockSpec(memory_space=pl.ANY)
    share = qkv.shape[0]
    return pl.pallas_call(
        functools.partial(first_gather_kernel, count),
        out_shape=(
            jax.ShapeDtypeStruct((4,) + normed.shape, BF),
            jax.ShapeDtypeStruct((count, 2) + qkv.shape, BF),
            jax.ShapeDtypeStruct((count,) + turned_out.shape, BF),
            jax.ShapeDtypeStruct(wide.shape, BF),
            jax.ShapeDtypeStruct(wide.shape, BF),
        ),
        in_specs=[anywhere] * 4,
        out_specs=(anywhere,) * 5,
        scratch_shapes=[
            pltpu.SemaphoreType.DMA((slots,)),
            pltpu.SemaphoreType.DMA((slots,)),
            pltpu.SemaphoreType.DMA((3,)),
        ],
        compiler_params=pltpu.CompilerParams(collective_id=1, has_side_effects=True),
    )(normed, qkv, turned_out, wide)


def in_pieces(rows, body, size=16):
    lax.fori_loop(0, rows // size, lambda i, carry: (body(pl.ds(i * size, size)), carry)[1], 0)


class Spread:
    def __init__(self, mail, own, at):
        self.mail, self.own, self.at = mail, own, at
        self.c, self.t = lax.axis_index("cp"), lax.axis_index("tp")
        self.beside, self.yonder = self.t + 1 - 2 * (self.t % 2), (self.t + 2) % 4
        self.x = [mail.slot() for _ in range(3)]
        self.y = [mail.slot() for _ in range(3)]
        self.core = {}

    def to_core(self, c_is_own, t_is_own, piece):
        slot = self.core[c_is_own, t_is_own, piece] = self.mail.slot()
        c = self.c if c_is_own else 1 - self.c
        t = self.t if t_is_own else self.yonder
        source = self.own(piece) if c_is_own and t_is_own else self.at(c, t, piece)
        self.mail.start(slot, source, self.at(c, t, piece), tp=self.beside)

    def begin(self, piece):
        c, t = self.c, self.t
        if piece == 0:
            self.mail.start(self.x[0], self.own(0), self.at(c, t, 0), cp=1 - c)
        else:
            self.mail.start(self.y[0], self.own(1), self.at(c, t, 1), tp=self.yonder)
            self.mail.start(self.x[1], self.own(1), self.at(c, t, 1), cp=1 - c)
            self.mail.start(self.y[1], self.own(0), self.at(c, t, 0), tp=self.yonder)
        self.to_core(True, True, piece)

    def turn(self):
        c, t, mail, yonder = self.c, self.t, self.mail, self.yonder
        mail.arrive(self.x[0], self.at(1 - c, t, 0), cp=1 - c)
        mail.start(self.y[2], self.at(1 - c, t, 0), self.at(1 - c, t, 0), tp=yonder)
        self.to_core(False, True, 0)
        mail.arrive(self.y[0], self.at(c, yonder, 1), tp=yonder)
        mail.start(self.x[2], self.at(c, yonder, 1), self.at(c, yonder, 1), cp=1 - c)
        self.to_core(True, False, 1)

    def end(self):
        c, t, mail, yonder = self.c, self.t, self.mail, self.yonder
        mail.arrive(self.x[1], self.at(1 - c, t, 1), cp=1 - c)
        self.to_core(False, True, 1)
        mail.arrive(self.y[1], self.at(c, yonder, 0), tp=yonder)
        self.to_core(True, False, 0)
        mail.arrive(self.x[2], self.at(1 - c, yonder, 1), cp=1 - c)
        self.to_core(False, False, 1)
        mail.arrive(self.y[2], self.at(1 - c, yonder, 0), tp=yonder)
        self.to_core(False, False, 0)
        far = (self.beside + 2) % 4
        for (c_is_own, t_is_own, piece), slot in self.core.items():
            place = self.at(
                c if c_is_own else 1 - c, self.beside if t_is_own else far, piece
            )
            mail.arrive(slot, place, tp=self.beside)


def second_gather_kernel(
    count, part, tokens, gain, wide, wide_low, wide_high, wide_other,
    middle, normed_full, wide_full,
    own, from_core, to_yonder, from_yonder, normed,
    send, recv, local,
):
    z, c, t = lax.axis_index("fsdp"), lax.axis_index("cp"), lax.axis_index("tp")
    beside, yonder = t + 1 - 2 * (t % 2), (t + 2) % 4
    far = (beside + 2) % 4
    rows = tokens.shape[0]
    half = rows // 2
    mail = Mail(send, recv)
    greet(count)

    mine = Line(mail, count, None, lambda j: wide_full.at[:, j, c], wide_low, wide_high)
    other = Line(mail, count, wide_other, lambda j: wide_full.at[:, j, 1 - c])
    core = [mail.slot() for _ in range(2)]
    across = [mail.slot() for _ in range(2)]
    spread = Spread(
        mail, lambda piece: normed.at[piece], lambda c, t, piece: normed_full.at[c, t, piece]
    )

    mail.start(core[1], part.at[far], from_core.at[1], tp=beside)
    mail.start(core[0], part.at[beside], from_core.at[0], tp=beside)
    kept = [
        (pltpu.make_async_copy(part.at[yonder], own.at[1], local.at[0]), None),
        (pltpu.make_async_copy(part.at[t], own.at[0], local.at[1]), None),
        (pltpu.make_async_copy(wide, wide_full.at[:, z, c], local.at[2]), None),
        (pltpu.make_async_copy(wide_other, wide_full.at[:, z, 1 - c], local.at[3]), None),
        (
            pltpu.make_async_copy(
                wide_low, wide_full.at[:, jnp.maximum(z - 1, 0), c], local.at[4]
            ),
            z > 0,
        ),
        (
            pltpu.make_async_copy(
                wide_high, wide_full.at[:, jnp.minimum(z + 1, count - 1), c], local.at[5]
            ),
            z < count - 1,
        ),
    ]
    for copy, when in kept:
        copy.start() if when is None else pl.when(when)(copy.start)
    if count > 2:
        mine.send(2)
    if count > 1:
        other.send(1)

    kept[0][0].wait()
    mail.arrive(core[1], from_core.at[1], tp=beside)
    for piece in range(2):

        def add(place, piece=piece):
            place = pl.ds(place.start + piece * half, place.size)
            to_yonder[place, :] = (
                own[1, place, :].astype(F32) + from_core[1, place, :].astype(F32)
            ).astype(BF)

        in_pieces(half, add)
        block = pl.ds(piece * half, half)
        mail.start(across[piece], to_yonder.at[block], from_yonder.at[block], tp=yonder)

    kept[1][0].wait()
    mail.arrive(core[0], from_core.at[0], tp=beside)
    for piece in range(2):
        block = pl.ds(piece * half, half)
        mail.arrive(across[piece], from_yonder.at[block], tp=yonder)

        def norm(place, piece=piece):
            row = pl.ds(place.start + piece * half, place.size)
            attended = (
                own[0, row, :].astype(F32)
                + from_core[0, row, :].astype(F32)
                + from_yonder[row, :].astype(F32)
            )
            values = tokens[row, :].astype(F32) + BRANCH * attended
            middle[row, :] = values
            normed[piece, place, :] = (normalize(values) * gain[...]).astype(BF)

        in_pieces(half, norm)
        spread.begin(piece)
    keep_normed = pltpu.make_async_copy(normed, normed_full.at[c, t], local.at[0])
    keep_normed.start()
    spread.turn()

    for hop in range(1, count):
        if hop + 1 < count:
            mine.arrive(hop + 1)
            if hop + 2 < count:
                mine.send(hop + 2)
        other.arrive(hop)
        if hop + 1 < count:
            other.send(hop + 1)
        if hop == 1:
            spread.end()
    if count == 1:
        spread.end()
    keep_normed.wait()
    for copy, when in kept[2:]:
        copy.wait() if when is None else pl.when(when)(copy.wait)
    mail.finish()


def second_gather(count, part, tokens, gain, wide, wide_low, wide_high, wide_other):
    slots = 4 * count + 20
    rows, width = tokens.shape
    anywhere = pl.BlockSpec(memory_space=pl.ANY)
    vmem = pl.BlockSpec(memory_space=pltpu.VMEM)
    return pl.pallas_call(
        functools.partial(second_gather_kernel, count),
        out_shape=(
            jax.ShapeDtypeStruct((rows, width), F32),
            jax.ShapeDtypeStruct((2, 4, 2, rows // 2, width), BF),
            jax.ShapeDtypeStruct((3, count, 2) + wide.shape[1:], BF),
        ),
        in_specs=[anywhere, vmem, vmem] + [anywhere] * 4,
        out_specs=(vmem, anywhere, anywhere),
        scratch_shapes=[
            pltpu.VMEM((2, rows, width), BF),
            pltpu.VMEM((2, rows, width), BF),
            pltpu.VMEM((rows, width), BF),
            pltpu.VMEM((rows, width), BF),
            pltpu.VMEM((2, rows // 2, width), BF),
            pltpu.SemaphoreType.DMA((slots,)),
            pltpu.SemaphoreType.DMA((slots,)),
            pltpu.SemaphoreType.DMA((6,)),
        ],
        compiler_params=pltpu.CompilerParams(
            collective_id=2, has_side_effects=True, vmem_limit_bytes=40 << 20
        ),
    )(part, tokens, gain, wide, wide_low, wide_high, wide_other)


def normalize(values):
    return values * lax.rsqrt(jnp.mean(values * values, axis=-1, keepdims=True) + EPSILON)


def scaled_norm(values, gain_values):
    return normalize(values) * gain_values


def silu_product(gate_pre, up_pre):
    return gate_pre / (1.0 + jnp.exp(-gate_pre)) * up_pre


def matmul(left, right):
    return jnp.dot(left, right, preferred_element_type=F32)


def rows_inner(left, right):
    return lax.dot_general(left, right, (((0,), (0,)), ((), ())), preferred_element_type=F32)


def cols_inner(left, right):
    return lax.dot_general(left, right, (((1,), (1,)), ((), ())), preferred_element_type=F32)


def after(value, *earlier):
    return lax.optimization_barrier((value, *earlier))[0]


def swap(value):
    return lax.ppermute(value, "cp", [(0, 1), (1, 0)])


def in_order(place, mine, other, axis):
    return jnp.where(
        place == 0,
        jnp.concatenate([mine, other], axis=axis),
        jnp.concatenate([other, mine], axis=axis),
    )


def gather_line(block, gates=None):
    count = lax.axis_size("fsdp")
    z = lax.axis_index("fsdp")
    from_low, from_high = [], []
    low = high = block
    for step in range(1, count):
        if gates is not None and step - 1 < len(gates):
            low, high = after((low, high), *gates[step - 1])
        low = lax.ppermute(low, "fsdp", [(i, i + 1) for i in range(step - 1, count - 1)])
        high = lax.ppermute(high, "fsdp", [(i, i - 1) for i in range(1, count - step + 1)])
        from_low.append(low)
        from_high.append(high)
    blocks = [block]
    for step in range(1, count):
        blocks.append(jnp.where(z >= step, from_low[step - 1], from_high[count - step - 1]))
    return blocks, list(zip(from_low, from_high))


def placed(blocks, axis=0):
    count = lax.axis_size("fsdp")
    z = lax.axis_index("fsdp")
    rows = blocks[0].shape[axis]
    shape = list(blocks[0].shape)
    shape[axis] = rows * count
    full = jnp.zeros(shape, blocks[0].dtype)
    for step, block in enumerate(blocks):
        start = lax.rem(z - step + count, count) * rows
        full = lax.dynamic_update_slice_in_dim(full, block, start, axis)
    return full


def reduce_line(part):
    count = lax.axis_size("fsdp")
    z = lax.axis_index("fsdp")
    low = high = None
    for step in range(1, count):
        up_part = part(jnp.clip(z + count - step, 0, count - 1))
        down_part = part(jnp.clip(z - count + step, 0, count - 1))
        if low is not None:
            up_part = (up_part.astype(F32) + low.astype(F32)).astype(BF)
            down_part = (down_part.astype(F32) + high.astype(F32)).astype(BF)
        low = lax.ppermute(up_part, "fsdp", [(i, i + 1) for i in range(0, step)])
        high = lax.ppermute(down_part, "fsdp", [(i, i - 1) for i in range(count - step, count)])
    total = part(z).astype(F32)
    if low is not None:
        total = total + low.astype(F32) + high.astype(F32)
    return total


def farthest_first(count):
    return np.array(
        [sorted(range(count), key=lambda j: (-abs(j - z), j)) for z in range(count)], np.int32
    )


def on_device(
    tokens,
    seq_lengths,
    attention_gain,
    query_weight,
    key_weight,
    value_weight,
    out_weight,
    feedforward_gain,
    gate_weight,
    up_weight,
    down_weight,
    cotangent,
):
    c = lax.axis_index("cp")
    z = lax.axis_index("fsdp")
    sets = lax.axis_size("cp")
    count = lax.axis_size("fsdp")
    lanes = lax.axis_size("tp")
    slots, local, width = tokens.shape
    share = query_weight.shape[0]
    heads_width = query_weight.shape[1]
    head_count = heads_width // HD
    hidden_width = gate_weight.shape[1] // sets
    rows = sets * local
    seq = rows * lanes
    blocks = row_blocks(seq, sets, local)
    everyone = ("cp", "tp")

    def pick(value, which, axis=0):
        return lax.dynamic_index_in_dim(value, which, axis, keepdims=False)

    def to_sequence(value):
        mine = pick(value, c)
        other = swap(pick(value, 1 - c))
        return in_order(c, mine, other, 0)

    def from_sequence(value):
        value = value.reshape(sets, local, width)
        mine = pick(value, c)
        other = swap(pick(value, 1 - c))
        return in_order(c, mine[None], other[None], 0)

    token_rows = to_sequence(tokens)
    inputs = token_rows.astype(F32)
    upstream = to_sequence(cotangent).astype(F32)
    length = pick(seq_lengths, c)[None]
    gain_one = attention_gain.astype(F32)
    gain_two = feedforward_gain.astype(F32)

    def normed_rows(values):
        return (normalize(values.astype(F32)) * gain_one).astype(BF)

    qkv = jnp.concatenate([query_weight, key_weight, value_weight], axis=1)
    wide = jnp.stack([gate_weight, up_weight, down_weight.T]).reshape(3, share, sets, hidden_width)
    own_wide = pick(wide, c, 2)
    normed_one, full_qkv, out_half, wide_low, wide_high = first_gather(
        count, normed_rows(tokens), qkv, out_weight.T, own_wide
    )
    normed_one = normed_one.reshape(seq, width)
    full_qkv = full_qkv.reshape(width, 3 * heads_width)
    out_other, wide_other = after((out_half, pick(wide, 1 - c, 2)), full_qkv)
    wide_other = swap(wide_other)
    full_out = in_order(c, out_half[:, None], swap(out_other)[:, None], 1)
    full_out = full_out.reshape(width, heads_width)

    cosine_table, sine_table = tables(seq)
    projected = matmul(normed_one, full_qkv)
    context, q_heads, k_heads, v_heads, level = attention(
        blocks, head_count, length, projected, cosine_table, sine_table
    )
    part = cols_inner(context, full_out).astype(BF)

    middle, normed_two, full_wide = second_gather(
        count, part.reshape(lanes, rows, width), token_rows, gain_two[None], own_wide,
        wide_low, wide_high, wide_other,
    )
    normed_two = normed_two.reshape(sets * seq, width)
    full_gate, full_up, full_down = full_wide.reshape(3, width, hidden_width)
    _, norm_two_back = jax.vjp(scaled_norm, middle, gain_two)
    _, norm_one_back = jax.vjp(scaled_norm, inputs, gain_one)
    grad_branch = lax.all_gather((BRANCH * upstream).astype(BF), everyone, axis=0, tiled=True)
    gate_pre = matmul(normed_two, full_gate)
    up_pre = matmul(normed_two, full_up)
    hidden_exact, silu_back = jax.vjp(silu_product, gate_pre, up_pre)
    hidden = hidden_exact.astype(BF)

    def line_part(gradient):
        pieces = gradient.reshape(count, gradient.shape[0] // count, gradient.shape[1])
        return lambda j: pick(pieces, j)

    def reduced_halves(gradient):
        total = reduce_line(line_part(gradient))
        total = total.reshape(sets, share, hidden_width)
        mine = pick(total, c)
        other = swap(pick(total, 1 - c).astype(BF)).astype(F32)
        return in_order(c, mine, other, 1)

    grad_down = reduced_halves(rows_inner(grad_branch, hidden).astype(BF)).T
    grad_hidden = matmul(grad_branch, full_down)
    grad_gate_exact, grad_up_exact = silu_back(grad_hidden)
    grad_gate_pre = grad_gate_exact.astype(BF)
    grad_up_pre = grad_up_exact.astype(BF)
    grad_normed_two = cols_inner(grad_gate_pre, full_gate) + cols_inner(grad_up_pre, full_up)
    grad_norm_two = lax.psum_scatter(
        grad_normed_two.astype(BF), everyone, scatter_dimension=0, tiled=True
    ).astype(F32)
    grad_gate = reduced_halves(rows_inner(normed_two, grad_gate_pre).astype(BF))
    grad_up = reduced_halves(rows_inner(normed_two, grad_up_pre).astype(BF))

    grad_middle_norm, grad_gain_two = norm_two_back(grad_norm_two)
    grad_middle = upstream + grad_middle_norm
    grad_attention = lax.all_gather((BRANCH * grad_middle).astype(BF), "tp", axis=0, tiled=True)

    feedforward = lax.psum_scatter(
        after(cols_inner(hidden, full_down).astype(BF), grad_attention),
        everyone, scatter_dimension=0, tiled=True,
    )
    output = from_sequence((middle + BRANCH * feedforward.astype(F32)).astype(BF))

    order = jnp.asarray(farthest_first(count))[z]

    def reduced_rows(gradient):
        pieces = gradient.reshape(count, sets, share, gradient.shape[1])
        mine = pick(pieces, c, 1)
        other = pick(pieces, 1 - c, 1)
        summed = []
        for k in range(count):
            got = swap(pick(other, order[k]))
            summed.append((pick(mine, order[k]).astype(F32) + got.astype(F32)).astype(BF))

        def part(j):
            found = summed[0]
            for k in range(1, count):
                found = jnp.where(order[k] == j, summed[k], found)
            return found

        return reduce_line(part)

    grad_out = reduced_rows(rows_inner(grad_attention, context).astype(BF)).T
    grad_context = matmul(grad_attention, full_out).astype(BF)
    grad_projected = attention_back(
        blocks, head_count, length, grad_context, q_heads, k_heads, v_heads, level,
        cosine_table, sine_table,
    )
    grad_qkv = reduced_rows(rows_inner(normed_one, grad_projected).astype(BF))
    grad_norm_one = lax.psum_scatter(
        cols_inner(grad_projected, full_qkv).astype(BF), "tp", scatter_dimension=0, tiled=True
    ).astype(F32)
    grad_inputs_norm, grad_gain_one = norm_one_back(grad_norm_one)
    grad_tokens = from_sequence((grad_middle + grad_inputs_norm).astype(BF))
    gain_sums = lax.psum(jnp.stack([grad_gain_one, grad_gain_two]), ("fsdp", "cp", "tp"))
    return (
        output,
        grad_tokens,
        grad_qkv[:, :heads_width],
        grad_qkv[:, heads_width : 2 * heads_width],
        grad_qkv[:, 2 * heads_width :],
        grad_out,
        gain_sums[0],
        grad_gate,
        grad_up,
        grad_down,
        gain_sums[1],
    )


def solution(mesh):
    in_specs = (
        P("fsdp", ("cp", "tp"), None),
        P("fsdp"),
        P(),
        P(("fsdp", "cp"), "tp"),
        P(("fsdp", "cp"), "tp"),
        P(("fsdp", "cp"), "tp"),
        P("tp", ("fsdp", "cp")),
        P(),
        P(("fsdp", "cp"), "tp"),
        P(("fsdp", "cp"), "tp"),
        P("tp", ("fsdp", "cp")),
        P("fsdp", ("cp", "tp"), None),
    )
    out_specs = (
        P("fsdp", ("cp", "tp"), None),
        P("fsdp", ("cp", "tp"), None),
        P(("fsdp", "cp"), "tp"),
        P(("fsdp", "cp"), "tp"),
        P(("fsdp", "cp"), "tp"),
        P("tp", ("fsdp", "cp")),
        P(),
        P(("fsdp", "cp"), "tp"),
        P(("fsdp", "cp"), "tp"),
        P("tp", ("fsdp", "cp")),
        P(),
    )
    return jax.shard_map(
        on_device, mesh=mesh, in_specs=in_specs, out_specs=out_specs, check_vma=False
    )
```

time: 2560 us -> 1170 us (0.46)
  waiting for transfers between devices: 1980 us -> 269 us
  Pallas kernels: 0 us -> 358 us
  matrix products: 355 us -> 172 us
  starting transfers between devices: 20.9 us -> 115 us
  local copies, waits for them, and re-layouts: 23.7 us -> 79.2 us
  other arithmetic: 112 us -> 77.3 us
    reduce_scatter x15 -> x3, waiting for transfers between devices: 1300 us -> 74.9 us  [the longest x1 74.9 us: on_device(): lax.psum_scatter(grad_normed_two.astype(BF), everyone, scatter_dimension=...]
    all_gather x15 -> x2, waiting for transfers between devices: 638 us -> 37.6 us  [the longest x1 37.6 us: on_device(): lax.all_gather((BRANCH * grad_middle).astype(BF), 'tp', axis=0, tiled=True)]
    pallas_call x0 -> x4, Pallas kernels: none -> 358 us  [the longest x1 146 us: second_gather(): pl.pallas_call(functools.partial(second_gather_kernel, count), out_shape=...]
    dot_general x26 -> x5, matrix products: 201 us -> 61.8 us  [matmul(): return jnp.dot(left, right, preferred_element_type=F32)]
    ppermute x8 -> x47, waiting for transfers between devices: 42.2 us -> 156 us  [the longest x17 108 us: swap(): return lax.ppermute(value, 'cp', [(0, 1), (1, 0)])]
    ppermute x8 -> x47, starting transfers between devices: 17.7 us -> 114 us  [the longest x15 72.5 us: reduce_line(): low = lax.ppermute(up_part, 'fsdp', [(i, i + 1) for i in range(0, step)])]
    reduce_sum x6 -> x0, other arithmetic: 62.7 us -> none  [the longest x2 29.3 us: softmax_rows(): exponent = jnp.exp(scores - row_top)]
    convert_element_type x0 -> x9, local copies, waits for them, and re-layouts: none -> 31.3 us  [the longest x1 11.6 us: on_device(): grad_qkv = reduced_rows(rows_inner(normed_one, grad_projected).astype(BF))]
  transfers between devices with their start and end apart: 38 -> 52, of which waited for: 28 -> 18; matrix products, arithmetic and copies ran while one was open for 15% -> 19% of each run, Pallas kernels for 0% -> 28%
where the time goes in v1:
time: 1170 us; the launch traced here: 1160 us
  Pallas kernels  358 us (31%)
  waiting for transfers between devices  269 us (23%)
  matrix products  172 us (15%)
  starting transfers between devices  115 us (10%)
  local copies, waits for them, and re-layouts  79.2 us (7%)
  other arithmetic  77.3 us (7%)
  blocking collectives  53.4 us (5%)
  between operations  36.7 us (3%)
    pallas_call x1, Pallas kernels, second_gather(): pl.pallas_call(functools.partial(second_gather_kernel, count), out_shape=...  146 us
    pallas_call x1, Pallas kernels, first_gather(): pl.pallas_call(functools.partial(first_gather_kernel, count), out_shape=(...  138 us
    ppermute x17, waiting for transfers between devices, swap(): return lax.ppermute(value, 'cp', [(0, 1), (1, 0)])  108 us
    reduce_scatter x1, waiting for transfers between devices, on_device(): lax.psum_scatter(grad_normed_two.astype(BF), everyone, scatter_dimension=...  74.9 us
    ppermute x15, starting transfers between devices, reduce_line(): low = lax.ppermute(up_part, 'fsdp', [(i, i + 1) for i in range(0, step)])  72.5 us
    dot_general x5, matrix products, matmul(): return jnp.dot(left, right, preferred_element_type=F32)  61.8 us
    dot_general x5, matrix products, cols_inner(): lax.dot_general(left, right, (((1,), (1,)), ((), ())), preferred_element_...  58.4 us
    psum x1, blocking collectives, on_device(): lax.psum(jnp.stack([grad_gain_one, grad_gain_two]), ('fsdp', 'cp', 'tp'))  53.4 us
  transfers between devices with their start and end apart: 52, of which 18 were waited for; matrix products, arithmetic and copies ran while one was open for 19% of the time, Pallas kernels for 28%

profile of v1, /device:TPU:0, one launch (start us, length us, event | category | flops | bytes accessed | tf_op | source)
XLA Modules:
  0.0 1160.3 jit_solution(8766679357512125220)
XLA Ops:
  11.6 13.3 %collective-permute-done.3 = bf16[128,2304]{1,0:T(8,128)(2,1)S(1)} collective-permute-done((bf16[128,2304]{1,0:T(8,128)(2,1)S(1)}, bf16[128,2304]{1,0:T(8,128)(2,1)S(1)}, u32[]{:S(2)}, u32[]{:S(2)}) %collective-permute-start.3) | collective-permute-done | bytes 589856 | tf_op jit(solution)/shard_map/ppermute | solution.py:653
  40.3 138.0 %shard_map.212 = (bf16[4,2,128,2304]{3,2,1,0:T(8,128)(2,1)}, bf16[4,2,288,1728]{3,2,1,0:T(8,128)(2,1)}, bf16[4,288,576]{2,1,0:T(8,128)(2,1)}, bf16[3,288,720]{2,1,0:T(8,128)(2,1)}, bf16[3,288,720]{2,1,0:T(8,128)(2,1)}) custom-call(bf16[2,128,2304]{2,1,0:T(8,128)(2,1)} %fusion.6.normed, bf16[288,1728]{1,0:T(8,128)(2,1)} %concatenate.55.qkv, ...), custom_call_target="tpu_custom_call" | custom-call | tf_op jit(solution)/shard_map/pallas_call | solution.py:413
  181.7 14.9 %fusion.57.projected = f32[1024,1728]{1,0:T(8,128)} fusion(bf16[1024,2304]{1,0:T(8,128)(2,1)} %bitcast.246, bf16[2304,1728]{1,0:T(8,128)(2,1)} %bitcast.244), kind=kOutput, calls=%fused_computation.171 | convolution fusion | flops 8153726976 | bytes 19759104 | tf_op jit(solution)/shard_map/dot_general | solution.py:637
  204.1 34.8 %shard_map.213 = (bf16[1024,576]{1,0:T(8,128)(2,1)S(1)}, bf16[9,1024,64]{2,1,0:T(8,128)(2,1)S(1)}, bf16[9,1024,64]{2,1,0:T(8,128)(2,1)}, bf16[9,1024,64]{2,1,0:T(8,128)(2,1)}, f32[9,1,1024]{2,1,0:T(1,128)S(1)}) custom-call(s32[1]{0:T(128)} %dynamic_slice.178.length_ref, f32[1024,1728]{1,0:T(8,128)} %fusion.57.projected, f32[1024,128]{1,0:T(8,128)S(1)} %copy.80.cosine, ...), custom_call_target="tpu_custom_call" | custom-call | flops 2415919104 | bytes 20971520 | tf_op jit(solution)/shard_map/pallas_call | solution.py:106
  238.9 14.6 %collective-permute-done.1 = bf16[128,2304]{1,0:T(8,128)(2,1)} collective-permute-done((bf16[128,2304]{1,0:T(8,128)(2,1)}, bf16[128,2304]{1,0:T(8,128)(2,1)}, u32[]{:S(2)}, u32[]{:S(2)}) %collective-permute-start.1) | collective-permute-done | bytes 589856 | tf_op jit(solution)/shard_map/ppermute | solution.py:653
  265.4 146.4 %shard_map.214 = (f32[256,2304]{1,0:T(8,128)S(1)}, bf16[2,4,2,128,2304]{4,3,2,1,0:T(8,128)(2,1)}, bf16[3,4,2,288,720]{4,3,2,1,0:T(8,128)(2,1)}) custom-call(bf16[4,256,2304]{2,1,0:T(8,128)(2,1)S(1)} %bitcast.196, bf16[256,2304]{1,0:T(8,128)(2,1)S(1)} %get-tuple-element.60.tokens, f32[1,2304]{1,0:T(1,128)S(1)} %broadcast_in_dim.16.gain, ...), custom_call_target="tpu_custom_call" | custom-call | tf_op jit(solution)/shard_map/pallas_call | solution.py:599
  432.5 12.4 %fusion.59 = f32[2048,720]{0,1:T(8,128)} fusion(bf16[2048,2304]{1,0:T(8,128)(2,1)} %all-gather.3.cloned.1.call-done, bf16[2304,720]{1,0:T(8,128)(2,1)} %bitcast.226), kind=kOutput, calls=%fused_computation.173 | convolution fusion | flops 6794772480 | bytes 18653184 | tf_op jit(solution)/shard_map/dot_general | solution.py:637
  444.9 19.1 %add_convert_fusion.1 = (bf16[2048,720]{0,1:T(8,128)(2,1)}, bf16[2048,720]{0,1:T(8,128)(2,1)}, bf16[2048,720]{0,1:T(8,128)(2,1)}) fusion(f32[2048,720]{0,1:T(8,128)} %fusion.59, f32[2048,720]{0,1:T(8,128)} %fusion.58, bf16[2048,2304]{1,0:T(8,128)(2,1)} %bitcast.240, bf16[2304,720]{1,0:T(8,128)(2,1)} %bitcast.228), kind=kOutput, calls=%fused_computation.4 | convolution fusion | flops 6821314560 | bytes 33398784 | tf_op jit(solution)/shard_map/dot_general | solution.py:637
  464.0 13.9 %fusion.60 = f32[2048,2304]{1,0:T(8,128)} fusion(bf16[2048,720]{0,1:T(8,128)(2,1)} %get-tuple-element.62, bf16[2304,720]{1,0:T(8,128)(2,1)} %bitcast.231), kind=kOutput, calls=%fused_computation.174 | convolution fusion | flops 6794772480 | bytes 25141248 | tf_op jit(solution)/shard_map/dot_general | solution.py:645
  477.9 15.5 %add_convert_fusion = bf16[2048,2304]{1,0:T(8,128)(2,1)} fusion(f32[2048,2304]{1,0:T(8,128)} %fusion.60, bf16[2048,720]{0,1:T(8,128)(2,1)} %get-tuple-element.61, bf16[2304,720]{1,0:T(8,128)(2,1)} %bitcast.229), kind=kOutput, calls=%fused_computation | convolution fusion | flops 6804209664 | bytes 34578432 | tf_op jit(solution)/shard_map/dot_general | solution.py:645
  494.4 74.9 %reduce-scatter.4.cloned.1.call-done = bf16[256,2304]{1,0:T(8,128)(2,1)} async-done(((bf16[2048,2304]{1,0:T(8,128)(2,1)}), bf16[256,2304]{1,0:T(8,128)(2,1)}) %reduce-scatter.4.cloned.1.call-update) | async-done | bytes 1179664 | tf_op jit(solution)/shard_map/reduce_scatter | solution.py:823
  574.8 37.6 %all-gather.5.cloned.1.call-done = bf16[1024,2304]{1,0:T(8,128)(2,1)} async-done(((bf16[256,2304]{1,0:T(8,128)(2,1)}), bf16[1024,2304]{1,0:T(8,128)(2,1)}) %all-gather.5.cloned.1.call-update) | async-done | bytes 4718608 | tf_op jit(solution)/shard_map/all_gather | solution.py:831
  620.3 39.1 %shard_map.215 = bf16[1024,1728]{1,0:T(8,128)(2,1)} custom-call(s32[1]{0:T(128)} %dynamic_slice.178.length_ref, bf16[1024,576]{1,0:T(8,128)(2,1)} %copy.82.grad_context, bf16[9,1024,64]{2,1,0:T(8,128)(2,1)} %copy-done.11, bf16[9,1024,64]{2,1,0:T(8,128)(2,1)} %get-tuple-element.40.k_heads, bf16[9,1024,64]{2,1,0:T(8,128)(2,1)} %get-tuple-element.41.v_heads, ...), custom_call_target="tpu_custom_call" | custom-call | flops 6039797760 | bytes 20971520 | tf_op jit(solution)/shard_map/pallas_call | solution.py:185
  659.4 14.7 %convolution_convert_fusion.2 = bf16[1024,2304]{1,0:T(8,128)(2,1)} fusion(bf16[1024,1728]{1,0:T(8,128)(2,1)} %shard_map.215, bf16[2304,1728]{1,0:T(8,128)(2,1)} %bitcast.245), kind=kOutput, calls=%fused_computation.8 | convolution fusion | flops 8156086272 | bytes 16220160 | tf_op jit(solution)/shard_map/dot_general | solution.py:645
  675.9 12.1 %convolution_convert_fusion.4 = bf16[2304,720]{0,1:T(8,128)(2,1)} fusion(bf16[2048,720]{0,1:T(8,128)(2,1)S(1)} %copy-done.55, bf16[2048,2304]{1,0:T(8,128)(2,1)} %all-gather.3.cloned.1.call-done), kind=kOutput, calls=%fused_computation.10 | convolution fusion | flops 6796431360 | bytes 15704064 | tf_op jit(solution)/shard_map/dot_general | solution.py:641
  698.5 12.1 %convolution_convert_fusion.5 = bf16[2304,720]{0,1:T(8,128)(2,1)} fusion(bf16[2048,720]{0,1:T(8,128)(2,1)S(1)} %copy-done.53, bf16[2048,2304]{1,0:T(8,128)(2,1)} %bitcast.241), kind=kOutput, calls=%fused_computation.11 | convolution fusion | flops 6796431360 | bytes 15704064 | tf_op jit(solution)/shard_map/dot_general | solution.py:641
  719.0 12.4 %convolution_convert_fusion.6 = bf16[2304,720]{0,1:T(8,128)(2,1)} fusion(bf16[2048,720]{0,1:T(8,128)(2,1)S(1)} %copy-done.54, bf16[2048,2304]{1,0:T(8,128)(2,1)} %bitcast.242), kind=kOutput, calls=%fused_computation.12 | convolution fusion | flops 6796431360 | bytes 15704064 | tf_op jit(solution)/shard_map/dot_general | solution.py:641
  787.1 13.1 %collective-permute-done.34 = bf16[576,720]{1,0:T(8,128)(2,1)} collective-permute-done((bf16[576,720]{1,0:T(8,128)(2,1)}, bf16[576,720]{1,0:T(8,128)(2,1)}, u32[]{:S(2)}, u32[]{:S(2)}) %collective-permute-start.34) | collective-permute-done | bytes 829472 | tf_op jit(solution)/shard_map/ppermute | solution.py:705
  885.4 17.1 %collective-permute-start.28 = (bf16[576,720]{1,0:T(8,128)(2,1)}, bf16[576,720]{1,0:T(8,128)(2,1)}, u32[]{:S(2)}, u32[]{:S(2)}) collective-permute-start(bf16[576,720]{1,0:T(8,128)(2,1)} %get-tuple-element.81), channel_id=1, source_target_pairs={{0,8},{8,16},{16,24},{1,9},{9,17},{17,25},{2,10},{10,18},{18,26},{... | collective-permute-start | bytes 2488328 | tf_op jit(solution)/shard_map/ppermute | solution.py:705
  907.3 15.6 %collective-permute-done.7 = bf16[288,1728]{1,0:T(8,128)(2,1)S(1)} collective-permute-done((bf16[288,1728]{1,0:T(8,128)(2,1)S(1)}, bf16[288,1728]{1,0:T(8,128)(2,1)S(1)}, u32[]{:S(2)}, u32[]{:S(2)}) %collective-permute-start.7) | collective-permute-done | bytes 995360 | tf_op jit(solution)/shard_map/ppermute | solution.py:653
  923.0 22.1 %collective-permute-done.8 = bf16[288,1728]{1,0:T(8,128)(2,1)S(1)} collective-permute-done((bf16[288,1728]{1,0:T(8,128)(2,1)S(1)}, bf16[288,1728]{1,0:T(8,128)(2,1)S(1)}, u32[]{:S(2)}, u32[]{:S(2)}) %collective-permute-start.8) | collective-permute-done | bytes 995360 | tf_op jit(solution)/shard_map/ppermute | solution.py:653
  945.1 19.0 %collective-permute-done.9 = bf16[288,1728]{1,0:T(8,128)(2,1)S(1)} collective-permute-done((bf16[288,1728]{1,0:T(8,128)(2,1)S(1)}, bf16[288,1728]{1,0:T(8,128)(2,1)S(1)}, u32[]{:S(2)}, u32[]{:S(2)}) %collective-permute-start.9) | collective-permute-done | bytes 995360 | tf_op jit(solution)/shard_map/ppermute | solution.py:653
  1067.3 13.3 %collective-permute-done.25 = bf16[288,576]{1,0:T(8,128)(2,1)S(1)} collective-permute-done((bf16[288,576]{1,0:T(8,128)(2,1)S(1)}, bf16[288,576]{1,0:T(8,128)(2,1)S(1)}, u32[]{:S(2)}, u32[]{:S(2)}) %collective-permute-start.25) | collective-permute-done | bytes 331808 | tf_op jit(solution)/shard_map/ppermute | solution.py:706
  1096.1 53.4 %psum.7 = f32[2,2304]{1,0:T(2,128)} all-reduce(f32[2,2304]{1,0:T(2,128)} %pad_maximum_fusion.1), channel_id=1, replica_groups=mesh['fsdp'=4,'cp'=2,'tp'=4] {'fsdp','cp','tp'}, use_global_device_ids=true, to_apply=%region_10.11 | all-reduce | flops 4608 | bytes 36864 | tf_op jit(solution)/shard_map/psum | solution.py:870
  (328 shorter events, 344.1 us)
Async XLA Ops:
  7.2 425.3 %all-gather.3.cloned.1.call-start = ((), (), s32[]{:S(2)}) async-start(), calls=%async_computation.3 | async-start | bytes 10616832 | tf_op jit(solution)/shard_map/all_gather | solution.py:800
  26.3 543.0 %reduce-scatter.4.cloned.1.call-start = ((), (), s32[]{:S(2)}) async-start(), calls=%async_computation.4 | async-start | bytes 10616832 | tf_op jit(solution)/shard_map/reduce_scatter | solution.py:823
  178.3 77.5 %collective-permute-start = (bf16[4,288,576]{2,1,0:T(8,128)(2,1)}, bf16[4,288,576]{2,1,0:T(8,128)(2,1)}, u32[]{:S(2)}, u32[]{:S(2)}) collective-permute-start(bf16[4,288,576]{2,1,0:T(8,128)(2,1)} %get-tuple-element.31), channel_id=1, source_target_pairs={{0,4},{4,0},{1,5},{5,1},{2,6},{6,2},{3,7},{7,3},{8,12},{12,8},{9,1... | collective-permute-start | bytes 3981320 | tf_op jit(solution)/shard_map/ppermute | solution.py:653
  178.7 84.3 %collective-permute-start.2 = (bf16[3,288,720]{2,1,0:T(8,128)(2,1)}, bf16[3,288,720]{2,1,0:T(8,128)(2,1)S(1)}, u32[]{:S(2)}, u32[]{:S(2)}) collective-permute-start(bf16[3,288,720]{2,1,0:T(8,128)(2,1)} %get-tuple-element.34), channel_id=1, source_target_pairs={{0,4},{4,0},{1,5},{5,1},{2,6},{6,2},{3,7},{7,3},{8,12},{12,8},{9,1... | collective-permute-start | bytes 3732488 | tf_op jit(solution)/shard_map/ppermute | solution.py:653
  181.3 72.2 %collective-permute-start.1 = (bf16[128,2304]{1,0:T(8,128)(2,1)}, bf16[128,2304]{1,0:T(8,128)(2,1)}, u32[]{:S(2)}, u32[]{:S(2)}) collective-permute-start(bf16[128,2304]{1,0:T(8,128)(2,1)} %get-tuple-element.104), channel_id=1, source_target_pairs={{0,4},{4,0},{1,5},{5,1},{2,6},{6,2},{3,7},{7,3},{8,12},{12,8},{9,1... | collective-permute-start | bytes 1769480 | tf_op jit(solution)/shard_map/ppermute | solution.py:653
  493.5 118.9 %all-gather.5.cloned.1.call-start = ((), (), s32[]{:S(2)}) async-start(), calls=%async_computation.5 | async-start | bytes 5898240 | tf_op jit(solution)/shard_map/all_gather | solution.py:831
  574.8 509.4 %reduce-scatter.8.cloned.1.call-start = ((), (), s32[]{:S(2)}) async-start(), calls=%async_computation.7 | async-start | bytes 5898240 | tf_op jit(solution)/shard_map/reduce_scatter | solution.py:865
  674.1 414.6 %reduce-scatter.6.cloned.1.call-start = ((), (), s32[]{:S(2)}) async-start(), calls=%async_computation.6 | async-start | bytes 10616832 | tf_op jit(solution)/shard_map/reduce_scatter | solution.py:833
  693.9 49.1 %collective-permute-start.40 = (bf16[576,720]{1,0:T(8,128)(2,1)}, bf16[576,720]{1,0:T(8,128)(2,1)}, u32[]{:S(2)}, u32[]{:S(2)}) collective-permute-start(bf16[576,720]{1,0:T(8,128)(2,1)} %get-tuple-element.75), channel_id=1, source_target_pairs={{0,8},{1,9},{2,10},{3,11},{4,12},{5,13},{6,14},{7,15}} | collective-permute-start | bytes 2488328 | tf_op jit(solution)/shard_map/ppermute | solution.py:705
  733.0 54.1 %collective-permute-start.36 = (bf16[576,720]{1,0:T(8,128)(2,1)}, bf16[576,720]{1,0:T(8,128)(2,1)}, u32[]{:S(2)}, u32[]{:S(2)}) collective-permute-start(bf16[576,720]{1,0:T(8,128)(2,1)} %get-tuple-element.80), channel_id=1, source_target_pairs={{24,16},{25,17},{26,18},{27,19},{28,20},{29,21},{30,22},{31,23}} | collective-permute-start | bytes 2488328 | tf_op jit(solution)/shard_map/ppermute | solution.py:706
  750.6 49.6 %collective-permute-start.34 = (bf16[576,720]{1,0:T(8,128)(2,1)}, bf16[576,720]{1,0:T(8,128)(2,1)}, u32[]{:S(2)}, u32[]{:S(2)}) collective-permute-start(bf16[576,720]{1,0:T(8,128)(2,1)} %fusion.26), channel_id=1, source_target_pairs={{0,8},{8,16},{1,9},{9,17},{2,10},{10,18},{3,11},{11,19},{4,12},{12... | collective-permute-start | bytes 2488328 | tf_op jit(solution)/shard_map/ppermute | solution.py:705
  763.6 68.9 %collective-permute-start.29 = (bf16[576,720]{1,0:T(8,128)(2,1)}, bf16[576,720]{1,0:T(8,128)(2,1)}, u32[]{:S(2)}, u32[]{:S(2)}) collective-permute-start(bf16[576,720]{1,0:T(8,128)(2,1)} %get-tuple-element.84), channel_id=1, source_target_pairs={{24,16},{25,17},{26,18},{27,19},{28,20},{29,21},{30,22},{31,23}} | collective-permute-start | bytes 2488328 | tf_op jit(solution)/shard_map/ppermute | solution.py:706
  767.6 69.8 %collective-permute-start.27 = (bf16[576,720]{1,0:T(8,128)(2,1)}, bf16[576,720]{1,0:T(8,128)(2,1)}, u32[]{:S(2)}, u32[]{:S(2)}) collective-permute-start(bf16[576,720]{1,0:T(8,128)(2,1)} %fusion.31), channel_id=1, source_target_pairs={{0,8},{8,16},{1,9},{9,17},{2,10},{10,18},{3,11},{11,19},{4,12},{12... | collective-permute-start | bytes 2488328 | tf_op jit(solution)/shard_map/ppermute | solution.py:705
  785.4 56.8 %collective-permute-start.44 = (bf16[576,720]{1,0:T(8,128)(2,1)}, bf16[576,720]{1,0:T(8,128)(2,1)}, u32[]{:S(2)}, u32[]{:S(2)}) collective-permute-start(bf16[576,720]{1,0:T(8,128)(2,1)} %get-tuple-element.74), channel_id=1, source_target_pairs={{16,8},{24,16},{17,9},{25,17},{18,10},{26,18},{19,11},{27,19},{20,... | collective-permute-start | bytes 2488328 | tf_op jit(solution)/shard_map/ppermute | solution.py:706
  827.6 47.4 %collective-permute-start.42 = (bf16[576,720]{1,0:T(8,128)(2,1)}, bf16[576,720]{1,0:T(8,128)(2,1)}, u32[]{:S(2)}, u32[]{:S(2)}) collective-permute-start(bf16[576,720]{1,0:T(8,128)(2,1)} %get-tuple-element.73), channel_id=1, source_target_pairs={{0,8},{8,16},{16,24},{1,9},{9,17},{17,25},{2,10},{10,18},{18,26},{... | collective-permute-start | bytes 2488328 | tf_op jit(solution)/shard_map/ppermute | solution.py:705
  832.5 44.0 %collective-permute-start.35 = (bf16[576,720]{1,0:T(8,128)(2,1)}, bf16[576,720]{1,0:T(8,128)(2,1)}, u32[]{:S(2)}, u32[]{:S(2)}) collective-permute-start(bf16[576,720]{1,0:T(8,128)(2,1)} %get-tuple-element.77), channel_id=1, source_target_pairs={{0,8},{8,16},{16,24},{1,9},{9,17},{17,25},{2,10},{10,18},{18,26},{... | collective-permute-start | bytes 2488328 | tf_op jit(solution)/shard_map/ppermute | solution.py:705
  876.5 46.4 %collective-permute-start.7 = (bf16[288,1728]{1,0:T(8,128)(2,1)S(1)}, bf16[288,1728]{1,0:T(8,128)(2,1)S(1)}, u32[]{:S(2)}, u32[]{:S(2)}) collective-permute-start(bf16[288,1728]{1,0:T(8,128)(2,1)S(1)} %get-tuple-element.69), channel_id=1, source_target_pairs={{0,4},{4,0},{1,5},{5,1},{2,6},{6,2},{3,7},{7,3},{8,12},{12,8},{9,1... | collective-permute-start | bytes 2985992 | tf_op jit(solution)/shard_map/ppermute | solution.py:653
  877.1 68.0 %collective-permute-start.8 = (bf16[288,1728]{1,0:T(8,128)(2,1)S(1)}, bf16[288,1728]{1,0:T(8,128)(2,1)S(1)}, u32[]{:S(2)}, u32[]{:S(2)}) collective-permute-start(bf16[288,1728]{1,0:T(8,128)(2,1)S(1)} %get-tuple-element.70), channel_id=1, source_target_pairs={{0,4},{4,0},{1,5},{5,1},{2,6},{6,2},{3,7},{7,3},{8,12},{12,8},{9,1... | collective-permute-start | bytes 2985992 | tf_op jit(solution)/shard_map/ppermute | solution.py:653
  878.6 85.5 %collective-permute-start.9 = (bf16[288,1728]{1,0:T(8,128)(2,1)S(1)}, bf16[288,1728]{1,0:T(8,128)(2,1)S(1)}, u32[]{:S(2)}, u32[]{:S(2)}) collective-permute-start(bf16[288,1728]{1,0:T(8,128)(2,1)S(1)} %get-tuple-element.68), channel_id=1, source_target_pairs={{0,4},{4,0},{1,5},{5,1},{2,6},{6,2},{3,7},{7,3},{8,12},{12,8},{9,1... | collective-permute-start | bytes 2985992 | tf_op jit(solution)/shard_map/ppermute | solution.py:653
  885.4 111.7 %collective-permute-start.28 = (bf16[576,720]{1,0:T(8,128)(2,1)}, bf16[576,720]{1,0:T(8,128)(2,1)}, u32[]{:S(2)}, u32[]{:S(2)}) collective-permute-start(bf16[576,720]{1,0:T(8,128)(2,1)} %get-tuple-element.81), channel_id=1, source_target_pairs={{0,8},{8,16},{16,24},{1,9},{9,17},{17,25},{2,10},{10,18},{18,26},{... | collective-permute-start | bytes 2488328 | tf_op jit(solution)/shard_map/ppermute | solution.py:705
  905.9 91.2 %collective-permute-start.31 = (bf16[576,720]{1,0:T(8,128)(2,1)}, bf16[576,720]{1,0:T(8,128)(2,1)}, u32[]{:S(2)}, u32[]{:S(2)}) collective-permute-start(bf16[576,720]{1,0:T(8,128)(2,1)} %fusion.30), channel_id=1, source_target_pairs={{8,0},{16,8},{24,16},{9,1},{17,9},{25,17},{10,2},{18,10},{26,18},{... | collective-permute-start | bytes 2488328 | tf_op jit(solution)/shard_map/ppermute | solution.py:706
  984.9 44.3 %collective-permute-start.13 = (bf16[288,1728]{1,0:T(8,128)(2,1)S(1)}, bf16[288,1728]{1,0:T(8,128)(2,1)S(1)}, u32[]{:S(2)}, u32[]{:S(2)}) collective-permute-start(bf16[288,1728]{1,0:T(8,128)(2,1)S(1)} %select_select_fusion), channel_id=1, source_target_pairs={{24,16},{25,17},{26,18},{27,19},{28,20},{29,21},{30,22},{31,23}} | collective-permute-start | bytes 2985992 | tf_op jit(solution)/shard_map/ppermute | solution.py:706
  1092.6 58.4 %collective-permute-start.5 = (bf16[128,2304]{1,0:T(8,128)(2,1)S(1)}, bf16[128,2304]{1,0:T(8,128)(2,1)S(1)}, u32[]{:S(2)}, u32[]{:S(2)}) collective-permute-start(bf16[128,2304]{1,0:T(8,128)(2,1)S(1)} %get-tuple-element.99), channel_id=1, source_target_pairs={{0,4},{4,0},{1,5},{5,1},{2,6},{6,2},{3,7},{7,3},{8,12},{12,8},{9,1... | collective-permute-start | bytes 1769480 | tf_op jit(solution)/shard_map/ppermute | solution.py:653
  1095.4 56.8 %collective-permute-start.4 = (bf16[128,2304]{1,0:T(8,128)(2,1)S(1)}, bf16[128,2304]{1,0:T(8,128)(2,1)S(1)}, u32[]{:S(2)}, u32[]{:S(2)}) collective-permute-start(bf16[128,2304]{1,0:T(8,128)(2,1)S(1)} %get-tuple-element.101), channel_id=1, source_target_pairs={{0,4},{4,0},{1,5},{5,1},{2,6},{6,2},{3,7},{7,3},{8,12},{12,8},{9,1... | collective-permute-start | bytes 1769480 | tf_op jit(solution)/shard_map/ppermute | solution.py:653
  (91 other events, 2242.8 us)
Sparse Core Ops, SparseCore 0:
  26.4 93.0 all-gather.2
  493.6 75.5 reduce-scatter.3
  574.9 37.4 all-gather.4
  674.2 47.8 reduce-scatter.7
  767.7 75.6 reduce-scatter.5

commit v2 on v1

--- a/solution.py
+++ b/solution.py
@@ -431,6 +431,9 @@
 
 
 def in_pieces(rows, body, size=16):
+    if rows % size:
+        body(pl.ds(0, rows))
+        return
     lax.fori_loop(0, rows // size, lambda i, carry: (body(pl.ds(i * size, size)), carry)[1], 0)
 
 
@@ -621,12 +624,517 @@
     )(part, tokens, gain, wide, wide_low, wide_high, wide_other)
 
 
+class TensorSum:
+    def __init__(self, mail, part, own, from_core, to_yonder, from_yonder, local):
+        self.mail, self.part, self.own, self.from_core = mail, part, own, from_core
+        self.to_yonder, self.from_yonder, self.local = to_yonder, from_yonder, local
+        self.t = t = lax.axis_index("tp")
+        self.beside, self.yonder = t + 1 - 2 * (t % 2), (t + 2) % 4
+        self.core = [mail.slot() for _ in range(2)]
+        self.across = [mail.slot() for _ in range(2)]
+        self.half = from_yonder.shape[0] // 2
+
+    def begin(self):
+        part, far = self.part, (self.beside + 2) % 4
+        self.mail.start(self.core[1], part.at[far], self.from_core.at[1], tp=self.beside)
+        self.mail.start(self.core[0], part.at[self.beside], self.from_core.at[0], tp=self.beside)
+        self.kept = [
+            pltpu.make_async_copy(part.at[self.yonder], self.own.at[1], self.local.at[0]),
+            pltpu.make_async_copy(part.at[self.t], self.own.at[0], self.local.at[1]),
+        ]
+        for copy in self.kept:
+            copy.start()
+
+    def turn(self):
+        own, from_core = self.own, self.from_core
+        self.kept[0].wait()
+        self.mail.arrive(self.core[1], from_core.at[1], tp=self.beside)
+        for piece in range(2):
+
+            def add(place, piece=piece):
+                place = pl.ds(place.start + piece * self.half, place.size)
+                self.to_yonder[place, :] = (
+                    own[1, place, :].astype(F32) + from_core[1, place, :].astype(F32)
+                ).astype(BF)
+
+            in_pieces(self.half, add)
+            block = pl.ds(piece * self.half, self.half)
+            self.mail.start(
+                self.across[piece], self.to_yonder.at[block], self.from_yonder.at[block],
+                tp=self.yonder,
+            )
+        self.kept[1].wait()
+        self.mail.arrive(self.core[0], from_core.at[0], tp=self.beside)
+
+    def arrive(self, piece):
+        block = pl.ds(piece * self.half, self.half)
+        self.mail.arrive(self.across[piece], self.from_yonder.at[block], tp=self.yonder)
+
+    def rows(self, row):
+        return (
+            self.own[0, row, :].astype(F32)
+            + self.from_core[0, row, :].astype(F32)
+            + self.from_yonder[row, :].astype(F32)
+        )
+
+
+class Drain:
+    def __init__(self, mail, count, fill, total, landed):
+        self.mail, self.count, self.fill, self.total, self.landed = mail, count, fill, total, landed
+        self.z = lax.axis_index("fsdp")
+        self.slots = [[mail.slot() for _ in range(count)] for _ in range(2)]
+
+    def sends(self, hop, up):
+        z, count = self.z, self.count
+        return (z <= hop - 1) & (z < count - 1) if up else (z >= count - hop) & (z > 0)
+
+    def gets(self, hop, up):
+        z, count = self.z, self.count
+        return (z >= 1) & (z <= hop) if up else (z <= count - 2) & (z >= count - 1 - hop)
+
+    def block(self, hop, up):
+        z, count = self.z, self.count
+        return jnp.minimum(z + count - hop, count - 1) if up else jnp.maximum(z - count + hop, 0)
+
+    def arrive(self, hop):
+        for side, up in enumerate((True, False)):
+            self.mail.arrive(
+                self.slots[side][hop], self.landed(side, hop), when=self.gets(hop, up), fsdp=self.z
+            )
+
+    def gather(self, hop):
+        for side, up in enumerate((True, False)):
+            target = self.total(side, hop)
+
+            def work(side=side, up=up, target=target):
+                self.fill(hop, up, self.block(hop, up), target)
+                if hop > 1:
+
+                    def add():
+                        landed = self.landed(side, hop - 1)
+
+                        def one(place):
+                            target[place, :] = (
+                                target[place, :].astype(F32) + landed[place, :].astype(F32)
+                            ).astype(BF)
+
+                        in_pieces(target.shape[0], one)
+
+                    pl.when(self.gets(hop - 1, up))(add)
+
+            pl.when(self.sends(hop, up))(work)
+
+    def send(self, hop):
+        z, count = self.z, self.count
+        for side, up in enumerate((True, False)):
+            to = jnp.minimum(z + 1, count - 1) if up else jnp.maximum(z - 1, 0)
+            self.mail.start(
+                self.slots[side][hop], self.total(side, hop), self.landed(side, hop),
+                when=self.sends(hop, up), fsdp=to,
+            )
+
+
+def norm_back(values, gain, upstream):
+    scale = lax.rsqrt(jnp.mean(values * values, axis=-1, keepdims=True) + EPSILON)
+    norm = values * scale
+    scaled = upstream * gain
+    mean = jnp.mean(scaled * norm, axis=-1, keepdims=True)
+    return scale * (scaled - norm * mean), upstream * norm
+
+
+def first_sum_kernel(
+    count, part, gate_grad, up_grad, down_grad, middle, cotangent, gain,
+    grad_middle, attention_full, gain_rows, leaving,
+    own, from_core, first, second, grad_attention, totals, landed,
+    send, recv, local,
+):
+    z, c, t = lax.axis_index("fsdp"), lax.axis_index("cp"), lax.axis_index("tp")
+    beside, yonder = t + 1 - 2 * (t % 2), (t + 2) % 4
+    far = (beside + 2) % 4
+    half = middle.shape[0] // 2
+    width = middle.shape[1]
+    mail = Mail(send, recv)
+    greet(count)
+    last = count - 1
+
+    def fill_from(which):
+        def fill(hop, up, j, target):
+            copy = pltpu.make_async_copy((gate_grad, up_grad, down_grad)[which].at[j], target, local.at[4])
+            copy.start()
+            copy.wait()
+
+        return fill
+
+    drains = [
+        Drain(
+            mail, count, fill_from(which),
+            lambda side, hop, which=which: (
+                leaving.at[side, which] if hop == last else totals.at[side, hop - 1, which]
+            ),
+            lambda side, hop, which=which: landed.at[side, hop - 1, which],
+        )
+        for which in range(3)
+    ]
+
+    core = {}
+    mine = {}
+    order = ((1, 0), (0, 0), (0, 1), (1, 1))
+    for index, (c_own, t_own) in enumerate(order):
+        block_c = c if c_own else 1 - c
+        core[c_own, t_own] = mail.slot()
+        mail.start(
+            core[c_own, t_own], part.at[block_c, beside if t_own else far],
+            from_core.at[c_own, t_own], tp=beside,
+        )
+        mine[c_own, t_own] = pltpu.make_async_copy(
+            part.at[block_c, t if t_own else yonder], own.at[c_own, t_own], local.at[index]
+        )
+        mine[c_own, t_own].start()
+    if last > 1:
+        for drain in drains:
+            drain.gather(1)
+            drain.send(1)
+    for c_own, t_own in order:
+        mine[c_own, t_own].wait()
+        mail.arrive(core[c_own, t_own], from_core.at[c_own, t_own], tp=beside)
+
+        def add(place, c_own=c_own, t_own=t_own):
+            own[c_own, t_own, place, :] = (
+                own[c_own, t_own, place, :].astype(F32)
+                + from_core[c_own, t_own, place, :].astype(F32)
+            ).astype(BF)
+
+        in_pieces(2 * half, add)
+
+    top, low = pl.ds(0, half), pl.ds(half, half)
+    y_first = [mail.slot() for _ in range(2)]
+    x_first = [mail.slot() for _ in range(2)]
+    x_second, y_second = mail.slot(), mail.slot()
+    for c_own in (0, 1):
+        mail.start(y_first[c_own], own.at[c_own, 0, top], first.at[0, c_own], tp=yonder)
+    for t_own in (0, 1):
+        mail.start(x_first[t_own], own.at[0, t_own, low], first.at[1, t_own], cp=1 - c)
+
+    def add_first(side, index, c_own, t_own):
+        def one(place):
+            row = pl.ds(place.start + side * half, place.size)
+            own[c_own, t_own, row, :] = (
+                own[c_own, t_own, row, :].astype(F32) + first[side, index, place, :].astype(F32)
+            ).astype(BF)
+
+        in_pieces(half, one)
+
+    mail.arrive(y_first[0], first.at[0, 0], tp=yonder)
+    add_first(0, 0, 0, 1)
+    mail.start(x_second, own.at[0, 1, top], second.at[0], cp=1 - c)
+    mail.arrive(x_first[0], first.at[1, 0], cp=1 - c)
+    add_first(1, 0, 1, 0)
+    mail.start(y_second, own.at[1, 0, low], second.at[1], tp=yonder)
+    mail.arrive(y_first[1], first.at[0, 1], tp=yonder)
+    add_first(0, 1, 1, 1)
+    mail.arrive(x_first[1], first.at[1, 1], cp=1 - c)
+    add_first(1, 1, 1, 1)
+
+    gain_rows[...] = jnp.zeros_like(gain_rows)
+    ring_y = [mail.slot() for _ in range(2)]
+    ring_core = [mail.slot() for _ in range(4)]
+    keep = []
+    for piece in range(2):
+        if piece == 0:
+            mail.arrive(x_second, second.at[0], cp=1 - c)
+        else:
+            mail.arrive(y_second, second.at[1], tp=yonder)
+
+        def back(place, piece=piece):
+            row = pl.ds(place.start + piece * half, place.size)
+            summed = own[1, 1, row, :].astype(F32) + second[piece, place, :].astype(F32)
+            grad, rows = norm_back(middle[row, :], gain[...], summed)
+            grad = cotangent[row, :].astype(F32) + grad
+            grad_middle[row, :] = grad
+            grad_attention[piece, place, :] = (BRANCH * grad).astype(BF)
+            gain_rows[...] += jnp.sum(rows, axis=0, keepdims=True)
+
+        in_pieces(half, back)
+        mail.start(ring_y[piece], grad_attention.at[piece], attention_full.at[t, piece], tp=yonder)
+        mail.start(
+            ring_core[piece], grad_attention.at[piece], attention_full.at[t, piece], tp=beside
+        )
+    keep = pltpu.make_async_copy(grad_attention, attention_full.at[t], local.at[0])
+    keep.start()
+    for hop in range(2, last):
+        for drain in drains:
+            drain.arrive(hop - 1)
+            drain.gather(hop)
+            drain.send(hop)
+    for piece in range(2):
+        mail.arrive(ring_y[piece], attention_full.at[yonder, piece], tp=yonder)
+        mail.start(
+            ring_core[2 + piece], attention_full.at[yonder, piece],
+            attention_full.at[yonder, piece], tp=beside,
+        )
+    for piece in range(2):
+        mail.arrive(ring_core[piece], attention_full.at[beside, piece], tp=beside)
+        mail.arrive(ring_core[2 + piece], attention_full.at[far, piece], tp=beside)
+    for drain in drains:
+        if last > 1:
+            drain.arrive(last - 1)
+        if last > 0:
+            drain.gather(last)
+    keep.wait()
+    mail.finish()
+
+
+def first_sum(count, part, gate_grad, up_grad, down_grad, middle, cotangent, gain):
+    slots = 6 * count + 24
+    rows, width = middle.shape
+    block = gate_grad.shape[1:]
+    anywhere = pl.BlockSpec(memory_space=pl.ANY)
+    vmem = pl.BlockSpec(memory_space=pltpu.VMEM)
+    hops = max(count - 2, 1)
+    return pl.pallas_call(
+        functools.partial(first_sum_kernel, count),
+        out_shape=(
+            jax.ShapeDtypeStruct((rows, width), F32),
+            jax.ShapeDtypeStruct((4, 2, rows // 2, width), BF),
+            jax.ShapeDtypeStruct((1, width), F32),
+            jax.ShapeDtypeStruct((2, 3) + block, BF),
+        ),
+        in_specs=[anywhere] * 4 + [vmem] * 3,
+        out_specs=(vmem, anywhere, vmem, vmem),
+        scratch_shapes=[
+            pltpu.VMEM((2, 2, rows, width), BF),
+            pltpu.VMEM((2, 2, rows, width), BF),
+            pltpu.VMEM((2, 2, rows // 2, width), BF),
+            pltpu.VMEM((2, rows // 2, width), BF),
+            pltpu.VMEM((2, rows // 2, width), BF),
+            pltpu.VMEM((2, hops, 3) + block, BF),
+            pltpu.VMEM((2, hops, 3) + block, BF),
+            pltpu.SemaphoreType.DMA((slots,)),
+            pltpu.SemaphoreType.DMA((slots,)),
+            pltpu.SemaphoreType.DMA((5,)),
+        ],
+        compiler_params=pltpu.CompilerParams(
+            collective_id=3, has_side_effects=True, vmem_limit_bytes=60 << 20
+        ),
+    )(part, gate_grad, up_grad, down_grad, middle, cotangent, gain)
+
+
+def last_sum_kernel(
+    count, part, qkv_grad, out_grad, tokens, grad_middle, gain, gain_rows,
+    qkv_total, out_total, grad_tokens, gain_sums,
+    own, from_core, to_yonder, from_yonder, pieces,
+    from_x, heads_sum, heads_landed, outs_sum, outs_landed, final_out, gains, gain_line,
+    send, recv, local,
+):
+    z, c, t = lax.axis_index("fsdp"), lax.axis_index("cp"), lax.axis_index("tp")
+    beside, yonder = t + 1 - 2 * (t % 2), (t + 2) % 4
+    half = tokens.shape[0] // 2
+    last = count - 1
+    mail = Mail(send, recv)
+    greet(count)
+
+    summed = TensorSum(mail, part, own, from_core, to_yonder, from_yonder, local)
+
+    cross = [[mail.slot() for _ in range(count)] for _ in range(2)]
+    cross_own = mail.slot()
+
+    def fill_heads(hop, up, j, target):
+        side = 0 if up else 1
+        copy = pltpu.make_async_copy(qkv_grad.at[j, c], target, local.at[2])
+        copy.start()
+        mail.arrive(cross[side][hop], from_x.at[side, hop - 1], cp=1 - c)
+        copy.wait()
+
+        def one(place):
+            target[place, :] = (
+                target[place, :].astype(F32) + from_x[side, hop - 1, place, :].astype(F32)
+            ).astype(BF)
+
+        in_pieces(target.shape[0], one)
+
+    heads = Drain(
+        mail, count, fill_heads,
+        lambda side, hop: heads_sum.at[side, hop - 1],
+        lambda side, hop: heads_landed.at[side, hop - 1],
+    )
+
+    def fill_outs(hop, up, j, target):
+        copy = pltpu.make_async_copy(out_grad.at[j], target, local.at[3])
+        copy.start()
+        copy.wait()
+
+    outs = Drain(
+        mail, count, fill_outs,
+        lambda side, hop: outs_sum.at[side, hop - 1],
+        lambda side, hop: outs_landed.at[side, hop - 1],
+    )
+
+    def cross_send(hop):
+        if hop == count:
+            mail.start(cross_own, qkv_grad.at[z, 1 - c], from_x.at[0, last], cp=1 - c)
+        elif hop < count:
+            for side, up in enumerate((True, False)):
+                mail.start(
+                    cross[side][hop], qkv_grad.at[heads.block(hop, up), 1 - c],
+                    from_x.at[side, hop - 1], when=heads.sends(hop, up), cp=1 - c,
+                )
+
+    cross_send(1)
+    cross_send(2)
+    summed.begin()
+    outs.gather(1)
+    outs.send(1)
+    summed.turn()
+
+    keep = pltpu.make_async_copy(pieces.at[c], grad_tokens.at[c], local.at[0])
+    home = mail.slot()
+    gain_x, gain_y, gain_core = mail.slot(), mail.slot(), mail.slot()
+    line = Line(mail, count, gain_line.at[z], lambda j: gain_line.at[j])
+
+    def finish_rows():
+        gains[0, 0:1, :] = jnp.zeros_like(gain_rows)
+        gains[0, 1:2, :] = gain_rows[...]
+        for piece in range(2):
+            summed.arrive(piece)
+
+            def back(place, piece=piece):
+                row = pl.ds(place.start + piece * half, place.size)
+                grad, rows = norm_back(tokens[row, :].astype(F32), gain[...], summed.rows(row))
+                pieces[piece, place, :] = (grad_middle[row, :] + grad).astype(BF)
+                gains[0, 0:1, :] += jnp.sum(rows, axis=0, keepdims=True)
+
+            in_pieces(half, back)
+        mail.start(home, pieces.at[1 - c], grad_tokens.at[c], cp=1 - c)
+        keep.start()
+        mail.start(gain_core, gains.at[0], gains.at[1], tp=beside)
+
+    def gain_step(k):
+        if k == 0:
+            mail.arrive(gain_core, gains.at[1], tp=beside)
+            gains[2] = gains[0] + gains[1]
+            mail.start(gain_y, gains.at[2], gains.at[3], tp=yonder)
+        elif k == 1:
+            mail.arrive(gain_y, gains.at[3], tp=yonder)
+            gains[4] = gains[2] + gains[3]
+            mail.start(gain_x, gains.at[4], gains.at[5], cp=1 - c)
+        elif k == 2:
+            mail.arrive(gain_x, gains.at[5], cp=1 - c)
+            gain_line[z] = gains[4] + gains[5]
+            if count > 1:
+                line.send(1)
+        else:
+            hop = k - 2
+            line.arrive(hop)
+            if hop + 1 < count:
+                line.send(hop + 1)
+
+    for hop in range(1, count):
+        if hop > 1:
+            heads.arrive(hop - 1)
+        heads.gather(hop)
+        heads.send(hop)
+        cross_send(hop + 2)
+        if hop > 1:
+            outs.arrive(hop - 1)
+            outs.gather(hop)
+            outs.send(hop)
+        if hop == 1:
+            finish_rows()
+        if hop == 2:
+            gain_step(0)
+            gain_step(1)
+    if count == 1:
+        finish_rows()
+    if count <= 2:
+        gain_step(0)
+        gain_step(1)
+    gain_step(2)
+
+    own_copy = pltpu.make_async_copy(qkv_grad.at[z, c], from_x.at[1, last], local.at[2])
+    own_copy.start()
+    out_copy = pltpu.make_async_copy(out_grad.at[z], final_out, local.at[3])
+    out_copy.start()
+    mail.arrive(cross_own, from_x.at[0, last], cp=1 - c)
+    own_copy.wait()
+    out_copy.wait()
+
+    def start_heads(place):
+        qkv_total[place, :] = from_x[0, last, place, :].astype(F32) + from_x[
+            1, last, place, :
+        ].astype(F32)
+
+    in_pieces(qkv_total.shape[0], start_heads)
+
+    def start_outs(place):
+        out_total[place, :] = final_out[place, :].astype(F32)
+
+    in_pieces(out_total.shape[0], start_outs)
+    for hop in range(1, count):
+        gain_step(2 + hop)
+    if count > 1:
+        outs.arrive(last)
+        heads.arrive(last)
+        for drain, total in ((outs, out_total), (heads, qkv_total)):
+            for side, up in enumerate((True, False)):
+
+                def more(drain=drain, total=total, side=side):
+                    landed = drain.landed(side, last)
+
+                    def one(place):
+                        total[place, :] += landed[place, :].astype(F32)
+
+                    in_pieces(total.shape[0], one)
+
+                pl.when(drain.gets(last, up))(more)
+    gain_sums[...] = jnp.sum(gain_line[...], axis=0)
+    mail.arrive(home, grad_tokens.at[1 - c], cp=1 - c)
+    keep.wait()
+    mail.finish()
+
+
+def last_sum(count, part, qkv_grad, out_grad, tokens, grad_middle, gain, gain_rows):
+    slots = 8 * count + 16
+    rows, width = tokens.shape
+    hops = max(count - 1, 1)
+    block, out_block = qkv_grad.shape[2:], out_grad.shape[1:]
+    anywhere = pl.BlockSpec(memory_space=pl.ANY)
+    vmem = pl.BlockSpec(memory_space=pltpu.VMEM)
+    return pl.pallas_call(
+        functools.partial(last_sum_kernel, count),
+        out_shape=(
+            jax.ShapeDtypeStruct(block, F32),
+            jax.ShapeDtypeStruct(out_block, F32),
+            jax.ShapeDtypeStruct((2, rows // 2, width), BF),
+            jax.ShapeDtypeStruct((2, width), F32),
+        ),
+        in_specs=[anywhere] * 3 + [vmem] * 4,
+        out_specs=(vmem, vmem, anywhere, vmem),
+        scratch_shapes=[
+            pltpu.VMEM((2, rows, width), BF),
+            pltpu.VMEM((2, rows, width), BF),
+            pltpu.VMEM((rows, width), BF),
+            pltpu.VMEM((rows, width), BF),
+            pltpu.VMEM((2, rows // 2, width), BF),
+            pltpu.VMEM((2, count) + block, BF),
+            pltpu.VMEM((2, hops) + block, BF),
+            pltpu.VMEM((2, hops) + block, BF),
+            pltpu.VMEM((2, hops) + out_block, BF),
+            pltpu.VMEM((2, hops) + out_block, BF),
+            pltpu.VMEM(out_block, BF),
+            pltpu.VMEM((6, 2, width), F32),
+            pltpu.VMEM((count, 2, width), F32),
+            pltpu.SemaphoreType.DMA((slots,)),
+            pltpu.SemaphoreType.DMA((slots,)),
+            pltpu.SemaphoreType.DMA((4,)),
+        ],
+        compiler_params=pltpu.CompilerParams(
+            collective_id=4, has_side_effects=True, vmem_limit_bytes=60 << 20
+        ),
+    )(part, qkv_grad, out_grad, tokens, grad_middle, gain, gain_rows)
+
+
 def normalize(values):
     return values * lax.rsqrt(jnp.mean(values * values, axis=-1, keepdims=True) + EPSILON)
-
-
-def scaled_norm(values, gain_values):
-    return normalize(values) * gain_values
 
 
 def silu_product(gate_pre, up_pre):
@@ -658,61 +1166,6 @@
         place == 0,
         jnp.concatenate([mine, other], axis=axis),
         jnp.concatenate([other, mine], axis=axis),
-    )
-
-
-def gather_line(block, gates=None):
-    count = lax.axis_size("fsdp")
-    z = lax.axis_index("fsdp")
-    from_low, from_high = [], []
-    low = high = block
-    for step in range(1, count):
-        if gates is not None and step - 1 < len(gates):
-            low, high = after((low, high), *gates[step - 1])
-        low = lax.ppermute(low, "fsdp", [(i, i + 1) for i in range(step - 1, count - 1)])
-        high = lax.ppermute(high, "fsdp", [(i, i - 1) for i in range(1, count - step + 1)])
-        from_low.append(low)
-        from_high.append(high)
-    blocks = [block]
-    for step in range(1, count):
-        blocks.append(jnp.where(z >= step, from_low[step - 1], from_high[count - step - 1]))
-    return blocks, list(zip(from_low, from_high))
-
-
-def placed(blocks, axis=0):
-    count = lax.axis_size("fsdp")
-    z = lax.axis_index("fsdp")
-    rows = blocks[0].shape[axis]
-    shape = list(blocks[0].shape)
-    shape[axis] = rows * count
-    full = jnp.zeros(shape, blocks[0].dtype)
-    for step, block in enumerate(blocks):
-        start = lax.rem(z - step + count, count) * rows
-        full = lax.dynamic_update_slice_in_dim(full, block, start, axis)
-    return full
-
-
-def reduce_line(part):
-    count = lax.axis_size("fsdp")
-    z = lax.axis_index("fsdp")
-    low = high = None
-    for step in range(1, count):
-        up_part = part(jnp.clip(z + count - step, 0, count - 1))
-        down_part = part(jnp.clip(z - count + step, 0, count - 1))
-        if low is not None:
-            up_part = (up_part.astype(F32) + low.astype(F32)).astype(BF)
-            down_part = (down_part.astype(F32) + high.astype(F32)).astype(BF)
-        low = lax.ppermute(up_part, "fsdp", [(i, i + 1) for i in range(0, step)])
-        high = lax.ppermute(down_part, "fsdp", [(i, i - 1) for i in range(count - step, count)])
-    total = part(z).astype(F32)
-    if low is not None:
-        total = total + low.astype(F32) + high.astype(F32)
-    return total
-
-
-def farthest_first(count):
-    return np.array(
-        [sorted(range(count), key=lambda j: (-abs(j - z), j)) for z in range(count)], np.int32
     )
 
 
@@ -760,8 +1213,8 @@
         return in_order(c, mine[None], other[None], 0)
 
     token_rows = to_sequence(tokens)
-    inputs = token_rows.astype(F32)
-    upstream = to_sequence(cotangent).astype(F32)
+    cotangent_rows = to_sequence(cotangent)
+    upstream = cotangent_rows.astype(F32)
     length = pick(seq_lengths, c)[None]
     gain_one = attention_gain.astype(F32)
     gain_two = feedforward_gain.astype(F32)
@@ -795,86 +1248,77 @@
     )
     normed_two = normed_two.reshape(sets * seq, width)
     full_gate, full_up, full_down = full_wide.reshape(3, width, hidden_width)
-    _, norm_two_back = jax.vjp(scaled_norm, middle, gain_two)
-    _, norm_one_back = jax.vjp(scaled_norm, inputs, gain_one)
     grad_branch = lax.all_gather((BRANCH * upstream).astype(BF), everyone, axis=0, tiled=True)
     gate_pre = matmul(normed_two, full_gate)
     up_pre = matmul(normed_two, full_up)
     hidden_exact, silu_back = jax.vjp(silu_product, gate_pre, up_pre)
     hidden = hidden_exact.astype(BF)
 
-    def line_part(gradient):
-        pieces = gradient.reshape(count, gradient.shape[0] // count, gradient.shape[1])
-        return lambda j: pick(pieces, j)
-
-    def reduced_halves(gradient):
-        total = reduce_line(line_part(gradient))
-        total = total.reshape(sets, share, hidden_width)
-        mine = pick(total, c)
-        other = swap(pick(total, 1 - c).astype(BF)).astype(F32)
-        return in_order(c, mine, other, 1)
-
-    grad_down = reduced_halves(rows_inner(grad_branch, hidden).astype(BF)).T
+    def blocks_of(gradient):
+        return gradient.astype(BF).reshape(count, width // count, hidden_width)
+
+    down_blocks = blocks_of(rows_inner(grad_branch, hidden))
     grad_hidden = matmul(grad_branch, full_down)
     grad_gate_exact, grad_up_exact = silu_back(grad_hidden)
     grad_gate_pre = grad_gate_exact.astype(BF)
     grad_up_pre = grad_up_exact.astype(BF)
     grad_normed_two = cols_inner(grad_gate_pre, full_gate) + cols_inner(grad_up_pre, full_up)
-    grad_norm_two = lax.psum_scatter(
-        grad_normed_two.astype(BF), everyone, scatter_dimension=0, tiled=True
-    ).astype(F32)
-    grad_gate = reduced_halves(rows_inner(normed_two, grad_gate_pre).astype(BF))
-    grad_up = reduced_halves(rows_inner(normed_two, grad_up_pre).astype(BF))
-
-    grad_middle_norm, grad_gain_two = norm_two_back(grad_norm_two)
-    grad_middle = upstream + grad_middle_norm
-    grad_attention = lax.all_gather((BRANCH * grad_middle).astype(BF), "tp", axis=0, tiled=True)
-
+    gate_blocks = blocks_of(rows_inner(normed_two, grad_gate_pre))
+    up_blocks = blocks_of(rows_inner(normed_two, grad_up_pre))
+    grad_middle, grad_attention, gain_two_rows, leaving = first_sum(
+        count, grad_normed_two.astype(BF).reshape(sets, lanes, rows, width),
+        gate_blocks, up_blocks, down_blocks, middle, cotangent_rows, gain_two[None],
+    )
+    grad_attention = grad_attention.reshape(seq, width)
+
+    low = lax.ppermute(leaving[0], "fsdp", [(i, i + 1) for i in range(count - 1)])
+    high = lax.ppermute(leaving[1], "fsdp", [(i, i - 1) for i in range(1, count)])
+
+    def own_share(which, gradient):
+        total = pick(gradient, z).astype(F32)
+        if count > 1:
+            total = total + low[which].astype(F32) + high[which].astype(F32)
+        return total.reshape(sets, share, hidden_width)
+
+    shares = [
+        own_share(which, gradient)
+        for which, gradient in enumerate((gate_blocks, up_blocks, down_blocks))
+    ]
+    others = swap(jnp.stack([pick(total, 1 - c).astype(BF) for total in shares]))
+    grad_gate, grad_up, grad_down = (
+        in_order(c, pick(total, c), others[which].astype(F32), 1)
+        for which, total in enumerate(shares)
+    )
+    grad_down = grad_down.T
+
+    out_pieces = rows_inner(grad_attention, context).astype(BF)
+    out_pieces = out_pieces.reshape(count, sets, share, heads_width)
+    out_pieces = (
+        pick(out_pieces, c, 1).astype(F32) + swap(pick(out_pieces, 1 - c, 1)).astype(F32)
+    ).astype(BF)
+    grad_context = matmul(grad_attention, full_out).astype(BF)
     feedforward = lax.psum_scatter(
-        after(cols_inner(hidden, full_down).astype(BF), grad_attention),
+        cols_inner(after(hidden, grad_attention), full_down).astype(BF),
         everyone, scatter_dimension=0, tiled=True,
     )
     output = from_sequence((middle + BRANCH * feedforward.astype(F32)).astype(BF))
-
-    order = jnp.asarray(farthest_first(count))[z]
-
-    def reduced_rows(gradient):
-        pieces = gradient.reshape(count, sets, share, gradient.shape[1])
-        mine = pick(pieces, c, 1)
-        other = pick(pieces, 1 - c, 1)
-        summed = []
-        for k in range(count):
-            got = swap(pick(other, order[k]))
-            summed.append((pick(mine, order[k]).astype(F32) + got.astype(F32)).astype(BF))
-
-        def part(j):
-            found = summed[0]
-            for k in range(1, count):
-                found = jnp.where(order[k] == j, summed[k], found)
-            return found
-
-        return reduce_line(part)
-
-    grad_out = reduced_rows(rows_inner(grad_attention, context).astype(BF)).T
-    grad_context = matmul(grad_attention, full_out).astype(BF)
     grad_projected = attention_back(
         blocks, head_count, length, grad_context, q_heads, k_heads, v_heads, level,
         cosine_table, sine_table,
     )
-    grad_qkv = reduced_rows(rows_inner(normed_one, grad_projected).astype(BF))
-    grad_norm_one = lax.psum_scatter(
-        cols_inner(grad_projected, full_qkv).astype(BF), "tp", scatter_dimension=0, tiled=True
-    ).astype(F32)
-    grad_inputs_norm, grad_gain_one = norm_one_back(grad_norm_one)
-    grad_tokens = from_sequence((grad_middle + grad_inputs_norm).astype(BF))
-    gain_sums = lax.psum(jnp.stack([grad_gain_one, grad_gain_two]), ("fsdp", "cp", "tp"))
+    grad_qkv = rows_inner(normed_one, grad_projected).astype(BF)
+    grad_qkv, grad_out, grad_tokens, gain_sums = last_sum(
+        count, cols_inner(grad_projected, full_qkv).astype(BF).reshape(lanes, rows, width),
+        grad_qkv.reshape(count, sets, share, 3 * heads_width), out_pieces,
+        token_rows, grad_middle, gain_one[None], gain_two_rows,
+    )
     return (
         output,
         grad_tokens,
         grad_qkv[:, :heads_width],
         grad_qkv[:, heads_width : 2 * heads_width],
         grad_qkv[:, 2 * heads_width :],
-        grad_out,
+        grad_out.T,
         gain_sums[0],
         grad_gate,
         grad_up,

time: 1170 us -> 952 us (0.81)
  waiting for transfers between devices: 269 us -> 19.6 us
  Pallas kernels: 358 us -> 601 us
  starting transfers between devices: 115 us -> 19.9 us
  blocking collectives: 53.4 us -> 0 us
  other arithmetic: 77.3 us -> 30.4 us
  between operations: 36.7 us -> 15.2 us
    pallas_call x0 -> x2, Pallas kernels: none -> 243 us  [the longest x1 123 us: first_sum(): pl.pallas_call(functools.partial(first_sum_kernel, count), out_shape=(jax...]
    ppermute x17 -> x7, waiting for transfers between devices: 108 us -> 19.6 us  [swap(): return lax.ppermute(value, 'cp', [(0, 1), (1, 0)])]
    ppermute x30 -> x2, starting transfers between devices: 91.9 us -> 9.88 us  [the longest x1 8.6 us: on_device(): lax.ppermute(leaving[0], 'fsdp', [(i, i + 1) for i in range(count - 1)])]
    reduce_scatter x3 -> x1, waiting for transfers between devices: 74.9 us -> 0.01 us  [on_device(): lax.psum_scatter(cols_inner(after(hidden, grad_attention), full_down).ast...]
    psum x1 -> x0, blocking collectives: 53.4 us -> none  [on_device(): lax.psum(jnp.stack([grad_gain_one, grad_gain_two]), ('fsdp', 'cp', 'tp'))]
    ppermute x30 -> x2, waiting for transfers between devices: 48.2 us -> 0.01 us  [the longest x1 0.01 us: on_device(): lax.ppermute(leaving[0], 'fsdp', [(i, i + 1) for i in range(count - 1)])]
    all_gather x1 -> x0, waiting for transfers between devices: 37.6 us -> none  [on_device(): lax.all_gather((BRANCH * grad_middle).astype(BF), 'tp', axis=0, tiled=True)]
    convert_element_type x21 -> x3, other arithmetic: 36.3 us -> 7.4 us  [the longest x1 2.87 us: on_device(): out_pieces = (pick(out_pieces, c, 1).astype(F32) + swap(pick(out_pieces,...]
  transfers between devices with their start and end apart: 52 -> 11, of which waited for: 18 -> 3; matrix products, arithmetic and copies ran while one was open for 19% -> 17% of each run, Pallas kernels for 28% -> 51%
where the time goes in v2:
time: 952 us; the launch traced here: 945 us
  Pallas kernels  601 us (63%)
  matrix products  173 us (18%)
  local copies, waits for them, and re-layouts  85.3 us (9%)
  other arithmetic  30.4 us (3%)
  starting transfers between devices  19.9 us (2%)
  waiting for transfers between devices  19.6 us (2%)
  between operations  15.2 us (2%)
    pallas_call x1, Pallas kernels, second_gather(): pl.pallas_call(functools.partial(second_gather_kernel, count), out_shape=...  147 us
    pallas_call x1, Pallas kernels, first_gather(): pl.pallas_call(functools.partial(first_gather_kernel, count), out_shape=(...  137 us
    pallas_call x1, Pallas kernels, first_sum(): pl.pallas_call(functools.partial(first_sum_kernel, count), out_shape=(jax...  123 us
    pallas_call x1, Pallas kernels, last_sum(): pl.pallas_call(functools.partial(last_sum_kernel, count), out_shape=(jax....  120 us
    dot_general x5, matrix products, matmul(): return jnp.dot(left, right, preferred_element_type=F32)  63.4 us
    dot_general x5, matrix products, rows_inner(): lax.dot_general(left, right, (((0,), (0,)), ((), ())), preferred_element_...  55.2 us
    dot_general x5, matrix products, cols_inner(): lax.dot_general(left, right, (((1,), (1,)), ((), ())), preferred_element_...  54.3 us
    pallas_call x1, Pallas kernels, attention_back(): pl.pallas_call(functools.partial(attention_back_kernel, blocks), out_shap...  39.7 us
  transfers between devices with their start and end apart: 11, of which 3 were waited for; matrix products, arithmetic and copies ran while one was open for 17% of the time, Pallas kernels for 51%

profile of v2, /device:TPU:0, one launch (start us, length us, event | category | flops | bytes accessed | tf_op | source)
XLA Modules:
  0.0 944.8 jit_solution(9164123746693396460)
XLA Ops:
  11.6 13.3 %collective-permute-done.3 = bf16[128,2304]{1,0:T(8,128)(2,1)S(1)} collective-permute-done((bf16[128,2304]{1,0:T(8,128)(2,1)S(1)}, bf16[128,2304]{1,0:T(8,128)(2,1)S(1)}, u32[]{:S(2)}, u32[]{:S(2)}) %collective-permute-start.3) | collective-permute-done | bytes 589856 | tf_op jit(solution)/shard_map/ppermute | solution.py:1161
  45.2 136.9 %shard_map.203 = (bf16[4,2,128,2304]{3,2,1,0:T(8,128)(2,1)}, bf16[4,2,288,1728]{3,2,1,0:T(8,128)(2,1)}, bf16[4,288,576]{2,1,0:T(8,128)(2,1)}, bf16[3,288,720]{2,1,0:T(8,128)(2,1)}, bf16[3,288,720]{2,1,0:T(8,128)(2,1)}) custom-call(bf16[2,128,2304]{2,1,0:T(8,128)(2,1)} %fusion.3.normed, bf16[288,1728]{1,0:T(8,128)(2,1)} %concatenate.49.qkv, ...), custom_call_target="tpu_custom_call" | custom-call | tf_op jit(solution)/shard_map/pallas_call | solution.py:413
  184.3 14.7 %fusion.13.projected = f32[1024,1728]{1,0:T(8,128)} fusion(bf16[1024,2304]{1,0:T(8,128)(2,1)} %bitcast.148, bf16[2304,1728]{1,0:T(8,128)(2,1)} %bitcast.144), kind=kOutput, calls=%fused_computation.73 | convolution fusion | flops 8153726976 | bytes 19759104 | tf_op jit(solution)/shard_map/dot_general | solution.py:1145
  205.9 34.7 %shard_map.204 = (bf16[1024,576]{1,0:T(8,128)(2,1)S(1)}, bf16[9,1024,64]{2,1,0:T(8,128)(2,1)S(1)}, bf16[9,1024,64]{2,1,0:T(8,128)(2,1)}, bf16[9,1024,64]{2,1,0:T(8,128)(2,1)}, f32[9,1,1024]{2,1,0:T(1,128)S(1)}) custom-call(s32[1]{0:T(128)} %dynamic_slice.66.length_ref, f32[1024,1728]{1,0:T(8,128)} %fusion.13.projected, f32[1024,128]{1,0:T(8,128)S(1)} %copy.53.cosine, ...), custom_call_target="tpu_custom_call" | custom-call | flops 2415919104 | bytes 20971520 | tf_op jit(solution)/shard_map/pallas_call | solution.py:106
  251.8 146.6 %shard_map.205 = (f32[256,2304]{1,0:T(8,128)S(1)}, bf16[2,4,2,128,2304]{4,3,2,1,0:T(8,128)(2,1)}, bf16[3,4,2,288,720]{4,3,2,1,0:T(8,128)(2,1)}) custom-call(bf16[4,256,2304]{2,1,0:T(8,128)(2,1)S(1)} %bitcast.105, bf16[256,2304]{1,0:T(8,128)(2,1)S(1)} %maximum_select_fusion.4.tokens, f32[1,2304]{1,0:T(1,128)S(1)} %reshape.176.gain, ...), custom_call_target="tpu_custom_call" | custom-call | tf_op jit(solution)/shard_map/pallas_call | solution.py:602
  406.8 11.3 %fusion.14 = f32[2048,720]{0,1:T(8,128)} fusion(bf16[2048,2304]{1,0:T(8,128)(2,1)} %bitcast.140, bf16[2304,720]{1,0:T(8,128)(2,1)S(1)} %bitcast.128), kind=kOutput, calls=%fused_computation.74 | convolution fusion | flops 6794772480 | bytes 18653184 | tf_op jit(solution)/shard_map/dot_general | solution.py:1145
  418.2 11.3 %fusion.15 = f32[2048,720]{0,1:T(8,128)} fusion(bf16[2048,2304]{1,0:T(8,128)(2,1)} %all-gather.2.cloned.1.call-done, bf16[2304,720]{1,0:T(8,128)(2,1)S(1)} %bitcast.124), kind=kOutput, calls=%fused_computation.75 | convolution fusion | flops 6794772480 | bytes 18653184 | tf_op jit(solution)/shard_map/dot_general | solution.py:1145
  429.5 18.9 %add_convert_fusion.1 = (bf16[2048,720]{0,1:T(8,128)(2,1)}, bf16[2048,720]{0,1:T(8,128)(2,1)}, bf16[2048,720]{0,1:T(8,128)(2,1)}) fusion(f32[2048,720]{0,1:T(8,128)} %fusion.15, f32[2048,720]{0,1:T(8,128)} %fusion.14, bf16[2048,2304]{1,0:T(8,128)(2,1)} %bitcast.141, bf16[2304,720]{1,0:T(8,128)(2,1)} %bitcast.126), kind=kOutput, calls=%fused_computation.4 | convolution fusion | flops 6821314560 | bytes 33398784 | tf_op jit(solution)/shard_map/dot_general | solution.py:1145
  448.4 12.7 %convolution_convert_fusion.5 = bf16[2304,720]{0,1:T(8,128)(2,1)} fusion(bf16[2048,720]{0,1:T(8,128)(2,1)} %get-tuple-element.64, bf16[2048,2304]{1,0:T(8,128)(2,1)} %bitcast.142), kind=kOutput, calls=%fused_computation.11 | convolution fusion | flops 6796431360 | bytes 15704064 | tf_op jit(solution)/shard_map/dot_general | solution.py:1149
  461.1 11.1 %fusion.16 = f32[2048,2304]{1,0:T(8,128)} fusion(bf16[2048,720]{0,1:T(8,128)(2,1)S(1)} %copy-done.37, bf16[2304,720]{1,0:T(8,128)(2,1)S(1)} %bitcast.129), kind=kOutput, calls=%fused_computation.76 | convolution fusion | flops 6794772480 | bytes 25141248 | tf_op jit(solution)/shard_map/dot_general | solution.py:1153
  472.2 8.9 convolution_convert_fusion.4
  486.9 12.6 %convolution_convert_fusion.6 = bf16[2304,720]{0,1:T(8,128)(2,1)} fusion(bf16[2048,720]{0,1:T(8,128)(2,1)} %get-tuple-element.63, bf16[2048,2304]{1,0:T(8,128)(2,1)} %bitcast.143), kind=kOutput, calls=%fused_computation.12 | convolution fusion | flops 6796431360 | bytes 15704064 | tf_op jit(solution)/shard_map/dot_general | solution.py:1149
  510.8 15.2 %add_convert_fusion = bf16[2048,2304]{1,0:T(8,128)(2,1)} fusion(f32[2048,2304]{1,0:T(8,128)} %fusion.16, bf16[2048,720]{0,1:T(8,128)(2,1)} %get-tuple-element.63, bf16[2304,720]{1,0:T(8,128)(2,1)} %bitcast.127), kind=kOutput, calls=%fused_computation | convolution fusion | flops 6804209664 | bytes 34578432 | tf_op jit(solution)/shard_map/dot_general | solution.py:1153
  526.1 123.3 %shard_map.206 = (f32[256,2304]{1,0:T(8,128)}, bf16[4,2,128,2304]{3,2,1,0:T(8,128)(2,1)}, f32[1,2304]{1,0:T(1,128)}, bf16[2,3,576,720]{3,2,1,0:T(8,128)(2,1)}) custom-call(bf16[2,4,256,2304]{3,2,1,0:T(8,128)(2,1)} %bitcast.115, bf16[4,576,720]{2,1,0:T(8,128)(2,1)} %bitcast.111, bf16[4,576,720]{2,1,0:T(8,128)(2,1)} %bitcast.109, ...), custom_call_target="tpu_custom_call" | custom-call | tf_op jit(solution)/shard_map/pallas_call | solution.py:894
  649.3 12.0 %convolution_convert_fusion.1 = bf16[2048,2304]{1,0:T(8,128)(2,1)} fusion(bf16[2048,720]{0,1:T(8,128)(2,1)} %get-tuple-element.47, bf16[2304,720]{1,0:T(8,128)(2,1)S(1)} %bitcast.125), kind=kOutput, calls=%fused_computation.2 | convolution fusion | flops 6799491072 | bytes 15704064 | tf_op jit(solution)/shard_map/dot_general | solution.py:1153
  662.7 6.8 convolution_convert_fusion.7
  673.6 7.2 slice_bitcast_fusion.1
  680.8 8.6 collective-permute-start.6
  690.7 7.1 convolution_convert_fusion.8
  703.3 39.7 %shard_map.207 = bf16[1024,1728]{1,0:T(8,128)(2,1)} custom-call(s32[1]{0:T(128)} %dynamic_slice.66.length_ref, bf16[1024,576]{1,0:T(8,128)(2,1)} %copy.58.grad_context, bf16[9,1024,64]{2,1,0:T(8,128)(2,1)} %copy-done.9, bf16[9,1024,64]{2,1,0:T(8,128)(2,1)} %get-tuple-element.49.k_heads, bf16[9,1024,64]{2,1,0:T(8,128)(2,1)} %get-tuple-element.50.v_heads, ...), custom_call_target="tpu_custom_call" | custom-call | flops 6039797760 | bytes 20971520 | tf_op jit(solution)/shard_map/pallas_call | solution.py:185
  743.0 14.2 %convolution_convert_fusion = bf16[2304,1728]{0,1:T(8,128)(2,1)} fusion(bf16[1024,2304]{1,0:T(8,128)(2,1)} %bitcast.149, bf16[1024,1728]{1,0:T(8,128)(2,1)} %shard_map.207), kind=kOutput, calls=%fused_computation.1 | convolution fusion | flops 8157708288 | bytes 16220160 | tf_op jit(solution)/shard_map/dot_general | solution.py:1149
  765.6 11.9 %convolution_convert_fusion.2 = bf16[1024,2304]{1,0:T(8,128)(2,1)} fusion(bf16[1024,1728]{1,0:T(8,128)(2,1)} %shard_map.207, bf16[2304,1728]{1,0:T(8,128)(2,1)S(1)} %bitcast.147), kind=kOutput, calls=%fused_computation.8 | convolution fusion | flops 8156086272 | bytes 16220160 | tf_op jit(solution)/shard_map/dot_general | solution.py:1153
  777.5 11.6 %copy.60 = bf16[2304,1728]{1,0:T(8,128)(2,1)} copy(bf16[2304,1728]{0,1:T(8,128)(2,1)} %convolution_convert_fusion) | data formatting | bytes 15925248 | tf_op jit(solution)/shard_map/convert_element_type | solution.py:1309
  792.0 120.2 %shard_map.208 = (f32[288,1728]{1,0:T(8,128)}, f32[288,576]{1,0:T(8,128)}, bf16[2,128,2304]{2,1,0:T(8,128)(2,1)}, f32[2,2304]{1,0:T(2,128)}) custom-call(bf16[4,256,2304]{2,1,0:T(8,128)(2,1)} %bitcast.123, bf16[4,2,288,1728]{3,2,1,0:T(8,128)(2,1)} %bitcast.106, bf16[4,288,576]{2,1,0:T(8,128)(2,1)} %fusion.out_grad, bf16[256,2304]{1,0:T(8,128)(2,1)} %copy-done.1, ...), custom_call_target="tpu_custom_call" | custom-call | tf_op jit(solution)/shard_map/pallas_call | solution.py:1102
  (165 shorter events, 118.7 us)
Async XLA Ops:
  7.2 411.0 %all-gather.2.cloned.1.call-start = ((), (), s32[]{:S(2)}) async-start(), calls=%async_computation.1 | async-start | bytes 10616832 | tf_op jit(solution)/shard_map/all_gather | solution.py:1251
  8.6 18.2 %copy-start.13 = (bf16[2,128,2304]{2,1,0:T(8,128)(2,1)S(1)}, bf16[2,128,2304]{2,1,0:T(8,128)(2,1)}, u32[]{:S(2)}) copy-start(bf16[2,128,2304]{2,1,0:T(8,128)(2,1)} %param.12) | copy-start | bytes 3538948
  8.6 16.3 %collective-permute-start.3 = (bf16[128,2304]{1,0:T(8,128)(2,1)S(1)}, bf16[128,2304]{1,0:T(8,128)(2,1)S(1)}, u32[]{:S(2)}, u32[]{:S(2)}) collective-permute-start(bf16[128,2304]{1,0:T(8,128)(2,1)S(1)} %get-tuple-element.84), channel_id=1, source_target_pairs={{0,4},{4,0},{1,5},{5,1},{2,6},{6,2},{3,7},{7,3},{8,12},{12,8},{9,1... | collective-permute-start | bytes 1769480 | tf_op jit(solution)/shard_map/ppermute | solution.py:1161
  26.7 894.7 %reduce-scatter.2.cloned.1.call-start = ((), (), s32[]{:S(2)}) async-start(), calls=%async_computation.2 | async-start | bytes 10616832 | tf_op jit(solution)/shard_map/reduce_scatter | solution.py:1300
  27.7 213.1 %collective-permute-start.1 = (bf16[128,2304]{1,0:T(8,128)(2,1)}, bf16[128,2304]{1,0:T(8,128)(2,1)}, u32[]{:S(2)}, u32[]{:S(2)}) collective-permute-start(bf16[128,2304]{1,0:T(8,128)(2,1)} %get-tuple-element.87), channel_id=1, source_target_pairs={{0,4},{4,0},{1,5},{5,1},{2,6},{6,2},{3,7},{7,3},{8,12},{12,8},{9,1... | collective-permute-start | bytes 1769480 | tf_op jit(solution)/shard_map/ppermute | solution.py:1161
  182.2 69.6 %collective-permute-start.2 = (bf16[3,288,720]{2,1,0:T(8,128)(2,1)}, bf16[3,288,720]{2,1,0:T(8,128)(2,1)S(1)}, u32[]{:S(2)}, u32[]{:S(2)}) collective-permute-start(bf16[3,288,720]{2,1,0:T(8,128)(2,1)} %get-tuple-element.42), channel_id=1, source_target_pairs={{0,4},{4,0},{1,5},{5,1},{2,6},{6,2},{3,7},{7,3},{8,12},{12,8},{9,1... | collective-permute-start | bytes 3732488 | tf_op jit(solution)/shard_map/ppermute | solution.py:1161
  183.7 61.0 %collective-permute-start = (bf16[4,288,576]{2,1,0:T(8,128)(2,1)}, bf16[4,288,576]{2,1,0:T(8,128)(2,1)}, u32[]{:S(2)}, u32[]{:S(2)}) collective-permute-start(bf16[4,288,576]{2,1,0:T(8,128)(2,1)} %get-tuple-element.39), channel_id=1, source_target_pairs={{0,4},{4,0},{1,5},{5,1},{2,6},{6,2},{3,7},{7,3},{8,12},{12,8},{9,1... | collective-permute-start | bytes 3981320 | tf_op jit(solution)/shard_map/ppermute | solution.py:1161
  184.3 14.7 %copy-start.36 = (s32[2]{0:T(128)S(1)}, s32[2]{0:T(128)}, u32[]{:S(2)}) copy-start(s32[2]{0:T(128)} %param.13) | copy-start | bytes 28
  184.3 15.3 %copy-start.35 = (bf16[2304]{0:T(1024)(128)(2,1)S(1)}, bf16[2304]{0:T(1024)(128)(2,1)}, u32[]{:S(2)}) copy-start(bf16[2304]{0:T(1024)(128)(2,1)} %param.19) | copy-start | bytes 13828
  199.6 52.1 %copy-start.8 = (f32[1,2304]{1,0:T(1,128)}, f32[1,2304]{1,0:T(1,128)S(1)}, u32[]{:S(2)}) copy-start(f32[1,2304]{1,0:T(1,128)S(1)} %reshape.176.gain) | copy-start | bytes 27652
  205.4 35.3 %copy-start.7 = (f32[1024,128]{1,0:T(8,128)}, f32[1024,128]{1,0:T(8,128)S(1)}, u32[]{:S(2)}) copy-start(f32[1024,128]{1,0:T(8,128)S(1)} %copy.53.cosine) | copy-start | bytes 1572868
  205.9 34.8 %copy-start.6 = (f32[1024,128]{1,0:T(8,128)}, f32[1024,128]{1,0:T(8,128)S(1)}, u32[]{:S(2)}) copy-start(f32[1024,128]{1,0:T(8,128)S(1)} %pad_maximum_fusion.1.sine) | copy-start | bytes 1572868
  448.4 12.7 %copy-start.26 = (bf16[1,4,2,288,720]{4,3,2,1,0:T(8,128)(2,1)S(1)}, bf16[1,4,2,288,720]{4,3,2,1,0:T(8,128)(2,1)}, u32[]{:S(2)}) copy-start(bf16[1,4,2,288,720]{4,3,2,1,0:T(8,128)(2,1)} %copy-done.25) | copy-start | bytes 9953284
  448.4 12.7 %copy-start.37 = (bf16[2048,720]{0,1:T(8,128)(2,1)S(1)}, bf16[2048,720]{0,1:T(8,128)(2,1)}, u32[]{:S(2)}) copy-start(bf16[2048,720]{0,1:T(8,128)(2,1)} %get-tuple-element.64) | copy-start | bytes 8847364
  448.4 23.8 %slice-start = ((s8[9437184]{0:T(1024)(128)(4,1)}), s8[4194304]{0:T(1024)(128)(4,1)S(1)}, s32[]{:S(2)}) async-start(s8[9437184]{0:T(1024)(128)(4,1)} %bitcast.138), calls=%async_computation.3 | async-start | bytes 8388608
  448.4 23.8 %slice-start.1 = ((s8[9437184]{0:T(1024)(128)(4,1)}), s8[4194304]{0:T(1024)(128)(4,1)S(1)}, s32[]{:S(2)}) async-start(s8[9437184]{0:T(1024)(128)(4,1)} %bitcast.138), calls=%async_computation.4 | async-start | bytes 8388608
  673.6 17.1 %copy-start.28 = (bf16[4,2,288,576]{3,2,1,0:T(8,128)(2,1)S(1)}, bf16[4,2,288,576]{3,2,1,0:T(8,128)(2,1)}, u32[]{:S(2)}) copy-start(bf16[4,2,288,576]{3,2,1,0:T(8,128)(2,1)} %copy-done.27) | copy-start | bytes 7962628
  680.8 76.4 %collective-permute-start.6 = (bf16[3,576,720]{2,1,0:T(8,128)(2,1)}, bf16[3,576,720]{2,1,0:T(8,128)(2,1)}, u32[]{:S(2)}, u32[]{:S(2)}) collective-permute-start(bf16[3,576,720]{2,1,0:T(8,128)(2,1)} %get-tuple-element.72), channel_id=1, source_target_pairs={{0,8},{8,16},{16,24},{1,9},{9,17},{17,25},{2,10},{10,18},{18,26},{... | collective-permute-start | bytes 7464968 | tf_op jit(solution)/shard_map/ppermute | solution.py:1274
  689.4 67.8 %collective-permute-start.7 = (bf16[3,576,720]{2,1,0:T(8,128)(2,1)}, bf16[3,576,720]{2,1,0:T(8,128)(2,1)}, u32[]{:S(2)}, u32[]{:S(2)}) collective-permute-start(bf16[3,576,720]{2,1,0:T(8,128)(2,1)} %get-tuple-element.73), channel_id=1, source_target_pairs={{8,0},{16,8},{24,16},{9,1},{17,9},{25,17},{10,2},{18,10},{26,18},{... | collective-permute-start | bytes 7464968 | tf_op jit(solution)/shard_map/ppermute | solution.py:1275
  701.7 87.4 %collective-permute-start.5 = (bf16[4,288,576]{2,1,0:T(8,128)(2,1)}, bf16[4,288,576]{2,1,0:T(8,128)(2,1)}, u32[]{:S(2)}, u32[]{:S(2)}) collective-permute-start(bf16[4,288,576]{2,1,0:T(8,128)(2,1)} %dynamic-slice_bitcast_fusion), channel_id=1, source_target_pairs={{0,4},{4,0},{1,5},{5,1},{2,6},{6,2},{3,7},{7,3},{8,12},{12,8},{9,1... | collective-permute-start | bytes 3981320 | tf_op jit(solution)/shard_map/ppermute | solution.py:1161
  703.3 62.3 %slice-start.3 = ((s8[8257536]{0:T(1024)(128)(4,1)}), s8[4063232]{0:T(1024)(128)(4,1)S(1)}, s32[]{:S(2)}) async-start(s8[8257536]{0:T(1024)(128)(4,1)} %bitcast.145), calls=%async_computation.6 | async-start | bytes 8126464
  743.0 22.6 %slice-start.4 = ((s8[8257536]{0:T(1024)(128)(4,1)}), s8[4194304]{0:T(1024)(128)(4,1)S(1)}, s32[]{:S(2)}) async-start(s8[8257536]{0:T(1024)(128)(4,1)} %bitcast.145), calls=%async_computation.7 | async-start | bytes 8388608
  765.0 153.5 %collective-permute-start.8 = (bf16[3,288,720]{2,1,0:T(8,128)(2,1)}, bf16[3,288,720]{2,1,0:T(8,128)(2,1)}, u32[]{:S(2)}, u32[]{:S(2)}) collective-permute-start(bf16[3,288,720]{2,1,0:T(8,128)(2,1)} %pad_maximum_fusion), channel_id=1, source_target_pairs={{0,4},{4,0},{1,5},{5,1},{2,6},{6,2},{3,7},{7,3},{8,12},{12,8},{9,1... | collective-permute-start | bytes 3732488 | tf_op jit(solution)/shard_map/ppermute | solution.py:1161
  923.2 11.2 %collective-permute-start.4 = (bf16[128,2304]{1,0:T(8,128)(2,1)S(1)}, bf16[128,2304]{1,0:T(8,128)(2,1)S(1)}, u32[]{:S(2)}, u32[]{:S(2)}) collective-permute-start(bf16[128,2304]{1,0:T(8,128)(2,1)S(1)} %get-tuple-element.83), channel_id=1, source_target_pairs={{0,4},{4,0},{1,5},{5,1},{2,6},{6,2},{3,7},{7,3},{8,12},{12,8},{9,1... | collective-permute-start | bytes 1769480 | tf_op jit(solution)/shard_map/ppermute | solution.py:1161
  (31 other events, 140.0 us)
Sparse Core Ops, SparseCore 0:
  26.8 96.0 all-gather.1
  661.5 103.3 reduce-scatter.1

commit v3 on v2

--- a/solution.py
+++ b/solution.py
@@ -6,6 +6,7 @@
 import numpy as np
 from jax import lax
 from jax.experimental import pallas as pl
+from jax.experimental.layout import Layout, with_layout_constraint
 from jax.experimental.pallas import tpu as pltpu
 from jax.sharding import PartitionSpec as P
 
@@ -201,10 +202,12 @@
 
 
 def tables(seq):
-    frequency = jnp.power(10000.0, -2.0 * jnp.arange(HD // 2, dtype=F32) / HD)
-    angle = jnp.arange(seq, dtype=F32)[:, None] * frequency[None, :]
-    cosine, sine = jnp.cos(angle), jnp.sin(angle)
-    return jnp.tile(cosine, (1, 4)), jnp.concatenate([-sine, sine, -sine, sine], axis=1)
+    step = np.arange(HD // 2, dtype=np.float32)
+    frequency = np.power(np.float32(10000.0), np.float32(-2.0) * step / np.float32(HD))
+    angle = np.arange(seq, dtype=np.float32)[:, None] * frequency[None, :]
+    cosine, sine = np.cos(angle), np.sin(angle)
+    signed = np.concatenate([-sine, sine, -sine, sine], axis=1)
+    return jnp.asarray(np.tile(cosine, (1, 4))), jnp.asarray(signed)
 
 
 MESH = pl.DeviceIdType.MESH
@@ -268,9 +271,9 @@
 
 
 class Line:
-    def __init__(self, mail, count, own, at, low=None, high=None):
+    def __init__(self, mail, count, own, at, ready=()):
         self.mail, self.count, self.own, self.at = mail, count, own, at
-        self.low, self.high = low, high
+        self.ready = ready
         self.z = lax.axis_index("fsdp")
         self.up = [mail.slot() for _ in range(count)]
         self.down = [mail.slot() for _ in range(count)]
@@ -286,9 +289,9 @@
         low, high = jnp.maximum(z - hop + 1, 0), jnp.minimum(z + hop - 1, count - 1)
         from_low = from_high = self.own
         if hop > 1:
-            ready = hop == 2 and self.low is not None
-            from_low = self.low if ready else self.at(low)
-            from_high = self.high if ready else self.at(high)
+            from_low, from_high = self.at(low), self.at(high)
+        if 0 < hop - 1 <= len(self.ready):
+            from_low, from_high = self.ready[hop - 2]
         mail.start(
             self.up[hop], from_low, self.at(low),
             when=(z >= hop - 1) & (z < count - 1), fsdp=jnp.minimum(z + 1, count - 1),
@@ -306,6 +309,24 @@
         self.mail.arrive(
             self.down[hop], self.at(jnp.minimum(z + hop, count - 1)), when=self.has_high(hop), fsdp=z
         )
+
+
+    def keep(self, local, first):
+        z, count = self.z, self.count
+        made = [(pltpu.make_async_copy(self.own, self.at(z), local.at[first]), None)]
+        for index, (low, high) in enumerate(self.ready):
+            hop, place = index + 1, first + 2 * index + 1
+            to_low, to_high = jnp.maximum(z - hop, 0), jnp.minimum(z + hop, count - 1)
+            made.append(
+                (pltpu.make_async_copy(low, self.at(to_low), local.at[place]), self.has_low(hop))
+            )
+            made.append(
+                (
+                    pltpu.make_async_copy(high, self.at(to_high), local.at[place + 1]),
+                    self.has_high(hop),
+                )
+            )
+        return made
 
 
 class Across:
@@ -337,17 +358,18 @@
 
 
 def first_gather_kernel(
-    count, normed, qkv, turned_out, wide, normed_full, qkv_full, out_half, low, high,
-    send, recv, local,
+    count, tokens, tokens_away, gain, qkv, turned_out, wide, wide_away,
+    token_rows, normed_full, qkv_full, out_half, low_pair, high_pair,
+    landed, normed, send, recv, local,
 ):
     z, c, t = lax.axis_index("fsdp"), lax.axis_index("cp"), lax.axis_index("tp")
     beside, yonder = t + 1 - 2 * (t % 2), (t + 2) % 4
+    low, high, wide_other = low_pair.at[0], high_pair.at[0], low_pair.at[1]
     mail = Mail(send, recv)
     greet(count)
     kept = [
         pltpu.make_async_copy(qkv, qkv_full.at[z, c], local.at[0]),
         pltpu.make_async_copy(turned_out, out_half.at[z], local.at[1]),
-        pltpu.make_async_copy(normed.at[c], normed_full.at[t, c], local.at[2]),
     ]
     for copy in kept:
         copy.start()
@@ -358,18 +380,29 @@
     )
     outs = Line(mail, count, turned_out, lambda j: out_half.at[j])
     wide_up, wide_down = mail.slot(), mail.slot()
-    rows_x = mail.slot()
+    rows_x, wide_x = mail.slot(), mail.slot()
     rows_y = [mail.slot() for _ in range(2)]
     rows_core = [mail.slot() for _ in range(4)]
 
-    mail.start(rows_x, normed.at[1 - c], normed_full.at[t, c], cp=1 - c)
+    mail.start(rows_x, tokens_away, landed, cp=1 - c)
     heads.send(1)
     heads_across.send(0)
-    mail.start(rows_y[0], normed.at[c], normed_full.at[t, c], tp=yonder)
-    mail.start(rows_core[0], normed.at[c], normed_full.at[t, c], tp=beside)
-    mail.arrive(rows_x, normed_full.at[t, 1 - c], cp=1 - c)
-    mail.start(rows_y[1], normed_full.at[t, 1 - c], normed_full.at[t, 1 - c], tp=yonder)
-    mail.start(rows_core[1], normed_full.at[t, 1 - c], normed_full.at[t, 1 - c], tp=beside)
+
+    def rows_out(source, side, half):
+        def one(place):
+            rows = source[place, :]
+            token_rows[half, place, :] = rows
+            normed[half, place, :] = (normalize(rows.astype(F32)) * gain[...]).astype(BF)
+
+        in_pieces(source.shape[0], one)
+        mail.start(rows_y[side], normed.at[half], normed_full.at[t, half], tp=yonder)
+        mail.start(rows_core[side], normed.at[half], normed_full.at[t, half], tp=beside)
+
+    rows_out(tokens, 0, c)
+    mail.arrive(rows_x, landed, cp=1 - c)
+    rows_out(landed, 1, 1 - c)
+    kept.append(pltpu.make_async_copy(normed, normed_full.at[t], local.at[2]))
+    kept[-1].start()
 
     def rows_on(k, half):
         mail.arrive(rows_y[k], normed_full.at[yonder, half], tp=yonder)
@@ -385,6 +418,8 @@
             outs.arrive(hop - 1)
         outs.send(hop)
         heads_across.send(hop)
+        if hop == min(2, count - 1):
+            mail.start(wide_x, wide_away, wide_other, cp=1 - c)
         if hop == 1:
             rows_on(0, c)
             rows_on(1, 1 - c)
@@ -399,6 +434,9 @@
     far = (beside + 2) % 4
     mail.arrive(rows_core[2], normed_full.at[far, c], tp=beside)
     mail.arrive(rows_core[3], normed_full.at[far, 1 - c], tp=beside)
+    mail.arrive(wide_x, wide_other, cp=1 - c)
+    kept.append(pltpu.make_async_copy(wide_other, high_pair.at[1], local.at[3]))
+    kept[-1].start()
     mail.arrive(wide_up, low, when=z > 0, fsdp=z)
     mail.arrive(wide_down, high, when=z < count - 1, fsdp=z)
     for copy in kept:
@@ -406,28 +444,32 @@
     mail.finish()
 
 
-def first_gather(count, normed, qkv, turned_out, wide):
-    slots = 6 * count + 9
+def first_gather(count, tokens, tokens_away, gain, qkv, turned_out, wide, wide_away):
+    slots = 6 * count + 10
     anywhere = pl.BlockSpec(memory_space=pl.ANY)
-    share = qkv.shape[0]
+    vmem = pl.BlockSpec(memory_space=pltpu.VMEM)
+    pair = (2,) + tokens.shape
     return pl.pallas_call(
         functools.partial(first_gather_kernel, count),
         out_shape=(
-            jax.ShapeDtypeStruct((4,) + normed.shape, BF),
+            jax.ShapeDtypeStruct(pair, BF),
+            jax.ShapeDtypeStruct((4,) + pair, BF),
             jax.ShapeDtypeStruct((count, 2) + qkv.shape, BF),
             jax.ShapeDtypeStruct((count,) + turned_out.shape, BF),
-            jax.ShapeDtypeStruct(wide.shape, BF),
-            jax.ShapeDtypeStruct(wide.shape, BF),
+            jax.ShapeDtypeStruct((2,) + wide.shape, BF),
+            jax.ShapeDtypeStruct((2,) + wide.shape, BF),
         ),
-        in_specs=[anywhere] * 4,
-        out_specs=(anywhere,) * 5,
+        in_specs=[vmem, anywhere, vmem] + [anywhere] * 4,
+        out_specs=(vmem,) + (anywhere,) * 5,
         scratch_shapes=[
+            pltpu.VMEM(tokens.shape, BF),
+            pltpu.VMEM(pair, BF),
             pltpu.SemaphoreType.DMA((slots,)),
             pltpu.SemaphoreType.DMA((slots,)),
-            pltpu.SemaphoreType.DMA((3,)),
+            pltpu.SemaphoreType.DMA((4,)),
         ],
         compiler_params=pltpu.CompilerParams(collective_id=1, has_side_effects=True),
-    )(normed, qkv, turned_out, wide)
+    )(tokens, tokens_away, gain, qkv, turned_out, wide, wide_away)
 
 
 def in_pieces(rows, body, size=16):
@@ -491,123 +533,114 @@
 
 
 def second_gather_kernel(
-    count, part, tokens, gain, wide, wide_low, wide_high, wide_other,
-    middle, normed_full, wide_full,
-    own, from_core, to_yonder, from_yonder, normed,
-    send, recv, local,
+    count, part, tokens, gain, wide, first_low, first_high, second_low, second_high, *refs
 ):
-    z, c, t = lax.axis_index("fsdp"), lax.axis_index("cp"), lax.axis_index("tp")
-    beside, yonder = t + 1 - 2 * (t % 2), (t + 2) % 4
-    far = (beside + 2) % 4
+    hops_mine, hops_other = min(2, count - 1), 1
+    wide_other = first_low.at[1]
+    ready_mine = [first_low.at[0], first_high.at[0], second_low.at[0], second_high.at[0]]
+    ready_mine = ready_mine[: 2 * hops_mine]
+    ready_other = [second_low.at[1], second_high.at[1]]
+    middle, normed_full, gate_full, up_full, down_full = refs[:5]
+    own, from_core, to_yonder, from_yonder, normed, send, recv, local, local_line = refs[5:]
+    c, t = lax.axis_index("cp"), lax.axis_index("tp")
     rows = tokens.shape[0]
     half = rows // 2
     mail = Mail(send, recv)
     greet(count)
 
-    mine = Line(mail, count, None, lambda j: wide_full.at[:, j, c], wide_low, wide_high)
-    other = Line(mail, count, wide_other, lambda j: wide_full.at[:, j, 1 - c])
-    core = [mail.slot() for _ in range(2)]
-    across = [mail.slot() for _ in range(2)]
+    mine, other = [], []
+    for which, full in enumerate((gate_full, up_full, down_full)):
+        for lines, side, piece, ready in (
+            (mine, c, wide, ready_mine), (other, 1 - c, wide_other, ready_other),
+        ):
+            arrived = [
+                (ready[2 * hop].at[which], ready[2 * hop + 1].at[which])
+                for hop in range(len(ready) // 2)
+            ]
+            lines.append(
+                Line(
+                    mail, count, piece.at[which],
+                    lambda j, full=full, side=side: full.at[j, side], arrived,
+                )
+            )
+    summed = TensorSum(mail, part, own, from_core, to_yonder, from_yonder, local)
     spread = Spread(
-        mail, lambda piece: normed.at[piece], lambda c, t, piece: normed_full.at[c, t, piece]
-    )
-
-    mail.start(core[1], part.at[far], from_core.at[1], tp=beside)
-    mail.start(core[0], part.at[beside], from_core.at[0], tp=beside)
-    kept = [
-        (pltpu.make_async_copy(part.at[yonder], own.at[1], local.at[0]), None),
-        (pltpu.make_async_copy(part.at[t], own.at[0], local.at[1]), None),
-        (pltpu.make_async_copy(wide, wide_full.at[:, z, c], local.at[2]), None),
-        (pltpu.make_async_copy(wide_other, wide_full.at[:, z, 1 - c], local.at[3]), None),
-        (
-            pltpu.make_async_copy(
-                wide_low, wide_full.at[:, jnp.maximum(z - 1, 0), c], local.at[4]
-            ),
-            z > 0,
-        ),
-        (
-            pltpu.make_async_copy(
-                wide_high, wide_full.at[:, jnp.minimum(z + 1, count - 1), c], local.at[5]
-            ),
-            z < count - 1,
-        ),
-    ]
+        mail, lambda piece: normed.at[piece], lambda c, t, piece: normed_full.at[piece, t, c]
+    )
+
+    summed.begin()
+    kept = []
+    for lines, hops in ((mine, hops_mine), (other, hops_other)):
+        for line in lines:
+            kept += line.keep(local_line, len(kept))
     for copy, when in kept:
         copy.start() if when is None else pl.when(when)(copy.start)
-    if count > 2:
-        mine.send(2)
-    if count > 1:
-        other.send(1)
-
-    kept[0][0].wait()
-    mail.arrive(core[1], from_core.at[1], tp=beside)
+
+    def send_hop(lines, hop):
+        for line in lines:
+            if hop < count:
+                line.send(hop)
+
+    def arrive_hop(lines, hop):
+        for line in lines:
+            if hop < count:
+                line.arrive(hop)
+
+    send_hop(other, hops_other + 1)
+    send_hop(mine, hops_mine + 1)
+    summed.turn()
     for piece in range(2):
-
-        def add(place, piece=piece):
-            place = pl.ds(place.start + piece * half, place.size)
-            to_yonder[place, :] = (
-                own[1, place, :].astype(F32) + from_core[1, place, :].astype(F32)
-            ).astype(BF)
-
-        in_pieces(half, add)
-        block = pl.ds(piece * half, half)
-        mail.start(across[piece], to_yonder.at[block], from_yonder.at[block], tp=yonder)
-
-    kept[1][0].wait()
-    mail.arrive(core[0], from_core.at[0], tp=beside)
-    for piece in range(2):
-        block = pl.ds(piece * half, half)
-        mail.arrive(across[piece], from_yonder.at[block], tp=yonder)
+        summed.arrive(piece)
 
         def norm(place, piece=piece):
             row = pl.ds(place.start + piece * half, place.size)
-            attended = (
-                own[0, row, :].astype(F32)
-                + from_core[0, row, :].astype(F32)
-                + from_yonder[row, :].astype(F32)
-            )
-            values = tokens[row, :].astype(F32) + BRANCH * attended
+            values = tokens[row, :].astype(F32) + BRANCH * summed.rows(row)
             middle[row, :] = values
             normed[piece, place, :] = (normalize(values) * gain[...]).astype(BF)
 
         in_pieces(half, norm)
         spread.begin(piece)
-    keep_normed = pltpu.make_async_copy(normed, normed_full.at[c, t], local.at[0])
+    keep_normed = pltpu.make_async_copy(normed, normed_full.at[:, t, c], local.at[0])
     keep_normed.start()
     spread.turn()
-
-    for hop in range(1, count):
-        if hop + 1 < count:
-            mine.arrive(hop + 1)
-            if hop + 2 < count:
-                mine.send(hop + 2)
-        other.arrive(hop)
-        if hop + 1 < count:
-            other.send(hop + 1)
-        if hop == 1:
+    for step in range(1, count):
+        hop = hops_other + step
+        if hop < count:
+            for line_other, line_mine in zip(other, mine):
+                line_other.arrive(hop)
+                if hop + 1 < count:
+                    line_other.send(hop + 1)
+                if hops_mine + step < count:
+                    line_mine.arrive(hops_mine + step)
+                    if hops_mine + step + 1 < count:
+                        line_mine.send(hops_mine + step + 1)
+        if step == 1:
             spread.end()
     if count == 1:
         spread.end()
     keep_normed.wait()
-    for copy, when in kept[2:]:
+    for copy, when in kept:
         copy.wait() if when is None else pl.when(when)(copy.wait)
     mail.finish()
 
 
-def second_gather(count, part, tokens, gain, wide, wide_low, wide_high, wide_other):
-    slots = 4 * count + 20
+def second_gather(count, part, tokens, gain, wide, first_low, first_high, second_low, second_high):
+    slots = 12 * count + 20
     rows, width = tokens.shape
     anywhere = pl.BlockSpec(memory_space=pl.ANY)
     vmem = pl.BlockSpec(memory_space=pltpu.VMEM)
+    full = jax.ShapeDtypeStruct((count, 2) + wide.shape[1:], BF)
     return pl.pallas_call(
         functools.partial(second_gather_kernel, count),
         out_shape=(
             jax.ShapeDtypeStruct((rows, width), F32),
             jax.ShapeDtypeStruct((2, 4, 2, rows // 2, width), BF),
-            jax.ShapeDtypeStruct((3, count, 2) + wide.shape[1:], BF),
+            full,
+            full,
+            full,
         ),
-        in_specs=[anywhere, vmem, vmem] + [anywhere] * 4,
-        out_specs=(vmem, anywhere, anywhere),
+        in_specs=[anywhere, vmem, vmem] + [anywhere] * 5,
+        out_specs=(vmem,) + (anywhere,) * 4,
         scratch_shapes=[
             pltpu.VMEM((2, rows, width), BF),
             pltpu.VMEM((2, rows, width), BF),
@@ -616,12 +649,13 @@
             pltpu.VMEM((2, rows // 2, width), BF),
             pltpu.SemaphoreType.DMA((slots,)),
             pltpu.SemaphoreType.DMA((slots,)),
-            pltpu.SemaphoreType.DMA((6,)),
+            pltpu.SemaphoreType.DMA((2,)),
+            pltpu.SemaphoreType.DMA((24,)),
         ],
         compiler_params=pltpu.CompilerParams(
             collective_id=2, has_side_effects=True, vmem_limit_bytes=40 << 20
         ),
-    )(part, tokens, gain, wide, wide_low, wide_high, wide_other)
+    )(part, tokens, gain, wide, first_low, first_high, second_low, second_high)
 
 
 class TensorSum:
@@ -743,8 +777,8 @@
 
 
 def first_sum_kernel(
-    count, part, gate_grad, up_grad, down_grad, middle, cotangent, gain,
-    grad_middle, attention_full, gain_rows, leaving,
+    count, part, gate_grad, up_grad, middle, cotangent, gain,
+    grad_middle, attention_full, gain_rows, leaving_up, leaving_down,
     own, from_core, first, second, grad_attention, totals, landed,
     send, recv, local,
 ):
@@ -759,7 +793,7 @@
 
     def fill_from(which):
         def fill(hop, up, j, target):
-            copy = pltpu.make_async_copy((gate_grad, up_grad, down_grad)[which].at[j], target, local.at[4])
+            copy = pltpu.make_async_copy((gate_grad, up_grad)[which].at[j], target, local.at[4])
             copy.start()
             copy.wait()
 
@@ -769,11 +803,11 @@
         Drain(
             mail, count, fill_from(which),
             lambda side, hop, which=which: (
-                leaving.at[side, which] if hop == last else totals.at[side, hop - 1, which]
+                (leaving_up, leaving_down)[side].at[which] if hop == last else totals.at[side, hop - 1, which]
             ),
             lambda side, hop, which=which: landed.at[side, hop - 1, which],
         )
-        for which in range(3)
+        for which in range(2)
     ]
 
     core = {}
@@ -783,11 +817,11 @@
         block_c = c if c_own else 1 - c
         core[c_own, t_own] = mail.slot()
         mail.start(
-            core[c_own, t_own], part.at[block_c, beside if t_own else far],
+            core[c_own, t_own], part.at[:, beside if t_own else far, block_c],
             from_core.at[c_own, t_own], tp=beside,
         )
         mine[c_own, t_own] = pltpu.make_async_copy(
-            part.at[block_c, t if t_own else yonder], own.at[c_own, t_own], local.at[index]
+            part.at[:, t if t_own else yonder, block_c], own.at[c_own, t_own], local.at[index]
         )
         mine[c_own, t_own].start()
     if last > 1:
@@ -797,39 +831,39 @@
     for c_own, t_own in order:
         mine[c_own, t_own].wait()
         mail.arrive(core[c_own, t_own], from_core.at[c_own, t_own], tp=beside)
-
-        def add(place, c_own=c_own, t_own=t_own):
-            own[c_own, t_own, place, :] = (
-                own[c_own, t_own, place, :].astype(F32)
-                + from_core[c_own, t_own, place, :].astype(F32)
-            ).astype(BF)
-
-        in_pieces(2 * half, add)
-
-    top, low = pl.ds(0, half), pl.ds(half, half)
+        for piece in range(2):
+
+            def add(place, c_own=c_own, t_own=t_own, piece=piece):
+                own[c_own, t_own, piece, place, :] = (
+                    own[c_own, t_own, piece, place, :].astype(F32)
+                    + from_core[c_own, t_own, piece, place, :].astype(F32)
+                ).astype(BF)
+
+            in_pieces(half, add)
+
     y_first = [mail.slot() for _ in range(2)]
     x_first = [mail.slot() for _ in range(2)]
     x_second, y_second = mail.slot(), mail.slot()
     for c_own in (0, 1):
-        mail.start(y_first[c_own], own.at[c_own, 0, top], first.at[0, c_own], tp=yonder)
+        mail.start(y_first[c_own], own.at[c_own, 0, 0], first.at[0, c_own], tp=yonder)
     for t_own in (0, 1):
-        mail.start(x_first[t_own], own.at[0, t_own, low], first.at[1, t_own], cp=1 - c)
+        mail.start(x_first[t_own], own.at[0, t_own, 1], first.at[1, t_own], cp=1 - c)
 
     def add_first(side, index, c_own, t_own):
         def one(place):
-            row = pl.ds(place.start + side * half, place.size)
-            own[c_own, t_own, row, :] = (
-                own[c_own, t_own, row, :].astype(F32) + first[side, index, place, :].astype(F32)
+            own[c_own, t_own, side, place, :] = (
+                own[c_own, t_own, side, place, :].astype(F32)
+                + first[side, index, place, :].astype(F32)
             ).astype(BF)
 
         in_pieces(half, one)
 
     mail.arrive(y_first[0], first.at[0, 0], tp=yonder)
     add_first(0, 0, 0, 1)
-    mail.start(x_second, own.at[0, 1, top], second.at[0], cp=1 - c)
+    mail.start(x_second, own.at[0, 1, 0], second.at[0], cp=1 - c)
     mail.arrive(x_first[0], first.at[1, 0], cp=1 - c)
     add_first(1, 0, 1, 0)
-    mail.start(y_second, own.at[1, 0, low], second.at[1], tp=yonder)
+    mail.start(y_second, own.at[1, 0, 1], second.at[1], tp=yonder)
     mail.arrive(y_first[1], first.at[0, 1], tp=yonder)
     add_first(0, 1, 1, 1)
     mail.arrive(x_first[1], first.at[1, 1], cp=1 - c)
@@ -847,7 +881,7 @@
 
         def back(place, piece=piece):
             row = pl.ds(place.start + piece * half, place.size)
-            summed = own[1, 1, row, :].astype(F32) + second[piece, place, :].astype(F32)
+            summed = own[1, 1, piece, place, :].astype(F32) + second[piece, place, :].astype(F32)
             grad, rows = norm_back(middle[row, :], gain[...], summed)
             grad = cotangent[row, :].astype(F32) + grad
             grad_middle[row, :] = grad
@@ -884,7 +918,7 @@
     mail.finish()
 
 
-def first_sum(count, part, gate_grad, up_grad, down_grad, middle, cotangent, gain):
+def first_sum(count, part, gate_grad, up_grad, middle, cotangent, gain):
     slots = 6 * count + 24
     rows, width = middle.shape
     block = gate_grad.shape[1:]
@@ -897,18 +931,19 @@
             jax.ShapeDtypeStruct((rows, width), F32),
             jax.ShapeDtypeStruct((4, 2, rows // 2, width), BF),
             jax.ShapeDtypeStruct((1, width), F32),
-            jax.ShapeDtypeStruct((2, 3) + block, BF),
+            jax.ShapeDtypeStruct((2,) + block, BF),
+            jax.ShapeDtypeStruct((2,) + block, BF),
         ),
-        in_specs=[anywhere] * 4 + [vmem] * 3,
-        out_specs=(vmem, anywhere, vmem, vmem),
+        in_specs=[anywhere] * 3 + [vmem] * 3,
+        out_specs=(vmem, anywhere, vmem, vmem, vmem),
         scratch_shapes=[
-            pltpu.VMEM((2, 2, rows, width), BF),
-            pltpu.VMEM((2, 2, rows, width), BF),
+            pltpu.VMEM((2, 2, 2, rows // 2, width), BF),
+            pltpu.VMEM((2, 2, 2, rows // 2, width), BF),
             pltpu.VMEM((2, 2, rows // 2, width), BF),
             pltpu.VMEM((2, rows // 2, width), BF),
             pltpu.VMEM((2, rows // 2, width), BF),
-            pltpu.VMEM((2, hops, 3) + block, BF),
-            pltpu.VMEM((2, hops, 3) + block, BF),
+            pltpu.VMEM((2, hops, 2) + block, BF),
+            pltpu.VMEM((2, hops, 2) + block, BF),
             pltpu.SemaphoreType.DMA((slots,)),
             pltpu.SemaphoreType.DMA((slots,)),
             pltpu.SemaphoreType.DMA((5,)),
@@ -916,7 +951,7 @@
         compiler_params=pltpu.CompilerParams(
             collective_id=3, has_side_effects=True, vmem_limit_bytes=60 << 20
         ),
-    )(part, gate_grad, up_grad, down_grad, middle, cotangent, gain)
+    )(part, gate_grad, up_grad, middle, cotangent, gain)
 
 
 def last_sum_kernel(
@@ -1153,6 +1188,10 @@
     return lax.dot_general(left, right, (((1,), (1,)), ((), ())), preferred_element_type=F32)
 
 
+def row_major(value):
+    return with_layout_constraint(value, Layout(major_to_minor=(0, 1)))
+
+
 def after(value, *earlier):
     return lax.optimization_barrier((value, *earlier))[0]
 
@@ -1201,40 +1240,42 @@
     def pick(value, which, axis=0):
         return lax.dynamic_index_in_dim(value, which, axis, keepdims=False)
 
-    def to_sequence(value):
-        mine = pick(value, c)
-        other = swap(pick(value, 1 - c))
-        return in_order(c, mine, other, 0)
-
     def from_sequence(value):
         value = value.reshape(sets, local, width)
         mine = pick(value, c)
         other = swap(pick(value, 1 - c))
         return in_order(c, mine[None], other[None], 0)
 
-    token_rows = to_sequence(tokens)
-    cotangent_rows = to_sequence(cotangent)
-    upstream = cotangent_rows.astype(F32)
     length = pick(seq_lengths, c)[None]
     gain_one = attention_gain.astype(F32)
     gain_two = feedforward_gain.astype(F32)
 
-    def normed_rows(values):
-        return (normalize(values.astype(F32)) * gain_one).astype(BF)
-
     qkv = jnp.concatenate([query_weight, key_weight, value_weight], axis=1)
-    wide = jnp.stack([gate_weight, up_weight, down_weight.T]).reshape(3, share, sets, hidden_width)
-    own_wide = pick(wide, c, 2)
-    normed_one, full_qkv, out_half, wide_low, wide_high = first_gather(
-        count, normed_rows(tokens), qkv, out_weight.T, own_wide
-    )
+
+    def halves(weight):
+        return weight[:, :hidden_width], weight[:, hidden_width:]
+
+    parts = [halves(weight) for weight in (gate_weight, up_weight, down_weight.T)]
+    own_wide = jnp.stack([jnp.where(c == 0, low, high) for low, high in parts])
+    wide_away = jnp.stack([jnp.where(c == 0, high, low) for low, high in parts])
+    token_rows, normed_one, full_qkv, out_half, first_low, first_high = first_gather(
+        count, pick(tokens, c), pick(tokens, 1 - c), gain_one[None], qkv, out_weight.T,
+        own_wide, wide_away,
+    )
+    token_rows = token_rows.reshape(rows, width)
     normed_one = normed_one.reshape(seq, width)
     full_qkv = full_qkv.reshape(width, 3 * heads_width)
-    out_other, wide_other = after((out_half, pick(wide, 1 - c, 2)), full_qkv)
-    wide_other = swap(wide_other)
-    full_out = in_order(c, out_half[:, None], swap(out_other)[:, None], 1)
+
+    out_half, cotangent = after((out_half, cotangent), full_qkv)
+    cotangents = lax.all_gather(cotangent, everyone, axis=0).reshape(
+        sets, lanes, slots, local, width
+    )
+    full_out = in_order(c, out_half[:, None], swap(out_half)[:, None], 1)
     full_out = full_out.reshape(width, heads_width)
-
+    up_hop = [(i, i + 1) for i in range(count - 1)]
+    down_hop = [(i, i - 1) for i in range(1, count)]
+    second_low = lax.ppermute(first_low, "fsdp", up_hop)
+    second_high = lax.ppermute(first_high, "fsdp", down_hop)
     cosine_table, sine_table = tables(seq)
     projected = matmul(normed_one, full_qkv)
     context, q_heads, k_heads, v_heads, level = attention(
@@ -1242,22 +1283,38 @@
     )
     part = cols_inner(context, full_out).astype(BF)
 
-    middle, normed_two, full_wide = second_gather(
+    middle, normed_two, full_gate, full_up, full_down = second_gather(
         count, part.reshape(lanes, rows, width), token_rows, gain_two[None], own_wide,
-        wide_low, wide_high, wide_other,
+        first_low, first_high, second_low, second_high,
     )
     normed_two = normed_two.reshape(sets * seq, width)
-    full_gate, full_up, full_down = full_wide.reshape(3, width, hidden_width)
-    grad_branch = lax.all_gather((BRANCH * upstream).astype(BF), everyone, axis=0, tiled=True)
+    full_gate, full_up, full_down = (
+        full.reshape(width, hidden_width) for full in (full_gate, full_up, full_down)
+    )
+    t = lax.axis_index("tp")
+    grad_branch = (BRANCH * cotangents.astype(F32)).astype(BF).reshape(sets * seq, width)
+    middle_home = from_sequence(middle)
+    cotangent_rows = pick(pick(cotangents, t, 1), c, 1).reshape(rows, width)
     gate_pre = matmul(normed_two, full_gate)
     up_pre = matmul(normed_two, full_up)
     hidden_exact, silu_back = jax.vjp(silu_product, gate_pre, up_pre)
     hidden = hidden_exact.astype(BF)
 
     def blocks_of(gradient):
-        return gradient.astype(BF).reshape(count, width // count, hidden_width)
+        gradient = row_major(gradient.astype(BF))
+        return gradient.reshape(count, width // count, hidden_width)
 
     down_blocks = blocks_of(rows_inner(grad_branch, hidden))
+    low = high = None
+    for hop in range(1, count):
+        leaving_up = pick(down_blocks, jnp.minimum(z + count - hop, count - 1))
+        leaving_down = pick(down_blocks, jnp.maximum(z - count + hop, 0))
+        if hop > 1:
+            leaving_up = (leaving_up.astype(F32) + low.astype(F32)).astype(BF)
+            leaving_down = (leaving_down.astype(F32) + high.astype(F32)).astype(BF)
+        if hop < count - 1:
+            low = lax.ppermute(leaving_up, "fsdp", up_hop[:hop])
+            high = lax.ppermute(leaving_down, "fsdp", down_hop[count - 1 - hop :])
     grad_hidden = matmul(grad_branch, full_down)
     grad_gate_exact, grad_up_exact = silu_back(grad_hidden)
     grad_gate_pre = grad_gate_exact.astype(BF)
@@ -1265,14 +1322,23 @@
     grad_normed_two = cols_inner(grad_gate_pre, full_gate) + cols_inner(grad_up_pre, full_up)
     gate_blocks = blocks_of(rows_inner(normed_two, grad_gate_pre))
     up_blocks = blocks_of(rows_inner(normed_two, grad_up_pre))
-    grad_middle, grad_attention, gain_two_rows, leaving = first_sum(
-        count, grad_normed_two.astype(BF).reshape(sets, lanes, rows, width),
-        gate_blocks, up_blocks, down_blocks, middle, cotangent_rows, gain_two[None],
+    part = grad_normed_two.astype(BF).reshape(sets, lanes, slots, local, width)
+    if count > 1:
+        part, leaving_up, leaving_down = lax.optimization_barrier((part, leaving_up, leaving_down))
+    part, middle_home = lax.optimization_barrier((part, middle_home))
+    grad_middle, grad_attention, gain_two_rows, pair_up, pair_down = first_sum(
+        count, part, gate_blocks, up_blocks, middle, cotangent_rows, gain_two[None],
     )
     grad_attention = grad_attention.reshape(seq, width)
 
-    low = lax.ppermute(leaving[0], "fsdp", [(i, i + 1) for i in range(count - 1)])
-    high = lax.ppermute(leaving[1], "fsdp", [(i, i - 1) for i in range(1, count)])
+    if count > 1:
+        leaving_up, leaving_down = after((leaving_up, leaving_down), grad_attention)
+        low = [lax.ppermute(pair_up, "fsdp", up_hop), lax.ppermute(leaving_up, "fsdp", up_hop)]
+        high = [
+            lax.ppermute(pair_down, "fsdp", down_hop), lax.ppermute(leaving_down, "fsdp", down_hop),
+        ]
+        low = [low[0][0], low[0][1], low[1]]
+        high = [high[0][0], high[0][1], high[1]]
 
     def own_share(which, gradient):
         total = pick(gradient, z).astype(F32)
@@ -1291,22 +1357,23 @@
     )
     grad_down = grad_down.T
 
-    out_pieces = rows_inner(grad_attention, context).astype(BF)
+    out_pieces = row_major(rows_inner(grad_attention, context).astype(BF))
     out_pieces = out_pieces.reshape(count, sets, share, heads_width)
-    out_pieces = (
-        pick(out_pieces, c, 1).astype(F32) + swap(pick(out_pieces, 1 - c, 1)).astype(F32)
-    ).astype(BF)
-    grad_context = matmul(grad_attention, full_out).astype(BF)
+    out_other = swap(pick(out_pieces, 1 - c, 1))
+    out_pieces = (pick(out_pieces, c, 1).astype(F32) + out_other.astype(F32)).astype(BF)
+    grad_context = row_major(matmul(grad_attention, full_out).astype(BF))
     feedforward = lax.psum_scatter(
         cols_inner(after(hidden, grad_attention), full_down).astype(BF),
         everyone, scatter_dimension=0, tiled=True,
     )
-    output = from_sequence((middle + BRANCH * feedforward.astype(F32)).astype(BF))
+    feedforward = feedforward.reshape(slots, local, width)
+    output = (middle_home + BRANCH * feedforward.astype(F32)).astype(BF)
     grad_projected = attention_back(
         blocks, head_count, length, grad_context, q_heads, k_heads, v_heads, level,
         cosine_table, sine_table,
     )
-    grad_qkv = rows_inner(normed_one, grad_projected).astype(BF)
+    grad_projected = after(grad_projected, out_other, low[2], high[2])
+    grad_qkv = row_major(rows_inner(normed_one, grad_projected).astype(BF))
     grad_qkv, grad_out, grad_tokens, gain_sums = last_sum(
         count, cols_inner(grad_projected, full_qkv).astype(BF).reshape(lanes, rows, width),
         grad_qkv.reshape(count, sets, share, 3 * heads_width), out_pieces,

time: 952 us -> 891 us (0.936)
  local copies, waits for them, and re-layouts: 85.3 us -> 24.3 us
  Pallas kernels: 601 us -> 573 us
  starting transfers between devices: 19.9 us -> 40.1 us
  other arithmetic: 30.4 us -> 43 us
    pallas_call x1, Pallas kernels: 147 us -> 91 us  [second_gather(): pl.pallas_call(functools.partial(second_gather_kernel, count), out_shape=...]
    pallas_call x1, Pallas kernels: 137 us -> 179 us  [first_gather(): pl.pallas_call(functools.partial(first_gather_kernel, count), out_shape=(...]
    convert_element_type x6 -> x0, local copies, waits for them, and re-layouts: 35.3 us -> none  [the longest x3 17.1 us: blocks_of(): return gradient.astype(BF).reshape(count, width // count, hidden_width)]
    ppermute x2 -> x10, starting transfers between devices: 9.88 us -> 37 us  [the longest x1 11.7 us: on_device(): lax.ppermute(leaving_up, 'fsdp', up_hop)]
    pallas_call x1, Pallas kernels: 123 us -> 96.6 us  [first_sum(): pl.pallas_call(functools.partial(first_sum_kernel, count), out_shape=(jax...]
    another operation x7 -> x0, local copies, waits for them, and re-layouts: 17.4 us -> none  [the longest x4 7.77 us: on_device(): jnp.stack([gate_weight, up_weight, down_weight.T])]
    pallas_call x1, Pallas kernels: 120 us -> 133 us  [last_sum(): pl.pallas_call(functools.partial(last_sum_kernel, count), out_shape=(jax....]
    convert_element_type x5 -> x6, other arithmetic: 7.67 us -> 17.9 us  [the longest x1 9.61 us: on_device(): (BRANCH * cotangents.astype(F32)).astype(BF).reshape(sets * seq, width)]
  transfers between devices with their start and end apart: 11 -> 16, of which waited for: 3 -> 2; matrix products, arithmetic and copies ran while one was open for 17% -> 18% of each run, Pallas kernels for 51% -> 34%
where the time goes in v3:
time: 891 us; the launch traced here: 887 us
  Pallas kernels  573 us (64%)
  matrix products  178 us (20%)
  other arithmetic  43 us (5%)
  starting transfers between devices  40.1 us (5%)
  local copies, waits for them, and re-layouts  24.3 us (3%)
  between operations  14.9 us (2%)
  waiting for transfers between devices  13.8 us (2%)
    pallas_call x1, Pallas kernels, first_gather(): pl.pallas_call(functools.partial(first_gather_kernel, count), out_shape=(...  179 us
    pallas_call x1, Pallas kernels, last_sum(): pl.pallas_call(functools.partial(last_sum_kernel, count), out_shape=(jax....  133 us
    pallas_call x1, Pallas kernels, first_sum(): pl.pallas_call(functools.partial(first_sum_kernel, count), out_shape=(jax...  96.6 us
    pallas_call x1, Pallas kernels, second_gather(): pl.pallas_call(functools.partial(second_gather_kernel, count), out_shape=...  91 us
    dot_general x5, matrix products, matmul(): return jnp.dot(left, right, preferred_element_type=F32)  64.7 us
    dot_general x5, matrix products, cols_inner(): lax.dot_general(left, right, (((1,), (1,)), ((), ())), preferred_element_...  58.5 us
    dot_general x5, matrix products, rows_inner(): lax.dot_general(left, right, (((0,), (0,)), ((), ())), preferred_element_...  55 us
    pallas_call x1, Pallas kernels, attention_back(): pl.pallas_call(functools.partial(attention_back_kernel, blocks), out_shap...  39.2 us
  transfers between devices with their start and end apart: 16, of which 2 were waited for; matrix products, arithmetic and copies ran while one was open for 18% of the time, Pallas kernels for 34%

profile of v3, /device:TPU:0, one launch (start us, length us, event | category | flops | bytes accessed | tf_op | source)
XLA Modules:
  0.0 887.2 jit_solution(10660256204673916584)
XLA Ops:
  18.1 178.9 %shard_map.221 = (bf16[2,128,2304]{2,1,0:T(8,128)(2,1)}, bf16[4,2,128,2304]{3,2,1,0:T(8,128)(2,1)}, bf16[4,2,288,1728]{3,2,1,0:T(8,128)(2,1)}, bf16[4,288,576]{2...) custom-call(bf16[128,2304]{1,0:T(8,128)(2,1)} %get-tuple-element.103.tokens, ...), custom_call_target="tpu_custom_call" | custom-call | tf_op jit(solution)/shard_map/pallas_call | solution.py:452
  203.6 15.8 %fusion.11.projected = f32[1024,1728]{1,0:T(8,128)} fusion(bf16[1024,2304]{1,0:T(8,128)(2,1)} %bitcast.172, bf16[2304,1728]{1,0:T(8,128)(2,1)} %bitcast.170), kind=kOutput, calls=%fused_computation.70 | convolution fusion | flops 8153726976 | bytes 19759104 | tf_op jit(solution)/shard_map/dot_general | solution.py:1180
  219.4 34.7 %shard_map.222 = (bf16[1024,576]{1,0:T(8,128)(2,1)S(1)}, bf16[9,1024,64]{2,1,0:T(8,128)(2,1)S(1)}, bf16[9,1024,64]{2,1,0:T(8,128)(2,1)}, bf16[9,1024,64]{2,1,0:T(8,128)(2,1)}, f32[9,1,1024]{2,1,0:T(1,128)S(1)}) custom-call(s32[1]{0:T(128)} %dynamic_slice.80.length_ref, f32[1024,1728]{1,0:T(8,128)} %fusion.11.projected, f32[1024,128]{1,0:T(8,128)S(1)} %copy-done.7, ...), custom_call_target="tpu_custom_call" | custom-call | flops 2415919104 | bytes 20971520 | tf_op jit(solution)/shard_map/pallas_call | solution.py:107
  264.2 91.0 %shard_map.223 = (f32[256,2304]{1,0:T(8,128)S(1)}, bf16[2,4,2,128,2304]{4,3,2,1,0:T(8,128)(2,1)}, bf16[4,2,288,720]{3,2,1,0:T(8,128)(2,1)}, bf16[4,2,288,720]{3,2,1,0:T(8,128)(2,1)}, bf16[4,2,288,720]{3,2,1,0:T(8,128)(2,1)}) custom-call(bf16[4,256,2304]{2,1,0:T(8,128)(2,1)} %bitcast.155, bf16[256,2304]{1,0:T(8,128)(2,1)S(1)} %bitcast.132, ...), custom_call_target="tpu_custom_call" | custom-call | tf_op jit(solution)/shard_map/pallas_call | solution.py:633
  358.0 11.4 %fusion.13 = f32[2048,720]{0,1:T(8,128)} fusion(bf16[2048,2304]{1,0:T(8,128)(2,1)} %bitcast.166, bf16[2304,720]{1,0:T(8,128)(2,1)S(1)} %bitcast.179), kind=kOutput, calls=%fused_computation.72 | convolution fusion | flops 6794772480 | bytes 18653184 | tf_op jit(solution)/shard_map/dot_general | solution.py:1180
  369.4 12.3 %collective-permute-done.7 = f32[128,2304]{1,0:T(8,128)S(1)} collective-permute-done((f32[128,2304]{1,0:T(8,128)S(1)}, f32[128,2304]{1,0:T(8,128)S(1)}, u32[]{:S(2)}, u32[]{:S(2)}) %collective-permute-start.7) | collective-permute-done | bytes 1179680 | tf_op jit(solution)/shard_map/ppermute | solution.py:1200
  383.3 9.6 %multiply_convert_fusion = bf16[16,128,2304]{2,1,0:T(8,128)(2,1)} fusion(bf16[16,128,2304]{2,1,0:T(8,128)(2,1)} %all-gather.3.cloned.1.call-done), kind=kLoop, calls=%fused_computation | loop fusion | flops 14155776 | bytes 18874368 | tf_op jit(solution)/shard_map/convert_element_type | solution.py:1295
  392.9 11.2 %fusion.12 = f32[2048,720]{0,1:T(8,128)} fusion(bf16[2048,2304]{1,0:T(8,128)(2,1)} %bitcast.140, bf16[2304,720]{1,0:T(8,128)(2,1)S(1)} %bitcast.176), kind=kOutput, calls=%fused_computation.71 | convolution fusion | flops 6794772480 | bytes 18653184 | tf_op jit(solution)/shard_map/dot_general | solution.py:1180
  404.0 18.9 %multiply_convert_fusion.1 = (bf16[2048,720]{0,1:T(8,128)(2,1)}, bf16[2048,720]{0,1:T(8,128)(2,1)}, bf16[2048,720]{0,1:T(8,128)(2,1)}) fusion(f32[2048,720]{0,1:T(8,128)} %fusion.13, f32[2048,720]{0,1:T(8,128)} %fusion.12, bf16[2048,2304]{1,0:T(8,128)(2,1)} %bitcast.167, bf16[2304,720]{1,0:T(8,128)(2,1)} %bitcast.180), kind=kOutput, calls=%fused_computation.4 | convolution fusion | flops 6821314560 | bytes 33398784 | tf_op jit(solution)/shard_map/dot_general | solution.py:1180
  423.0 11.2 %convolution_convert_fusion.6 = bf16[2304,720]{1,0:T(8,128)(2,1)S(1)} fusion(bf16[2048,2304]{1,0:T(8,128)(2,1)} %bitcast.141, bf16[2048,720]{0,1:T(8,128)(2,1)} %get-tuple-element.65), kind=kOutput, calls=%fused_computation.13 | convolution fusion | flops 6796431360 | bytes 15704064 | tf_op jit(solution)/shard_map/dot_general | solution.py:1184
  438.9 11.3 %fusion.14 = f32[2048,2304]{1,0:T(8,128)} fusion(bf16[2048,720]{0,1:T(8,128)(2,1)S(1)} %copy-done.33, bf16[2304,720]{1,0:T(8,128)(2,1)S(1)} %bitcast.181), kind=kOutput, calls=%fused_computation.73 | convolution fusion | flops 6794772480 | bytes 25141248 | tf_op jit(solution)/shard_map/dot_general | solution.py:1188
  450.1 15.4 %add_convert_fusion = bf16[2048,2304]{1,0:T(8,128)(2,1)} fusion(f32[2048,2304]{1,0:T(8,128)} %fusion.14, bf16[2048,720]{0,1:T(8,128)(2,1)} %get-tuple-element.86, bf16[2304,720]{1,0:T(8,128)(2,1)} %bitcast.178), kind=kOutput, calls=%fused_computation.1 | convolution fusion | flops 6804209664 | bytes 34578432 | tf_op jit(solution)/shard_map/dot_general | solution.py:1188
  466.4 12.3 %convolution_convert_fusion.5 = bf16[2304,720]{1,0:T(8,128)(2,1)} fusion(bf16[2048,2304]{1,0:T(8,128)(2,1)} %bitcast.168, bf16[2048,720]{0,1:T(8,128)(2,1)} %get-tuple-element.86), kind=kOutput, calls=%fused_computation.12 | convolution fusion | flops 6796431360 | bytes 15704064 | tf_op jit(solution)/shard_map/dot_general | solution.py:1184
  481.5 8.4 collective-permute-start.4
  489.9 11.7 %convolution_convert_fusion.4 = bf16[2304,720]{1,0:T(8,128)(2,1)} fusion(bf16[2048,2304]{1,0:T(8,128)(2,1)} %bitcast.169, bf16[2048,720]{0,1:T(8,128)(2,1)S(1)} %copy-done.34), kind=kOutput, calls=%fused_computation.11 | convolution fusion | flops 6796431360 | bytes 15704064 | tf_op jit(solution)/shard_map/dot_general | solution.py:1184
  506.5 96.6 %shard_map.224 = (f32[256,2304]{1,0:T(8,128)}, bf16[4,2,128,2304]{3,2,1,0:T(8,128)(2,1)}, f32[1,2304]{1,0:T(1,128)}, bf16[2,576,720]{2,1,0:T(8,128)(2,1)}, bf16[2,576,720]{2,1,0:T(8,128)(2,1)}) custom-call(bf16[2,4,2,128,2304]{4,3,2,1,0:T(8,128)(2,1)} %bitcast.139, bf16[4,576,720]{2,1,0:T(8,128)(2,1)} %bitcast.144, bf16[4,576,720]{2,1,0:T(8,128)(2,1)} %bitcast.146, ...), custom_call_target="tpu_custom_call" | custom-call | tf_op jit(solution)/shard_map/pallas_call | solution.py:928
  603.2 11.9 %convolution_convert_fusion.1 = bf16[2048,2304]{1,0:T(8,128)(2,1)} fusion(bf16[2048,720]{0,1:T(8,128)(2,1)} %get-tuple-element.65, bf16[2304,720]{1,0:T(8,128)(2,1)S(1)} %bitcast.177), kind=kOutput, calls=%fused_computation.3 | convolution fusion | flops 6799491072 | bytes 15704064 | tf_op jit(solution)/shard_map/dot_general | solution.py:1188
  615.1 11.7 %collective-permute-start.9 = (bf16[576,720]{1,0:T(8,128)(2,1)}, bf16[576,720]{1,0:T(8,128)(2,1)S(1)}, u32[]{:S(2)}, u32[]{:S(2)}) collective-permute-start(bf16[576,720]{1,0:T(8,128)(2,1)} %fusion.6), channel_id=1, source_target_pairs={{0,8},{8,16},{16,24},{1,9},{9,17},{17,25},{2,10},{10,18},{18,26},{... | collective-permute-start | bytes 2488328 | tf_op jit(solution)/shard_map/ppermute | solution.py:1336
  628.5 7.0 convolution_convert_fusion.7
  638.5 7.5 convolution_convert_fusion.8.grad_context
  651.9 39.2 %shard_map.225 = bf16[1024,1728]{1,0:T(8,128)(2,1)} custom-call(s32[1]{0:T(128)} %dynamic_slice.80.length_ref, bf16[1024,576]{1,0:T(8,128)(2,1)} %convolution_convert_fusion.8.grad_context, bf16[9,1024,64]{2,1,0:T(8,128)(2,1)} %copy-done.8, bf16[9,1024,64]{2,1,0:T(8,128)(2,1)} %get-tuple-element.67.k_heads, bf16[9,1024,64]{2,1,0:T(8,128)(2,1)} %get-tuple-element.68.v_heads, ...), custom_call_target="tpu_custom_call" | custom-call | flops 6039797760 | bytes 20971520 | tf_op jit(solution)/shard_map/pallas_call | solution.py:186
  693.6 12.8 %convolution_convert_fusion = bf16[2304,1728]{1,0:T(8,128)(2,1)} fusion(bf16[1024,2304]{1,0:T(8,128)(2,1)} %bitcast.173, bf16[1024,1728]{1,0:T(8,128)(2,1)S(1)} %copy-done.32), kind=kOutput, calls=%fused_computation.2 | convolution fusion | flops 8157708288 | bytes 16220160 | tf_op jit(solution)/shard_map/dot_general | solution.py:1184
  714.2 13.9 %convolution_convert_fusion.2 = bf16[1024,2304]{1,0:T(8,128)(2,1)} fusion(bf16[1024,1728]{1,0:T(8,128)(2,1)S(1)} %copy-done.32, bf16[2304,1728]{1,0:T(8,128)(2,1)} %bitcast.171), kind=kOutput, calls=%fused_computation.9 | convolution fusion | flops 8156086272 | bytes 16220160 | tf_op jit(solution)/shard_map/dot_general | solution.py:1188
  730.9 132.5 %shard_map.226 = (f32[288,1728]{1,0:T(8,128)}, f32[288,576]{1,0:T(8,128)}, bf16[2,128,2304]{2,1,0:T(8,128)(2,1)}, f32[2,2304]{1,0:T(2,128)}) custom-call(bf16[4,256,2304]{2,1,0:T(8,128)(2,1)} %bitcast.156, bf16[4,2,288,1728]{3,2,1,0:T(8,128)(2,1)} %bitcast.143, bf16[4,288,576]{2,1,0:T(8,128)(2,1)} %fusion.out_grad, bf16[256,2304]{1,0:T(8,128)(2,1)} %bitcast.131, ...), custom_call_target="tpu_custom_call" | custom-call | tf_op jit(solution)/shard_map/pallas_call | solution.py:1137
  (140 shorter events, 85.4 us)
Async XLA Ops:
  7.2 376.1 %all-gather.3.cloned.1.call-start = ((), (), s32[]{:S(2)}) async-start(), calls=%async_computation.2 | async-start | bytes 10616832 | tf_op jit(solution)/shard_map/all_gather | solution.py:1270
  18.1 184.9 %copy-start.31 = (s32[2]{0:T(128)S(1)}, s32[2]{0:T(128)}, u32[]{:S(2)}) copy-start(s32[2]{0:T(128)} %param.15) | copy-start | bytes 28
  18.1 185.5 %copy-start.26 = (bf16[2304]{0:T(1024)(128)(2,1)S(1)}, bf16[2304]{0:T(1024)(128)(2,1)}, u32[]{:S(2)}) copy-start(bf16[2304]{0:T(1024)(128)(2,1)} %param.21) | copy-start | bytes 13828
  197.1 678.3 %reduce-scatter.2.cloned.1.call-start = ((), (), s32[]{:S(2)}) async-start(), calls=%async_computation.1 | async-start | bytes 10616832 | tf_op jit(solution)/shard_map/reduce_scatter | solution.py:1365
  197.1 57.0 %collective-permute-start = (bf16[4,288,576]{2,1,0:T(8,128)(2,1)}, bf16[4,288,576]{2,1,0:T(8,128)(2,1)}, u32[]{:S(2)}, u32[]{:S(2)}) collective-permute-start(bf16[4,288,576]{2,1,0:T(8,128)(2,1)} %get-tuple-element.52), channel_id=1, source_target_pairs={{0,4},{4,0},{1,5},{5,1},{2,6},{6,2},{3,7},{7,3},{8,12},{12,8},{9,1... | collective-permute-start | bytes 3981320 | tf_op jit(solution)/shard_map/ppermute | solution.py:1200
  197.7 66.4 %collective-permute-start.1 = (bf16[2,3,288,720]{3,2,1,0:T(8,128)(2,1)}, bf16[2,3,288,720]{3,2,1,0:T(8,128)(2,1)S(1)}, u32[]{:S(2)}, u32[]{:S(2)}) collective-permute-start(bf16[2,3,288,720]{3,2,1,0:T(8,128)(2,1)} %get-tuple-element.54.first_low), channel_id=1, source_target_pairs={{0,8},{8,16},{16,24},{1,9},{9,17},{17,25},{2,10},{10,18},{18,26},{... | collective-permute-start | bytes 7464968 | tf_op jit(solution)/shard_map/ppermute | solution.py:1277
  201.4 62.7 %collective-permute-start.2 = (bf16[2,3,288,720]{3,2,1,0:T(8,128)(2,1)}, bf16[2,3,288,720]{3,2,1,0:T(8,128)(2,1)}, u32[]{:S(2)}, u32[]{:S(2)}) collective-permute-start(bf16[2,3,288,720]{3,2,1,0:T(8,128)(2,1)} %get-tuple-element.55.first_high), channel_id=1, source_target_pairs={{8,0},{16,8},{24,16},{9,1},{17,9},{25,17},{10,2},{18,10},{26,18},{... | collective-permute-start | bytes 7464968 | tf_op jit(solution)/shard_map/ppermute | solution.py:1278
  203.6 60.5 %copy-start.5 = (f32[1,2304]{1,0:T(1,128)}, f32[1,2304]{1,0:T(1,128)S(1)}, u32[]{:S(2)}) copy-start(f32[1,2304]{1,0:T(1,128)S(1)} %reshape.168.gain) | copy-start | bytes 27652
  203.6 15.8 %copy-start.6 = (f32[1024,128]{1,0:T(8,128)S(1)}, f32[1024,128]{1,0:T(8,128)}, u32[]{:S(2)}) copy-start(f32[1024,128]{1,0:T(8,128)} %constant.137.clone.sine) | copy-start | bytes 1572868
  219.4 34.7 %copy-start.19 = (bf16[4,288,576]{2,1,0:T(8,128)(2,1)S(1)}, bf16[4,288,576]{2,1,0:T(8,128)(2,1)}, u32[]{:S(2)}) copy-start(bf16[4,288,576]{2,1,0:T(8,128)(2,1)} %get-tuple-element.52) | copy-start | bytes 3981316
  355.4 26.3 %collective-permute-start.7 = (f32[128,2304]{1,0:T(8,128)S(1)}, f32[128,2304]{1,0:T(8,128)S(1)}, u32[]{:S(2)}, u32[]{:S(2)}) collective-permute-start(f32[128,2304]{1,0:T(8,128)S(1)} %get-tuple-element.95), channel_id=1, source_target_pairs={{0,4},{4,0},{1,5},{5,1},{2,6},{6,2},{3,7},{7,3},{8,12},{12,8},{9,1... | collective-permute-start | bytes 3538952 | tf_op jit(solution)/shard_map/ppermute | solution.py:1200
  423.0 15.9 %copy-start.33 = (bf16[2048,720]{0,1:T(8,128)(2,1)S(1)}, bf16[2048,720]{0,1:T(8,128)(2,1)}, u32[]{:S(2)}) copy-start(bf16[2048,720]{0,1:T(8,128)(2,1)} %get-tuple-element.87) | copy-start | bytes 8847364
  434.2 71.2 %copy-start.12 = (bf16[2304,720]{1,0:T(8,128)(2,1)}, bf16[2304,720]{1,0:T(8,128)(2,1)S(1)}, u32[]{:S(2)}) copy-start(bf16[2304,720]{1,0:T(8,128)(2,1)S(1)} %convolution_convert_fusion.6) | copy-start | bytes 9953284
  435.5 30.0 %collective-permute-start.5 = (bf16[576,720]{1,0:T(8,128)(2,1)}, bf16[576,720]{1,0:T(8,128)(2,1)S(1)}, u32[]{:S(2)}, u32[]{:S(2)}) collective-permute-start(bf16[576,720]{1,0:T(8,128)(2,1)} %get-tuple-element.92), channel_id=1, source_target_pairs={{24,16},{25,17},{26,18},{27,19},{28,20},{29,21},{30,22},{31,23}} | collective-permute-start | bytes 2488328 | tf_op jit(solution)/shard_map/ppermute | solution.py:1317
  436.4 42.4 %collective-permute-start.3 = (bf16[576,720]{1,0:T(8,128)(2,1)}, bf16[576,720]{1,0:T(8,128)(2,1)}, u32[]{:S(2)}, u32[]{:S(2)}) collective-permute-start(bf16[576,720]{1,0:T(8,128)(2,1)} %get-tuple-element.93), channel_id=1, source_target_pairs={{0,8},{1,9},{2,10},{3,11},{4,12},{5,13},{6,14},{7,15}} | collective-permute-start | bytes 2488328 | tf_op jit(solution)/shard_map/ppermute | solution.py:1316
  465.7 13.0 %collective-permute-start.6 = (bf16[576,720]{1,0:T(8,128)(2,1)S(1)}, bf16[576,720]{1,0:T(8,128)(2,1)S(1)}, u32[]{:S(2)}, u32[]{:S(2)}) collective-permute-start(bf16[576,720]{1,0:T(8,128)(2,1)S(1)} %fusion.3), channel_id=1, source_target_pairs={{16,8},{24,16},{17,9},{25,17},{18,10},{26,18},{19,11},{27,19},{20,... | collective-permute-start | bytes 2488328 | tf_op jit(solution)/shard_map/ppermute | solution.py:1317
  481.5 23.9 %collective-permute-start.4 = (bf16[576,720]{1,0:T(8,128)(2,1)S(1)}, bf16[576,720]{1,0:T(8,128)(2,1)S(1)}, u32[]{:S(2)}, u32[]{:S(2)}) collective-permute-start(bf16[576,720]{1,0:T(8,128)(2,1)S(1)} %get-tuple-element.91), channel_id=1, source_target_pairs={{0,8},{8,16},{1,9},{9,17},{2,10},{10,18},{3,11},{11,19},{4,12},{12... | collective-permute-start | bytes 2488328 | tf_op jit(solution)/shard_map/ppermute | solution.py:1316
  506.5 96.6 %copy-start.28 = (bf16[4,2,288,720]{3,2,1,0:T(8,128)(2,1)S(1)}, bf16[4,2,288,720]{3,2,1,0:T(8,128)(2,1)}, u32[]{:S(2)}) copy-start(bf16[4,2,288,720]{3,2,1,0:T(8,128)(2,1)} %get-tuple-element.56) | copy-start | bytes 9953284
  615.1 76.0 %collective-permute-start.9 = (bf16[576,720]{1,0:T(8,128)(2,1)}, bf16[576,720]{1,0:T(8,128)(2,1)S(1)}, u32[]{:S(2)}, u32[]{:S(2)}) collective-permute-start(bf16[576,720]{1,0:T(8,128)(2,1)} %fusion.6), channel_id=1, source_target_pairs={{0,8},{8,16},{16,24},{1,9},{9,17},{17,25},{2,10},{10,18},{18,26},{... | collective-permute-start | bytes 2488328 | tf_op jit(solution)/shard_map/ppermute | solution.py:1336
  626.8 64.3 %collective-permute-start.10 = (bf16[576,720]{1,0:T(8,128)(2,1)}, bf16[576,720]{1,0:T(8,128)(2,1)}, u32[]{:S(2)}, u32[]{:S(2)}) collective-permute-start(bf16[576,720]{1,0:T(8,128)(2,1)} %get-tuple-element.73), channel_id=1, source_target_pairs={{8,0},{16,8},{24,16},{9,1},{17,9},{25,17},{10,2},{18,10},{26,18},{... | collective-permute-start | bytes 2488328 | tf_op jit(solution)/shard_map/ppermute | solution.py:1338
  636.8 56.2 %collective-permute-start.8 = (bf16[4,288,576]{2,1,0:T(8,128)(2,1)}, bf16[4,288,576]{2,1,0:T(8,128)(2,1)}, u32[]{:S(2)}, u32[]{:S(2)}) collective-permute-start(bf16[4,288,576]{2,1,0:T(8,128)(2,1)} %dynamic-slice_bitcast_fusion), channel_id=1, source_target_pairs={{0,4},{4,0},{1,5},{5,1},{2,6},{6,2},{3,7},{7,3},{8,12},{12,8},{9,1... | collective-permute-start | bytes 3981320 | tf_op jit(solution)/shard_map/ppermute | solution.py:1200
  645.9 60.6 %collective-permute-start.11 = (bf16[2,576,720]{2,1,0:T(8,128)(2,1)}, bf16[2,576,720]{2,1,0:T(8,128)(2,1)S(1)}, u32[]{:S(2)}, u32[]{:S(2)}) collective-permute-start(bf16[2,576,720]{2,1,0:T(8,128)(2,1)} %get-tuple-element.81), channel_id=1, source_target_pairs={{0,8},{8,16},{16,24},{1,9},{9,17},{17,25},{2,10},{10,18},{18,26},{... | collective-permute-start | bytes 4976648 | tf_op jit(solution)/shard_map/ppermute | solution.py:1336
  650.4 57.3 %collective-permute-start.12 = (bf16[2,576,720]{2,1,0:T(8,128)(2,1)}, bf16[2,576,720]{2,1,0:T(8,128)(2,1)}, u32[]{:S(2)}, u32[]{:S(2)}) collective-permute-start(bf16[2,576,720]{2,1,0:T(8,128)(2,1)} %get-tuple-element.82), channel_id=1, source_target_pairs={{8,0},{16,8},{24,16},{9,1},{17,9},{25,17},{10,2},{18,10},{26,18},{... | collective-permute-start | bytes 4976648 | tf_op jit(solution)/shard_map/ppermute | solution.py:1338
  713.4 155.1 %collective-permute-start.13 = (bf16[3,288,720]{2,1,0:T(8,128)(2,1)}, bf16[3,288,720]{2,1,0:T(8,128)(2,1)}, u32[]{:S(2)}, u32[]{:S(2)}) collective-permute-start(bf16[3,288,720]{2,1,0:T(8,128)(2,1)} %pad_maximum_fusion.2), channel_id=1, source_target_pairs={{0,4},{4,0},{1,5},{5,1},{2,6},{6,2},{3,7},{7,3},{8,12},{12,8},{9,1... | collective-permute-start | bytes 3732488 | tf_op jit(solution)/shard_map/ppermute | solution.py:1200
  (27 other events, 145.3 us)
Sparse Core Ops, SparseCore 0:
  197.2 73.3 all-gather.2
  615.2 105.2 reduce-scatter.1

commit v4 on v3

--- a/solution.py
+++ b/solution.py
@@ -270,6 +270,36 @@
                 pl.when(when)(made.wait_send)
 
 
+class Stage:
+    def __init__(self, pieces, stage, sems):
+        self.made = []
+        for k, (source, target, when) in enumerate(pieces):
+            self.made.append(
+                (
+                    pltpu.make_async_copy(source, stage.at[k], sems.at[0, k]),
+                    pltpu.make_async_copy(stage.at[k], target, sems.at[1, k]),
+                    when,
+                )
+            )
+
+    def begin(self):
+        for copy, _, when in self.made:
+            copy.start() if when is None else pl.when(when)(copy.start)
+
+    def turn(self):
+        for first, second, when in self.made:
+
+            def on(first=first, second=second):
+                first.wait()
+                second.start()
+
+            on() if when is None else pl.when(when)(on)
+
+    def end(self):
+        for _, copy, when in self.made:
+            copy.wait() if when is None else pl.when(when)(copy.wait)
+
+
 class Line:
     def __init__(self, mail, count, own, at, ready=()):
         self.mail, self.count, self.own, self.at = mail, count, own, at
@@ -311,21 +341,13 @@
         )
 
 
-    def keep(self, local, first):
+    def keep(self):
         z, count = self.z, self.count
-        made = [(pltpu.make_async_copy(self.own, self.at(z), local.at[first]), None)]
+        made = [(self.own, self.at(z), None)]
         for index, (low, high) in enumerate(self.ready):
-            hop, place = index + 1, first + 2 * index + 1
-            to_low, to_high = jnp.maximum(z - hop, 0), jnp.minimum(z + hop, count - 1)
-            made.append(
-                (pltpu.make_async_copy(low, self.at(to_low), local.at[place]), self.has_low(hop))
-            )
-            made.append(
-                (
-                    pltpu.make_async_copy(high, self.at(to_high), local.at[place + 1]),
-                    self.has_high(hop),
-                )
-            )
+            hop = index + 1
+            made.append((low, self.at(jnp.maximum(z - hop, 0)), self.has_low(hop)))
+            made.append((high, self.at(jnp.minimum(z + hop, count - 1)), self.has_high(hop)))
         return made
 
 
@@ -360,19 +382,17 @@
 def first_gather_kernel(
     count, tokens, tokens_away, gain, qkv, turned_out, wide, wide_away,
     token_rows, normed_full, qkv_full, out_half, low_pair, high_pair,
-    landed, normed, send, recv, local,
+    landed, normed, wide_landed, qkv_stage, out_stage,
+    send, recv, local, qkv_local, out_local,
 ):
     z, c, t = lax.axis_index("fsdp"), lax.axis_index("cp"), lax.axis_index("tp")
     beside, yonder = t + 1 - 2 * (t % 2), (t + 2) % 4
-    low, high, wide_other = low_pair.at[0], high_pair.at[0], low_pair.at[1]
+    low, high = low_pair.at[0], high_pair.at[0]
     mail = Mail(send, recv)
     greet(count)
-    kept = [
-        pltpu.make_async_copy(qkv, qkv_full.at[z, c], local.at[0]),
-        pltpu.make_async_copy(turned_out, out_half.at[z], local.at[1]),
-    ]
-    for copy in kept:
-        copy.start()
+    stage_qkv = Stage([(qkv, qkv_full.at[z, c], None)], qkv_stage, qkv_local)
+    stage_out = Stage([(turned_out, out_half.at[z], None)], out_stage, out_local)
+    kept = []
 
     heads = Line(mail, count, qkv, lambda j: qkv_full.at[j, c])
     heads_across = Across(
@@ -386,7 +406,6 @@
 
     mail.start(rows_x, tokens_away, landed, cp=1 - c)
     heads.send(1)
-    heads_across.send(0)
 
     def rows_out(source, side, half):
         def one(place):
@@ -398,8 +417,13 @@
         mail.start(rows_y[side], normed.at[half], normed_full.at[t, half], tp=yonder)
         mail.start(rows_core[side], normed.at[half], normed_full.at[t, half], tp=beside)
 
+    stage_qkv.begin()
+    stage_out.begin()
     rows_out(tokens, 0, c)
+    stage_qkv.turn()
+    stage_out.turn()
     mail.arrive(rows_x, landed, cp=1 - c)
+    heads_across.send(0)
     rows_out(landed, 1, 1 - c)
     kept.append(pltpu.make_async_copy(normed, normed_full.at[t], local.at[2]))
     kept[-1].start()
@@ -414,19 +438,19 @@
         heads.arrive(hop)
         if hop + 1 < count:
             heads.send(hop + 1)
-        if hop > 1:
-            outs.arrive(hop - 1)
-        outs.send(hop)
         heads_across.send(hop)
-        if hop == min(2, count - 1):
-            mail.start(wide_x, wide_away, wide_other, cp=1 - c)
         if hop == 1:
             rows_on(0, c)
             rows_on(1, 1 - c)
-    mail.start(wide_up, wide, low, when=z < count - 1, fsdp=jnp.minimum(z + 1, count - 1))
-    mail.start(wide_down, wide, high, when=z > 0, fsdp=jnp.maximum(z - 1, 0))
-    if count > 1:
-        outs.arrive(count - 1)
+            outs.send(1)
+        if hop == min(2, count - 1):
+            mail.start(wide_up, wide, low, when=z < count - 1, fsdp=jnp.minimum(z + 1, count - 1))
+            mail.start(wide_down, wide, high, when=z > 0, fsdp=jnp.maximum(z - 1, 0))
+    mail.start(wide_x, wide_away, wide_landed, cp=1 - c)
+    for hop in range(1, count):
+        outs.arrive(hop)
+        if hop + 1 < count:
+            outs.send(hop + 1)
     for hop in range(count):
         heads_across.arrive(hop)
     mail.arrive(rows_core[0], normed_full.at[beside, c], tp=beside)
@@ -434,13 +458,16 @@
     far = (beside + 2) % 4
     mail.arrive(rows_core[2], normed_full.at[far, c], tp=beside)
     mail.arrive(rows_core[3], normed_full.at[far, 1 - c], tp=beside)
-    mail.arrive(wide_x, wide_other, cp=1 - c)
-    kept.append(pltpu.make_async_copy(wide_other, high_pair.at[1], local.at[3]))
-    kept[-1].start()
+    mail.arrive(wide_x, wide_landed, cp=1 - c)
+    for pair, place in ((low_pair, 1), (high_pair, 3)):
+        kept.append(pltpu.make_async_copy(wide_landed, pair.at[1], local.at[place]))
+        kept[-1].start()
     mail.arrive(wide_up, low, when=z > 0, fsdp=z)
     mail.arrive(wide_down, high, when=z < count - 1, fsdp=z)
     for copy in kept:
         copy.wait()
+    stage_qkv.end()
+    stage_out.end()
     mail.finish()
 
 
@@ -464,11 +491,18 @@
         scratch_shapes=[
             pltpu.VMEM(tokens.shape, BF),
             pltpu.VMEM(pair, BF),
+            pltpu.VMEM(wide.shape, BF),
+            pltpu.VMEM((1,) + qkv.shape, BF),
+            pltpu.VMEM((1,) + turned_out.shape, BF),
             pltpu.SemaphoreType.DMA((slots,)),
             pltpu.SemaphoreType.DMA((slots,)),
             pltpu.SemaphoreType.DMA((4,)),
+            pltpu.SemaphoreType.DMA((2, 1)),
+            pltpu.SemaphoreType.DMA((2, 1)),
         ],
-        compiler_params=pltpu.CompilerParams(collective_id=1, has_side_effects=True),
+        compiler_params=pltpu.CompilerParams(
+            collective_id=1, has_side_effects=True, vmem_limit_bytes=32 << 20
+        ),
     )(tokens, tokens_away, gain, qkv, turned_out, wide, wide_away)
 
 
@@ -540,8 +574,8 @@
     ready_mine = [first_low.at[0], first_high.at[0], second_low.at[0], second_high.at[0]]
     ready_mine = ready_mine[: 2 * hops_mine]
     ready_other = [second_low.at[1], second_high.at[1]]
-    middle, normed_full, gate_full, up_full, down_full = refs[:5]
-    own, from_core, to_yonder, from_yonder, normed, send, recv, local, local_line = refs[5:]
+    middle, middle_home, normed_full, gate_full, up_full, down_full = refs[:6]
+    own, from_core, to_yonder, from_yonder, normed, stage, send, recv, local, local_line = refs[6:]
     c, t = lax.axis_index("cp"), lax.axis_index("tp")
     rows = tokens.shape[0]
     half = rows // 2
@@ -569,12 +603,8 @@
     )
 
     summed.begin()
-    kept = []
-    for lines, hops in ((mine, hops_mine), (other, hops_other)):
-        for line in lines:
-            kept += line.keep(local_line, len(kept))
-    for copy, when in kept:
-        copy.start() if when is None else pl.when(when)(copy.start)
+    placing = Stage([piece for line in mine + other for piece in line.keep()], stage, local_line)
+    placing.begin()
 
     def send_hop(lines, hop):
         for line in lines:
@@ -589,6 +619,7 @@
     send_hop(other, hops_other + 1)
     send_hop(mine, hops_mine + 1)
     summed.turn()
+    placing.turn()
     for piece in range(2):
         summed.arrive(piece)
 
@@ -602,7 +633,12 @@
         spread.begin(piece)
     keep_normed = pltpu.make_async_copy(normed, normed_full.at[:, t, c], local.at[0])
     keep_normed.start()
+    home = mail.slot()
+    stay, go = pl.ds(c * half, half), pl.ds((1 - c) * half, half)
+    keep_home = pltpu.make_async_copy(middle.at[stay], middle_home.at[c], local.at[1])
+    keep_home.start()
     spread.turn()
+    mail.start(home, middle.at[go], middle_home.at[c], cp=1 - c)
     for step in range(1, count):
         hop = hops_other + step
         if hop < count:
@@ -618,14 +654,15 @@
             spread.end()
     if count == 1:
         spread.end()
+    mail.arrive(home, middle_home.at[1 - c], cp=1 - c)
+    keep_home.wait()
     keep_normed.wait()
-    for copy, when in kept:
-        copy.wait() if when is None else pl.when(when)(copy.wait)
+    placing.end()
     mail.finish()
 
 
 def second_gather(count, part, tokens, gain, wide, first_low, first_high, second_low, second_high):
-    slots = 12 * count + 20
+    slots = 12 * count + 24
     rows, width = tokens.shape
     anywhere = pl.BlockSpec(memory_space=pl.ANY)
     vmem = pl.BlockSpec(memory_space=pltpu.VMEM)
@@ -634,23 +671,25 @@
         functools.partial(second_gather_kernel, count),
         out_shape=(
             jax.ShapeDtypeStruct((rows, width), F32),
+            jax.ShapeDtypeStruct((2, rows // 2, width), F32),
             jax.ShapeDtypeStruct((2, 4, 2, rows // 2, width), BF),
             full,
             full,
             full,
         ),
         in_specs=[anywhere, vmem, vmem] + [anywhere] * 5,
-        out_specs=(vmem,) + (anywhere,) * 4,
+        out_specs=(vmem,) + (anywhere,) * 5,
         scratch_shapes=[
             pltpu.VMEM((2, rows, width), BF),
             pltpu.VMEM((2, rows, width), BF),
             pltpu.VMEM((rows, width), BF),
             pltpu.VMEM((rows, width), BF),
             pltpu.VMEM((2, rows // 2, width), BF),
+            pltpu.VMEM((24,) + wide.shape[1:], BF),
             pltpu.SemaphoreType.DMA((slots,)),
             pltpu.SemaphoreType.DMA((slots,)),
             pltpu.SemaphoreType.DMA((2,)),
-            pltpu.SemaphoreType.DMA((24,)),
+            pltpu.SemaphoreType.DMA((2, 24)),
         ],
         compiler_params=pltpu.CompilerParams(
             collective_id=2, has_side_effects=True, vmem_limit_bytes=40 << 20
@@ -812,7 +851,7 @@
 
     core = {}
     mine = {}
-    order = ((1, 0), (0, 0), (0, 1), (1, 1))
+    order = ((0, 0), (0, 1), (1, 0), (1, 1))
     for index, (c_own, t_own) in enumerate(order):
         block_c = c if c_own else 1 - c
         core[c_own, t_own] = mail.slot()
@@ -828,87 +867,100 @@
         for drain in drains:
             drain.gather(1)
             drain.send(1)
-    for c_own, t_own in order:
-        mine[c_own, t_own].wait()
-        mail.arrive(core[c_own, t_own], from_core.at[c_own, t_own], tp=beside)
-        for piece in range(2):
-
-            def add(place, c_own=c_own, t_own=t_own, piece=piece):
-                own[c_own, t_own, piece, place, :] = (
-                    own[c_own, t_own, piece, place, :].astype(F32)
-                    + from_core[c_own, t_own, piece, place, :].astype(F32)
-                ).astype(BF)
-
-            in_pieces(half, add)
-
-    y_first = [mail.slot() for _ in range(2)]
-    x_first = [mail.slot() for _ in range(2)]
-    x_second, y_second = mail.slot(), mail.slot()
-    for c_own in (0, 1):
-        mail.start(y_first[c_own], own.at[c_own, 0, 0], first.at[0, c_own], tp=yonder)
+
+    quarter = half // 2
+    quarters = [(piece, pl.ds(side * quarter, quarter)) for piece in range(2) for side in range(2)]
+    x_first = [[mail.slot() for _ in range(2)] for _ in quarters]
+    y_second = [mail.slot() for _ in quarters]
+    ring_y = [mail.slot() for _ in quarters]
+    ring_core = [mail.slot() for _ in quarters]
+    ring_far = [mail.slot() for _ in quarters]
+
+    def core_add(c_own, t_own, piece, rows):
+        def one(place):
+            row = pl.ds(rows.start + place.start, place.size)
+            own[c_own, t_own, piece, row, :] = (
+                own[c_own, t_own, piece, row, :].astype(F32)
+                + from_core[c_own, t_own, piece, row, :].astype(F32)
+            ).astype(BF)
+
+        in_pieces(quarter, one)
+
     for t_own in (0, 1):
-        mail.start(x_first[t_own], own.at[0, t_own, 1], first.at[1, t_own], cp=1 - c)
-
-    def add_first(side, index, c_own, t_own):
+        mine[0, t_own].wait()
+        mail.arrive(core[0, t_own], from_core.at[0, t_own], tp=beside)
+    for k, (piece, rows) in enumerate(quarters):
+        for t_own in (0, 1):
+            core_add(0, t_own, piece, rows)
+            mail.start(
+                x_first[k][t_own], own.at[0, t_own, piece, rows], first.at[k, t_own], cp=1 - c
+            )
+    for t_own in (0, 1):
+        mine[1, t_own].wait()
+        mail.arrive(core[1, t_own], from_core.at[1, t_own], tp=beside)
+
+    def add_first(k, t_own):
+        piece, rows = quarters[k]
+
         def one(place):
-            own[c_own, t_own, side, place, :] = (
-                own[c_own, t_own, side, place, :].astype(F32)
-                + first[side, index, place, :].astype(F32)
+            row = pl.ds(rows.start + place.start, place.size)
+            own[1, t_own, piece, row, :] = (
+                own[1, t_own, piece, row, :].astype(F32)
+                + from_core[1, t_own, piece, row, :].astype(F32)
+                + first[k, t_own, place, :].astype(F32)
             ).astype(BF)
 
-        in_pieces(half, one)
-
-    mail.arrive(y_first[0], first.at[0, 0], tp=yonder)
-    add_first(0, 0, 0, 1)
-    mail.start(x_second, own.at[0, 1, 0], second.at[0], cp=1 - c)
-    mail.arrive(x_first[0], first.at[1, 0], cp=1 - c)
-    add_first(1, 0, 1, 0)
-    mail.start(y_second, own.at[1, 0, 1], second.at[1], tp=yonder)
-    mail.arrive(y_first[1], first.at[0, 1], tp=yonder)
-    add_first(0, 1, 1, 1)
-    mail.arrive(x_first[1], first.at[1, 1], cp=1 - c)
-    add_first(1, 1, 1, 1)
+        in_pieces(quarter, one)
 
     gain_rows[...] = jnp.zeros_like(gain_rows)
-    ring_y = [mail.slot() for _ in range(2)]
-    ring_core = [mail.slot() for _ in range(4)]
-    keep = []
-    for piece in range(2):
-        if piece == 0:
-            mail.arrive(x_second, second.at[0], cp=1 - c)
-        else:
-            mail.arrive(y_second, second.at[1], tp=yonder)
-
-        def back(place, piece=piece):
-            row = pl.ds(place.start + piece * half, place.size)
-            summed = own[1, 1, piece, place, :].astype(F32) + second[piece, place, :].astype(F32)
-            grad, rows = norm_back(middle[row, :], gain[...], summed)
+
+    def finish(k):
+        piece, rows = quarters[k]
+        mail.arrive(y_second[k], second.at[k], tp=yonder)
+
+        def back(place):
+            local_row = pl.ds(rows.start + place.start, place.size)
+            row = pl.ds(piece * half + rows.start + place.start, place.size)
+            summed = own[1, 1, piece, local_row, :].astype(F32) + second[k, place, :].astype(F32)
+            grad, products = norm_back(middle[row, :], gain[...], summed)
             grad = cotangent[row, :].astype(F32) + grad
             grad_middle[row, :] = grad
-            grad_attention[piece, place, :] = (BRANCH * grad).astype(BF)
-            gain_rows[...] += jnp.sum(rows, axis=0, keepdims=True)
-
-        in_pieces(half, back)
-        mail.start(ring_y[piece], grad_attention.at[piece], attention_full.at[t, piece], tp=yonder)
-        mail.start(
-            ring_core[piece], grad_attention.at[piece], attention_full.at[t, piece], tp=beside
-        )
-    keep = pltpu.make_async_copy(grad_attention, attention_full.at[t], local.at[0])
-    keep.start()
-    for hop in range(2, last):
+            grad_attention[piece, local_row, :] = (BRANCH * grad).astype(BF)
+            gain_rows[...] += jnp.sum(products, axis=0, keepdims=True)
+
+        in_pieces(quarter, back)
+        source = grad_attention.at[piece, rows]
+        mail.start(ring_y[k], source, attention_full.at[t, piece, rows], tp=yonder)
+        mail.start(ring_core[k], source, attention_full.at[t, piece, rows], tp=beside)
+
+    def z_hop(hop):
         for drain in drains:
             drain.arrive(hop - 1)
             drain.gather(hop)
             drain.send(hop)
-    for piece in range(2):
-        mail.arrive(ring_y[piece], attention_full.at[yonder, piece], tp=yonder)
-        mail.start(
-            ring_core[2 + piece], attention_full.at[yonder, piece],
-            attention_full.at[yonder, piece], tp=beside,
-        )
-    for piece in range(2):
-        mail.arrive(ring_core[piece], attention_full.at[beside, piece], tp=beside)
-        mail.arrive(ring_core[2 + piece], attention_full.at[far, piece], tp=beside)
+
+    for k, (piece, rows) in enumerate(quarters):
+        mail.arrive(x_first[k][0], first.at[k, 0], cp=1 - c)
+        add_first(k, 0)
+        mail.start(y_second[k], own.at[1, 0, piece, rows], second.at[k], tp=yonder)
+        mail.arrive(x_first[k][1], first.at[k, 1], cp=1 - c)
+        add_first(k, 1)
+        if k > 0:
+            finish(k - 1)
+        if k == 2 and last > 2:
+            z_hop(2)
+    finish(len(quarters) - 1)
+    keep = pltpu.make_async_copy(grad_attention, attention_full.at[t], local.at[0])
+    keep.start()
+    for hop in range(3, last):
+        z_hop(hop)
+    for k, (piece, rows) in enumerate(quarters):
+        arrived = attention_full.at[yonder, piece, rows]
+        mail.arrive(ring_y[k], arrived, tp=yonder)
+        mail.start(ring_far[k], arrived, arrived, tp=beside)
+    for k, (piece, rows) in enumerate(quarters):
+        mail.arrive(ring_core[k], attention_full.at[beside, piece, rows], tp=beside)
+        mail.arrive(ring_far[k], attention_full.at[far, piece, rows], tp=beside)
     for drain in drains:
         if last > 1:
             drain.arrive(last - 1)
@@ -919,7 +971,7 @@
 
 
 def first_sum(count, part, gate_grad, up_grad, middle, cotangent, gain):
-    slots = 6 * count + 24
+    slots = 6 * count + 32
     rows, width = middle.shape
     block = gate_grad.shape[1:]
     anywhere = pl.BlockSpec(memory_space=pl.ANY)
@@ -939,8 +991,8 @@
         scratch_shapes=[
             pltpu.VMEM((2, 2, 2, rows // 2, width), BF),
             pltpu.VMEM((2, 2, 2, rows // 2, width), BF),
-            pltpu.VMEM((2, 2, rows // 2, width), BF),
-            pltpu.VMEM((2, rows // 2, width), BF),
+            pltpu.VMEM((4, 2, rows // 4, width), BF),
+            pltpu.VMEM((4, rows // 4, width), BF),
             pltpu.VMEM((2, rows // 2, width), BF),
             pltpu.VMEM((2, hops, 2) + block, BF),
             pltpu.VMEM((2, hops, 2) + block, BF),
@@ -952,6 +1004,9 @@
             collective_id=3, has_side_effects=True, vmem_limit_bytes=60 << 20
         ),
     )(part, gate_grad, up_grad, middle, cotangent, gain)
+
+
+AHEAD = 4
 
 
 def last_sum_kernel(
@@ -970,28 +1025,34 @@
 
     summed = TensorSum(mail, part, own, from_core, to_yonder, from_yonder, local)
 
-    cross = [[mail.slot() for _ in range(count)] for _ in range(2)]
-    cross_own = mail.slot()
-
-    def fill_heads(hop, up, j, target):
-        side = 0 if up else 1
-        copy = pltpu.make_async_copy(qkv_grad.at[j, c], target, local.at[2])
-        copy.start()
-        mail.arrive(cross[side][hop], from_x.at[side, hop - 1], cp=1 - c)
-        copy.wait()
-
-        def one(place):
-            target[place, :] = (
-                target[place, :].astype(F32) + from_x[side, hop - 1, place, :].astype(F32)
-            ).astype(BF)
-
-        in_pieces(target.shape[0], one)
-
-    heads = Drain(
-        mail, count, fill_heads,
-        lambda side, hop: heads_sum.at[side, hop - 1],
-        lambda side, hop: heads_landed.at[side, hop - 1],
-    )
+    columns = qkv_total.shape[1]
+    split = -(-columns // (2 * TILE)) * TILE
+    parts = [pl.ds(0, split), pl.ds(split, columns - split)]
+    cross = [[[mail.slot() for _ in range(count)] for _ in range(2)] for _ in parts]
+    cross_own = [mail.slot() for _ in parts]
+
+    def head_drain(lanes):
+        def fill(hop, up, j, target):
+            side = 0 if up else 1
+            copy = pltpu.make_async_copy(qkv_grad.at[j, c, :, lanes], target, local.at[2])
+            copy.start()
+            copy.wait()
+            arrived = from_x.at[side, hop - 1, :, lanes]
+
+            def one(place):
+                target[place, :] = (
+                    target[place, :].astype(F32) + arrived[place, :].astype(F32)
+                ).astype(BF)
+
+            in_pieces(target.shape[0], one)
+
+        return Drain(
+            mail, count, fill,
+            lambda side, hop: heads_sum.at[side, hop - 1, :, lanes],
+            lambda side, hop: heads_landed.at[side, hop - 1, :, lanes],
+        )
+
+    heads = [head_drain(lanes) for lanes in parts]
 
     def fill_outs(hop, up, j, target):
         copy = pltpu.make_async_copy(out_grad.at[j], target, local.at[3])
@@ -1004,21 +1065,37 @@
         lambda side, hop: outs_landed.at[side, hop - 1],
     )
 
-    def cross_send(hop):
+    steps = [(hop, k) for hop in range(1, count + 1) for k in range(2)]
+
+    def cross_send(step):
+        if step >= len(steps):
+            return
+        hop, k = steps[step]
+        lanes = parts[k]
         if hop == count:
-            mail.start(cross_own, qkv_grad.at[z, 1 - c], from_x.at[0, last], cp=1 - c)
-        elif hop < count:
-            for side, up in enumerate((True, False)):
-                mail.start(
-                    cross[side][hop], qkv_grad.at[heads.block(hop, up), 1 - c],
-                    from_x.at[side, hop - 1], when=heads.sends(hop, up), cp=1 - c,
-                )
-
-    cross_send(1)
-    cross_send(2)
+            mail.start(
+                cross_own[k], qkv_grad.at[z, 1 - c, :, lanes], from_x.at[0, last, :, lanes], cp=1 - c
+            )
+            return
+        for side, up in enumerate((True, False)):
+            mail.start(
+                cross[k][side][hop], qkv_grad.at[heads[k].block(hop, up), 1 - c, :, lanes],
+                from_x.at[side, hop - 1, :, lanes], when=heads[k].sends(hop, up), cp=1 - c,
+            )
+
+    def cross_arrive(hop, k):
+        for side, up in enumerate((True, False)):
+            mail.arrive(
+                cross[k][side][hop], from_x.at[side, hop - 1, :, parts[k]],
+                when=heads[k].sends(hop, up), cp=1 - c,
+            )
+
+    for step in range(AHEAD):
+        cross_send(step)
     summed.begin()
-    outs.gather(1)
-    outs.send(1)
+    if count > 1:
+        outs.gather(1)
+        outs.send(1)
     summed.turn()
 
     keep = pltpu.make_async_copy(pieces.at[c], grad_tokens.at[c], local.at[0])
@@ -1063,20 +1140,29 @@
             if hop + 1 < count:
                 line.send(hop + 1)
 
-    for hop in range(1, count):
+    def outs_hop(hop):
+        outs.arrive(hop - 1)
+        outs.gather(hop)
+        outs.send(hop)
+
+    early = min(3, count)
+    for hop in range(2, early + 1):
+        if hop < count:
+            outs_hop(hop)
+    for step, (hop, k) in enumerate(steps[:-2]):
+        cross_arrive(hop, k)
+        cross_send(step + AHEAD)
         if hop > 1:
-            heads.arrive(hop - 1)
-        heads.gather(hop)
-        heads.send(hop)
-        cross_send(hop + 2)
-        if hop > 1:
-            outs.arrive(hop - 1)
-            outs.gather(hop)
-            outs.send(hop)
-        if hop == 1:
+            heads[k].arrive(hop - 1)
+        heads[k].gather(hop)
+        heads[k].send(hop)
+        if k == 1 and hop > early:
+            outs_hop(hop)
+        if step == 2 or step == 1 and count == 2:
             finish_rows()
-        if hop == 2:
+        if step == 4:
             gain_step(0)
+        if step == 5:
             gain_step(1)
     if count == 1:
         finish_rows()
@@ -1089,7 +1175,8 @@
     own_copy.start()
     out_copy = pltpu.make_async_copy(out_grad.at[z], final_out, local.at[3])
     out_copy.start()
-    mail.arrive(cross_own, from_x.at[0, last], cp=1 - c)
+    for k, lanes in enumerate(parts):
+        mail.arrive(cross_own[k], from_x.at[0, last, :, lanes], cp=1 - c)
     own_copy.wait()
     out_copy.wait()
 
@@ -1107,16 +1194,17 @@
     for hop in range(1, count):
         gain_step(2 + hop)
     if count > 1:
-        outs.arrive(last)
-        heads.arrive(last)
-        for drain, total in ((outs, out_total), (heads, qkv_total)):
+        chains = [(outs, pl.ds(0, out_total.shape[1]), out_total)]
+        chains += [(heads[k], lanes, qkv_total) for k, lanes in enumerate(parts)]
+        for drain, lanes, total in chains:
+            drain.arrive(last)
             for side, up in enumerate((True, False)):
 
-                def more(drain=drain, total=total, side=side):
+                def more(drain=drain, total=total, side=side, lanes=lanes):
                     landed = drain.landed(side, last)
 
                     def one(place):
-                        total[place, :] += landed[place, :].astype(F32)
+                        total[place, lanes] += landed[place, :].astype(F32)
 
                     in_pieces(total.shape[0], one)
 
@@ -1128,7 +1216,7 @@
 
 
 def last_sum(count, part, qkv_grad, out_grad, tokens, grad_middle, gain, gain_rows):
-    slots = 8 * count + 16
+    slots = 13 * count + 16
     rows, width = tokens.shape
     hops = max(count - 1, 1)
     block, out_block = qkv_grad.shape[2:], out_grad.shape[1:]
@@ -1240,12 +1328,6 @@
     def pick(value, which, axis=0):
         return lax.dynamic_index_in_dim(value, which, axis, keepdims=False)
 
-    def from_sequence(value):
-        value = value.reshape(sets, local, width)
-        mine = pick(value, c)
-        other = swap(pick(value, 1 - c))
-        return in_order(c, mine[None], other[None], 0)
-
     length = pick(seq_lengths, c)[None]
     gain_one = attention_gain.astype(F32)
     gain_two = feedforward_gain.astype(F32)
@@ -1283,7 +1365,7 @@
     )
     part = cols_inner(context, full_out).astype(BF)
 
-    middle, normed_two, full_gate, full_up, full_down = second_gather(
+    middle, middle_home, normed_two, full_gate, full_up, full_down = second_gather(
         count, part.reshape(lanes, rows, width), token_rows, gain_two[None], own_wide,
         first_low, first_high, second_low, second_high,
     )
@@ -1292,8 +1374,7 @@
         full.reshape(width, hidden_width) for full in (full_gate, full_up, full_down)
     )
     t = lax.axis_index("tp")
-    grad_branch = (BRANCH * cotangents.astype(F32)).astype(BF).reshape(sets * seq, width)
-    middle_home = from_sequence(middle)
+    cotangents_all = cotangents.reshape(sets * seq, width)
     cotangent_rows = pick(pick(cotangents, t, 1), c, 1).reshape(rows, width)
     gate_pre = matmul(normed_two, full_gate)
     up_pre = matmul(normed_two, full_up)
@@ -1304,7 +1385,7 @@
         gradient = row_major(gradient.astype(BF))
         return gradient.reshape(count, width // count, hidden_width)
 
-    down_blocks = blocks_of(rows_inner(grad_branch, hidden))
+    down_blocks = blocks_of(BRANCH * rows_inner(cotangents_all, hidden))
     low = high = None
     for hop in range(1, count):
         leaving_up = pick(down_blocks, jnp.minimum(z + count - hop, count - 1))
@@ -1315,7 +1396,7 @@
         if hop < count - 1:
             low = lax.ppermute(leaving_up, "fsdp", up_hop[:hop])
             high = lax.ppermute(leaving_down, "fsdp", down_hop[count - 1 - hop :])
-    grad_hidden = matmul(grad_branch, full_down)
+    grad_hidden = BRANCH * matmul(cotangents_all, full_down)
     grad_gate_exact, grad_up_exact = silu_back(grad_hidden)
     grad_gate_pre = grad_gate_exact.astype(BF)
     grad_up_pre = grad_up_exact.astype(BF)
@@ -1325,7 +1406,6 @@
     part = grad_normed_two.astype(BF).reshape(sets, lanes, slots, local, width)
     if count > 1:
         part, leaving_up, leaving_down = lax.optimization_barrier((part, leaving_up, leaving_down))
-    part, middle_home = lax.optimization_barrier((part, middle_home))
     grad_middle, grad_attention, gain_two_rows, pair_up, pair_down = first_sum(
         count, part, gate_blocks, up_blocks, middle, cotangent_rows, gain_two[None],
     )

time: 891 us -> 832 us (0.934)
  Pallas kernels: 573 us -> 528 us
  other arithmetic: 43 us -> 28.6 us
  waiting for transfers between devices: 13.8 us -> 2.25 us
  local copies, waits for them, and re-layouts: 24.3 us -> 34.1 us
    pallas_call x1, Pallas kernels: 179 us -> 136 us  [first_gather(): pl.pallas_call(functools.partial(first_gather_kernel, count), out_shape=(...]
    ppermute x4 -> x3, waiting for transfers between devices: 12.3 us -> 0.01 us  [swap(): return lax.ppermute(value, 'cp', [(0, 1), (1, 0)])]
    unnamed x72 -> x94, local copies, waits for them, and re-layouts: 7.75 us -> 17.7 us
    convert_element_type x1 -> x0, other arithmetic: 9.61 us -> none  [on_device(): (BRANCH * cotangents.astype(F32)).astype(BF).reshape(sets * seq, width)]
  transfers between devices with their start and end apart: 16 -> 15, of which waited for: 2 -> 1; matrix products, arithmetic and copies ran while one was open for 18% -> 18% of each run, Pallas kernels for 34% -> 36%
where the time goes in v4:
time: 832 us; the launch traced here: 827 us
  Pallas kernels  528 us (63%)
  matrix products  177 us (21%)
  starting transfers between devices  42 us (5%)
  local copies, waits for them, and re-layouts  34.1 us (4%)
  other arithmetic  28.6 us (3%)
  between operations  14.9 us (2%)
    pallas_call x1, Pallas kernels, first_gather(): pl.pallas_call(functools.partial(first_gather_kernel, count), out_shape=(...  136 us
    pallas_call x1, Pallas kernels, last_sum(): pl.pallas_call(functools.partial(last_sum_kernel, count), out_shape=(jax....  130 us
    pallas_call x1, Pallas kernels, second_gather(): pl.pallas_call(functools.partial(second_gather_kernel, count), out_shape=...  94.4 us
    pallas_call x1, Pallas kernels, first_sum(): pl.pallas_call(functools.partial(first_sum_kernel, count), out_shape=(jax...  93.3 us
    dot_general x5, matrix products, matmul(): return jnp.dot(left, right, preferred_element_type=F32)  65.8 us
    dot_general x5, matrix products, cols_inner(): lax.dot_general(left, right, (((1,), (1,)), ((), ())), preferred_element_...  58.5 us
    dot_general x5, matrix products, rows_inner(): lax.dot_general(left, right, (((0,), (0,)), ((), ())), preferred_element_...  52.8 us
    pallas_call x1, Pallas kernels, attention_back(): pl.pallas_call(functools.partial(attention_back_kernel, blocks), out_shap...  39.9 us
  transfers between devices with their start and end apart: 15, of which 1 were waited for; matrix products, arithmetic and copies ran while one was open for 18% of the time, Pallas kernels for 36%

profile of v4, /device:TPU:0, one launch (start us, length us, event | category | flops | bytes accessed | tf_op | source)
XLA Modules:
  0.0 827.5 jit_solution(5864925028399024360)
XLA Ops:
  18.7 135.9 %shard_map.221 = (bf16[2,128,2304]{2,1,0:T(8,128)(2,1)S(1)}, bf16[4,2,128,2304]{3,2,1,0:T(8,128)(2,1)S(1)}, bf16[4,2,288,1728]{3,2,1,0:T(8,128)(2,1)}, bf16[4,28...) custom-call(bf16[128,2304]{1,0:T(8,128)(2,1)S(1)} %get-tuple-element.99.tokens, ...), custom_call_target="tpu_custom_call" | custom-call | tf_op jit(solution)/shard_map/pallas_call | solution.py:479
  163.5 5.0 collective-permute-start.1
  170.8 15.3 %fusion.11.projected = f32[1024,1728]{1,0:T(8,128)} fusion(bf16[1024,2304]{1,0:T(8,128)(2,1)} %bitcast.130, bf16[2304,1728]{1,0:T(8,128)(2,1)} %bitcast.169), kind=kOutput, calls=%fused_computation.66 | convolution fusion | flops 8153726976 | bytes 19759104 | tf_op jit(solution)/shard_map/dot_general | solution.py:1268
  186.1 34.6 %shard_map.222 = (bf16[1024,576]{1,0:T(8,128)(2,1)S(1)}, bf16[9,1024,64]{2,1,0:T(8,128)(2,1)S(1)}, bf16[9,1024,64]{2,1,0:T(8,128)(2,1)}, bf16[9,1024,64]{2,1,0:T(8,128)(2,1)}, f32[9,1,1024]{2,1,0:T(1,128)S(1)}) custom-call(s32[1]{0:T(128)} %dynamic_slice.71.length_ref, f32[1024,1728]{1,0:T(8,128)} %fusion.11.projected, f32[1024,128]{1,0:T(8,128)S(1)} %copy-done.17, ...), custom_call_target="tpu_custom_call" | custom-call | flops 2415919104 | bytes 20971520 | tf_op jit(solution)/shard_map/pallas_call | solution.py:107
  222.6 6.0 convolution_convert_fusion.3
  228.7 94.4 %shard_map.223 = (f32[256,2304]{1,0:T(8,128)S(1)}, f32[2,128,2304]{2,1,0:T(8,128)S(1)}, bf16[2,4,2,128,2304]{4,3,2,1,0:T(8,128)(2,1)}, bf16[4,2,288,720]{3,2,1,0...) custom-call(bf16[4,256,2304]{2,1,0:T(8,128)(2,1)} %bitcast.153, ...), custom_call_target="tpu_custom_call" | custom-call | tf_op jit(solution)/shard_map/pallas_call | solution.py:670
  325.9 12.5 %fusion.12 = f32[2048,720]{0,1:T(8,128)} fusion(bf16[2048,2304]{1,0:T(8,128)(2,1)} %bitcast.165, bf16[2304,720]{1,0:T(8,128)(2,1)} %bitcast.177), kind=kOutput, calls=%fused_computation.67 | convolution fusion | flops 6794772480 | bytes 18653184 | tf_op jit(solution)/shard_map/dot_general | solution.py:1268
  338.4 11.3 %fusion.13 = f32[2048,720]{0,1:T(8,128)} fusion(bf16[2048,2304]{1,0:T(8,128)(2,1)} %bitcast.162, bf16[2304,720]{1,0:T(8,128)(2,1)S(1)} %bitcast.173), kind=kOutput, calls=%fused_computation.68 | convolution fusion | flops 6794772480 | bytes 18653184 | tf_op jit(solution)/shard_map/dot_general | solution.py:1268
  349.7 19.2 %add_convert_fusion.1 = (bf16[2048,720]{0,1:T(8,128)(2,1)}, bf16[2048,720]{0,1:T(8,128)(2,1)}, bf16[2048,720]{0,1:T(8,128)(2,1)}) fusion(f32[2048,720]{0,1:T(8,128)} %fusion.12, f32[2048,720]{0,1:T(8,128)} %fusion.13, bf16[2048,2304]{1,0:T(8,128)(2,1)} %bitcast.166, bf16[2304,720]{1,0:T(8,128)(2,1)} %bitcast.175), kind=kOutput, calls=%fused_computation.5 | convolution fusion | flops 6822789120 | bytes 33398784 | tf_op jit(solution)/shard_map/dot_general | solution.py:1268
  368.9 11.2 %multiply_convert_fusion = bf16[2304,720]{1,0:T(8,128)(2,1)S(1)} fusion(bf16[2048,2304]{1,0:T(8,128)(2,1)} %bitcast.163, bf16[2048,720]{0,1:T(8,128)(2,1)} %get-tuple-element.63), kind=kOutput, calls=%fused_computation.3 | convolution fusion | flops 6798090240 | bytes 15704064 | tf_op jit(solution)/shard_map/dot_general | solution.py:1272
  384.8 11.2 %fusion.14 = f32[2048,2304]{1,0:T(8,128)} fusion(bf16[2048,720]{0,1:T(8,128)(2,1)S(1)} %copy-done.42, bf16[2304,720]{1,0:T(8,128)(2,1)S(1)} %bitcast.178), kind=kOutput, calls=%fused_computation.69 | convolution fusion | flops 6794772480 | bytes 25141248 | tf_op jit(solution)/shard_map/dot_general | solution.py:1276
  396.0 15.4 %add_convert_fusion = bf16[2048,2304]{1,0:T(8,128)(2,1)} fusion(f32[2048,2304]{1,0:T(8,128)} %fusion.14, bf16[2048,720]{0,1:T(8,128)(2,1)} %get-tuple-element.83, bf16[2304,720]{1,0:T(8,128)(2,1)} %bitcast.176), kind=kOutput, calls=%fused_computation | convolution fusion | flops 6804209664 | bytes 34578432 | tf_op jit(solution)/shard_map/dot_general | solution.py:1276
  412.4 12.4 %convolution_convert_fusion.5 = bf16[2304,720]{1,0:T(8,128)(2,1)} fusion(bf16[2048,2304]{1,0:T(8,128)(2,1)} %bitcast.167, bf16[2048,720]{0,1:T(8,128)(2,1)} %get-tuple-element.83), kind=kOutput, calls=%fused_computation.12 | convolution fusion | flops 6796431360 | bytes 15704064 | tf_op jit(solution)/shard_map/dot_general | solution.py:1272
  427.5 9.2 %collective-permute-start.4 = (bf16[576,720]{1,0:T(8,128)(2,1)S(1)}, bf16[576,720]{1,0:T(8,128)(2,1)S(1)}, u32[]{:S(2)}, u32[]{:S(2)}) collective-permute-start(bf16[576,720]{1,0:T(8,128)(2,1)S(1)} %get-tuple-element.89), channel_id=1, source_target_pairs={{0,8},{8,16},{1,9},{9,17},{2,10},{10,18},{3,11},{11,19},{4,12},{12... | collective-permute-start | bytes 2488328 | tf_op jit(solution)/shard_map/ppermute | solution.py:1397
  436.7 11.9 %convolution_convert_fusion.4 = bf16[2304,720]{1,0:T(8,128)(2,1)} fusion(bf16[2048,2304]{1,0:T(8,128)(2,1)} %bitcast.168, bf16[2048,720]{0,1:T(8,128)(2,1)S(1)} %copy-done.43), kind=kOutput, calls=%fused_computation.11 | convolution fusion | flops 6796431360 | bytes 15704064 | tf_op jit(solution)/shard_map/dot_general | solution.py:1272
  454.2 93.3 %shard_map.224 = (f32[256,2304]{1,0:T(8,128)}, bf16[4,2,128,2304]{3,2,1,0:T(8,128)(2,1)}, f32[1,2304]{1,0:T(1,128)}, bf16[2,576,720]{2,1,0:T(8,128)(2,1)}, bf16[2,576,720]{2,1,0:T(8,128)(2,1)}) custom-call(bf16[2,4,2,128,2304]{4,3,2,1,0:T(8,128)(2,1)} %bitcast.139, bf16[4,576,720]{2,1,0:T(8,128)(2,1)} %bitcast.142, bf16[4,576,720]{2,1,0:T(8,128)(2,1)} %bitcast.144, ...), custom_call_target="tpu_custom_call" | custom-call | tf_op jit(solution)/shard_map/pallas_call | solution.py:980
  547.5 11.8 %convolution_convert_fusion.1 = bf16[2048,2304]{1,0:T(8,128)(2,1)} fusion(bf16[2048,720]{0,1:T(8,128)(2,1)} %get-tuple-element.63, bf16[2304,720]{1,0:T(8,128)(2,1)S(1)} %bitcast.174), kind=kOutput, calls=%fused_computation.2 | convolution fusion | flops 6799491072 | bytes 15704064 | tf_op jit(solution)/shard_map/dot_general | solution.py:1276
  559.4 8.6 %collective-permute-start.8 = (bf16[576,720]{1,0:T(8,128)(2,1)}, bf16[576,720]{1,0:T(8,128)(2,1)}, u32[]{:S(2)}, u32[]{:S(2)}) collective-permute-start(bf16[576,720]{1,0:T(8,128)(2,1)} %fusion.6), channel_id=1, source_target_pairs={{0,8},{8,16},{16,24},{1,9},{9,17},{17,25},{2,10},{10,18},{18,26},{... | collective-permute-start | bytes 2488328 | tf_op jit(solution)/shard_map/ppermute | solution.py:1416
  569.5 6.4 convolution_convert_fusion.6
  579.8 7.5 convolution_convert_fusion.7.grad_context
  593.5 39.9 %shard_map.225 = bf16[1024,1728]{1,0:T(8,128)(2,1)} custom-call(s32[1]{0:T(128)} %dynamic_slice.71.length_ref, bf16[1024,576]{1,0:T(8,128)(2,1)} %convolution_convert_fusion.7.grad_context, bf16[9,1024,64]{2,1,0:T(8,128)(2,1)} %copy-done.18, bf16[9,1024,64]{2,1,0:T(8,128)(2,1)} %get-tuple-element.65.k_heads, bf16[9,1024,64]{2,1,0:T(8,128)(2,1)} %get-tuple-element.66.v_heads, ...), custom_call_target="tpu_custom_call" | custom-call | flops 6039797760 | bytes 20971520 | tf_op jit(solution)/shard_map/pallas_call | solution.py:186
  636.3 11.0 %convolution_convert_fusion = bf16[2304,1728]{1,0:T(8,128)(2,1)} fusion(bf16[1024,2304]{1,0:T(8,128)(2,1)S(1)} %bitcast.133, bf16[1024,1728]{1,0:T(8,128)(2,1)S(1)} %copy-done.40), kind=kOutput, calls=%fused_computation.1 | convolution fusion | flops 8157708288 | bytes 16220160 | tf_op jit(solution)/shard_map/dot_general | solution.py:1272
  656.3 14.1 %convolution_convert_fusion.2 = bf16[1024,2304]{1,0:T(8,128)(2,1)} fusion(bf16[1024,1728]{1,0:T(8,128)(2,1)S(1)} %copy-done.41, bf16[2304,1728]{1,0:T(8,128)(2,1)} %bitcast.170), kind=kOutput, calls=%fused_computation.9 | convolution fusion | flops 8156086272 | bytes 16220160 | tf_op jit(solution)/shard_map/dot_general | solution.py:1276
  673.3 130.4 %shard_map.226 = (f32[288,1728]{1,0:T(8,128)}, f32[288,576]{1,0:T(8,128)}, bf16[2,128,2304]{2,1,0:T(8,128)(2,1)}, f32[2,2304]{1,0:T(2,128)}) custom-call(bf16[4,256,2304]{2,1,0:T(8,128)(2,1)} %bitcast.154, bf16[4,2,288,1728]{3,2,1,0:T(8,128)(2,1)} %bitcast.141, bf16[4,288,576]{2,1,0:T(8,128)(2,1)} %fusion.out_grad, bf16[256,2304]{1,0:T(8,128)(2,1)} %bitcast.126, ...), custom_call_target="tpu_custom_call" | custom-call | tf_op jit(solution)/shard_map/pallas_call | solution.py:1225
  (158 shorter events, 84.2 us)
Async XLA Ops:
  7.2 331.2 %all-gather.3.cloned.1.call-start = ((), (), s32[]{:S(2)}) async-start(), calls=%async_computation.2 | async-start | bytes 10616832 | tf_op jit(solution)/shard_map/all_gather | solution.py:1352
  18.7 151.4 %copy-start.39 = (s32[2]{0:T(128)S(1)}, s32[2]{0:T(128)}, u32[]{:S(2)}) copy-start(s32[2]{0:T(128)} %param.15) | copy-start | bytes 28
  18.7 152.0 %copy-start.35 = (bf16[2304]{0:T(1024)(128)(2,1)S(1)}, bf16[2304]{0:T(1024)(128)(2,1)}, u32[]{:S(2)}) copy-start(bf16[2304]{0:T(1024)(128)(2,1)} %param.21) | copy-start | bytes 13828
  161.9 653.7 %reduce-scatter.2.cloned.1.call-start = ((), (), s32[]{:S(2)}) async-start(), calls=%async_computation.1 | async-start | bytes 10616832 | tf_op jit(solution)/shard_map/reduce_scatter | solution.py:1445
  162.0 58.8 %collective-permute-start = (bf16[4,288,576]{2,1,0:T(8,128)(2,1)}, bf16[4,288,576]{2,1,0:T(8,128)(2,1)S(1)}, u32[]{:S(2)}, u32[]{:S(2)}) collective-permute-start(bf16[4,288,576]{2,1,0:T(8,128)(2,1)} %copy-done.10), channel_id=1, source_target_pairs={{0,4},{4,0},{1,5},{5,1},{2,6},{6,2},{3,7},{7,3},{8,12},{12,8},{9,1... | collective-permute-start | bytes 3981320 | tf_op jit(solution)/shard_map/ppermute | solution.py:1288
  163.5 65.1 %collective-permute-start.1 = (bf16[2,3,288,720]{3,2,1,0:T(8,128)(2,1)}, bf16[2,3,288,720]{3,2,1,0:T(8,128)(2,1)}, u32[]{:S(2)}, u32[]{:S(2)}) collective-permute-start(bf16[2,3,288,720]{3,2,1,0:T(8,128)(2,1)} %copy-done.3), channel_id=1, source_target_pairs={{0,8},{8,16},{16,24},{1,9},{9,17},{17,25},{2,10},{10,18},{18,26},{... | collective-permute-start | bytes 7464968 | tf_op jit(solution)/shard_map/ppermute | solution.py:1359
  168.5 60.1 %collective-permute-start.2 = (bf16[2,3,288,720]{3,2,1,0:T(8,128)(2,1)}, bf16[2,3,288,720]{3,2,1,0:T(8,128)(2,1)}, u32[]{:S(2)}, u32[]{:S(2)}) collective-permute-start(bf16[2,3,288,720]{3,2,1,0:T(8,128)(2,1)} %copy-done.5), channel_id=1, source_target_pairs={{8,0},{16,8},{24,16},{9,1},{17,9},{25,17},{10,2},{18,10},{26,18},{... | collective-permute-start | bytes 7464968 | tf_op jit(solution)/shard_map/ppermute | solution.py:1360
  170.7 57.9 %copy-start.13 = (f32[1,2304]{1,0:T(1,128)}, f32[1,2304]{1,0:T(1,128)S(1)}, u32[]{:S(2)}) copy-start(f32[1,2304]{1,0:T(1,128)S(1)} %reshape.157.gain) | copy-start | bytes 27652
  186.1 34.7 %copy-start.11 = (bf16[4,288,576]{2,1,0:T(8,128)(2,1)S(1)}, bf16[4,288,576]{2,1,0:T(8,128)(2,1)}, u32[]{:S(2)}) copy-start(bf16[4,288,576]{2,1,0:T(8,128)(2,1)} %copy-done.10) | copy-start | bytes 3981316
  380.1 73.0 %copy-start.22 = (bf16[2304,720]{1,0:T(8,128)(2,1)}, bf16[2304,720]{1,0:T(8,128)(2,1)S(1)}, u32[]{:S(2)}) copy-start(bf16[2304,720]{1,0:T(8,128)(2,1)S(1)} %multiply_convert_fusion) | copy-start | bytes 9953284
  381.5 30.0 %collective-permute-start.5 = (bf16[576,720]{1,0:T(8,128)(2,1)}, bf16[576,720]{1,0:T(8,128)(2,1)S(1)}, u32[]{:S(2)}, u32[]{:S(2)}) collective-permute-start(bf16[576,720]{1,0:T(8,128)(2,1)} %get-tuple-element.90), channel_id=1, source_target_pairs={{24,16},{25,17},{26,18},{27,19},{28,20},{29,21},{30,22},{31,23}} | collective-permute-start | bytes 2488328 | tf_op jit(solution)/shard_map/ppermute | solution.py:1398
  382.3 42.4 %collective-permute-start.3 = (bf16[576,720]{1,0:T(8,128)(2,1)}, bf16[576,720]{1,0:T(8,128)(2,1)}, u32[]{:S(2)}, u32[]{:S(2)}) collective-permute-start(bf16[576,720]{1,0:T(8,128)(2,1)} %get-tuple-element.91), channel_id=1, source_target_pairs={{0,8},{1,9},{2,10},{3,11},{4,12},{5,13},{6,14},{7,15}} | collective-permute-start | bytes 2488328 | tf_op jit(solution)/shard_map/ppermute | solution.py:1397
  411.6 13.1 %collective-permute-start.6 = (bf16[576,720]{1,0:T(8,128)(2,1)S(1)}, bf16[576,720]{1,0:T(8,128)(2,1)S(1)}, u32[]{:S(2)}, u32[]{:S(2)}) collective-permute-start(bf16[576,720]{1,0:T(8,128)(2,1)S(1)} %fusion.3), channel_id=1, source_target_pairs={{16,8},{24,16},{17,9},{25,17},{18,10},{26,18},{19,11},{27,19},{20,... | collective-permute-start | bytes 2488328 | tf_op jit(solution)/shard_map/ppermute | solution.py:1398
  427.5 25.6 %collective-permute-start.4 = (bf16[576,720]{1,0:T(8,128)(2,1)S(1)}, bf16[576,720]{1,0:T(8,128)(2,1)S(1)}, u32[]{:S(2)}, u32[]{:S(2)}) collective-permute-start(bf16[576,720]{1,0:T(8,128)(2,1)S(1)} %get-tuple-element.89), channel_id=1, source_target_pairs={{0,8},{8,16},{1,9},{9,17},{2,10},{10,18},{3,11},{11,19},{4,12},{12... | collective-permute-start | bytes 2488328 | tf_op jit(solution)/shard_map/ppermute | solution.py:1397
  454.2 93.3 %copy-start.37 = (bf16[4,2,288,720]{3,2,1,0:T(8,128)(2,1)S(1)}, bf16[4,2,288,720]{3,2,1,0:T(8,128)(2,1)}, u32[]{:S(2)}) copy-start(bf16[4,2,288,720]{3,2,1,0:T(8,128)(2,1)} %get-tuple-element.59) | copy-start | bytes 9953284
  559.4 74.0 %collective-permute-start.8 = (bf16[576,720]{1,0:T(8,128)(2,1)}, bf16[576,720]{1,0:T(8,128)(2,1)}, u32[]{:S(2)}, u32[]{:S(2)}) collective-permute-start(bf16[576,720]{1,0:T(8,128)(2,1)} %fusion.6), channel_id=1, source_target_pairs={{0,8},{8,16},{16,24},{1,9},{9,17},{17,25},{2,10},{10,18},{18,26},{... | collective-permute-start | bytes 2488328 | tf_op jit(solution)/shard_map/ppermute | solution.py:1416
  568.0 65.4 %collective-permute-start.9 = (bf16[576,720]{1,0:T(8,128)(2,1)}, bf16[576,720]{1,0:T(8,128)(2,1)}, u32[]{:S(2)}, u32[]{:S(2)}) collective-permute-start(bf16[576,720]{1,0:T(8,128)(2,1)} %get-tuple-element.71), channel_id=1, source_target_pairs={{8,0},{16,8},{24,16},{9,1},{17,9},{25,17},{10,2},{18,10},{26,18},{... | collective-permute-start | bytes 2488328 | tf_op jit(solution)/shard_map/ppermute | solution.py:1418
  577.1 58.4 %collective-permute-start.7 = (bf16[4,288,576]{2,1,0:T(8,128)(2,1)}, bf16[4,288,576]{2,1,0:T(8,128)(2,1)}, u32[]{:S(2)}, u32[]{:S(2)}) collective-permute-start(bf16[4,288,576]{2,1,0:T(8,128)(2,1)} %dynamic-slice_bitcast_fusion), channel_id=1, source_target_pairs={{0,4},{4,0},{1,5},{5,1},{2,6},{6,2},{3,7},{7,3},{8,12},{12,8},{9,1... | collective-permute-start | bytes 3981320 | tf_op jit(solution)/shard_map/ppermute | solution.py:1288
  587.3 60.0 %collective-permute-start.10 = (bf16[2,576,720]{2,1,0:T(8,128)(2,1)}, bf16[2,576,720]{2,1,0:T(8,128)(2,1)S(1)}, u32[]{:S(2)}, u32[]{:S(2)}) collective-permute-start(bf16[2,576,720]{2,1,0:T(8,128)(2,1)} %get-tuple-element.79), channel_id=1, source_target_pairs={{0,8},{8,16},{16,24},{1,9},{9,17},{17,25},{2,10},{10,18},{18,26},{... | collective-permute-start | bytes 4976648 | tf_op jit(solution)/shard_map/ppermute | solution.py:1416
  592.1 56.3 %collective-permute-start.11 = (bf16[2,576,720]{2,1,0:T(8,128)(2,1)}, bf16[2,576,720]{2,1,0:T(8,128)(2,1)}, u32[]{:S(2)}, u32[]{:S(2)}) collective-permute-start(bf16[2,576,720]{2,1,0:T(8,128)(2,1)} %get-tuple-element.80), channel_id=1, source_target_pairs={{8,0},{16,8},{24,16},{9,1},{17,9},{25,17},{10,2},{18,10},{26,18},{... | collective-permute-start | bytes 4976648 | tf_op jit(solution)/shard_map/ppermute | solution.py:1418
  593.4 42.1 %slice-start = ((s8[4718592]{0:T(1024)(128)(4,1)}), s8[4194304]{0:T(1024)(128)(4,1)S(1)}, s32[]{:S(2)}) async-start(s8[4718592]{0:T(1024)(128)(4,1)} %bitcast.131), calls=%async_computation.3 | async-start | bytes 8388608
  593.5 42.1 %slice-start.1 = ((s8[4718592]{0:T(1024)(128)(4,1)}), s8[524288]{0:T(1024)(128)(4,1)S(1)}, s32[]{:S(2)}) async-start(s8[4718592]{0:T(1024)(128)(4,1)} %bitcast.131), calls=%async_computation.4 | async-start | bytes 1048576
  654.1 16.4 %copy-start.26 = (bf16[2304,576]{1,0:T(8,128)(2,1)S(1)}, bf16[2304,576]{1,0:T(8,128)(2,1)}, u32[]{:S(2)}) copy-start(bf16[2304,576]{1,0:T(8,128)(2,1)} %copy-done.25) | copy-start | bytes 7962628
  654.1 154.7 %collective-permute-start.12 = (bf16[3,288,720]{2,1,0:T(8,128)(2,1)}, bf16[3,288,720]{2,1,0:T(8,128)(2,1)}, u32[]{:S(2)}, u32[]{:S(2)}) collective-permute-start(bf16[3,288,720]{2,1,0:T(8,128)(2,1)} %pad_maximum_fusion.2), channel_id=1, source_target_pairs={{0,4},{4,0},{1,5},{5,1},{2,6},{6,2},{3,7},{7,3},{8,12},{12,8},{9,1... | collective-permute-start | bytes 3732488 | tf_op jit(solution)/shard_map/ppermute | solution.py:1288
  (37 other events, 184.5 us)
Sparse Core Ops, SparseCore 0:
  162.0 73.1 all-gather.2
  559.5 106.3 reduce-scatter.1

commit v5 on v4

--- a/solution.py
+++ b/solution.py
@@ -816,10 +816,10 @@
 
 
 def first_sum_kernel(
-    count, part, gate_grad, up_grad, middle, cotangent, gain,
-    grad_middle, attention_full, gain_rows, leaving_up, leaving_down,
-    own, from_core, first, second, grad_attention, totals, landed,
-    send, recv, local,
+    count, part, gate_grad, up_grad, hidden, middle, cotangent, gain, down,
+    grad_middle, attention_full, gain_rows, leaving_up, leaving_down, feedforward,
+    own, from_core, first, second, grad_attention, totals, landed, hidden_rows, product,
+    send, recv, local, hidden_local,
 ):
     z, c, t = lax.axis_index("fsdp"), lax.axis_index("cp"), lax.axis_index("tp")
     beside, yonder = t + 1 - 2 * (t % 2), (t + 2) % 4
@@ -868,6 +868,43 @@
             drain.gather(1)
             drain.send(1)
 
+    block_rows = product.shape[1]
+    blocks = hidden.shape[0] // block_rows
+
+    def hidden_copy(block):
+        return pltpu.make_async_copy(
+            hidden.at[pl.ds(block * block_rows, block_rows)], hidden_rows.at[block % 2],
+            hidden_local.at[0, block % 2],
+        )
+
+    def product_copy(block):
+        return pltpu.make_async_copy(
+            product.at[block % 2], feedforward.at[pl.ds(block * block_rows, block_rows)],
+            hidden_local.at[1, block % 2],
+        )
+
+    def product_block(block):
+        hidden_copy(block).wait()
+        if block + 1 < blocks:
+            hidden_copy(block + 1).start()
+        if block > 1:
+            product_copy(block - 2).wait()
+
+        def one(k, carry):
+            columns = pl.ds(pl.multiple_of(k * 2 * TILE, 2 * TILE), 2 * TILE)
+            value = lax.dot_general(
+                hidden_rows[block % 2], down[columns, :], (((1,), (1,)), ((), ())),
+                preferred_element_type=F32,
+            )
+            product[block % 2, :, columns] = value.astype(BF)
+            return carry
+
+        lax.fori_loop(0, width // (2 * TILE), one, 0)
+        product_copy(block).start()
+
+    hidden_copy(0).start()
+    product_block(0)
+
     quarter = half // 2
     quarters = [(piece, pl.ds(side * quarter, quarter)) for piece in range(2) for side in range(2)]
     x_first = [[mail.slot() for _ in range(2)] for _ in quarters]
@@ -949,7 +986,10 @@
             finish(k - 1)
         if k == 2 and last > 2:
             z_hop(2)
+        product_block(k + 1)
     finish(len(quarters) - 1)
+    for block in range(len(quarters) + 1, blocks):
+        product_block(block)
     keep = pltpu.make_async_copy(grad_attention, attention_full.at[t], local.at[0])
     keep.start()
     for hop in range(3, last):
@@ -967,10 +1007,12 @@
         if last > 0:
             drain.gather(last)
     keep.wait()
+    for block in range(blocks - 2, blocks):
+        product_copy(block).wait()
     mail.finish()
 
 
-def first_sum(count, part, gate_grad, up_grad, middle, cotangent, gain):
+def first_sum(count, part, gate_grad, up_grad, hidden, middle, cotangent, gain, down):
     slots = 6 * count + 32
     rows, width = middle.shape
     block = gate_grad.shape[1:]
@@ -985,9 +1027,10 @@
             jax.ShapeDtypeStruct((1, width), F32),
             jax.ShapeDtypeStruct((2,) + block, BF),
             jax.ShapeDtypeStruct((2,) + block, BF),
+            jax.ShapeDtypeStruct((hidden.shape[0], width), BF),
         ),
-        in_specs=[anywhere] * 3 + [vmem] * 3,
-        out_specs=(vmem, anywhere, vmem, vmem, vmem),
+        in_specs=[anywhere] * 4 + [vmem] * 4,
+        out_specs=(vmem, anywhere, vmem, vmem, vmem, anywhere),
         scratch_shapes=[
             pltpu.VMEM((2, 2, 2, rows // 2, width), BF),
             pltpu.VMEM((2, 2, 2, rows // 2, width), BF),
@@ -996,25 +1039,28 @@
             pltpu.VMEM((2, rows // 2, width), BF),
             pltpu.VMEM((2, hops, 2) + block, BF),
             pltpu.VMEM((2, hops, 2) + block, BF),
+            pltpu.VMEM((2, hidden.shape[0] // 8, hidden.shape[1]), BF),
+            pltpu.VMEM((2, hidden.shape[0] // 8, width), BF),
             pltpu.SemaphoreType.DMA((slots,)),
             pltpu.SemaphoreType.DMA((slots,)),
             pltpu.SemaphoreType.DMA((5,)),
+            pltpu.SemaphoreType.DMA((2, 2)),
         ],
         compiler_params=pltpu.CompilerParams(
             collective_id=3, has_side_effects=True, vmem_limit_bytes=60 << 20
         ),
-    )(part, gate_grad, up_grad, middle, cotangent, gain)
-
-
-AHEAD = 4
+    )(part, gate_grad, up_grad, hidden, middle, cotangent, gain, down)
+
+
+AHEAD = 6
 
 
 def last_sum_kernel(
-    count, part, qkv_grad, out_grad, tokens, grad_middle, gain, gain_rows,
+    count, grad_projected, qkv_full, qkv_grad, out_grad, tokens, grad_middle, gain, gain_rows,
     qkv_total, out_total, grad_tokens, gain_sums,
     own, from_core, to_yonder, from_yonder, pieces,
     from_x, heads_sum, heads_landed, outs_sum, outs_landed, final_out, gains, gain_line,
-    send, recv, local,
+    part, weights, send, recv, local, weights_local,
 ):
     z, c, t = lax.axis_index("fsdp"), lax.axis_index("cp"), lax.axis_index("tp")
     beside, yonder = t + 1 - 2 * (t % 2), (t + 2) % 4
@@ -1092,11 +1138,34 @@
 
     for step in range(AHEAD):
         cross_send(step)
-    summed.begin()
     if count > 1:
         outs.gather(1)
         outs.send(1)
-    summed.turn()
+
+    wide_block = weights.shape[1]
+    blocks = qkv_full.shape[0] // wide_block
+
+    def weights_copy(block, slot):
+        return pltpu.make_async_copy(
+            qkv_full.at[pl.ds(block * wide_block, wide_block)], weights.at[slot],
+            weights_local.at[slot],
+        )
+
+    def product(block, carry):
+        slot = lax.rem(block, 2)
+        weights_copy(block, slot).wait()
+        pl.when(block + 1 < blocks)(lambda: weights_copy(block + 1, 1 - slot).start())
+        columns = pl.ds(pl.multiple_of(block * wide_block, wide_block), wide_block)
+        value = lax.dot_general(
+            grad_projected[...], weights[slot], (((1,), (1,)), ((), ())),
+            preferred_element_type=F32,
+        )
+        part[:, :, columns] = value.astype(BF).reshape(part.shape[:2] + (wide_block,))
+        return carry
+
+    weights_copy(0, 0).start()
+    thirds = [blocks * k // 3 for k in range(4)]
+    lax.fori_loop(thirds[0], thirds[1], product, 0)
 
     keep = pltpu.make_async_copy(pieces.at[c], grad_tokens.at[c], local.at[0])
     home = mail.slot()
@@ -1146,9 +1215,15 @@
         outs.send(hop)
 
     early = min(3, count)
-    for hop in range(2, early + 1):
+    for k, hop in enumerate(range(2, early + 1)):
         if hop < count:
             outs_hop(hop)
+        if k == 0:
+            lax.fori_loop(thirds[1], thirds[2], product, 0)
+    if early < 2:
+        lax.fori_loop(thirds[1], thirds[2], product, 0)
+    lax.fori_loop(thirds[2], thirds[3], product, 0)
+    summed.begin()
     for step, (hop, k) in enumerate(steps[:-2]):
         cross_arrive(hop, k)
         cross_send(step + AHEAD)
@@ -1158,13 +1233,15 @@
         heads[k].send(hop)
         if k == 1 and hop > early:
             outs_hop(hop)
-        if step == 2 or step == 1 and count == 2:
+        if step == 0:
+            summed.turn()
+        if step == 3 or step == 1 and count == 2:
             finish_rows()
-        if step == 4:
+        if step == 5:
             gain_step(0)
-        if step == 5:
             gain_step(1)
     if count == 1:
+        summed.turn()
         finish_rows()
     if count <= 2:
         gain_step(0)
@@ -1215,7 +1292,7 @@
     mail.finish()
 
 
-def last_sum(count, part, qkv_grad, out_grad, tokens, grad_middle, gain, gain_rows):
+def last_sum(count, grad_projected, qkv_full, qkv_grad, out_grad, tokens, grad_middle, gain, gain_rows):
     slots = 13 * count + 16
     rows, width = tokens.shape
     hops = max(count - 1, 1)
@@ -1230,7 +1307,7 @@
             jax.ShapeDtypeStruct((2, rows // 2, width), BF),
             jax.ShapeDtypeStruct((2, width), F32),
         ),
-        in_specs=[anywhere] * 3 + [vmem] * 4,
+        in_specs=[vmem] + [anywhere] * 3 + [vmem] * 4,
         out_specs=(vmem, vmem, anywhere, vmem),
         scratch_shapes=[
             pltpu.VMEM((2, rows, width), BF),
@@ -1246,14 +1323,17 @@
             pltpu.VMEM(out_block, BF),
             pltpu.VMEM((6, 2, width), F32),
             pltpu.VMEM((count, 2, width), F32),
+            pltpu.VMEM((4, rows, width), BF),
+            pltpu.VMEM((2, 2 * TILE, qkv_full.shape[1]), BF),
             pltpu.SemaphoreType.DMA((slots,)),
             pltpu.SemaphoreType.DMA((slots,)),
             pltpu.SemaphoreType.DMA((4,)),
+            pltpu.SemaphoreType.DMA((2,)),
         ],
         compiler_params=pltpu.CompilerParams(
             collective_id=4, has_side_effects=True, vmem_limit_bytes=60 << 20
         ),
-    )(part, qkv_grad, out_grad, tokens, grad_middle, gain, gain_rows)
+    )(grad_projected, qkv_full, qkv_grad, out_grad, tokens, grad_middle, gain, gain_rows)
 
 
 def normalize(values):
@@ -1400,14 +1480,16 @@
     grad_gate_exact, grad_up_exact = silu_back(grad_hidden)
     grad_gate_pre = grad_gate_exact.astype(BF)
     grad_up_pre = grad_up_exact.astype(BF)
-    grad_normed_two = cols_inner(grad_gate_pre, full_gate) + cols_inner(grad_up_pre, full_up)
+    gate_part = lax.optimization_barrier(cols_inner(grad_gate_pre, full_gate).astype(BF))
+    grad_normed_two = gate_part.astype(F32) + cols_inner(grad_up_pre, full_up)
     gate_blocks = blocks_of(rows_inner(normed_two, grad_gate_pre))
     up_blocks = blocks_of(rows_inner(normed_two, grad_up_pre))
     part = grad_normed_two.astype(BF).reshape(sets, lanes, slots, local, width)
     if count > 1:
         part, leaving_up, leaving_down = lax.optimization_barrier((part, leaving_up, leaving_down))
-    grad_middle, grad_attention, gain_two_rows, pair_up, pair_down = first_sum(
-        count, part, gate_blocks, up_blocks, middle, cotangent_rows, gain_two[None],
+    grad_middle, grad_attention, gain_two_rows, pair_up, pair_down, feedforward = first_sum(
+        count, part, gate_blocks, up_blocks, hidden, middle, cotangent_rows, gain_two[None],
+        full_down,
     )
     grad_attention = grad_attention.reshape(seq, width)
 
@@ -1442,10 +1524,7 @@
     out_other = swap(pick(out_pieces, 1 - c, 1))
     out_pieces = (pick(out_pieces, c, 1).astype(F32) + out_other.astype(F32)).astype(BF)
     grad_context = row_major(matmul(grad_attention, full_out).astype(BF))
-    feedforward = lax.psum_scatter(
-        cols_inner(after(hidden, grad_attention), full_down).astype(BF),
-        everyone, scatter_dimension=0, tiled=True,
-    )
+    feedforward = lax.psum_scatter(feedforward, everyone, scatter_dimension=0, tiled=True)
     feedforward = feedforward.reshape(slots, local, width)
     output = (middle_home + BRANCH * feedforward.astype(F32)).astype(BF)
     grad_projected = attention_back(
@@ -1455,8 +1534,7 @@
     grad_projected = after(grad_projected, out_other, low[2], high[2])
     grad_qkv = row_major(rows_inner(normed_one, grad_projected).astype(BF))
     grad_qkv, grad_out, grad_tokens, gain_sums = last_sum(
-        count, cols_inner(grad_projected, full_qkv).astype(BF).reshape(lanes, rows, width),
-        grad_qkv.reshape(count, sets, share, 3 * heads_width), out_pieces,
+        count, grad_projected, full_qkv, grad_qkv.reshape(count, sets, share, 3 * heads_width), out_pieces,
         token_rows, grad_middle, gain_one[None], gain_two_rows,
     )
     return (

time: 832 us -> 806 us (0.969)
  matrix products: 177 us -> 144 us
  Pallas kernels: 528 us -> 539 us
    dot_general x5 -> x3, matrix products: 58.5 us -> 28.6 us  [cols_inner(): lax.dot_general(left, right, (((1,), (1,)), ((), ())), preferred_element_...]
    pallas_call x1, Pallas kernels: 130 us -> 142 us  [last_sum(): pl.pallas_call(functools.partial(last_sum_kernel, count), out_shape=(jax....]
  transfers between devices with their start and end apart: 15 -> 15, of which waited for: 1 -> 1; matrix products, arithmetic and copies ran while one was open for 18% -> 16% of each run, Pallas kernels for 36% -> 39%
where the time goes in v5:
time: 806 us; the launch traced here: 800 us
  Pallas kernels  539 us (67%)
  matrix products  144 us (18%)
  starting transfers between devices  40.4 us (5%)
  local copies, waits for them, and re-layouts  32.3 us (4%)
  other arithmetic  27.1 us (3%)
  between operations  14.9 us (2%)
    pallas_call x1, Pallas kernels, last_sum(): pl.pallas_call(functools.partial(last_sum_kernel, count), out_shape=(jax....  142 us
    pallas_call x1, Pallas kernels, first_gather(): pl.pallas_call(functools.partial(first_gather_kernel, count), out_shape=(...  136 us
    pallas_call x1, Pallas kernels, second_gather(): pl.pallas_call(functools.partial(second_gather_kernel, count), out_shape=...  94.4 us
    pallas_call x1, Pallas kernels, first_sum(): pl.pallas_call(functools.partial(first_sum_kernel, count), out_shape=(jax...  92.7 us
    dot_general x5, matrix products, matmul(): return jnp.dot(left, right, preferred_element_type=F32)  61.2 us
    dot_general x5, matrix products, rows_inner(): lax.dot_general(left, right, (((0,), (0,)), ((), ())), preferred_element_...  53.9 us
    pallas_call x1, Pallas kernels, attention_back(): pl.pallas_call(functools.partial(attention_back_kernel, blocks), out_shap...  40.1 us
    pallas_call x1, Pallas kernels, attention(): pl.pallas_call(functools.partial(attention_kernel, blocks), out_shape=(ja...  34.7 us
  transfers between devices with their start and end apart: 15, of which 1 were waited for; matrix products, arithmetic and copies ran while one was open for 16% of the time, Pallas kernels for 39%

profile of v5, /device:TPU:0, one launch (start us, length us, event | category | flops | bytes accessed | tf_op | source)
XLA Modules:
  0.0 800.3 jit_solution(523963165994323434)
XLA Ops:
  18.7 135.9 %shard_map.221 = (bf16[2,128,2304]{2,1,0:T(8,128)(2,1)S(1)}, bf16[4,2,128,2304]{3,2,1,0:T(8,128)(2,1)S(1)}, bf16[4,2,288,1728]{3,2,1,0:T(8,128)(2,1)}, bf16[4,28...) custom-call(bf16[128,2304]{1,0:T(8,128)(2,1)S(1)} %get-tuple-element.99.tokens, ...), custom_call_target="tpu_custom_call" | custom-call | tf_op jit(solution)/shard_map/pallas_call | solution.py:479
  163.6 5.0 collective-permute-start.1
  170.8 15.3 %fusion.11.projected = f32[1024,1728]{1,0:T(8,128)} fusion(bf16[1024,2304]{1,0:T(8,128)(2,1)} %bitcast.125, bf16[2304,1728]{1,0:T(8,128)(2,1)} %bitcast.136), kind=kOutput, calls=%fused_computation.65 | convolution fusion | flops 8153726976 | bytes 19759104 | tf_op jit(solution)/shard_map/dot_general | solution.py:1348
  186.1 34.7 %shard_map.222 = (bf16[1024,576]{1,0:T(8,128)(2,1)S(1)}, bf16[9,1024,64]{2,1,0:T(8,128)(2,1)S(1)}, bf16[9,1024,64]{2,1,0:T(8,128)(2,1)}, bf16[9,1024,64]{2,1,0:T(8,128)(2,1)}, f32[9,1,1024]{2,1,0:T(1,128)S(1)}) custom-call(s32[1]{0:T(128)} %dynamic_slice.71.length_ref, f32[1024,1728]{1,0:T(8,128)} %fusion.11.projected, f32[1024,128]{1,0:T(8,128)S(1)} %copy-done.17, ...), custom_call_target="tpu_custom_call" | custom-call | flops 2415919104 | bytes 20971520 | tf_op jit(solution)/shard_map/pallas_call | solution.py:107
  222.6 5.8 convolution_convert_fusion.2
  228.5 94.4 %shard_map.223 = (f32[256,2304]{1,0:T(8,128)S(1)}, f32[2,128,2304]{2,1,0:T(8,128)S(1)}, bf16[2,4,2,128,2304]{4,3,2,1,0:T(8,128)(2,1)}, bf16[4,2,288,720]{3,2,1,0...) custom-call(bf16[4,256,2304]{2,1,0:T(8,128)(2,1)} %bitcast.150, ...), custom_call_target="tpu_custom_call" | custom-call | tf_op jit(solution)/shard_map/pallas_call | solution.py:670
  325.6 12.9 %fusion.13 = f32[2048,720]{1,0:T(8,128)} fusion(bf16[2048,2304]{1,0:T(8,128)(2,1)} %bitcast.163, bf16[2304,720]{1,0:T(8,128)(2,1)} %bitcast.171), kind=kOutput, calls=%fused_computation.67 | convolution fusion | flops 6794772480 | bytes 18653184 | tf_op jit(solution)/shard_map/dot_general | solution.py:1348
  338.5 11.8 %fusion.12 = f32[2048,720]{1,0:T(8,128)} fusion(bf16[2048,2304]{1,0:T(8,128)(2,1)} %bitcast.160, bf16[2304,720]{1,0:T(8,128)(2,1)S(1)} %bitcast.152), kind=kOutput, calls=%fused_computation.66 | convolution fusion | flops 6794772480 | bytes 18653184 | tf_op jit(solution)/shard_map/dot_general | solution.py:1348
  350.4 16.2 %multiply_convert_fusion.1 = (bf16[2048,720]{1,0:T(8,128)(2,1)S(1)}, bf16[2048,720]{1,0:T(8,128)(2,1)}, bf16[2048,720]{1,0:T(8,128)(2,1)}) fusion(f32[2048,720]{1,0:T(8,128)} %fusion.13, f32[2048,720]{1,0:T(8,128)} %fusion.12, bf16[2048,2304]{1,0:T(8,128)(2,1)S(1)} %bitcast.166, bf16[2304,720]{1,0:T(8,128)(2,1)} %bitcast.169), kind=kOutput, calls=%fused_computation.4 | convolution fusion | flops 6822789120 | bytes 33398784 | tf_op jit(solution)/shard_map/dot_general | solution.py:1348
  366.6 11.9 %multiply_convert_fusion = bf16[2304,720]{1,0:T(8,128)(2,1)S(1)} fusion(bf16[2048,2304]{1,0:T(8,128)(2,1)} %bitcast.161, bf16[2048,720]{1,0:T(8,128)(2,1)S(1)} %get-tuple-element.83.hidden), kind=kOutput, calls=%fused_computation.3 | convolution fusion | flops 6798090240 | bytes 15704064 | tf_op jit(solution)/shard_map/dot_general | solution.py:1352
  381.8 9.9 %convolution_convert_fusion.1 = bf16[2048,2304]{1,0:T(8,128)(2,1)} fusion(bf16[2048,720]{1,0:T(8,128)(2,1)S(1)} %copy-done.43, bf16[2304,720]{1,0:T(8,128)(2,1)S(1)} %bitcast.172), kind=kOutput, calls=%fused_computation.2 | convolution fusion | flops 6799491072 | bytes 15704064 | tf_op jit(solution)/shard_map/dot_general | solution.py:1356
  391.7 13.0 %add_convert_fusion = bf16[2048,2304]{1,0:T(8,128)(2,1)} fusion(bf16[2048,2304]{1,0:T(8,128)(2,1)} %convolution_convert_fusion.1, bf16[2048,720]{1,0:T(8,128)(2,1)} %get-tuple-element.85, bf16[2304,720]{1,0:T(8,128)(2,1)S(1)} %bitcast.170), kind=kOutput, calls=%fused_computation | convolution fusion | flops 6808928256 | bytes 25141248 | tf_op jit(solution)/shard_map/dot_general | solution.py:1356
  405.6 12.5 %convolution_convert_fusion.4 = bf16[2304,720]{1,0:T(8,128)(2,1)} fusion(bf16[2048,2304]{1,0:T(8,128)(2,1)} %bitcast.164, bf16[2048,720]{1,0:T(8,128)(2,1)} %get-tuple-element.84), kind=kOutput, calls=%fused_computation.11 | convolution fusion | flops 6796431360 | bytes 15704064 | tf_op jit(solution)/shard_map/dot_general | solution.py:1352
  419.5 9.9 %collective-permute-start.4 = (bf16[576,720]{1,0:T(8,128)(2,1)S(1)}, bf16[576,720]{1,0:T(8,128)(2,1)S(1)}, u32[]{:S(2)}, u32[]{:S(2)}) collective-permute-start(bf16[576,720]{1,0:T(8,128)(2,1)S(1)} %get-tuple-element.89), channel_id=1, source_target_pairs={{0,8},{8,16},{1,9},{9,17},{2,10},{10,18},{3,11},{11,19},{4,12},{12... | collective-permute-start | bytes 2488328 | tf_op jit(solution)/shard_map/ppermute | solution.py:1477
  429.5 11.4 %convolution_convert_fusion.3 = bf16[2304,720]{1,0:T(8,128)(2,1)} fusion(bf16[2048,2304]{1,0:T(8,128)(2,1)} %bitcast.165, bf16[2048,720]{1,0:T(8,128)(2,1)S(1)} %copy-done.42), kind=kOutput, calls=%fused_computation.10 | convolution fusion | flops 6796431360 | bytes 15704064 | tf_op jit(solution)/shard_map/dot_general | solution.py:1352
  447.1 92.7 %shard_map.224 = (f32[256,2304]{1,0:T(8,128)}, bf16[4,2,128,2304]{3,2,1,0:T(8,128)(2,1)}, f32[1,2304]{1,0:T(1,128)}, bf16[2,576,720]{2,1,0:T(8,128)(2,1)}, bf16[...) custom-call(bf16[2,4,2,128,2304]{4,3,2,1,0:T(8,128)(2,1)} %bitcast.134, bf16[4,576,720]{2,1,0:T(8,128)(2,1)} %bitcast.139, ...), custom_call_target="tpu_custom_call" | custom-call | tf_op jit(solution)/shard_map/pallas_call | solution.py:1022
  539.8 9.2 %collective-permute-start.8 = (bf16[576,720]{1,0:T(8,128)(2,1)}, bf16[576,720]{1,0:T(8,128)(2,1)S(1)}, u32[]{:S(2)}, u32[]{:S(2)}) collective-permute-start(bf16[576,720]{1,0:T(8,128)(2,1)} %fusion.6), channel_id=1, source_target_pairs={{0,8},{8,16},{16,24},{1,9},{9,17},{17,25},{2,10},{10,18},{18,26},{... | collective-permute-start | bytes 2488328 | tf_op jit(solution)/shard_map/ppermute | solution.py:1498
  550.4 7.0 convolution_convert_fusion.5
  561.3 4.0 collective-permute-start.10
  566.7 4.9 convolution_convert_fusion.6.grad_context
  571.6 40.1 %shard_map.225.grad_projected = bf16[1024,1728]{1,0:T(8,128)(2,1)} custom-call(s32[1]{0:T(128)} %dynamic_slice.71.length_ref, bf16[1024,576]{1,0:T(8,128)(2,1)} %convolution_convert_fusion.6.grad_context, bf16[9,1024,64]{2,1,0:T(8,128)(2,1)} %copy-done.18, bf16[9,1024,64]{2,1,0:T(8,128)(2,1)} %get-tuple-element.65.k_heads, ...), custom_call_target="tpu_custom_call" | custom-call | flops 6039797760 | bytes 20971520 | tf_op jit(solution)/shard_map/pallas_call | solution.py:186
  621.1 11.0 %convolution_convert_fusion = bf16[2304,1728]{1,0:T(8,128)(2,1)} fusion(bf16[1024,2304]{1,0:T(8,128)(2,1)S(1)} %bitcast.128, bf16[1024,1728]{1,0:T(8,128)(2,1)S(1)} %copy-done.25), kind=kOutput, calls=%fused_computation.1 | convolution fusion | flops 8157708288 | bytes 16220160 | tf_op jit(solution)/shard_map/dot_general | solution.py:1352
  635.0 141.6 %shard_map.226 = (f32[288,1728]{1,0:T(8,128)}, f32[288,576]{1,0:T(8,128)}, bf16[2,128,2304]{2,1,0:T(8,128)(2,1)}, f32[2,2304]{1,0:T(2,128)}) custom-call(bf16[1024,1728]{1,0:T(8,128)(2,1)} %shard_map.225.grad_projected, bf16[2304,1728]{1,0:T(8,128)(2,1)} %bitcast.137, bf16[4,2,288,1728]{3,2,1,0:T(8,128)(2,1)} %bitcast.138, ...), custom_call_target="tpu_custom_call" | custom-call | tf_op jit(solution)/shard_map/pallas_call | solution.py:1302
  778.0 3.4 fusion.10
  (156 shorter events, 70.8 us)
Async XLA Ops:
  7.2 331.4 %all-gather.3.cloned.1.call-start = ((), (), s32[]{:S(2)}) async-start(), calls=%async_computation.2 | async-start | bytes 10616832 | tf_op jit(solution)/shard_map/all_gather | solution.py:1432
  18.7 151.5 %copy-start.41 = (s32[2]{0:T(128)S(1)}, s32[2]{0:T(128)}, u32[]{:S(2)}) copy-start(s32[2]{0:T(128)} %param.15) | copy-start | bytes 28
  18.7 152.0 %copy-start.36 = (bf16[2304]{0:T(1024)(128)(2,1)S(1)}, bf16[2304]{0:T(1024)(128)(2,1)}, u32[]{:S(2)}) copy-start(bf16[2304]{0:T(1024)(128)(2,1)} %param.21) | copy-start | bytes 13828
  162.0 626.6 %reduce-scatter.2.cloned.1.call-start = ((), (), s32[]{:S(2)}) async-start(), calls=%async_computation.1 | async-start | bytes 10616832 | tf_op jit(solution)/shard_map/reduce_scatter | solution.py:1527
  162.0 58.8 %collective-permute-start = (bf16[4,288,576]{2,1,0:T(8,128)(2,1)}, bf16[4,288,576]{2,1,0:T(8,128)(2,1)S(1)}, u32[]{:S(2)}, u32[]{:S(2)}) collective-permute-start(bf16[4,288,576]{2,1,0:T(8,128)(2,1)} %copy-done.10), channel_id=1, source_target_pairs={{0,4},{4,0},{1,5},{5,1},{2,6},{6,2},{3,7},{7,3},{8,12},{12,8},{9,1... | collective-permute-start | bytes 3981320 | tf_op jit(solution)/shard_map/ppermute | solution.py:1368
  163.6 64.9 %collective-permute-start.1 = (bf16[2,3,288,720]{3,2,1,0:T(8,128)(2,1)}, bf16[2,3,288,720]{3,2,1,0:T(8,128)(2,1)}, u32[]{:S(2)}, u32[]{:S(2)}) collective-permute-start(bf16[2,3,288,720]{3,2,1,0:T(8,128)(2,1)} %copy-done.3), channel_id=1, source_target_pairs={{0,8},{8,16},{16,24},{1,9},{9,17},{17,25},{2,10},{10,18},{18,26},{... | collective-permute-start | bytes 7464968 | tf_op jit(solution)/shard_map/ppermute | solution.py:1439
  168.6 59.8 %collective-permute-start.2 = (bf16[2,3,288,720]{3,2,1,0:T(8,128)(2,1)}, bf16[2,3,288,720]{3,2,1,0:T(8,128)(2,1)}, u32[]{:S(2)}, u32[]{:S(2)}) collective-permute-start(bf16[2,3,288,720]{3,2,1,0:T(8,128)(2,1)} %copy-done.5), channel_id=1, source_target_pairs={{8,0},{16,8},{24,16},{9,1},{17,9},{25,17},{10,2},{18,10},{26,18},{... | collective-permute-start | bytes 7464968 | tf_op jit(solution)/shard_map/ppermute | solution.py:1440
  170.7 57.7 %copy-start.13 = (f32[1,2304]{1,0:T(1,128)}, f32[1,2304]{1,0:T(1,128)S(1)}, u32[]{:S(2)}) copy-start(f32[1,2304]{1,0:T(1,128)S(1)} %reshape.153.gain) | copy-start | bytes 27652
  170.7 15.4 %copy-start.16 = (f32[1024,128]{1,0:T(8,128)S(1)}, f32[1024,128]{1,0:T(8,128)}, u32[]{:S(2)}) copy-start(f32[1024,128]{1,0:T(8,128)} %constant.132.clone.sine) | copy-start | bytes 1572868
  170.7 15.3 %copy-start.17 = (f32[1024,128]{1,0:T(8,128)S(1)}, f32[1024,128]{1,0:T(8,128)}, u32[]{:S(2)}) copy-start(f32[1024,128]{1,0:T(8,128)} %constant.131.clone.cosine) | copy-start | bytes 1572868
  186.1 34.7 %copy-start.11 = (bf16[4,288,576]{2,1,0:T(8,128)(2,1)S(1)}, bf16[4,288,576]{2,1,0:T(8,128)(2,1)}, u32[]{:S(2)}) copy-start(bf16[4,288,576]{2,1,0:T(8,128)(2,1)} %copy-done.10) | copy-start | bytes 3981316
  366.6 14.8 %copy-start.43 = (bf16[2048,720]{1,0:T(8,128)(2,1)S(1)}, bf16[2048,720]{1,0:T(8,128)(2,1)}, u32[]{:S(2)}) copy-start(bf16[2048,720]{1,0:T(8,128)(2,1)} %get-tuple-element.84) | copy-start | bytes 8847364
  378.5 67.4 %copy-start.22 = (bf16[2304,720]{1,0:T(8,128)(2,1)}, bf16[2304,720]{1,0:T(8,128)(2,1)S(1)}, u32[]{:S(2)}) copy-start(bf16[2304,720]{1,0:T(8,128)(2,1)S(1)} %multiply_convert_fusion) | copy-start | bytes 9953284
  378.7 26.0 %collective-permute-start.5 = (bf16[576,720]{1,0:T(8,128)(2,1)S(1)}, bf16[576,720]{1,0:T(8,128)(2,1)S(1)}, u32[]{:S(2)}, u32[]{:S(2)}) collective-permute-start(bf16[576,720]{1,0:T(8,128)(2,1)S(1)} %get-tuple-element.90), channel_id=1, source_target_pairs={{24,16},{25,17},{26,18},{27,19},{28,20},{29,21},{30,22},{31,23}} | collective-permute-start | bytes 2488328 | tf_op jit(solution)/shard_map/ppermute | solution.py:1478
  379.5 38.6 %collective-permute-start.3 = (bf16[576,720]{1,0:T(8,128)(2,1)S(1)}, bf16[576,720]{1,0:T(8,128)(2,1)S(1)}, u32[]{:S(2)}, u32[]{:S(2)}) collective-permute-start(bf16[576,720]{1,0:T(8,128)(2,1)S(1)} %get-tuple-element.91), channel_id=1, source_target_pairs={{0,8},{1,9},{2,10},{3,11},{4,12},{5,13},{6,14},{7,15}} | collective-permute-start | bytes 2488328 | tf_op jit(solution)/shard_map/ppermute | solution.py:1477
  404.9 13.3 %collective-permute-start.6 = (bf16[576,720]{1,0:T(8,128)(2,1)S(1)}, bf16[576,720]{1,0:T(8,128)(2,1)S(1)}, u32[]{:S(2)}, u32[]{:S(2)}) collective-permute-start(bf16[576,720]{1,0:T(8,128)(2,1)S(1)} %fusion.3), channel_id=1, source_target_pairs={{16,8},{24,16},{17,9},{25,17},{18,10},{26,18},{19,11},{27,19},{20,... | collective-permute-start | bytes 2488328 | tf_op jit(solution)/shard_map/ppermute | solution.py:1478
  419.5 26.4 %collective-permute-start.4 = (bf16[576,720]{1,0:T(8,128)(2,1)S(1)}, bf16[576,720]{1,0:T(8,128)(2,1)S(1)}, u32[]{:S(2)}, u32[]{:S(2)}) collective-permute-start(bf16[576,720]{1,0:T(8,128)(2,1)S(1)} %get-tuple-element.89), channel_id=1, source_target_pairs={{0,8},{8,16},{1,9},{9,17},{2,10},{10,18},{3,11},{11,19},{4,12},{12... | collective-permute-start | bytes 2488328 | tf_op jit(solution)/shard_map/ppermute | solution.py:1477
  539.8 71.8 %collective-permute-start.8 = (bf16[576,720]{1,0:T(8,128)(2,1)}, bf16[576,720]{1,0:T(8,128)(2,1)S(1)}, u32[]{:S(2)}, u32[]{:S(2)}) collective-permute-start(bf16[576,720]{1,0:T(8,128)(2,1)} %fusion.6), channel_id=1, source_target_pairs={{0,8},{8,16},{16,24},{1,9},{9,17},{17,25},{2,10},{10,18},{18,26},{... | collective-permute-start | bytes 2488328 | tf_op jit(solution)/shard_map/ppermute | solution.py:1498
  549.1 62.6 %collective-permute-start.9 = (bf16[576,720]{1,0:T(8,128)(2,1)}, bf16[576,720]{1,0:T(8,128)(2,1)}, u32[]{:S(2)}, u32[]{:S(2)}) collective-permute-start(bf16[576,720]{1,0:T(8,128)(2,1)} %get-tuple-element.71), channel_id=1, source_target_pairs={{8,0},{16,8},{24,16},{9,1},{17,9},{25,17},{10,2},{18,10},{26,18},{... | collective-permute-start | bytes 2488328 | tf_op jit(solution)/shard_map/ppermute | solution.py:1500
  550.4 16.3 %copy-start.38 = (bf16[4,2,128,2304]{3,2,1,0:T(8,128)(2,1)S(1)}, bf16[4,2,128,2304]{3,2,1,0:T(8,128)(2,1)}, u32[]{:S(2)}) copy-start(bf16[4,2,128,2304]{3,2,1,0:T(8,128)(2,1)} %get-tuple-element.63) | copy-start | bytes 14155780
  558.6 54.9 %collective-permute-start.7 = (bf16[4,288,576]{2,1,0:T(8,128)(2,1)}, bf16[4,288,576]{2,1,0:T(8,128)(2,1)}, u32[]{:S(2)}, u32[]{:S(2)}) collective-permute-start(bf16[4,288,576]{2,1,0:T(8,128)(2,1)} %dynamic-slice_bitcast_fusion), channel_id=1, source_target_pairs={{0,4},{4,0},{1,5},{5,1},{2,6},{6,2},{3,7},{7,3},{8,12},{12,8},{9,1... | collective-permute-start | bytes 3981320 | tf_op jit(solution)/shard_map/ppermute | solution.py:1368
  561.3 52.2 %collective-permute-start.10 = (bf16[2,576,720]{2,1,0:T(8,128)(2,1)}, bf16[2,576,720]{2,1,0:T(8,128)(2,1)S(1)}, u32[]{:S(2)}, u32[]{:S(2)}) collective-permute-start(bf16[2,576,720]{2,1,0:T(8,128)(2,1)} %get-tuple-element.79), channel_id=1, source_target_pairs={{0,8},{8,16},{16,24},{1,9},{9,17},{17,25},{2,10},{10,18},{18,26},{... | collective-permute-start | bytes 4976648 | tf_op jit(solution)/shard_map/ppermute | solution.py:1498
  565.4 49.4 %collective-permute-start.11 = (bf16[2,576,720]{2,1,0:T(8,128)(2,1)}, bf16[2,576,720]{2,1,0:T(8,128)(2,1)}, u32[]{:S(2)}, u32[]{:S(2)}) collective-permute-start(bf16[2,576,720]{2,1,0:T(8,128)(2,1)} %get-tuple-element.80), channel_id=1, source_target_pairs={{8,0},{16,8},{24,16},{9,1},{17,9},{25,17},{10,2},{18,10},{26,18},{... | collective-permute-start | bytes 4976648 | tf_op jit(solution)/shard_map/ppermute | solution.py:1500
  620.4 161.2 %collective-permute-start.12 = (bf16[3,288,720]{2,1,0:T(8,128)(2,1)}, bf16[3,288,720]{2,1,0:T(8,128)(2,1)}, u32[]{:S(2)}, u32[]{:S(2)}) collective-permute-start(bf16[3,288,720]{2,1,0:T(8,128)(2,1)} %pad_maximum_fusion.2), channel_id=1, source_target_pairs={{0,4},{4,0},{1,5},{5,1},{2,6},{6,2},{3,7},{7,3},{8,12},{12,8},{9,1... | collective-permute-start | bytes 3732488 | tf_op jit(solution)/shard_map/ppermute | solution.py:1368
  (37 other events, 175.3 us)
Sparse Core Ops, SparseCore 0:
  162.1 73.9 all-gather.2
  539.9 115.6 reduce-scatter.1

commit v6 on v5

--- a/solution.py
+++ b/solution.py
@@ -16,7 +16,7 @@
 BF = jnp.bfloat16
 F32 = jnp.float32
 TILE = 128
-QUERY_ROWS = 256
+QUERY_ROWS = 512
 
 
 def turned(values, cosine, sine):
@@ -83,15 +83,15 @@
             top = jnp.max(scores, axis=0, keepdims=True)
             exponent = jnp.exp(scores - top)
             total = jnp.sum(exponent, axis=0, keepdims=True)
-            probabilities = (exponent * (1.0 / total)).astype(BF)
+            probabilities = exponent.astype(BF)
             level[head, :, first:most] = top + jnp.log(total)
             mixed = lax.dot_general(
                 values, probabilities, (((0,), (0,)), ((), ())), preferred_element_type=F32
             )
-            kept[head, first:most, :] = mixed.T.astype(BF)
+            kept[head, first:most, :] = (mixed * (1.0 / total)).T.astype(BF)
         return carry
 
-    lax.fori_loop(0, heads, one_head, 0)
+    lax.fori_loop(0, heads, one_head, 0, unroll=True)
     for gathered, ordered in blocks:
         source, target = pl.ds(ordered, local), pl.ds(gathered, local)
         for head in range(0, heads, 2):
@@ -167,7 +167,7 @@
             dq[head, first:most, :] = grad_queries.T * (1.0 / math.sqrt(HD))
         return carry
 
-    lax.fori_loop(0, heads, one_head, 0)
+    lax.fori_loop(0, heads, one_head, 0, unroll=True)
     sources = [dq] * heads + [dk] * heads + [dv] * heads
     for gathered, ordered in blocks:
         source, target = pl.ds(ordered, local), pl.ds(gathered, local)
@@ -1060,7 +1060,8 @@
     qkv_total, out_total, grad_tokens, gain_sums,
     own, from_core, to_yonder, from_yonder, pieces,
     from_x, heads_sum, heads_landed, outs_sum, outs_landed, final_out, gains, gain_line,
-    part, weights, send, recv, local, weights_local,
+    part, weights, give_sum, give_landed, give_own, give_total,
+    send, recv, local, weights_local,
 ):
     z, c, t = lax.axis_index("fsdp"), lax.axis_index("cp"), lax.axis_index("tp")
     beside, yonder = t + 1 - 2 * (t % 2), (t + 2) % 4
@@ -1072,8 +1073,10 @@
     summed = TensorSum(mail, part, own, from_core, to_yonder, from_yonder, local)
 
     columns = qkv_total.shape[1]
-    split = -(-columns // (2 * TILE)) * TILE
-    parts = [pl.ds(0, split), pl.ds(split, columns - split)]
+    behind = columns * 5 // 6 // TILE * TILE
+    split = -(-behind // (2 * TILE)) * TILE
+    parts = [pl.ds(0, split), pl.ds(split, behind - split)]
+    late = pl.ds(behind, columns - behind)
     cross = [[[mail.slot() for _ in range(count)] for _ in range(2)] for _ in parts]
     cross_own = [mail.slot() for _ in parts]
 
@@ -1099,6 +1102,26 @@
         )
 
     heads = [head_drain(lanes) for lanes in parts]
+
+    def late_fill(side_c):
+        def fill(hop, up, j, target):
+            copy = pltpu.make_async_copy(qkv_grad.at[j, side_c, :, late], target, local.at[2])
+            copy.start()
+            copy.wait()
+
+        return fill
+
+    stay = Drain(
+        mail, count, late_fill(c),
+        lambda side, hop: heads_sum.at[side, hop - 1, :, late],
+        lambda side, hop: heads_landed.at[side, hop - 1, :, late],
+    )
+    give = Drain(
+        mail, count, late_fill(1 - c),
+        lambda side, hop: give_sum.at[side, hop - 1],
+        lambda side, hop: give_landed.at[side, hop - 1],
+    )
+    give_slot = mail.slot()
 
     def fill_outs(hop, up, j, target):
         copy = pltpu.make_async_copy(out_grad.at[j], target, local.at[3])
@@ -1138,9 +1161,11 @@
 
     for step in range(AHEAD):
         cross_send(step)
+    early_chains = (outs, give, stay)
     if count > 1:
-        outs.gather(1)
-        outs.send(1)
+        for drain in early_chains:
+            drain.gather(1)
+            drain.send(1)
 
     wide_block = weights.shape[1]
     blocks = qkv_full.shape[0] // wide_block
@@ -1165,7 +1190,6 @@
 
     weights_copy(0, 0).start()
     thirds = [blocks * k // 3 for k in range(4)]
-    lax.fori_loop(thirds[0], thirds[1], product, 0)
 
     keep = pltpu.make_async_copy(pieces.at[c], grad_tokens.at[c], local.at[0])
     home = mail.slot()
@@ -1210,43 +1234,61 @@
                 line.send(hop + 1)
 
     def outs_hop(hop):
-        outs.arrive(hop - 1)
-        outs.gather(hop)
-        outs.send(hop)
-
-    early = min(3, count)
-    for k, hop in enumerate(range(2, early + 1)):
-        if hop < count:
-            outs_hop(hop)
-        if k == 0:
-            lax.fori_loop(thirds[1], thirds[2], product, 0)
-    if early < 2:
-        lax.fori_loop(thirds[1], thirds[2], product, 0)
-    lax.fori_loop(thirds[2], thirds[3], product, 0)
-    summed.begin()
+        for drain in early_chains:
+            drain.arrive(hop - 1)
+            drain.gather(hop)
+            drain.send(hop)
+
+    def give_away():
+        copy = pltpu.make_async_copy(qkv_grad.at[z, 1 - c, :, late], give_own, local.at[3])
+        copy.start()
+        copy.wait()
+        if count > 1:
+            give.arrive(last)
+
+        def one(place):
+            total = give_own[place, :].astype(F32)
+            for side, up in enumerate((True, False)):
+                if count > 1:
+                    landed = give.landed(side, last)[place, :].astype(F32)
+                    total += jnp.where(give.gets(last, up), landed, 0.0)
+            give_total[place, :] = total.astype(BF)
+
+        in_pieces(give_own.shape[0], one)
+        mail.start(give_slot, give_total, from_x.at[0, last, :, late], cp=1 - c)
+
     for step, (hop, k) in enumerate(steps[:-2]):
+        if step < 3:
+            lax.fori_loop(thirds[step], thirds[step + 1], product, 0)
+        if count == 2 and step == 1:
+            lax.fori_loop(thirds[2], thirds[3], product, 0)
+        if step == 2 or count == 2 and step == 1:
+            summed.begin()
         cross_arrive(hop, k)
         cross_send(step + AHEAD)
         if hop > 1:
             heads[k].arrive(hop - 1)
         heads[k].gather(hop)
         heads[k].send(hop)
-        if k == 1 and hop > early:
-            outs_hop(hop)
-        if step == 0:
+        if k == 1 and hop + 1 < count:
+            outs_hop(hop + 1)
+        if step == 2 or count == 2 and step == 1:
             summed.turn()
-        if step == 3 or step == 1 and count == 2:
+        if step == 3 or count == 2 and step == 1:
             finish_rows()
-        if step == 5:
+        if step == 5 or step == 3 and count == 3:
             gain_step(0)
             gain_step(1)
     if count == 1:
+        lax.fori_loop(thirds[0], thirds[3], product, 0)
+        summed.begin()
         summed.turn()
         finish_rows()
     if count <= 2:
         gain_step(0)
         gain_step(1)
     gain_step(2)
+    give_away()
 
     own_copy = pltpu.make_async_copy(qkv_grad.at[z, c], from_x.at[1, last], local.at[2])
     own_copy.start()
@@ -1254,6 +1296,7 @@
     out_copy.start()
     for k, lanes in enumerate(parts):
         mail.arrive(cross_own[k], from_x.at[0, last, :, lanes], cp=1 - c)
+    mail.arrive(give_slot, from_x.at[0, last, :, late], cp=1 - c)
     own_copy.wait()
     out_copy.wait()
 
@@ -1272,6 +1315,7 @@
         gain_step(2 + hop)
     if count > 1:
         chains = [(outs, pl.ds(0, out_total.shape[1]), out_total)]
+        chains += [(stay, late, qkv_total)]
         chains += [(heads[k], lanes, qkv_total) for k, lanes in enumerate(parts)]
         for drain, lanes, total in chains:
             drain.arrive(last)
@@ -1293,10 +1337,12 @@
 
 
 def last_sum(count, grad_projected, qkv_full, qkv_grad, out_grad, tokens, grad_middle, gain, gain_rows):
-    slots = 13 * count + 16
+    slots = 17 * count + 17
     rows, width = tokens.shape
     hops = max(count - 1, 1)
     block, out_block = qkv_grad.shape[2:], out_grad.shape[1:]
+    columns = block[1]
+    give_block = (block[0], columns - columns * 5 // 6 // TILE * TILE)
     anywhere = pl.BlockSpec(memory_space=pl.ANY)
     vmem = pl.BlockSpec(memory_space=pltpu.VMEM)
     return pl.pallas_call(
@@ -1325,6 +1371,10 @@
             pltpu.VMEM((count, 2, width), F32),
             pltpu.VMEM((4, rows, width), BF),
             pltpu.VMEM((2, 2 * TILE, qkv_full.shape[1]), BF),
+            pltpu.VMEM((2, hops) + give_block, BF),
+            pltpu.VMEM((2, hops) + give_block, BF),
+            pltpu.VMEM(give_block, BF),
+            pltpu.VMEM(give_block, BF),
             pltpu.SemaphoreType.DMA((slots,)),
             pltpu.SemaphoreType.DMA((slots,)),
             pltpu.SemaphoreType.DMA((4,)),

time: 806 us -> 797 us (0.989)
  Pallas kernels: 539 us -> 495 us
  waiting for transfers between devices: 2.69 us -> 27.3 us
    pallas_call x1, Pallas kernels: 34.7 us -> 18.6 us  [attention(): pl.pallas_call(functools.partial(attention_kernel, blocks), out_shape=(ja...]
    ppermute x3, waiting for transfers between devices: 0.01 us -> 13.7 us  [swap(): return lax.ppermute(value, 'cp', [(0, 1), (1, 0)])]
    pallas_call x1, Pallas kernels: 142 us -> 128 us  [last_sum(): pl.pallas_call(functools.partial(last_sum_kernel, count), out_shape=(jax....]
    pallas_call x1, Pallas kernels: 40.1 us -> 28.6 us  [attention_back(): pl.pallas_call(functools.partial(attention_back_kernel, blocks), out_shap...]
  transfers between devices with their start and end apart: 15 -> 15, of which waited for: 1 -> 5; matrix products, arithmetic and copies ran while one was open for 16% -> 17% of each run, Pallas kernels for 39% -> 34%
where the time goes in v6:
time: 797 us; the launch traced here: 786 us
  Pallas kernels  495 us (62%)
  matrix products  143 us (18%)
  starting transfers between devices  46.8 us (6%)
  local copies, waits for them, and re-layouts  31.3 us (4%)
  other arithmetic  27.4 us (3%)
  waiting for transfers between devices  27.3 us (3%)
  between operations  15.1 us (2%)
    pallas_call x1, Pallas kernels, first_gather(): pl.pallas_call(functools.partial(first_gather_kernel, count), out_shape=(...  136 us
    pallas_call x1, Pallas kernels, last_sum(): pl.pallas_call(functools.partial(last_sum_kernel, count), out_shape=(jax....  128 us
    pallas_call x1, Pallas kernels, first_sum(): pl.pallas_call(functools.partial(first_sum_kernel, count), out_shape=(jax...  92.5 us
    pallas_call x1, Pallas kernels, second_gather(): pl.pallas_call(functools.partial(second_gather_kernel, count), out_shape=...  91.9 us
    dot_general x5, matrix products, matmul(): return jnp.dot(left, right, preferred_element_type=F32)  61.4 us
    dot_general x5, matrix products, rows_inner(): lax.dot_general(left, right, (((0,), (0,)), ((), ())), preferred_element_...  53.1 us
    pallas_call x1, Pallas kernels, attention_back(): pl.pallas_call(functools.partial(attention_back_kernel, blocks), out_shap...  28.6 us
    dot_general x3, matrix products, cols_inner(): lax.dot_general(left, right, (((1,), (1,)), ((), ())), preferred_element_...  28.5 us
  transfers between devices with their start and end apart: 15, of which 5 were waited for; matrix products, arithmetic and copies ran while one was open for 17% of the time, Pallas kernels for 34%

profile of v6, /device:TPU:0, one launch (start us, length us, event | category | flops | bytes accessed | tf_op | source)
XLA Modules:
  0.0 786.2 jit_solution(16168492161731012338)
XLA Ops:
  18.7 135.9 %shard_map.221 = (bf16[2,128,2304]{2,1,0:T(8,128)(2,1)S(1)}, bf16[4,2,128,2304]{3,2,1,0:T(8,128)(2,1)S(1)}, bf16[4,2,288,1728]{3,2,1,0:T(8,128)(2,1)}, bf16[4,28...) custom-call(bf16[128,2304]{1,0:T(8,128)(2,1)S(1)} %get-tuple-element.99.tokens, ...), custom_call_target="tpu_custom_call" | custom-call | tf_op jit(solution)/shard_map/pallas_call | solution.py:479
  170.6 15.6 %fusion.11.projected = f32[1024,1728]{1,0:T(8,128)} fusion(bf16[1024,2304]{1,0:T(8,128)(2,1)} %bitcast.125, bf16[2304,1728]{1,0:T(8,128)(2,1)} %bitcast.136), kind=kOutput, calls=%fused_computation.65 | convolution fusion | flops 8153726976 | bytes 19759104 | tf_op jit(solution)/shard_map/dot_general | solution.py:1398
  186.2 18.6 %shard_map.222 = (bf16[1024,576]{1,0:T(8,128)(2,1)S(1)}, bf16[9,1024,64]{2,1,0:T(8,128)(2,1)S(1)}, bf16[9,1024,64]{2,1,0:T(8,128)(2,1)}, bf16[9,1024,64]{2,1,0:T(8,128)(2,1)}, f32[9,1,1024]{2,1,0:T(1,128)S(1)}) custom-call(s32[1]{0:T(128)} %dynamic_slice.71.length_ref, f32[1024,1728]{1,0:T(8,128)} %fusion.11.projected, f32[1024,128]{1,0:T(8,128)S(1)} %copy-done.17, ...), custom_call_target="tpu_custom_call" | custom-call | flops 2415919104 | bytes 20971520 | tf_op jit(solution)/shard_map/pallas_call | solution.py:107
  204.8 5.3 collective-permute-done
  211.2 5.6 convolution_convert_fusion.2
  216.8 5.7 collective-permute-done.1.second_low
  222.5 5.7 collective-permute-done.2.second_high
  228.2 91.9 %shard_map.223 = (f32[256,2304]{1,0:T(8,128)S(1)}, f32[2,128,2304]{2,1,0:T(8,128)S(1)}, bf16[2,4,2,128,2304]{4,3,2,1,0:T(8,128)(2,1)}, bf16[4,2,288,720]{3,2,1,0...) custom-call(bf16[4,256,2304]{2,1,0:T(8,128)(2,1)} %bitcast.150, ...), custom_call_target="tpu_custom_call" | custom-call | tf_op jit(solution)/shard_map/pallas_call | solution.py:670
  322.9 12.9 %fusion.13 = f32[2048,720]{1,0:T(8,128)} fusion(bf16[2048,2304]{1,0:T(8,128)(2,1)} %bitcast.163, bf16[2304,720]{1,0:T(8,128)(2,1)} %bitcast.171), kind=kOutput, calls=%fused_computation.67 | convolution fusion | flops 6794772480 | bytes 18653184 | tf_op jit(solution)/shard_map/dot_general | solution.py:1398
  335.8 11.8 %fusion.12 = f32[2048,720]{1,0:T(8,128)} fusion(bf16[2048,2304]{1,0:T(8,128)(2,1)} %bitcast.160, bf16[2304,720]{1,0:T(8,128)(2,1)S(1)} %bitcast.152), kind=kOutput, calls=%fused_computation.66 | convolution fusion | flops 6794772480 | bytes 18653184 | tf_op jit(solution)/shard_map/dot_general | solution.py:1398
  347.6 16.2 %multiply_convert_fusion.1 = (bf16[2048,720]{1,0:T(8,128)(2,1)S(1)}, bf16[2048,720]{1,0:T(8,128)(2,1)}, bf16[2048,720]{1,0:T(8,128)(2,1)}) fusion(f32[2048,720]{1,0:T(8,128)} %fusion.13, f32[2048,720]{1,0:T(8,128)} %fusion.12, bf16[2048,2304]{1,0:T(8,128)(2,1)S(1)} %bitcast.166, bf16[2304,720]{1,0:T(8,128)(2,1)} %bitcast.169), kind=kOutput, calls=%fused_computation.4 | convolution fusion | flops 6822789120 | bytes 33398784 | tf_op jit(solution)/shard_map/dot_general | solution.py:1398
  363.9 11.6 %multiply_convert_fusion = bf16[2304,720]{1,0:T(8,128)(2,1)S(1)} fusion(bf16[2048,2304]{1,0:T(8,128)(2,1)} %bitcast.161, bf16[2048,720]{1,0:T(8,128)(2,1)S(1)} %get-tuple-element.83.hidden), kind=kOutput, calls=%fused_computation.3 | convolution fusion | flops 6798090240 | bytes 15704064 | tf_op jit(solution)/shard_map/dot_general | solution.py:1402
  378.7 9.9 %convolution_convert_fusion.1 = bf16[2048,2304]{1,0:T(8,128)(2,1)} fusion(bf16[2048,720]{1,0:T(8,128)(2,1)S(1)} %copy-done.43, bf16[2304,720]{1,0:T(8,128)(2,1)S(1)} %bitcast.172), kind=kOutput, calls=%fused_computation.2 | convolution fusion | flops 6799491072 | bytes 15704064 | tf_op jit(solution)/shard_map/dot_general | solution.py:1406
  388.6 13.0 %add_convert_fusion = bf16[2048,2304]{1,0:T(8,128)(2,1)} fusion(bf16[2048,2304]{1,0:T(8,128)(2,1)} %convolution_convert_fusion.1, bf16[2048,720]{1,0:T(8,128)(2,1)} %get-tuple-element.85, bf16[2304,720]{1,0:T(8,128)(2,1)S(1)} %bitcast.170), kind=kOutput, calls=%fused_computation | convolution fusion | flops 6808928256 | bytes 25141248 | tf_op jit(solution)/shard_map/dot_general | solution.py:1406
  402.5 12.8 %convolution_convert_fusion.4 = bf16[2304,720]{1,0:T(8,128)(2,1)} fusion(bf16[2048,2304]{1,0:T(8,128)(2,1)} %bitcast.164, bf16[2048,720]{1,0:T(8,128)(2,1)} %get-tuple-element.84), kind=kOutput, calls=%fused_computation.11 | convolution fusion | flops 6796431360 | bytes 15704064 | tf_op jit(solution)/shard_map/dot_general | solution.py:1402
  416.7 9.2 %collective-permute-start.4 = (bf16[576,720]{1,0:T(8,128)(2,1)S(1)}, bf16[576,720]{1,0:T(8,128)(2,1)S(1)}, u32[]{:S(2)}, u32[]{:S(2)}) collective-permute-start(bf16[576,720]{1,0:T(8,128)(2,1)S(1)} %get-tuple-element.89), channel_id=1, source_target_pairs={{0,8},{8,16},{1,9},{9,17},{2,10},{10,18},{3,11},{11,19},{4,12},{12... | collective-permute-start | bytes 2488328 | tf_op jit(solution)/shard_map/ppermute | solution.py:1527
  425.9 11.4 %convolution_convert_fusion.3 = bf16[2304,720]{1,0:T(8,128)(2,1)} fusion(bf16[2048,2304]{1,0:T(8,128)(2,1)} %bitcast.165, bf16[2048,720]{1,0:T(8,128)(2,1)S(1)} %copy-done.42), kind=kOutput, calls=%fused_computation.10 | convolution fusion | flops 6796431360 | bytes 15704064 | tf_op jit(solution)/shard_map/dot_general | solution.py:1402
  443.0 92.5 %shard_map.224 = (f32[256,2304]{1,0:T(8,128)}, bf16[4,2,128,2304]{3,2,1,0:T(8,128)(2,1)}, f32[1,2304]{1,0:T(1,128)}, bf16[2,576,720]{2,1,0:T(8,128)(2,1)}, bf16[...) custom-call(bf16[2,4,2,128,2304]{4,3,2,1,0:T(8,128)(2,1)} %bitcast.134, bf16[4,576,720]{2,1,0:T(8,128)(2,1)} %bitcast.139, ...), custom_call_target="tpu_custom_call" | custom-call | tf_op jit(solution)/shard_map/pallas_call | solution.py:1022
  535.6 11.0 %collective-permute-start.8 = (bf16[576,720]{1,0:T(8,128)(2,1)}, bf16[576,720]{1,0:T(8,128)(2,1)S(1)}, u32[]{:S(2)}, u32[]{:S(2)}) collective-permute-start(bf16[576,720]{1,0:T(8,128)(2,1)} %fusion.6), channel_id=1, source_target_pairs={{0,8},{8,16},{16,24},{1,9},{9,17},{17,25},{2,10},{10,18},{18,26},{... | collective-permute-start | bytes 2488328 | tf_op jit(solution)/shard_map/ppermute | solution.py:1548
  547.9 6.4 convolution_convert_fusion.5
  571.9 28.6 %shard_map.225.grad_projected = bf16[1024,1728]{1,0:T(8,128)(2,1)} custom-call(s32[1]{0:T(128)} %dynamic_slice.71.length_ref, bf16[1024,576]{1,0:T(8,128)(2,1)} %convolution_convert_fusion.6.grad_context, bf16[9,1024,64]{2,1,0:T(8,128)(2,1)} %copy-done.18, bf16[9,1024,64]{2,1,0:T(8,128)(2,1)} %get-tuple-element.65.k_heads, ...), custom_call_target="tpu_custom_call" | custom-call | flops 6039797760 | bytes 20971520 | tf_op jit(solution)/shard_map/pallas_call | solution.py:186
  602.5 8.5 %collective-permute-done.7 = bf16[4,288,576]{2,1,0:T(8,128)(2,1)} collective-permute-done((bf16[4,288,576]{2,1,0:T(8,128)(2,1)}, bf16[4,288,576]{2,1,0:T(8,128)(2,1)}, u32[]{:S(2)}, u32[]{:S(2)}) %collective-permute-start.7) | collective-permute-done | bytes 1327136 | tf_op jit(solution)/shard_map/ppermute | solution.py:1418
  620.5 10.9 %convolution_convert_fusion = bf16[2304,1728]{1,0:T(8,128)(2,1)} fusion(bf16[1024,2304]{1,0:T(8,128)(2,1)S(1)} %bitcast.128, bf16[1024,1728]{1,0:T(8,128)(2,1)S(1)} %copy-done.25), kind=kOutput, calls=%fused_computation.1 | convolution fusion | flops 8157708288 | bytes 16220160 | tf_op jit(solution)/shard_map/dot_general | solution.py:1402
  634.3 128.0 %shard_map.226 = (f32[288,1728]{1,0:T(8,128)}, f32[288,576]{1,0:T(8,128)}, bf16[2,128,2304]{2,1,0:T(8,128)(2,1)}, f32[2,2304]{1,0:T(2,128)}) custom-call(bf16[1024,1728]{1,0:T(8,128)(2,1)} %shard_map.225.grad_projected, bf16[2304,1728]{1,0:T(8,128)(2,1)} %bitcast.137, bf16[4,2,288,1728]{3,2,1,0:T(8,128)(2,1)} %bitcast.138, ...), custom_call_target="tpu_custom_call" | custom-call | tf_op jit(solution)/shard_map/pallas_call | solution.py:1348
  (156 shorter events, 92.3 us)
Async XLA Ops:
  7.2 328.6 %all-gather.3.cloned.1.call-start = ((), (), s32[]{:S(2)}) async-start(), calls=%async_computation.2 | async-start | bytes 10616832 | tf_op jit(solution)/shard_map/all_gather | solution.py:1482
  18.7 151.3 %copy-start.41 = (s32[2]{0:T(128)S(1)}, s32[2]{0:T(128)}, u32[]{:S(2)}) copy-start(s32[2]{0:T(128)} %param.15) | copy-start | bytes 28
  18.7 151.9 %copy-start.36 = (bf16[2304]{0:T(1024)(128)(2,1)S(1)}, bf16[2304]{0:T(1024)(128)(2,1)}, u32[]{:S(2)}) copy-start(bf16[2304]{0:T(1024)(128)(2,1)} %param.21) | copy-start | bytes 13828
  162.0 612.3 %reduce-scatter.2.cloned.1.call-start = ((), (), s32[]{:S(2)}) async-start(), calls=%async_computation.1 | async-start | bytes 10616832 | tf_op jit(solution)/shard_map/reduce_scatter | solution.py:1577
  162.0 48.0 %collective-permute-start = (bf16[4,288,576]{2,1,0:T(8,128)(2,1)}, bf16[4,288,576]{2,1,0:T(8,128)(2,1)S(1)}, u32[]{:S(2)}, u32[]{:S(2)}) collective-permute-start(bf16[4,288,576]{2,1,0:T(8,128)(2,1)} %copy-done.10), channel_id=1, source_target_pairs={{0,4},{4,0},{1,5},{5,1},{2,6},{6,2},{3,7},{7,3},{8,12},{12,8},{9,1... | collective-permute-start | bytes 3981320 | tf_op jit(solution)/shard_map/ppermute | solution.py:1418
  163.6 58.9 %collective-permute-start.1 = (bf16[2,3,288,720]{3,2,1,0:T(8,128)(2,1)}, bf16[2,3,288,720]{3,2,1,0:T(8,128)(2,1)}, u32[]{:S(2)}, u32[]{:S(2)}) collective-permute-start(bf16[2,3,288,720]{3,2,1,0:T(8,128)(2,1)} %copy-done.3), channel_id=1, source_target_pairs={{0,8},{8,16},{16,24},{1,9},{9,17},{17,25},{2,10},{10,18},{18,26},{... | collective-permute-start | bytes 7464968 | tf_op jit(solution)/shard_map/ppermute | solution.py:1489
  168.6 59.5 %collective-permute-start.2 = (bf16[2,3,288,720]{3,2,1,0:T(8,128)(2,1)}, bf16[2,3,288,720]{3,2,1,0:T(8,128)(2,1)}, u32[]{:S(2)}, u32[]{:S(2)}) collective-permute-start(bf16[2,3,288,720]{3,2,1,0:T(8,128)(2,1)} %copy-done.5), channel_id=1, source_target_pairs={{8,0},{16,8},{24,16},{9,1},{17,9},{25,17},{10,2},{18,10},{26,18},{... | collective-permute-start | bytes 7464968 | tf_op jit(solution)/shard_map/ppermute | solution.py:1490
  170.6 57.6 %copy-start.13 = (f32[1,2304]{1,0:T(1,128)}, f32[1,2304]{1,0:T(1,128)S(1)}, u32[]{:S(2)}) copy-start(f32[1,2304]{1,0:T(1,128)S(1)} %reshape.153.gain) | copy-start | bytes 27652
  186.2 23.9 %copy-start.11 = (bf16[4,288,576]{2,1,0:T(8,128)(2,1)S(1)}, bf16[4,288,576]{2,1,0:T(8,128)(2,1)}, u32[]{:S(2)}) copy-start(bf16[4,288,576]{2,1,0:T(8,128)(2,1)} %copy-done.10) | copy-start | bytes 3981316
  211.1 17.0 %copy-start.1 = (bf16[2,128,2304]{2,1,0:T(8,128)(2,1)S(1)}, bf16[2,128,2304]{2,1,0:T(8,128)(2,1)}, u32[]{:S(2)}) copy-start(bf16[2,128,2304]{2,1,0:T(8,128)(2,1)} %copy-done) | copy-start | bytes 3538948
  375.5 66.4 %copy-start.22 = (bf16[2304,720]{1,0:T(8,128)(2,1)}, bf16[2304,720]{1,0:T(8,128)(2,1)S(1)}, u32[]{:S(2)}) copy-start(bf16[2304,720]{1,0:T(8,128)(2,1)S(1)} %multiply_convert_fusion) | copy-start | bytes 9953284
  375.6 26.0 %collective-permute-start.5 = (bf16[576,720]{1,0:T(8,128)(2,1)S(1)}, bf16[576,720]{1,0:T(8,128)(2,1)S(1)}, u32[]{:S(2)}, u32[]{:S(2)}) collective-permute-start(bf16[576,720]{1,0:T(8,128)(2,1)S(1)} %get-tuple-element.90), channel_id=1, source_target_pairs={{24,16},{25,17},{26,18},{27,19},{28,20},{29,21},{30,22},{31,23}} | collective-permute-start | bytes 2488328 | tf_op jit(solution)/shard_map/ppermute | solution.py:1528
  376.5 38.9 %collective-permute-start.3 = (bf16[576,720]{1,0:T(8,128)(2,1)S(1)}, bf16[576,720]{1,0:T(8,128)(2,1)S(1)}, u32[]{:S(2)}, u32[]{:S(2)}) collective-permute-start(bf16[576,720]{1,0:T(8,128)(2,1)S(1)} %get-tuple-element.91), channel_id=1, source_target_pairs={{0,8},{1,9},{2,10},{3,11},{4,12},{5,13},{6,14},{7,15}} | collective-permute-start | bytes 2488328 | tf_op jit(solution)/shard_map/ppermute | solution.py:1527
  401.8 13.5 %collective-permute-start.6 = (bf16[576,720]{1,0:T(8,128)(2,1)S(1)}, bf16[576,720]{1,0:T(8,128)(2,1)S(1)}, u32[]{:S(2)}, u32[]{:S(2)}) collective-permute-start(bf16[576,720]{1,0:T(8,128)(2,1)S(1)} %fusion.3), channel_id=1, source_target_pairs={{16,8},{24,16},{17,9},{25,17},{18,10},{26,18},{19,11},{27,19},{20,... | collective-permute-start | bytes 2488328 | tf_op jit(solution)/shard_map/ppermute | solution.py:1528
  416.7 25.2 %collective-permute-start.4 = (bf16[576,720]{1,0:T(8,128)(2,1)S(1)}, bf16[576,720]{1,0:T(8,128)(2,1)S(1)}, u32[]{:S(2)}, u32[]{:S(2)}) collective-permute-start(bf16[576,720]{1,0:T(8,128)(2,1)S(1)} %get-tuple-element.89), channel_id=1, source_target_pairs={{0,8},{8,16},{1,9},{9,17},{2,10},{10,18},{3,11},{11,19},{4,12},{12... | collective-permute-start | bytes 2488328 | tf_op jit(solution)/shard_map/ppermute | solution.py:1527
  535.6 65.0 %collective-permute-start.8 = (bf16[576,720]{1,0:T(8,128)(2,1)}, bf16[576,720]{1,0:T(8,128)(2,1)S(1)}, u32[]{:S(2)}, u32[]{:S(2)}) collective-permute-start(bf16[576,720]{1,0:T(8,128)(2,1)} %fusion.6), channel_id=1, source_target_pairs={{0,8},{8,16},{16,24},{1,9},{9,17},{17,25},{2,10},{10,18},{18,26},{... | collective-permute-start | bytes 2488328 | tf_op jit(solution)/shard_map/ppermute | solution.py:1548
  546.5 54.0 %collective-permute-start.9 = (bf16[576,720]{1,0:T(8,128)(2,1)}, bf16[576,720]{1,0:T(8,128)(2,1)}, u32[]{:S(2)}, u32[]{:S(2)}) collective-permute-start(bf16[576,720]{1,0:T(8,128)(2,1)} %get-tuple-element.71), channel_id=1, source_target_pairs={{8,0},{16,8},{24,16},{9,1},{17,9},{25,17},{10,2},{18,10},{26,18},{... | collective-permute-start | bytes 2488328 | tf_op jit(solution)/shard_map/ppermute | solution.py:1550
  547.9 19.1 %copy-start.38 = (bf16[4,2,128,2304]{3,2,1,0:T(8,128)(2,1)S(1)}, bf16[4,2,128,2304]{3,2,1,0:T(8,128)(2,1)}, u32[]{:S(2)}) copy-start(bf16[4,2,128,2304]{3,2,1,0:T(8,128)(2,1)} %get-tuple-element.63) | copy-start | bytes 14155780
  555.5 55.4 %collective-permute-start.7 = (bf16[4,288,576]{2,1,0:T(8,128)(2,1)}, bf16[4,288,576]{2,1,0:T(8,128)(2,1)}, u32[]{:S(2)}, u32[]{:S(2)}) collective-permute-start(bf16[4,288,576]{2,1,0:T(8,128)(2,1)} %dynamic-slice_bitcast_fusion), channel_id=1, source_target_pairs={{0,4},{4,0},{1,5},{5,1},{2,6},{6,2},{3,7},{7,3},{8,12},{12,8},{9,1... | collective-permute-start | bytes 3981320 | tf_op jit(solution)/shard_map/ppermute | solution.py:1418
  560.6 50.4 %collective-permute-start.10 = (bf16[2,576,720]{2,1,0:T(8,128)(2,1)}, bf16[2,576,720]{2,1,0:T(8,128)(2,1)S(1)}, u32[]{:S(2)}, u32[]{:S(2)}) collective-permute-start(bf16[2,576,720]{2,1,0:T(8,128)(2,1)} %get-tuple-element.79), channel_id=1, source_target_pairs={{0,8},{8,16},{16,24},{1,9},{9,17},{17,25},{2,10},{10,18},{18,26},{... | collective-permute-start | bytes 4976648 | tf_op jit(solution)/shard_map/ppermute | solution.py:1548
  565.5 46.6 %collective-permute-start.11 = (bf16[2,576,720]{2,1,0:T(8,128)(2,1)}, bf16[2,576,720]{2,1,0:T(8,128)(2,1)}, u32[]{:S(2)}, u32[]{:S(2)}) collective-permute-start(bf16[2,576,720]{2,1,0:T(8,128)(2,1)} %get-tuple-element.80), channel_id=1, source_target_pairs={{8,0},{16,8},{24,16},{9,1},{17,9},{25,17},{10,2},{18,10},{26,18},{... | collective-permute-start | bytes 4976648 | tf_op jit(solution)/shard_map/ppermute | solution.py:1550
  600.6 20.0 %slice-start = ((s8[4718592]{0:T(1024)(128)(4,1)}), s8[4194304]{0:T(1024)(128)(4,1)S(1)}, s32[]{:S(2)}) async-start(s8[4718592]{0:T(1024)(128)(4,1)} %bitcast.126), calls=%async_computation.3 | async-start | bytes 8388608
  602.4 18.1 %slice-start.1 = ((s8[4718592]{0:T(1024)(128)(4,1)}), s8[524288]{0:T(1024)(128)(4,1)S(1)}, s32[]{:S(2)}) async-start(s8[4718592]{0:T(1024)(128)(4,1)} %bitcast.126), calls=%async_computation.4 | async-start | bytes 1048576
  618.1 149.2 %collective-permute-start.12 = (bf16[3,288,720]{2,1,0:T(8,128)(2,1)}, bf16[3,288,720]{2,1,0:T(8,128)(2,1)}, u32[]{:S(2)}, u32[]{:S(2)}) collective-permute-start(bf16[3,288,720]{2,1,0:T(8,128)(2,1)} %pad_maximum_fusion.2), channel_id=1, source_target_pairs={{0,4},{4,0},{1,5},{5,1},{2,6},{6,2},{3,7},{7,3},{8,12},{12,8},{9,1... | collective-permute-start | bytes 3732488 | tf_op jit(solution)/shard_map/ppermute | solution.py:1418
  (37 other events, 240.5 us)
Sparse Core Ops, SparseCore 0:
  162.1 72.8 all-gather.2
  535.7 118.4 reduce-scatter.1

commit v7 on v6

--- a/solution.py
+++ b/solution.py
@@ -210,6 +210,7 @@
     return jnp.asarray(np.tile(cosine, (1, 4))), jnp.asarray(signed)
 
 
+COST = pl.CostEstimate(flops=0, transcendentals=0, bytes_accessed=300 << 20)
 MESH = pl.DeviceIdType.MESH
 
 
@@ -500,6 +501,7 @@
             pltpu.SemaphoreType.DMA((2, 1)),
             pltpu.SemaphoreType.DMA((2, 1)),
         ],
+        cost_estimate=COST,
         compiler_params=pltpu.CompilerParams(
             collective_id=1, has_side_effects=True, vmem_limit_bytes=32 << 20
         ),
@@ -691,6 +693,7 @@
             pltpu.SemaphoreType.DMA((2,)),
             pltpu.SemaphoreType.DMA((2, 24)),
         ],
+        cost_estimate=COST,
         compiler_params=pltpu.CompilerParams(
             collective_id=2, has_side_effects=True, vmem_limit_bytes=40 << 20
         ),
@@ -1046,6 +1049,7 @@
             pltpu.SemaphoreType.DMA((5,)),
             pltpu.SemaphoreType.DMA((2, 2)),
         ],
+        cost_estimate=COST,
         compiler_params=pltpu.CompilerParams(
             collective_id=3, has_side_effects=True, vmem_limit_bytes=60 << 20
         ),
@@ -1380,6 +1384,7 @@
             pltpu.SemaphoreType.DMA((4,)),
             pltpu.SemaphoreType.DMA((2,)),
         ],
+        cost_estimate=COST,
         compiler_params=pltpu.CompilerParams(
             collective_id=4, has_side_effects=True, vmem_limit_bytes=60 << 20
         ),
@@ -1516,16 +1521,23 @@
         return gradient.reshape(count, width // count, hidden_width)
 
     down_blocks = blocks_of(BRANCH * rows_inner(cotangents_all, hidden))
-    low = high = None
-    for hop in range(1, count):
+    def leaving(hop, low, high):
         leaving_up = pick(down_blocks, jnp.minimum(z + count - hop, count - 1))
         leaving_down = pick(down_blocks, jnp.maximum(z - count + hop, 0))
         if hop > 1:
             leaving_up = (leaving_up.astype(F32) + low.astype(F32)).astype(BF)
             leaving_down = (leaving_down.astype(F32) + high.astype(F32)).astype(BF)
-        if hop < count - 1:
-            low = lax.ppermute(leaving_up, "fsdp", up_hop[:hop])
-            high = lax.ppermute(leaving_down, "fsdp", down_hop[count - 1 - hop :])
+        return leaving_up, leaving_down
+
+    def sent(hop, leaving_up, leaving_down):
+        return (
+            lax.ppermute(leaving_up, "fsdp", up_hop[:hop]),
+            lax.ppermute(leaving_down, "fsdp", down_hop[count - 1 - hop :]),
+        )
+
+    gone = leaving(1, None, None)
+    for hop in range(2, count - 1):
+        gone = leaving(hop, *sent(hop - 1, *gone))
     grad_hidden = BRANCH * matmul(cotangents_all, full_down)
     grad_gate_exact, grad_up_exact = silu_back(grad_hidden)
     grad_gate_pre = grad_gate_exact.astype(BF)
@@ -1535,8 +1547,7 @@
     gate_blocks = blocks_of(rows_inner(normed_two, grad_gate_pre))
     up_blocks = blocks_of(rows_inner(normed_two, grad_up_pre))
     part = grad_normed_two.astype(BF).reshape(sets, lanes, slots, local, width)
-    if count > 1:
-        part, leaving_up, leaving_down = lax.optimization_barrier((part, leaving_up, leaving_down))
+    part, gone = lax.optimization_barrier((part, gone))
     grad_middle, grad_attention, gain_two_rows, pair_up, pair_down, feedforward = first_sum(
         count, part, gate_blocks, up_blocks, hidden, middle, cotangent_rows, gain_two[None],
         full_down,
@@ -1544,7 +1555,10 @@
     grad_attention = grad_attention.reshape(seq, width)
 
     if count > 1:
-        leaving_up, leaving_down = after((leaving_up, leaving_down), grad_attention)
+        if count > 2:
+            arrived = after(sent(count - 2, *gone), grad_attention)
+            gone = leaving(count - 1, *arrived)
+        leaving_up, leaving_down = after(gone, grad_attention)
         low = [lax.ppermute(pair_up, "fsdp", up_hop), lax.ppermute(leaving_up, "fsdp", up_hop)]
         high = [
             lax.ppermute(pair_down, "fsdp", down_hop), lax.ppermute(leaving_down, "fsdp", down_hop),

time: 797 us -> 789 us (0.990)
  starting transfers between devices: 46.8 us -> 36.2 us
  Pallas kernels: 495 us -> 504 us
    ppermute x1, waiting for transfers between devices: 0.01 us -> 9.23 us  [on_device(): lax.ppermute(leaving_up, 'fsdp', up_hop)]
    ppermute x3, waiting for transfers between devices: 13.7 us -> 5.19 us  [swap(): return lax.ppermute(value, 'cp', [(0, 1), (1, 0)])]
    unnamed x94 -> x104, local copies, waits for them, and re-layouts: 16.1 us -> 15.8 us
  transfers between devices with their start and end apart: 15 -> 15, of which waited for: 5 -> 5; matrix products, arithmetic and copies ran while one was open for 17% -> 14% of each run, Pallas kernels for 34% -> 35%
where the time goes in v7:
time: 789 us; the launch traced here: 783 us
  Pallas kernels  504 us (64%)
  matrix products  142 us (18%)
  starting transfers between devices  36.2 us (5%)
  local copies, waits for them, and re-layouts  30.5 us (4%)
  other arithmetic  28.2 us (4%)
  waiting for transfers between devices  27.3 us (3%)
  between operations  15.2 us (2%)
    pallas_call x1, Pallas kernels, first_gather(): pl.pallas_call(functools.partial(first_gather_kernel, count), out_shape=(...  136 us
    pallas_call x1, Pallas kernels, last_sum(): pl.pallas_call(functools.partial(last_sum_kernel, count), out_shape=(jax....  135 us
    pallas_call x1, Pallas kernels, first_sum(): pl.pallas_call(functools.partial(first_sum_kernel, count), out_shape=(jax...  93.1 us
    pallas_call x1, Pallas kernels, second_gather(): pl.pallas_call(functools.partial(second_gather_kernel, count), out_shape=...  91.9 us
    dot_general x5, matrix products, matmul(): return jnp.dot(left, right, preferred_element_type=F32)  61.5 us
    dot_general x5, matrix products, rows_inner(): lax.dot_general(left, right, (((0,), (0,)), ((), ())), preferred_element_...  51.8 us
    pallas_call x1, Pallas kernels, attention_back(): pl.pallas_call(functools.partial(attention_back_kernel, blocks), out_shap...  29.1 us
    dot_general x3, matrix products, cols_inner(): lax.dot_general(left, right, (((1,), (1,)), ((), ())), preferred_element_...  28.6 us
  transfers between devices with their start and end apart: 15, of which 5 were waited for; matrix products, arithmetic and copies ran while one was open for 14% of the time, Pallas kernels for 35%

profile of v7, /device:TPU:0, one launch (start us, length us, event | category | flops | bytes accessed | tf_op | source)
XLA Modules:
  0.0 782.8 jit_solution(16133760601847422355)
XLA Ops:
  18.7 135.9 %shard_map.221 = (bf16[2,128,2304]{2,1,0:T(8,128)(2,1)S(1)}, bf16[4,2,128,2304]{3,2,1,0:T(8,128)(2,1)S(1)}, bf16[4,2,288,1728]{3,2,1,0:T(8,128)(2,1)}, bf16[4,28...) custom-call(bf16[128,2304]{1,0:T(8,128)(2,1)S(1)} %get-tuple-element.105.tokens, ...), custom_call_target="tpu_custom_call" | custom-call | bytes 314572800 | tf_op jit(solution)/shard_map/pallas_call | solution.py:480
  170.5 15.6 %fusion.11.projected = f32[1024,1728]{1,0:T(8,128)} fusion(bf16[1024,2304]{1,0:T(8,128)(2,1)} %bitcast.125, bf16[2304,1728]{1,0:T(8,128)(2,1)} %bitcast.135), kind=kOutput, calls=%fused_computation.65 | convolution fusion | flops 8153726976 | bytes 19759104 | tf_op jit(solution)/shard_map/dot_general | solution.py:1403
  186.2 18.6 %shard_map.222 = (bf16[1024,576]{1,0:T(8,128)(2,1)S(1)}, bf16[9,1024,64]{2,1,0:T(8,128)(2,1)S(1)}, bf16[9,1024,64]{2,1,0:T(8,128)(2,1)}, bf16[9,1024,64]{2,1,0:T(8,128)(2,1)}, f32[9,1,1024]{2,1,0:T(1,128)S(1)}) custom-call(s32[1]{0:T(128)} %dynamic_slice.71.length_ref, f32[1024,1728]{1,0:T(8,128)} %fusion.11.projected, f32[1024,128]{1,0:T(8,128)S(1)} %copy-done.17, ...), custom_call_target="tpu_custom_call" | custom-call | flops 2415919104 | bytes 20971520 | tf_op jit(solution)/shard_map/pallas_call | solution.py:107
  211.1 5.6 convolution_convert_fusion.2
  216.7 5.7 collective-permute-done.1.second_low
  222.4 5.6 collective-permute-done.2.second_high
  228.1 91.9 %shard_map.223 = (f32[256,2304]{1,0:T(8,128)S(1)}, f32[2,128,2304]{2,1,0:T(8,128)S(1)}, bf16[2,4,2,128,2304]{4,3,2,1,0:T(8,128)(2,1)}, bf16[4,2,288,720]{3,2,1,0...) custom-call(bf16[4,256,2304]{2,1,0:T(8,128)(2,1)} %bitcast.149, ...), custom_call_target="tpu_custom_call" | custom-call | bytes 314572800 | tf_op jit(solution)/shard_map/pallas_call | solution.py:672
  322.9 12.9 %fusion.13 = f32[2048,720]{1,0:T(8,128)} fusion(bf16[2048,2304]{1,0:T(8,128)(2,1)} %bitcast.164, bf16[2304,720]{1,0:T(8,128)(2,1)} %bitcast.172), kind=kOutput, calls=%fused_computation.67 | convolution fusion | flops 6794772480 | bytes 18653184 | tf_op jit(solution)/shard_map/dot_general | solution.py:1403
  335.7 11.8 %fusion.12 = f32[2048,720]{1,0:T(8,128)} fusion(bf16[2048,2304]{1,0:T(8,128)(2,1)} %bitcast.159, bf16[2304,720]{1,0:T(8,128)(2,1)S(1)} %bitcast.151), kind=kOutput, calls=%fused_computation.66 | convolution fusion | flops 6794772480 | bytes 18653184 | tf_op jit(solution)/shard_map/dot_general | solution.py:1403
  347.6 16.2 %multiply_convert_fusion.1 = (bf16[2048,720]{1,0:T(8,128)(2,1)S(1)}, bf16[2048,720]{1,0:T(8,128)(2,1)}, bf16[2048,720]{1,0:T(8,128)(2,1)}) fusion(f32[2048,720]{1,0:T(8,128)} %fusion.13, f32[2048,720]{1,0:T(8,128)} %fusion.12, bf16[2048,2304]{1,0:T(8,128)(2,1)S(1)} %bitcast.167, bf16[2304,720]{1,0:T(8,128)(2,1)} %bitcast.170), kind=kOutput, calls=%fused_computation.4 | convolution fusion | flops 6822789120 | bytes 33398784 | tf_op jit(solution)/shard_map/dot_general | solution.py:1403
  363.8 13.8 %convolution_convert_fusion.4 = bf16[2304,720]{1,0:T(8,128)(2,1)} fusion(bf16[2048,2304]{1,0:T(8,128)(2,1)} %bitcast.165, bf16[2048,720]{1,0:T(8,128)(2,1)} %get-tuple-element.88), kind=kOutput, calls=%fused_computation.11 | convolution fusion | flops 6796431360 | bytes 15704064 | tf_op jit(solution)/shard_map/dot_general | solution.py:1407
  377.6 9.9 %convolution_convert_fusion.1 = bf16[2048,2304]{1,0:T(8,128)(2,1)} fusion(bf16[2048,720]{1,0:T(8,128)(2,1)S(1)} %copy-done.45, bf16[2304,720]{1,0:T(8,128)(2,1)S(1)} %bitcast.173), kind=kOutput, calls=%fused_computation.2 | convolution fusion | flops 6799491072 | bytes 15704064 | tf_op jit(solution)/shard_map/dot_general | solution.py:1411
  387.5 8.1 %multiply_convert_fusion = bf16[2304,720]{1,0:T(8,128)(2,1)S(1)} fusion(bf16[2048,2304]{1,0:T(8,128)(2,1)S(1)} %bitcast.163, bf16[2048,720]{1,0:T(8,128)(2,1)S(1)} %get-tuple-element.87.hidden), kind=kOutput, calls=%fused_computation.3 | convolution fusion | flops 6798090240 | bytes 15704064 | tf_op jit(solution)/shard_map/dot_general | solution.py:1407
  398.9 13.2 %add_convert_fusion = bf16[2048,2304]{1,0:T(8,128)(2,1)} fusion(bf16[2048,2304]{1,0:T(8,128)(2,1)} %convolution_convert_fusion.1, bf16[2048,720]{1,0:T(8,128)(2,1)} %get-tuple-element.89, bf16[2304,720]{1,0:T(8,128)(2,1)S(1)} %bitcast.171), kind=kOutput, calls=%fused_computation | convolution fusion | flops 6808928256 | bytes 25141248 | tf_op jit(solution)/shard_map/dot_general | solution.py:1411
  412.1 12.4 %convolution_convert_fusion.3 = bf16[2304,720]{1,0:T(8,128)(2,1)} fusion(bf16[2048,2304]{1,0:T(8,128)(2,1)} %bitcast.166, bf16[2048,720]{1,0:T(8,128)(2,1)} %get-tuple-element.89), kind=kOutput, calls=%fused_computation.10 | convolution fusion | flops 6796431360 | bytes 15704064 | tf_op jit(solution)/shard_map/dot_general | solution.py:1407
  428.5 93.1 %shard_map.224 = (f32[256,2304]{1,0:T(8,128)}, bf16[4,2,128,2304]{3,2,1,0:T(8,128)(2,1)}, f32[1,2304]{1,0:T(1,128)}, bf16[2,576,720]{2,1,0:T(8,128)(2,1)}, bf16[...) custom-call(bf16[2,4,2,128,2304]{4,3,2,1,0:T(8,128)(2,1)} %bitcast.133, bf16[4,576,720]{2,1,0:T(8,128)(2,1)} %bitcast.138, ...), custom_call_target="tpu_custom_call" | custom-call | bytes 314572800 | tf_op jit(solution)/shard_map/pallas_call | solution.py:1025
  521.7 7.8 collective-permute-start.6
  530.6 6.4 convolution_convert_fusion.5
  539.5 6.3 collective-permute-start.10
  553.9 5.6 collective-permute-start.8
  560.9 29.1 %shard_map.225.grad_projected = bf16[1024,1728]{1,0:T(8,128)(2,1)} custom-call(s32[1]{0:T(128)} %dynamic_slice.71.length_ref, bf16[1024,576]{1,0:T(8,128)(2,1)} %convolution_convert_fusion.6.grad_context, bf16[9,1024,64]{2,1,0:T(8,128)(2,1)} %copy-done.18, bf16[9,1024,64]{2,1,0:T(8,128)(2,1)} %get-tuple-element.67.k_heads, ...), custom_call_target="tpu_custom_call" | custom-call | flops 6039797760 | bytes 20971520 | tf_op jit(solution)/shard_map/pallas_call | solution.py:186
  592.9 9.2 %collective-permute-done.8 = bf16[576,720]{1,0:T(8,128)(2,1)} collective-permute-done((bf16[576,720]{1,0:T(8,128)(2,1)}, bf16[576,720]{1,0:T(8,128)(2,1)}, u32[]{:S(2)}, u32[]{:S(2)}) %collective-permute-start.8) | collective-permute-done | bytes 829472 | tf_op jit(solution)/shard_map/ppermute | solution.py:1562
  613.3 11.2 %convolution_convert_fusion = bf16[2304,1728]{1,0:T(8,128)(2,1)} fusion(bf16[1024,2304]{1,0:T(8,128)(2,1)S(1)} %bitcast.128, bf16[1024,1728]{1,0:T(8,128)(2,1)S(1)} %copy-done.25), kind=kOutput, calls=%fused_computation.1 | convolution fusion | flops 8157708288 | bytes 16220160 | tf_op jit(solution)/shard_map/dot_general | solution.py:1407
  624.4 134.9 %shard_map.226 = (f32[288,1728]{1,0:T(8,128)}, f32[288,576]{1,0:T(8,128)}, bf16[2,128,2304]{2,1,0:T(8,128)(2,1)}, f32[2,2304]{1,0:T(2,128)}) custom-call(bf16[1024,1728]{1,0:T(8,128)(2,1)} %shard_map.225.grad_projected, bf16[2304,1728]{1,0:T(8,128)(2,1)} %bitcast.136, bf16[4,2,288,1728]{3,2,1,0:T(8,128)(2,1)} %bitcast.137, ...), custom_call_target="tpu_custom_call" | custom-call | bytes 314572800 | tf_op jit(solution)/shard_map/pallas_call | solution.py:1352
  (166 shorter events, 86.9 us)
Async XLA Ops:
  7.2 328.6 %all-gather.3.cloned.1.call-start = ((), (), s32[]{:S(2)}) async-start(), calls=%async_computation.2 | async-start | bytes 10616832 | tf_op jit(solution)/shard_map/all_gather | solution.py:1487
  18.7 151.2 %copy-start.44 = (s32[2]{0:T(128)S(1)}, s32[2]{0:T(128)}, u32[]{:S(2)}) copy-start(s32[2]{0:T(128)} %param.15) | copy-start | bytes 28
  18.7 151.8 %copy-start.39 = (bf16[2304]{0:T(1024)(128)(2,1)S(1)}, bf16[2304]{0:T(1024)(128)(2,1)}, u32[]{:S(2)}) copy-start(bf16[2304]{0:T(1024)(128)(2,1)} %param.21) | copy-start | bytes 13828
  161.9 608.9 %reduce-scatter.2.cloned.1.call-start = ((), (), s32[]{:S(2)}) async-start(), calls=%async_computation.1 | async-start | bytes 10616832 | tf_op jit(solution)/shard_map/reduce_scatter | solution.py:1591
  162.0 48.0 %collective-permute-start = (bf16[4,288,576]{2,1,0:T(8,128)(2,1)}, bf16[4,288,576]{2,1,0:T(8,128)(2,1)S(1)}, u32[]{:S(2)}, u32[]{:S(2)}) collective-permute-start(bf16[4,288,576]{2,1,0:T(8,128)(2,1)} %copy-done.10), channel_id=1, source_target_pairs={{0,4},{4,0},{1,5},{5,1},{2,6},{6,2},{3,7},{7,3},{8,12},{12,8},{9,1... | collective-permute-start | bytes 3981320 | tf_op jit(solution)/shard_map/ppermute | solution.py:1423
  163.5 58.9 %collective-permute-start.1 = (bf16[2,3,288,720]{3,2,1,0:T(8,128)(2,1)}, bf16[2,3,288,720]{3,2,1,0:T(8,128)(2,1)}, u32[]{:S(2)}, u32[]{:S(2)}) collective-permute-start(bf16[2,3,288,720]{3,2,1,0:T(8,128)(2,1)} %copy-done.3), channel_id=1, source_target_pairs={{0,8},{8,16},{16,24},{1,9},{9,17},{17,25},{2,10},{10,18},{18,26},{... | collective-permute-start | bytes 7464968 | tf_op jit(solution)/shard_map/ppermute | solution.py:1494
  168.6 59.5 %collective-permute-start.2 = (bf16[2,3,288,720]{3,2,1,0:T(8,128)(2,1)}, bf16[2,3,288,720]{3,2,1,0:T(8,128)(2,1)}, u32[]{:S(2)}, u32[]{:S(2)}) collective-permute-start(bf16[2,3,288,720]{3,2,1,0:T(8,128)(2,1)} %copy-done.5), channel_id=1, source_target_pairs={{8,0},{16,8},{24,16},{9,1},{17,9},{25,17},{10,2},{18,10},{26,18},{... | collective-permute-start | bytes 7464968 | tf_op jit(solution)/shard_map/ppermute | solution.py:1495
  170.5 57.6 %copy-start.13 = (f32[1,2304]{1,0:T(1,128)}, f32[1,2304]{1,0:T(1,128)S(1)}, u32[]{:S(2)}) copy-start(f32[1,2304]{1,0:T(1,128)S(1)} %reshape.153.gain) | copy-start | bytes 27652
  186.2 23.8 %copy-start.11 = (bf16[4,288,576]{2,1,0:T(8,128)(2,1)S(1)}, bf16[4,288,576]{2,1,0:T(8,128)(2,1)}, u32[]{:S(2)}) copy-start(bf16[4,288,576]{2,1,0:T(8,128)(2,1)} %copy-done.10) | copy-start | bytes 3981316
  363.8 23.7 %copy-start.27 = (bf16[2048,720]{1,0:T(8,128)(2,1)}, bf16[2048,720]{1,0:T(8,128)(2,1)S(1)}, u32[]{:S(2)}) copy-start(bf16[2048,720]{1,0:T(8,128)(2,1)S(1)} %get-tuple-element.87.hidden) | copy-start | bytes 8847364
  363.8 23.7 %slice-start.2 = ((s8[9437184]{0:T(1024)(128)(4,1)}), s8[4194304]{0:T(1024)(128)(4,1)S(1)}, s32[]{:S(2)}) async-start(s8[9437184]{0:T(1024)(128)(4,1)} %bitcast.161), calls=%async_computation.5 | async-start | bytes 8388608
  363.8 23.7 %slice-start.3 = ((s8[9437184]{0:T(1024)(128)(4,1)}), s8[4194304]{0:T(1024)(128)(4,1)S(1)}, s32[]{:S(2)}) async-start(s8[9437184]{0:T(1024)(128)(4,1)} %bitcast.161), calls=%async_computation.6 | async-start | bytes 8388608
  395.6 31.2 %copy-start.22 = (bf16[2304,720]{1,0:T(8,128)(2,1)}, bf16[2304,720]{1,0:T(8,128)(2,1)S(1)}, u32[]{:S(2)}) copy-start(bf16[2304,720]{1,0:T(8,128)(2,1)S(1)} %multiply_convert_fusion) | copy-start | bytes 9953284
  395.8 31.0 %collective-permute-start.4 = (bf16[576,720]{1,0:T(8,128)(2,1)S(1)}, bf16[576,720]{1,0:T(8,128)(2,1)S(1)}, u32[]{:S(2)}, u32[]{:S(2)}) collective-permute-start(bf16[576,720]{1,0:T(8,128)(2,1)S(1)} %get-tuple-element.96), channel_id=1, source_target_pairs={{24,16},{25,17},{26,18},{27,19},{28,20},{29,21},{30,22},{31,23}} | collective-permute-start | bytes 2488328 | tf_op jit(solution)/shard_map/ppermute | solution.py:1535
  396.6 30.2 %collective-permute-start.3 = (bf16[576,720]{1,0:T(8,128)(2,1)S(1)}, bf16[576,720]{1,0:T(8,128)(2,1)S(1)}, u32[]{:S(2)}, u32[]{:S(2)}) collective-permute-start(bf16[576,720]{1,0:T(8,128)(2,1)S(1)} %get-tuple-element.97), channel_id=1, source_target_pairs={{0,8},{1,9},{2,10},{3,11},{4,12},{5,13},{6,14},{7,15}} | collective-permute-start | bytes 2488328 | tf_op jit(solution)/shard_map/ppermute | solution.py:1534
  521.7 30.6 %collective-permute-start.6 = (bf16[576,720]{1,0:T(8,128)(2,1)}, bf16[576,720]{1,0:T(8,128)(2,1)S(1)}, u32[]{:S(2)}, u32[]{:S(2)}) collective-permute-start(bf16[576,720]{1,0:T(8,128)(2,1)} %get-tuple-element.70), channel_id=1, source_target_pairs={{0,8},{8,16},{1,9},{9,17},{2,10},{10,18},{3,11},{11,19},{4,12},{12... | collective-permute-start | bytes 2488328 | tf_op jit(solution)/shard_map/ppermute | solution.py:1534
  529.5 22.8 %collective-permute-start.7 = (bf16[576,720]{1,0:T(8,128)(2,1)}, bf16[576,720]{1,0:T(8,128)(2,1)S(1)}, u32[]{:S(2)}, u32[]{:S(2)}) collective-permute-start(bf16[576,720]{1,0:T(8,128)(2,1)} %get-tuple-element.71), channel_id=1, source_target_pairs={{16,8},{24,16},{17,9},{25,17},{18,10},{26,18},{19,11},{27,19},{20,... | collective-permute-start | bytes 2488328 | tf_op jit(solution)/shard_map/ppermute | solution.py:1535
  538.3 51.8 %collective-permute-start.5 = (bf16[4,288,576]{2,1,0:T(8,128)(2,1)}, bf16[4,288,576]{2,1,0:T(8,128)(2,1)}, u32[]{:S(2)}, u32[]{:S(2)}) collective-permute-start(bf16[4,288,576]{2,1,0:T(8,128)(2,1)} %dynamic-slice_bitcast_fusion), channel_id=1, source_target_pairs={{0,4},{4,0},{1,5},{5,1},{2,6},{6,2},{3,7},{7,3},{8,12},{12,8},{9,1... | collective-permute-start | bytes 3981320 | tf_op jit(solution)/shard_map/ppermute | solution.py:1423
  539.5 64.0 %collective-permute-start.10 = (bf16[2,576,720]{2,1,0:T(8,128)(2,1)}, bf16[2,576,720]{2,1,0:T(8,128)(2,1)S(1)}, u32[]{:S(2)}, u32[]{:S(2)}) collective-permute-start(bf16[2,576,720]{2,1,0:T(8,128)(2,1)} %get-tuple-element.83), channel_id=1, source_target_pairs={{0,8},{8,16},{16,24},{1,9},{9,17},{17,25},{2,10},{10,18},{18,26},{... | collective-permute-start | bytes 4976648 | tf_op jit(solution)/shard_map/ppermute | solution.py:1562
  545.8 59.0 %collective-permute-start.11 = (bf16[2,576,720]{2,1,0:T(8,128)(2,1)}, bf16[2,576,720]{2,1,0:T(8,128)(2,1)}, u32[]{:S(2)}, u32[]{:S(2)}) collective-permute-start(bf16[2,576,720]{2,1,0:T(8,128)(2,1)} %get-tuple-element.84), channel_id=1, source_target_pairs={{8,0},{16,8},{24,16},{9,1},{17,9},{25,17},{10,2},{18,10},{26,18},{... | collective-permute-start | bytes 4976648 | tf_op jit(solution)/shard_map/ppermute | solution.py:1564
  553.9 48.2 %collective-permute-start.8 = (bf16[576,720]{1,0:T(8,128)(2,1)}, bf16[576,720]{1,0:T(8,128)(2,1)}, u32[]{:S(2)}, u32[]{:S(2)}) collective-permute-start(bf16[576,720]{1,0:T(8,128)(2,1)} %get-tuple-element.74), channel_id=1, source_target_pairs={{0,8},{8,16},{16,24},{1,9},{9,17},{17,25},{2,10},{10,18},{18,26},{... | collective-permute-start | bytes 2488328 | tf_op jit(solution)/shard_map/ppermute | solution.py:1562
  559.5 44.1 %collective-permute-start.9 = (bf16[576,720]{1,0:T(8,128)(2,1)}, bf16[576,720]{1,0:T(8,128)(2,1)}, u32[]{:S(2)}, u32[]{:S(2)}) collective-permute-start(bf16[576,720]{1,0:T(8,128)(2,1)} %get-tuple-element.75), channel_id=1, source_target_pairs={{8,0},{16,8},{24,16},{9,1},{17,9},{25,17},{10,2},{18,10},{26,18},{... | collective-permute-start | bytes 2488328 | tf_op jit(solution)/shard_map/ppermute | solution.py:1564
  560.9 29.1 %copy-start.29 = (bf16[2304,576]{1,0:T(8,128)(2,1)S(1)}, bf16[2304,576]{1,0:T(8,128)(2,1)}, u32[]{:S(2)}) copy-start(bf16[2304,576]{1,0:T(8,128)(2,1)} %copy-done.28) | copy-start | bytes 7962628
  611.8 152.1 %collective-permute-start.12 = (bf16[3,288,720]{2,1,0:T(8,128)(2,1)}, bf16[3,288,720]{2,1,0:T(8,128)(2,1)}, u32[]{:S(2)}, u32[]{:S(2)}) collective-permute-start(bf16[3,288,720]{2,1,0:T(8,128)(2,1)} %pad_maximum_fusion.2), channel_id=1, source_target_pairs={{0,4},{4,0},{1,5},{5,1},{2,6},{6,2},{3,7},{7,3},{8,12},{12,8},{9,1... | collective-permute-start | bytes 3732488 | tf_op jit(solution)/shard_map/ppermute | solution.py:1423
  (42 other events, 288.6 us)
Sparse Core Ops, SparseCore 0:
  162.0 72.8 all-gather.2
  521.8 112.1 reduce-scatter.1

commit v8 on v7

--- a/solution.py
+++ b/solution.py
@@ -381,7 +381,8 @@
 
 
 def first_gather_kernel(
-    count, tokens, tokens_away, gain, qkv, turned_out, wide, wide_away,
+    count, tokens, tokens_away, gain, qkv, turned_out,
+    wide_0, wide_1, wide_2, away_0, away_1, away_2,
     token_rows, normed_full, qkv_full, out_half, low_pair, high_pair,
     landed, normed, wide_landed, qkv_stage, out_stage,
     send, recv, local, qkv_local, out_local,
@@ -389,6 +390,7 @@
     z, c, t = lax.axis_index("fsdp"), lax.axis_index("cp"), lax.axis_index("tp")
     beside, yonder = t + 1 - 2 * (t % 2), (t + 2) % 4
     low, high = low_pair.at[0], high_pair.at[0]
+    wide, wide_away = (wide_0, wide_1, wide_2), (away_0, away_1, away_2)
     mail = Mail(send, recv)
     greet(count)
     stage_qkv = Stage([(qkv, qkv_full.at[z, c], None)], qkv_stage, qkv_local)
@@ -400,8 +402,8 @@
         heads, qkv, lambda j: qkv_full.at[j, c], lambda j: qkv_full.at[j, 1 - c]
     )
     outs = Line(mail, count, turned_out, lambda j: out_half.at[j])
-    wide_up, wide_down = mail.slot(), mail.slot()
-    rows_x, wide_x = mail.slot(), mail.slot()
+    wide_up, wide_down, wide_x = ([mail.slot() for _ in wide] for _ in range(3))
+    rows_x = mail.slot()
     rows_y = [mail.slot() for _ in range(2)]
     rows_core = [mail.slot() for _ in range(4)]
 
@@ -445,9 +447,13 @@
             rows_on(1, 1 - c)
             outs.send(1)
         if hop == min(2, count - 1):
-            mail.start(wide_up, wide, low, when=z < count - 1, fsdp=jnp.minimum(z + 1, count - 1))
-            mail.start(wide_down, wide, high, when=z > 0, fsdp=jnp.maximum(z - 1, 0))
-    mail.start(wide_x, wide_away, wide_landed, cp=1 - c)
+            for k, piece in enumerate(wide):
+                mail.start(
+                    wide_up[k], piece, low.at[k], when=z < count - 1, fsdp=jnp.minimum(z + 1, count - 1)
+                )
+                mail.start(wide_down[k], piece, high.at[k], when=z > 0, fsdp=jnp.maximum(z - 1, 0))
+    for k, piece in enumerate(wide_away):
+        mail.start(wide_x[k], piece, wide_landed.at[k], cp=1 - c)
     for hop in range(1, count):
         outs.arrive(hop)
         if hop + 1 < count:
@@ -459,12 +465,14 @@
     far = (beside + 2) % 4
     mail.arrive(rows_core[2], normed_full.at[far, c], tp=beside)
     mail.arrive(rows_core[3], normed_full.at[far, 1 - c], tp=beside)
-    mail.arrive(wide_x, wide_landed, cp=1 - c)
+    for k in range(len(wide)):
+        mail.arrive(wide_x[k], wide_landed.at[k], cp=1 - c)
     for pair, place in ((low_pair, 1), (high_pair, 3)):
         kept.append(pltpu.make_async_copy(wide_landed, pair.at[1], local.at[place]))
         kept[-1].start()
-    mail.arrive(wide_up, low, when=z > 0, fsdp=z)
-    mail.arrive(wide_down, high, when=z < count - 1, fsdp=z)
+    for k in range(len(wide)):
+        mail.arrive(wide_up[k], low.at[k], when=z > 0, fsdp=z)
+        mail.arrive(wide_down[k], high.at[k], when=z < count - 1, fsdp=z)
     for copy in kept:
         copy.wait()
     stage_qkv.end()
@@ -473,10 +481,11 @@
 
 
 def first_gather(count, tokens, tokens_away, gain, qkv, turned_out, wide, wide_away):
-    slots = 6 * count + 10
+    slots = 6 * count + 16
     anywhere = pl.BlockSpec(memory_space=pl.ANY)
     vmem = pl.BlockSpec(memory_space=pltpu.VMEM)
     pair = (2,) + tokens.shape
+    wide_shape = (3,) + wide[0].shape
     return pl.pallas_call(
         functools.partial(first_gather_kernel, count),
         out_shape=(
@@ -484,15 +493,15 @@
             jax.ShapeDtypeStruct((4,) + pair, BF),
             jax.ShapeDtypeStruct((count, 2) + qkv.shape, BF),
             jax.ShapeDtypeStruct((count,) + turned_out.shape, BF),
-            jax.ShapeDtypeStruct((2,) + wide.shape, BF),
-            jax.ShapeDtypeStruct((2,) + wide.shape, BF),
+            jax.ShapeDtypeStruct((2,) + wide_shape, BF),
+            jax.ShapeDtypeStruct((2,) + wide_shape, BF),
         ),
-        in_specs=[vmem, anywhere, vmem] + [anywhere] * 4,
+        in_specs=[vmem, anywhere, vmem] + [anywhere] * 8,
         out_specs=(vmem,) + (anywhere,) * 5,
         scratch_shapes=[
             pltpu.VMEM(tokens.shape, BF),
             pltpu.VMEM(pair, BF),
-            pltpu.VMEM(wide.shape, BF),
+            pltpu.VMEM(wide_shape, BF),
             pltpu.VMEM((1,) + qkv.shape, BF),
             pltpu.VMEM((1,) + turned_out.shape, BF),
             pltpu.SemaphoreType.DMA((slots,)),
@@ -505,7 +514,7 @@
         compiler_params=pltpu.CompilerParams(
             collective_id=1, has_side_effects=True, vmem_limit_bytes=32 << 20
         ),
-    )(tokens, tokens_away, gain, qkv, turned_out, wide, wide_away)
+    )(tokens, tokens_away, gain, qkv, turned_out, *wide, *wide_away)
 
 
 def in_pieces(rows, body, size=16):
@@ -569,10 +578,12 @@
 
 
 def second_gather_kernel(
-    count, part, tokens, gain, wide, first_low, first_high, second_low, second_high, *refs
+    count, part, tokens, gain, wide_0, wide_1, wide_2,
+    first_low, first_high, second_low, second_high, *refs
 ):
     hops_mine, hops_other = min(2, count - 1), 1
-    wide_other = first_low.at[1]
+    wide = (wide_0, wide_1, wide_2)
+    wide_other = [first_low.at[1, which] for which in range(3)]
     ready_mine = [first_low.at[0], first_high.at[0], second_low.at[0], second_high.at[0]]
     ready_mine = ready_mine[: 2 * hops_mine]
     ready_other = [second_low.at[1], second_high.at[1]]
@@ -595,7 +606,7 @@
             ]
             lines.append(
                 Line(
-                    mail, count, piece.at[which],
+                    mail, count, piece[which],
                     lambda j, full=full, side=side: full.at[j, side], arrived,
                 )
             )
@@ -668,7 +679,7 @@
     rows, width = tokens.shape
     anywhere = pl.BlockSpec(memory_space=pl.ANY)
     vmem = pl.BlockSpec(memory_space=pltpu.VMEM)
-    full = jax.ShapeDtypeStruct((count, 2) + wide.shape[1:], BF)
+    full = jax.ShapeDtypeStruct((count, 2) + wide[0].shape, BF)
     return pl.pallas_call(
         functools.partial(second_gather_kernel, count),
         out_shape=(
@@ -679,7 +690,7 @@
             full,
             full,
         ),
-        in_specs=[anywhere, vmem, vmem] + [anywhere] * 5,
+        in_specs=[anywhere, vmem, vmem] + [anywhere] * 7,
         out_specs=(vmem,) + (anywhere,) * 5,
         scratch_shapes=[
             pltpu.VMEM((2, rows, width), BF),
@@ -687,7 +698,7 @@
             pltpu.VMEM((rows, width), BF),
             pltpu.VMEM((rows, width), BF),
             pltpu.VMEM((2, rows // 2, width), BF),
-            pltpu.VMEM((24,) + wide.shape[1:], BF),
+            pltpu.VMEM((24,) + wide[0].shape, BF),
             pltpu.SemaphoreType.DMA((slots,)),
             pltpu.SemaphoreType.DMA((slots,)),
             pltpu.SemaphoreType.DMA((2,)),
@@ -697,7 +708,7 @@
         compiler_params=pltpu.CompilerParams(
             collective_id=2, has_side_effects=True, vmem_limit_bytes=40 << 20
         ),
-    )(part, tokens, gain, wide, first_low, first_high, second_low, second_high)
+    )(part, tokens, gain, *wide, first_low, first_high, second_low, second_high)
 
 
 class TensorSum:
@@ -819,16 +830,22 @@
 
 
 def first_sum_kernel(
-    count, part, gate_grad, up_grad, hidden, middle, cotangent, gain, down,
+    count, part, gate_grad, up_grad, hidden, middle_from, cotangent_from, down_from, gain,
     grad_middle, attention_full, gain_rows, leaving_up, leaving_down, feedforward,
-    own, from_core, first, second, grad_attention, totals, landed, hidden_rows, product,
-    send, recv, local, hidden_local,
+    own, from_core, first, second, grad_attention, totals, landed, hidden_rows, product, middle, cotangent, down,
+    send, recv, local, hidden_local, loads_local,
 ):
     z, c, t = lax.axis_index("fsdp"), lax.axis_index("cp"), lax.axis_index("tp")
     beside, yonder = t + 1 - 2 * (t % 2), (t + 2) % 4
     far = (beside + 2) % 4
     half = middle.shape[0] // 2
     width = middle.shape[1]
+    loads = [
+        pltpu.make_async_copy(source, target, loads_local.at[k])
+        for k, (source, target) in enumerate(
+            ((down_from, down), (middle_from, middle), (cotangent_from, cotangent))
+        )
+    ]
     mail = Mail(send, recv)
     greet(count)
     last = count - 1
@@ -906,6 +923,9 @@
         product_copy(block).start()
 
     hidden_copy(0).start()
+    for copy in loads:
+        copy.start()
+    loads[0].wait()
     product_block(0)
 
     quarter = half // 2
@@ -953,6 +973,8 @@
         in_pieces(quarter, one)
 
     gain_rows[...] = jnp.zeros_like(gain_rows)
+    loads[1].wait()
+    loads[2].wait()
 
     def finish(k):
         piece, rows = quarters[k]
@@ -1032,7 +1054,7 @@
             jax.ShapeDtypeStruct((2,) + block, BF),
             jax.ShapeDtypeStruct((hidden.shape[0], width), BF),
         ),
-        in_specs=[anywhere] * 4 + [vmem] * 4,
+        in_specs=[anywhere] * 7 + [vmem],
         out_specs=(vmem, anywhere, vmem, vmem, vmem, anywhere),
         scratch_shapes=[
             pltpu.VMEM((2, 2, 2, rows // 2, width), BF),
@@ -1044,28 +1066,32 @@
             pltpu.VMEM((2, hops, 2) + block, BF),
             pltpu.VMEM((2, hidden.shape[0] // 8, hidden.shape[1]), BF),
             pltpu.VMEM((2, hidden.shape[0] // 8, width), BF),
+            pltpu.VMEM((rows, width), F32),
+            pltpu.VMEM((rows, width), BF),
+            pltpu.VMEM(down.shape, BF),
             pltpu.SemaphoreType.DMA((slots,)),
             pltpu.SemaphoreType.DMA((slots,)),
             pltpu.SemaphoreType.DMA((5,)),
             pltpu.SemaphoreType.DMA((2, 2)),
+            pltpu.SemaphoreType.DMA((3,)),
         ],
         cost_estimate=COST,
         compiler_params=pltpu.CompilerParams(
             collective_id=3, has_side_effects=True, vmem_limit_bytes=60 << 20
         ),
-    )(part, gate_grad, up_grad, hidden, middle, cotangent, gain, down)
+    )(part, gate_grad, up_grad, hidden, middle, cotangent, down, gain)
 
 
 AHEAD = 6
 
 
 def last_sum_kernel(
-    count, grad_projected, qkv_full, qkv_grad, out_grad, tokens, grad_middle, gain, gain_rows,
+    count, projected_from, qkv_full, qkv_grad, out_grad, tokens_from, middle_from, gain, gain_rows,
     qkv_total, out_total, grad_tokens, gain_sums,
     own, from_core, to_yonder, from_yonder, pieces,
     from_x, heads_sum, heads_landed, outs_sum, outs_landed, final_out, gains, gain_line,
-    part, weights, give_sum, give_landed, give_own, give_total,
-    send, recv, local, weights_local,
+    part, weights, give_sum, give_landed, give_own, give_total, grad_projected, tokens, grad_middle,
+    send, recv, local, weights_local, loads_local,
 ):
     z, c, t = lax.axis_index("fsdp"), lax.axis_index("cp"), lax.axis_index("tp")
     beside, yonder = t + 1 - 2 * (t % 2), (t + 2) % 4
@@ -1192,7 +1218,20 @@
         part[:, :, columns] = value.astype(BF).reshape(part.shape[:2] + (wide_block,))
         return carry
 
+    loads = [
+        pltpu.make_async_copy(source, target, loads_local.at[k])
+        for k, (source, target) in enumerate(
+            (
+                (projected_from, grad_projected),
+                (tokens_from, tokens),
+                (middle_from, grad_middle),
+            )
+        )
+    ]
     weights_copy(0, 0).start()
+    for copy in loads:
+        copy.start()
+    loads[0].wait()
     thirds = [blocks * k // 3 for k in range(4)]
 
     keep = pltpu.make_async_copy(pieces.at[c], grad_tokens.at[c], local.at[0])
@@ -1201,6 +1240,8 @@
     line = Line(mail, count, gain_line.at[z], lambda j: gain_line.at[j])
 
     def finish_rows():
+        loads[1].wait()
+        loads[2].wait()
         gains[0, 0:1, :] = jnp.zeros_like(gain_rows)
         gains[0, 1:2, :] = gain_rows[...]
         for piece in range(2):
@@ -1357,7 +1398,7 @@
             jax.ShapeDtypeStruct((2, rows // 2, width), BF),
             jax.ShapeDtypeStruct((2, width), F32),
         ),
-        in_specs=[vmem] + [anywhere] * 3 + [vmem] * 4,
+        in_specs=[anywhere] * 6 + [vmem] * 2,
         out_specs=(vmem, vmem, anywhere, vmem),
         scratch_shapes=[
             pltpu.VMEM((2, rows, width), BF),
@@ -1379,10 +1420,14 @@
             pltpu.VMEM((2, hops) + give_block, BF),
             pltpu.VMEM(give_block, BF),
             pltpu.VMEM(give_block, BF),
+            pltpu.VMEM(grad_projected.shape, BF),
+            pltpu.VMEM(tokens.shape, BF),
+            pltpu.VMEM(grad_middle.shape, F32),
             pltpu.SemaphoreType.DMA((slots,)),
             pltpu.SemaphoreType.DMA((slots,)),
             pltpu.SemaphoreType.DMA((4,)),
             pltpu.SemaphoreType.DMA((2,)),
+            pltpu.SemaphoreType.DMA((3,)),
         ],
         cost_estimate=COST,
         compiler_params=pltpu.CompilerParams(
@@ -1473,8 +1518,8 @@
         return weight[:, :hidden_width], weight[:, hidden_width:]
 
     parts = [halves(weight) for weight in (gate_weight, up_weight, down_weight.T)]
-    own_wide = jnp.stack([jnp.where(c == 0, low, high) for low, high in parts])
-    wide_away = jnp.stack([jnp.where(c == 0, high, low) for low, high in parts])
+    own_wide = [jnp.where(c == 0, low, high) for low, high in parts]
+    wide_away = [jnp.where(c == 0, high, low) for low, high in parts]
     token_rows, normed_one, full_qkv, out_half, first_low, first_high = first_gather(
         count, pick(tokens, c), pick(tokens, 1 - c), gain_one[None], qkv, out_weight.T,
         own_wide, wide_away,

time: 789 us -> 789 us (level)
    unnamed x104 -> x102, local copies, waits for them, and re-layouts: 15.8 us -> 18 us
where the time goes in v8:
time: 789 us; the launch traced here: 782 us
  Pallas kernels  502 us (64%)
  matrix products  142 us (18%)
  starting transfers between devices  35.8 us (5%)
  local copies, waits for them, and re-layouts  31.1 us (4%)
  other arithmetic  30.7 us (4%)
  waiting for transfers between devices  25.3 us (3%)
  between operations  15.2 us (2%)
    pallas_call x1, Pallas kernels, first_gather(): pl.pallas_call(functools.partial(first_gather_kernel, count), out_shape=(...  136 us
    pallas_call x1, Pallas kernels, last_sum(): pl.pallas_call(functools.partial(last_sum_kernel, count), out_shape=(jax....  134 us
    pallas_call x1, Pallas kernels, first_sum(): pl.pallas_call(functools.partial(first_sum_kernel, count), out_shape=(jax...  92.5 us
    pallas_call x1, Pallas kernels, second_gather(): pl.pallas_call(functools.partial(second_gather_kernel, count), out_shape=...  92 us
    dot_general x5, matrix products, matmul(): return jnp.dot(left, right, preferred_element_type=F32)  61.3 us
    dot_general x5, matrix products, rows_inner(): lax.dot_general(left, right, (((0,), (0,)), ((), ())), preferred_element_...  51.8 us
    pallas_call x1, Pallas kernels, attention_back(): pl.pallas_call(functools.partial(attention_back_kernel, blocks), out_shap...  29.1 us
    dot_general x3, matrix products, cols_inner(): lax.dot_general(left, right, (((1,), (1,)), ((), ())), preferred_element_...  28.6 us
  transfers between devices with their start and end apart: 15, of which 5 were waited for; matrix products, arithmetic and copies ran while one was open for 14% of the time, Pallas kernels for 35%

profile of v8, /device:TPU:0, one launch (start us, length us, event | category | flops | bytes accessed | tf_op | source)
XLA Modules:
  0.0 782.4 jit_solution(6162072209842293526)
XLA Ops:
  19.8 136.0 %shard_map.221 = (bf16[2,128,2304]{2,1,0:T(8,128)(2,1)S(1)}, bf16[4,2,128,2304]{3,2,1,0:T(8,128)(2,1)S(1)}, bf16[4,2,288,1728]{3,2,1,0:T(8,128)(2,1)}, bf16[4,28...) custom-call(bf16[128,2304]{1,0:T(8,128)(2,1)S(1)} %get-tuple-element.105.tokens, ...), custom_call_target="tpu_custom_call" | custom-call | bytes 314572800 | tf_op jit(solution)/shard_map/pallas_call | solution.py:489
  163.8 5.0 collective-permute-start.1
  171.4 15.5 %fusion.11.projected = f32[1024,1728]{1,0:T(8,128)} fusion(bf16[1024,2304]{1,0:T(8,128)(2,1)} %bitcast.113, bf16[2304,1728]{1,0:T(8,128)(2,1)} %bitcast.123), kind=kOutput, calls=%fused_computation.63 | convolution fusion | flops 8153726976 | bytes 19759104 | tf_op jit(solution)/shard_map/dot_general | solution.py:1448
  186.9 18.4 %shard_map.222 = (bf16[1024,576]{1,0:T(8,128)(2,1)S(1)}, bf16[9,1024,64]{2,1,0:T(8,128)(2,1)S(1)}, bf16[9,1024,64]{2,1,0:T(8,128)(2,1)}, bf16[9,1024,64]{2,1,0:T(8,128)(2,1)}, f32[9,1,1024]{2,1,0:T(1,128)S(1)}) custom-call(s32[1]{0:T(128)} %dynamic_slice.71.length_ref, f32[1024,1728]{1,0:T(8,128)} %fusion.11.projected, f32[1024,128]{1,0:T(8,128)S(1)} %copy-done.18, ...), custom_call_target="tpu_custom_call" | custom-call | flops 2415919104 | bytes 20971520 | tf_op jit(solution)/shard_map/pallas_call | solution.py:107
  213.1 5.6 convolution_convert_fusion.2
  222.7 5.6 collective-permute-done.2.second_high
  228.4 92.0 %shard_map.223 = (f32[256,2304]{1,0:T(8,128)S(1)}, f32[2,128,2304]{2,1,0:T(8,128)S(1)}, bf16[2,4,2,128,2304]{4,3,2,1,0:T(8,128)(2,1)}, bf16[4,2,288,720]{3,2,1,0...) custom-call(bf16[4,256,2304]{2,1,0:T(8,128)(2,1)} %bitcast.137, ...), custom_call_target="tpu_custom_call" | custom-call | bytes 314572800 | tf_op jit(solution)/shard_map/pallas_call | solution.py:683
  323.2 12.9 %fusion.13 = f32[2048,720]{1,0:T(8,128)} fusion(bf16[2048,2304]{1,0:T(8,128)(2,1)} %bitcast.151, bf16[2304,720]{1,0:T(8,128)(2,1)} %bitcast.159), kind=kOutput, calls=%fused_computation.65 | convolution fusion | flops 6794772480 | bytes 18653184 | tf_op jit(solution)/shard_map/dot_general | solution.py:1448
  336.1 11.8 %fusion.12 = f32[2048,720]{1,0:T(8,128)} fusion(bf16[2048,2304]{1,0:T(8,128)(2,1)} %bitcast.146, bf16[2304,720]{1,0:T(8,128)(2,1)S(1)} %bitcast.139), kind=kOutput, calls=%fused_computation.64 | convolution fusion | flops 6794772480 | bytes 18653184 | tf_op jit(solution)/shard_map/dot_general | solution.py:1448
  347.9 16.2 %multiply_convert_fusion.1 = (bf16[2048,720]{1,0:T(8,128)(2,1)S(1)}, bf16[2048,720]{1,0:T(8,128)(2,1)}, bf16[2048,720]{1,0:T(8,128)(2,1)}) fusion(f32[2048,720]{1,0:T(8,128)} %fusion.13, f32[2048,720]{1,0:T(8,128)} %fusion.12, bf16[2048,2304]{1,0:T(8,128)(2,1)S(1)} %bitcast.154, bf16[2304,720]{1,0:T(8,128)(2,1)} %bitcast.157), kind=kOutput, calls=%fused_computation.4 | convolution fusion | flops 6822789120 | bytes 33398784 | tf_op jit(solution)/shard_map/dot_general | solution.py:1448
  364.2 13.8 %convolution_convert_fusion.4 = bf16[2304,720]{1,0:T(8,128)(2,1)} fusion(bf16[2048,2304]{1,0:T(8,128)(2,1)} %bitcast.152, bf16[2048,720]{1,0:T(8,128)(2,1)} %get-tuple-element.88), kind=kOutput, calls=%fused_computation.11 | convolution fusion | flops 6796431360 | bytes 15704064 | tf_op jit(solution)/shard_map/dot_general | solution.py:1452
  378.0 9.9 %convolution_convert_fusion.1 = bf16[2048,2304]{1,0:T(8,128)(2,1)} fusion(bf16[2048,720]{1,0:T(8,128)(2,1)S(1)} %copy-done.44, bf16[2304,720]{1,0:T(8,128)(2,1)S(1)} %bitcast.160), kind=kOutput, calls=%fused_computation.2 | convolution fusion | flops 6799491072 | bytes 15704064 | tf_op jit(solution)/shard_map/dot_general | solution.py:1456
  387.9 8.1 %multiply_convert_fusion = bf16[2304,720]{1,0:T(8,128)(2,1)S(1)} fusion(bf16[2048,2304]{1,0:T(8,128)(2,1)S(1)} %bitcast.150, bf16[2048,720]{1,0:T(8,128)(2,1)S(1)} %get-tuple-element.87.hidden), kind=kOutput, calls=%fused_computation.3 | convolution fusion | flops 6798090240 | bytes 15704064 | tf_op jit(solution)/shard_map/dot_general | solution.py:1452
  399.3 13.1 %add_convert_fusion = bf16[2048,2304]{1,0:T(8,128)(2,1)} fusion(bf16[2048,2304]{1,0:T(8,128)(2,1)} %convolution_convert_fusion.1, bf16[2048,720]{1,0:T(8,128)(2,1)} %get-tuple-element.89, bf16[2304,720]{1,0:T(8,128)(2,1)S(1)} %bitcast.158), kind=kOutput, calls=%fused_computation | convolution fusion | flops 6808928256 | bytes 25141248 | tf_op jit(solution)/shard_map/dot_general | solution.py:1456
  412.4 12.4 %convolution_convert_fusion.3 = bf16[2304,720]{1,0:T(8,128)(2,1)} fusion(bf16[2048,2304]{1,0:T(8,128)(2,1)} %bitcast.153, bf16[2048,720]{1,0:T(8,128)(2,1)} %get-tuple-element.89), kind=kOutput, calls=%fused_computation.10 | convolution fusion | flops 6796431360 | bytes 15704064 | tf_op jit(solution)/shard_map/dot_general | solution.py:1452
  428.9 92.5 %shard_map.224 = (f32[256,2304]{1,0:T(8,128)}, bf16[4,2,128,2304]{3,2,1,0:T(8,128)(2,1)}, f32[1,2304]{1,0:T(1,128)}, bf16[2,576,720]{2,1,0:T(8,128)(2,1)}, bf16[...) custom-call(bf16[2,4,2,128,2304]{4,3,2,1,0:T(8,128)(2,1)} %bitcast.121, bf16[4,576,720]{2,1,0:T(8,128)(2,1)} %bitcast.126, ...), custom_call_target="tpu_custom_call" | custom-call | bytes 314572800 | tf_op jit(solution)/shard_map/pallas_call | solution.py:1047
  521.4 7.8 collective-permute-start.6
  530.4 6.4 convolution_convert_fusion.5
  539.2 6.3 collective-permute-start.10
  553.6 5.6 collective-permute-start.8
  560.6 29.1 %shard_map.225.projected_from = bf16[1024,1728]{1,0:T(8,128)(2,1)} custom-call(s32[1]{0:T(128)} %dynamic_slice.71.length_ref, bf16[1024,576]{1,0:T(8,128)(2,1)} %convolution_convert_fusion.6.grad_context, bf16[9,1024,64]{2,1,0:T(8,128)(2,1)} %copy-done.19, bf16[9,1024,64]{2,1,0:T(8,128)(2,1)} %get-tuple-element.67.k_heads, ...), custom_call_target="tpu_custom_call" | custom-call | flops 6039797760 | bytes 20971520 | tf_op jit(solution)/shard_map/pallas_call | solution.py:186
  592.6 8.8 %collective-permute-done.8 = bf16[576,720]{1,0:T(8,128)(2,1)} collective-permute-done((bf16[576,720]{1,0:T(8,128)(2,1)}, bf16[576,720]{1,0:T(8,128)(2,1)}, u32[]{:S(2)}, u32[]{:S(2)}) %collective-permute-start.8) | collective-permute-done | bytes 829472 | tf_op jit(solution)/shard_map/ppermute | solution.py:1607
  613.3 11.2 %convolution_convert_fusion = bf16[2304,1728]{1,0:T(8,128)(2,1)} fusion(bf16[1024,2304]{1,0:T(8,128)(2,1)S(1)} %bitcast.116, bf16[1024,1728]{1,0:T(8,128)(2,1)S(1)} %copy-done.26), kind=kOutput, calls=%fused_computation.1 | convolution fusion | flops 8157708288 | bytes 16220160 | tf_op jit(solution)/shard_map/dot_general | solution.py:1452
  624.4 134.5 %shard_map.226 = (f32[288,1728]{1,0:T(8,128)}, f32[288,576]{1,0:T(8,128)}, bf16[2,128,2304]{2,1,0:T(8,128)(2,1)}, f32[2,2304]{1,0:T(2,128)}) custom-call(bf16[1024,1728]{1,0:T(8,128)(2,1)} %shard_map.225.projected_from, bf16[2304,1728]{1,0:T(8,128)(2,1)} %bitcast.124, bf16[4,2,288,1728]{3,2,1,0:T(8,128)(2,1)} %bitcast.125, ...), custom_call_target="tpu_custom_call" | custom-call | bytes 314572800 | tf_op jit(solution)/shard_map/pallas_call | solution.py:1393
  (162 shorter events, 88.8 us)
Async XLA Ops:
  7.2 328.9 %all-gather.3.cloned.1.call-start = ((), (), s32[]{:S(2)}) async-start(), calls=%async_computation.2 | async-start | bytes 10616832 | tf_op jit(solution)/shard_map/all_gather | solution.py:1532
  19.8 150.3 %copy-start.43 = (s32[2]{0:T(128)S(1)}, s32[2]{0:T(128)}, u32[]{:S(2)}) copy-start(s32[2]{0:T(128)} %param.15) | copy-start | bytes 28
  162.1 66.2 %copy-start = (bf16[2,128,2304]{2,1,0:T(8,128)(2,1)}, bf16[2,128,2304]{2,1,0:T(8,128)(2,1)S(1)}, u32[]{:S(2)}) copy-start(bf16[2,128,2304]{2,1,0:T(8,128)(2,1)S(1)} %get-tuple-element.53) | copy-start | bytes 3538948
  162.2 608.2 %reduce-scatter.2.cloned.1.call-start = ((), (), s32[]{:S(2)}) async-start(), calls=%async_computation.1 | async-start | bytes 10616832 | tf_op jit(solution)/shard_map/reduce_scatter | solution.py:1636
  162.2 48.0 %collective-permute-start = (bf16[4,288,576]{2,1,0:T(8,128)(2,1)}, bf16[4,288,576]{2,1,0:T(8,128)(2,1)}, u32[]{:S(2)}, u32[]{:S(2)}) collective-permute-start(bf16[4,288,576]{2,1,0:T(8,128)(2,1)} %copy-done.11), channel_id=1, source_target_pairs={{0,4},{4,0},{1,5},{5,1},{2,6},{6,2},{3,7},{7,3},{8,12},{12,8},{9,1... | collective-permute-start | bytes 3981320 | tf_op jit(solution)/shard_map/ppermute | solution.py:1468
  163.8 58.9 %collective-permute-start.1 = (bf16[2,3,288,720]{3,2,1,0:T(8,128)(2,1)}, bf16[2,3,288,720]{3,2,1,0:T(8,128)(2,1)}, u32[]{:S(2)}, u32[]{:S(2)}) collective-permute-start(bf16[2,3,288,720]{3,2,1,0:T(8,128)(2,1)} %copy-done.1), channel_id=1, source_target_pairs={{0,8},{8,16},{16,24},{1,9},{9,17},{17,25},{2,10},{10,18},{18,26},{... | collective-permute-start | bytes 7464968 | tf_op jit(solution)/shard_map/ppermute | solution.py:1539
  168.8 59.5 %collective-permute-start.2 = (bf16[2,3,288,720]{3,2,1,0:T(8,128)(2,1)}, bf16[2,3,288,720]{3,2,1,0:T(8,128)(2,1)}, u32[]{:S(2)}, u32[]{:S(2)}) collective-permute-start(bf16[2,3,288,720]{3,2,1,0:T(8,128)(2,1)} %copy-done.3), channel_id=1, source_target_pairs={{8,0},{16,8},{24,16},{9,1},{17,9},{25,17},{10,2},{18,10},{26,18},{... | collective-permute-start | bytes 7464968 | tf_op jit(solution)/shard_map/ppermute | solution.py:1540
  171.4 56.9 %copy-start.14 = (f32[1,2304]{1,0:T(1,128)}, f32[1,2304]{1,0:T(1,128)S(1)}, u32[]{:S(2)}) copy-start(f32[1,2304]{1,0:T(1,128)S(1)} %reshape.153.gain) | copy-start | bytes 27652
  186.9 23.3 %copy-start.12 = (bf16[4,288,576]{2,1,0:T(8,128)(2,1)S(1)}, bf16[4,288,576]{2,1,0:T(8,128)(2,1)}, u32[]{:S(2)}) copy-start(bf16[4,288,576]{2,1,0:T(8,128)(2,1)} %copy-done.11) | copy-start | bytes 3981316
  364.2 23.7 %copy-start.28 = (bf16[2048,720]{1,0:T(8,128)(2,1)}, bf16[2048,720]{1,0:T(8,128)(2,1)S(1)}, u32[]{:S(2)}) copy-start(bf16[2048,720]{1,0:T(8,128)(2,1)S(1)} %get-tuple-element.87.hidden) | copy-start | bytes 8847364
  364.2 23.7 %slice-start.2 = ((s8[9437184]{0:T(1024)(128)(4,1)}), s8[4194304]{0:T(1024)(128)(4,1)S(1)}, s32[]{:S(2)}) async-start(s8[9437184]{0:T(1024)(128)(4,1)} %bitcast.148), calls=%async_computation.5 | async-start | bytes 8388608
  364.2 23.6 %slice-start.3 = ((s8[9437184]{0:T(1024)(128)(4,1)}), s8[4194304]{0:T(1024)(128)(4,1)S(1)}, s32[]{:S(2)}) async-start(s8[9437184]{0:T(1024)(128)(4,1)} %bitcast.148), calls=%async_computation.6 | async-start | bytes 8388608
  396.0 31.2 %copy-start.23 = (bf16[2304,720]{1,0:T(8,128)(2,1)}, bf16[2304,720]{1,0:T(8,128)(2,1)S(1)}, u32[]{:S(2)}) copy-start(bf16[2304,720]{1,0:T(8,128)(2,1)S(1)} %multiply_convert_fusion) | copy-start | bytes 9953284
  396.1 31.0 %collective-permute-start.4 = (bf16[576,720]{1,0:T(8,128)(2,1)S(1)}, bf16[576,720]{1,0:T(8,128)(2,1)S(1)}, u32[]{:S(2)}, u32[]{:S(2)}) collective-permute-start(bf16[576,720]{1,0:T(8,128)(2,1)S(1)} %get-tuple-element.96), channel_id=1, source_target_pairs={{24,16},{25,17},{26,18},{27,19},{28,20},{29,21},{30,22},{31,23}} | collective-permute-start | bytes 2488328 | tf_op jit(solution)/shard_map/ppermute | solution.py:1580
  397.0 30.2 %collective-permute-start.3 = (bf16[576,720]{1,0:T(8,128)(2,1)S(1)}, bf16[576,720]{1,0:T(8,128)(2,1)S(1)}, u32[]{:S(2)}, u32[]{:S(2)}) collective-permute-start(bf16[576,720]{1,0:T(8,128)(2,1)S(1)} %get-tuple-element.97), channel_id=1, source_target_pairs={{0,8},{1,9},{2,10},{3,11},{4,12},{5,13},{6,14},{7,15}} | collective-permute-start | bytes 2488328 | tf_op jit(solution)/shard_map/ppermute | solution.py:1579
  521.4 30.5 %collective-permute-start.6 = (bf16[576,720]{1,0:T(8,128)(2,1)}, bf16[576,720]{1,0:T(8,128)(2,1)S(1)}, u32[]{:S(2)}, u32[]{:S(2)}) collective-permute-start(bf16[576,720]{1,0:T(8,128)(2,1)} %get-tuple-element.70), channel_id=1, source_target_pairs={{0,8},{8,16},{1,9},{9,17},{2,10},{10,18},{3,11},{11,19},{4,12},{12... | collective-permute-start | bytes 2488328 | tf_op jit(solution)/shard_map/ppermute | solution.py:1579
  529.2 22.8 %collective-permute-start.7 = (bf16[576,720]{1,0:T(8,128)(2,1)}, bf16[576,720]{1,0:T(8,128)(2,1)S(1)}, u32[]{:S(2)}, u32[]{:S(2)}) collective-permute-start(bf16[576,720]{1,0:T(8,128)(2,1)} %get-tuple-element.71), channel_id=1, source_target_pairs={{16,8},{24,16},{17,9},{25,17},{18,10},{26,18},{19,11},{27,19},{20,... | collective-permute-start | bytes 2488328 | tf_op jit(solution)/shard_map/ppermute | solution.py:1580
  538.0 51.7 %collective-permute-start.5 = (bf16[4,288,576]{2,1,0:T(8,128)(2,1)}, bf16[4,288,576]{2,1,0:T(8,128)(2,1)}, u32[]{:S(2)}, u32[]{:S(2)}) collective-permute-start(bf16[4,288,576]{2,1,0:T(8,128)(2,1)} %dynamic-slice_bitcast_fusion), channel_id=1, source_target_pairs={{0,4},{4,0},{1,5},{5,1},{2,6},{6,2},{3,7},{7,3},{8,12},{12,8},{9,1... | collective-permute-start | bytes 3981320 | tf_op jit(solution)/shard_map/ppermute | solution.py:1468
  539.2 64.1 %collective-permute-start.10 = (bf16[2,576,720]{2,1,0:T(8,128)(2,1)}, bf16[2,576,720]{2,1,0:T(8,128)(2,1)S(1)}, u32[]{:S(2)}, u32[]{:S(2)}) collective-permute-start(bf16[2,576,720]{2,1,0:T(8,128)(2,1)} %get-tuple-element.83), channel_id=1, source_target_pairs={{0,8},{8,16},{16,24},{1,9},{9,17},{17,25},{2,10},{10,18},{18,26},{... | collective-permute-start | bytes 4976648 | tf_op jit(solution)/shard_map/ppermute | solution.py:1607
  545.5 59.0 %collective-permute-start.11 = (bf16[2,576,720]{2,1,0:T(8,128)(2,1)}, bf16[2,576,720]{2,1,0:T(8,128)(2,1)}, u32[]{:S(2)}, u32[]{:S(2)}) collective-permute-start(bf16[2,576,720]{2,1,0:T(8,128)(2,1)} %get-tuple-element.84), channel_id=1, source_target_pairs={{8,0},{16,8},{24,16},{9,1},{17,9},{25,17},{10,2},{18,10},{26,18},{... | collective-permute-start | bytes 4976648 | tf_op jit(solution)/shard_map/ppermute | solution.py:1609
  553.6 47.8 %collective-permute-start.8 = (bf16[576,720]{1,0:T(8,128)(2,1)}, bf16[576,720]{1,0:T(8,128)(2,1)}, u32[]{:S(2)}, u32[]{:S(2)}) collective-permute-start(bf16[576,720]{1,0:T(8,128)(2,1)} %get-tuple-element.74), channel_id=1, source_target_pairs={{0,8},{8,16},{16,24},{1,9},{9,17},{17,25},{2,10},{10,18},{18,26},{... | collective-permute-start | bytes 2488328 | tf_op jit(solution)/shard_map/ppermute | solution.py:1607
  559.2 44.1 %collective-permute-start.9 = (bf16[576,720]{1,0:T(8,128)(2,1)}, bf16[576,720]{1,0:T(8,128)(2,1)}, u32[]{:S(2)}, u32[]{:S(2)}) collective-permute-start(bf16[576,720]{1,0:T(8,128)(2,1)} %get-tuple-element.75), channel_id=1, source_target_pairs={{8,0},{16,8},{24,16},{9,1},{17,9},{25,17},{10,2},{18,10},{26,18},{... | collective-permute-start | bytes 2488328 | tf_op jit(solution)/shard_map/ppermute | solution.py:1609
  560.6 29.1 %copy-start.30 = (bf16[2304,576]{1,0:T(8,128)(2,1)S(1)}, bf16[2304,576]{1,0:T(8,128)(2,1)}, u32[]{:S(2)}) copy-start(bf16[2304,576]{1,0:T(8,128)(2,1)} %copy-done.29) | copy-start | bytes 7962628
  611.8 151.7 %collective-permute-start.12 = (bf16[3,288,720]{2,1,0:T(8,128)(2,1)}, bf16[3,288,720]{2,1,0:T(8,128)(2,1)}, u32[]{:S(2)}, u32[]{:S(2)}) collective-permute-start(bf16[3,288,720]{2,1,0:T(8,128)(2,1)} %pad_maximum_fusion), channel_id=1, source_target_pairs={{0,4},{4,0},{1,5},{5,1},{2,6},{6,2},{3,7},{7,3},{8,12},{12,8},{9,1... | collective-permute-start | bytes 3732488 | tf_op jit(solution)/shard_map/ppermute | solution.py:1468
  (41 other events, 269.5 us)
Sparse Core Ops, SparseCore 0:
  162.3 72.8 all-gather.2
  521.5 111.8 reduce-scatter.1

commit v9 on v8

--- a/solution.py
+++ b/solution.py
@@ -1617,16 +1617,15 @@
             total = total + low[which].astype(F32) + high[which].astype(F32)
         return total.reshape(sets, share, hidden_width)
 
-    shares = [
-        own_share(which, gradient)
-        for which, gradient in enumerate((gate_blocks, up_blocks, down_blocks))
-    ]
-    others = swap(jnp.stack([pick(total, 1 - c).astype(BF) for total in shares]))
-    grad_gate, grad_up, grad_down = (
-        in_order(c, pick(total, c), others[which].astype(F32), 1)
-        for which, total in enumerate(shares)
-    )
-    grad_down = grad_down.T
+    def halved(total):
+        return pick(total, c), pick(total, 1 - c).astype(BF)
+
+    gate_kept, gate_given = halved(own_share(0, gate_blocks))
+    up_kept, up_given = halved(own_share(1, up_blocks))
+    pair_given = jnp.stack([gate_given, up_given])
+    pair_got = swap(pair_given).astype(F32)
+    grad_gate = in_order(c, gate_kept, pair_got[0], 1)
+    grad_up = in_order(c, up_kept, pair_got[1], 1)
 
     out_pieces = row_major(rows_inner(grad_attention, context).astype(BF))
     out_pieces = out_pieces.reshape(count, sets, share, heads_width)
@@ -1640,8 +1639,13 @@
         blocks, head_count, length, grad_context, q_heads, k_heads, v_heads, level,
         cosine_table, sine_table,
     )
-    grad_projected = after(grad_projected, out_other, low[2], high[2])
+    grad_projected = after(grad_projected, out_other, pair_given)
     grad_qkv = row_major(rows_inner(normed_one, grad_projected).astype(BF))
+    if count > 1:
+        low[2], high[2] = after((low[2], high[2]), grad_qkv)
+    down_kept, down_given = halved(own_share(2, down_blocks))
+    grad_qkv, down_given = lax.optimization_barrier((grad_qkv, down_given))
+    grad_down = in_order(c, down_kept, swap(down_given).astype(F32), 1).T
     grad_qkv, grad_out, grad_tokens, gain_sums = last_sum(
         count, grad_projected, full_qkv, grad_qkv.reshape(count, sets, share, 3 * heads_width), out_pieces,
         token_rows, grad_middle, gain_one[None], gain_two_rows,

time: 789 us -> 777 us (0.985)
  waiting for transfers between devices: 25.3 us -> 14.4 us
    ppermute x1, waiting for transfers between devices: 8.84 us -> 0.01 us  [on_device(): lax.ppermute(leaving_up, 'fsdp', up_hop)]
    unnamed x102 -> x98, local copies, waits for them, and re-layouts: 18 us -> 16.8 us
  transfers between devices with their start and end apart: 15 -> 16, of which waited for: 5 -> 3; matrix products, arithmetic and copies ran while one was open for 14% -> 14% of each run, Pallas kernels for 35% -> 36%
where the time goes in v9:
time: 777 us; the launch traced here: 765 us
  Pallas kernels  501 us (64%)
  matrix products  143 us (18%)
  starting transfers between devices  35.8 us (5%)
  local copies, waits for them, and re-layouts  29.3 us (4%)
  other arithmetic  27.3 us (4%)
  between operations  14.9 us (2%)
  waiting for transfers between devices  14.4 us (2%)
    pallas_call x1, Pallas kernels, first_gather(): pl.pallas_call(functools.partial(first_gather_kernel, count), out_shape=(...  136 us
    pallas_call x1, Pallas kernels, last_sum(): pl.pallas_call(functools.partial(last_sum_kernel, count), out_shape=(jax....  133 us
    pallas_call x1, Pallas kernels, first_sum(): pl.pallas_call(functools.partial(first_sum_kernel, count), out_shape=(jax...  92.5 us
    pallas_call x1, Pallas kernels, second_gather(): pl.pallas_call(functools.partial(second_gather_kernel, count), out_shape=...  92 us
    dot_general x5, matrix products, matmul(): return jnp.dot(left, right, preferred_element_type=F32)  61.3 us
    dot_general x5, matrix products, rows_inner(): lax.dot_general(left, right, (((0,), (0,)), ((), ())), preferred_element_...  52.4 us
    pallas_call x1, Pallas kernels, attention_back(): pl.pallas_call(functools.partial(attention_back_kernel, blocks), out_shap...  29.7 us
    dot_general x3, matrix products, cols_inner(): lax.dot_general(left, right, (((1,), (1,)), ((), ())), preferred_element_...  28.7 us
  transfers between devices with their start and end apart: 16, of which 3 were waited for; matrix products, arithmetic and copies ran while one was open for 14% of the time, Pallas kernels for 36%

profile of v9, /device:TPU:0, one launch (start us, length us, event | category | flops | bytes accessed | tf_op | source)
XLA Modules:
  0.0 765.4 jit_solution(4792423102466664880)
XLA Ops:
  19.8 136.0 %shard_map.221 = (bf16[2,128,2304]{2,1,0:T(8,128)(2,1)S(1)}, bf16[4,2,128,2304]{3,2,1,0:T(8,128)(2,1)S(1)}, bf16[4,2,288,1728]{3,2,1,0:T(8,128)(2,1)}, bf16[4,28...) custom-call(bf16[128,2304]{1,0:T(8,128)(2,1)S(1)} %get-tuple-element.112.tokens, ...), custom_call_target="tpu_custom_call" | custom-call | bytes 314572800 | tf_op jit(solution)/shard_map/pallas_call | solution.py:489
  163.8 5.0 collective-permute-start.1
  171.4 15.6 %fusion.9.projected = f32[1024,1728]{1,0:T(8,128)} fusion(bf16[1024,2304]{1,0:T(8,128)(2,1)} %bitcast.104, bf16[2304,1728]{1,0:T(8,128)(2,1)} %bitcast.114), kind=kOutput, calls=%fused_computation.60 | convolution fusion | flops 8153726976 | bytes 19759104 | tf_op jit(solution)/shard_map/dot_general | solution.py:1448
  187.0 18.5 %shard_map.222 = (bf16[1024,576]{1,0:T(8,128)(2,1)S(1)}, bf16[9,1024,64]{2,1,0:T(8,128)(2,1)S(1)}, bf16[9,1024,64]{2,1,0:T(8,128)(2,1)}, bf16[9,1024,64]{2,1,0:T(8,128)(2,1)}, f32[9,1,1024]{2,1,0:T(1,128)S(1)}) custom-call(s32[1]{0:T(128)} %dynamic_slice.71.length_ref, f32[1024,1728]{1,0:T(8,128)} %fusion.9.projected, f32[1024,128]{1,0:T(8,128)S(1)} %copy-done.18, ...), custom_call_target="tpu_custom_call" | custom-call | flops 2415919104 | bytes 20971520 | tf_op jit(solution)/shard_map/pallas_call | solution.py:107
  205.6 4.7 collective-permute-done
  213.1 5.6 convolution_convert_fusion.2
  222.7 5.6 collective-permute-done.2.second_high
  228.3 92.0 %shard_map.223 = (f32[256,2304]{1,0:T(8,128)S(1)}, f32[2,128,2304]{2,1,0:T(8,128)S(1)}, bf16[2,4,2,128,2304]{4,3,2,1,0:T(8,128)(2,1)}, bf16[4,2,288,720]{3,2,1,0...) custom-call(bf16[4,256,2304]{2,1,0:T(8,128)(2,1)} %bitcast.128, ...), custom_call_target="tpu_custom_call" | custom-call | bytes 314572800 | tf_op jit(solution)/shard_map/pallas_call | solution.py:683
  323.2 12.9 %fusion.11 = f32[2048,720]{1,0:T(8,128)} fusion(bf16[2048,2304]{1,0:T(8,128)(2,1)} %bitcast.142, bf16[2304,720]{1,0:T(8,128)(2,1)} %bitcast.150), kind=kOutput, calls=%fused_computation.62 | convolution fusion | flops 6794772480 | bytes 18653184 | tf_op jit(solution)/shard_map/dot_general | solution.py:1448
  336.1 11.8 %fusion.10 = f32[2048,720]{1,0:T(8,128)} fusion(bf16[2048,2304]{1,0:T(8,128)(2,1)} %bitcast.137, bf16[2304,720]{1,0:T(8,128)(2,1)S(1)} %bitcast.130), kind=kOutput, calls=%fused_computation.61 | convolution fusion | flops 6794772480 | bytes 18653184 | tf_op jit(solution)/shard_map/dot_general | solution.py:1448
  347.9 16.2 %multiply_convert_fusion.1 = (bf16[2048,720]{1,0:T(8,128)(2,1)S(1)}, bf16[2048,720]{1,0:T(8,128)(2,1)}, bf16[2048,720]{1,0:T(8,128)(2,1)}) fusion(f32[2048,720]{1,0:T(8,128)} %fusion.11, f32[2048,720]{1,0:T(8,128)} %fusion.10, bf16[2048,2304]{1,0:T(8,128)(2,1)S(1)} %bitcast.145, bf16[2304,720]{1,0:T(8,128)(2,1)} %bitcast.148), kind=kOutput, calls=%fused_computation.4 | convolution fusion | flops 6822789120 | bytes 33398784 | tf_op jit(solution)/shard_map/dot_general | solution.py:1448
  364.1 13.8 %convolution_convert_fusion.4 = bf16[2304,720]{1,0:T(8,128)(2,1)} fusion(bf16[2048,2304]{1,0:T(8,128)(2,1)} %bitcast.143, bf16[2048,720]{1,0:T(8,128)(2,1)} %get-tuple-element.96), kind=kOutput, calls=%fused_computation.11 | convolution fusion | flops 6796431360 | bytes 15704064 | tf_op jit(solution)/shard_map/dot_general | solution.py:1452
  377.9 9.8 %convolution_convert_fusion.1 = bf16[2048,2304]{1,0:T(8,128)(2,1)} fusion(bf16[2048,720]{1,0:T(8,128)(2,1)S(1)} %copy-done.42, bf16[2304,720]{1,0:T(8,128)(2,1)S(1)} %bitcast.151), kind=kOutput, calls=%fused_computation.2 | convolution fusion | flops 6799491072 | bytes 15704064 | tf_op jit(solution)/shard_map/dot_general | solution.py:1456
  387.8 8.1 %multiply_convert_fusion = bf16[2304,720]{1,0:T(8,128)(2,1)S(1)} fusion(bf16[2048,2304]{1,0:T(8,128)(2,1)S(1)} %bitcast.141, bf16[2048,720]{1,0:T(8,128)(2,1)S(1)} %get-tuple-element.95.hidden), kind=kOutput, calls=%fused_computation.3 | convolution fusion | flops 6798090240 | bytes 15704064 | tf_op jit(solution)/shard_map/dot_general | solution.py:1452
  399.2 13.3 %add_convert_fusion = bf16[2048,2304]{1,0:T(8,128)(2,1)} fusion(bf16[2048,2304]{1,0:T(8,128)(2,1)} %convolution_convert_fusion.1, bf16[2048,720]{1,0:T(8,128)(2,1)} %get-tuple-element.97, bf16[2304,720]{1,0:T(8,128)(2,1)S(1)} %bitcast.149), kind=kOutput, calls=%fused_computation | convolution fusion | flops 6808928256 | bytes 25141248 | tf_op jit(solution)/shard_map/dot_general | solution.py:1456
  412.5 12.5 %convolution_convert_fusion.3 = bf16[2304,720]{1,0:T(8,128)(2,1)} fusion(bf16[2048,2304]{1,0:T(8,128)(2,1)} %bitcast.144, bf16[2048,720]{1,0:T(8,128)(2,1)} %get-tuple-element.97), kind=kOutput, calls=%fused_computation.10 | convolution fusion | flops 6796431360 | bytes 15704064 | tf_op jit(solution)/shard_map/dot_general | solution.py:1452
  429.0 92.5 %shard_map.224 = (f32[256,2304]{1,0:T(8,128)}, bf16[4,2,128,2304]{3,2,1,0:T(8,128)(2,1)}, f32[1,2304]{1,0:T(1,128)}, bf16[2,576,720]{2,1,0:T(8,128)(2,1)}, bf16[...) custom-call(bf16[2,4,2,128,2304]{4,3,2,1,0:T(8,128)(2,1)} %bitcast.112, bf16[4,576,720]{2,1,0:T(8,128)(2,1)} %bitcast.117, ...), custom_call_target="tpu_custom_call" | custom-call | bytes 314572800 | tf_op jit(solution)/shard_map/pallas_call | solution.py:1047
  521.6 8.7 %collective-permute-start.8 = (bf16[576,720]{1,0:T(8,128)(2,1)}, bf16[576,720]{1,0:T(8,128)(2,1)}, u32[]{:S(2)}, u32[]{:S(2)}) collective-permute-start(bf16[576,720]{1,0:T(8,128)(2,1)} %get-tuple-element.77), channel_id=1, source_target_pairs={{0,8},{8,16},{1,9},{9,17},{2,10},{10,18},{3,11},{11,19},{4,12},{12... | collective-permute-start | bytes 2488328 | tf_op jit(solution)/shard_map/ppermute | solution.py:1579
  531.9 7.1 convolution_convert_fusion.5
  545.7 4.9 convolution_convert_fusion.6.grad_context
  550.6 29.7 %shard_map.225.projected_from = bf16[1024,1728]{1,0:T(8,128)(2,1)} custom-call(s32[1]{0:T(128)} %dynamic_slice.71.length_ref, bf16[1024,576]{1,0:T(8,128)(2,1)} %convolution_convert_fusion.6.grad_context, bf16[9,1024,64]{2,1,0:T(8,128)(2,1)} %copy-done.19, bf16[9,1024,64]{2,1,0:T(8,128)(2,1)} %get-tuple-element.71.k_heads, ...), custom_call_target="tpu_custom_call" | custom-call | flops 6039797760 | bytes 20971520 | tf_op jit(solution)/shard_map/pallas_call | solution.py:186
  582.3 5.0 collective-permute-start.10
  595.8 11.0 %convolution_convert_fusion = bf16[2304,1728]{1,0:T(8,128)(2,1)} fusion(bf16[1024,2304]{1,0:T(8,128)(2,1)S(1)} %bitcast.107, bf16[1024,1728]{1,0:T(8,128)(2,1)S(1)} %copy-done.25), kind=kOutput, calls=%fused_computation.1 | convolution fusion | flops 8157708288 | bytes 16220160 | tf_op jit(solution)/shard_map/dot_general | solution.py:1452
  609.4 132.6 %shard_map.226 = (f32[288,1728]{1,0:T(8,128)}, f32[288,576]{1,0:T(8,128)}, bf16[2,128,2304]{2,1,0:T(8,128)(2,1)}, f32[2,2304]{1,0:T(2,128)}) custom-call(bf16[1024,1728]{1,0:T(8,128)(2,1)} %shard_map.225.projected_from, bf16[2304,1728]{1,0:T(8,128)(2,1)} %bitcast.115, bf16[4,2,288,1728]{3,2,1,0:T(8,128)(2,1)} %bitcast.116, ...), custom_call_target="tpu_custom_call" | custom-call | bytes 314572800 | tf_op jit(solution)/shard_map/pallas_call | solution.py:1393
  (162 shorter events, 77.6 us)
Async XLA Ops:
  7.2 328.9 %all-gather.3.cloned.1.call-start = ((), (), s32[]{:S(2)}) async-start(), calls=%async_computation.2 | async-start | bytes 10616832 | tf_op jit(solution)/shard_map/all_gather | solution.py:1532
  19.8 150.3 %copy-start.41 = (s32[2]{0:T(128)S(1)}, s32[2]{0:T(128)}, u32[]{:S(2)}) copy-start(s32[2]{0:T(128)} %param.15) | copy-start | bytes 28
  162.1 66.2 %copy-start = (bf16[2,128,2304]{2,1,0:T(8,128)(2,1)}, bf16[2,128,2304]{2,1,0:T(8,128)(2,1)S(1)}, u32[]{:S(2)}) copy-start(bf16[2,128,2304]{2,1,0:T(8,128)(2,1)S(1)} %get-tuple-element.57) | copy-start | bytes 3538948
  162.2 591.5 %reduce-scatter.2.cloned.1.call-start = ((), (), s32[]{:S(2)}) async-start(), calls=%async_computation.1 | async-start | bytes 10616832 | tf_op jit(solution)/shard_map/reduce_scatter | solution.py:1635
  162.2 48.0 %collective-permute-start = (bf16[4,288,576]{2,1,0:T(8,128)(2,1)}, bf16[4,288,576]{2,1,0:T(8,128)(2,1)}, u32[]{:S(2)}, u32[]{:S(2)}) collective-permute-start(bf16[4,288,576]{2,1,0:T(8,128)(2,1)} %copy-done.11), channel_id=1, source_target_pairs={{0,4},{4,0},{1,5},{5,1},{2,6},{6,2},{3,7},{7,3},{8,12},{12,8},{9,1... | collective-permute-start | bytes 3981320 | tf_op jit(solution)/shard_map/ppermute | solution.py:1468
  163.8 58.9 %collective-permute-start.1 = (bf16[2,3,288,720]{3,2,1,0:T(8,128)(2,1)}, bf16[2,3,288,720]{3,2,1,0:T(8,128)(2,1)}, u32[]{:S(2)}, u32[]{:S(2)}) collective-permute-start(bf16[2,3,288,720]{3,2,1,0:T(8,128)(2,1)} %copy-done.1), channel_id=1, source_target_pairs={{0,8},{8,16},{16,24},{1,9},{9,17},{17,25},{2,10},{10,18},{18,26},{... | collective-permute-start | bytes 7464968 | tf_op jit(solution)/shard_map/ppermute | solution.py:1539
  168.8 59.5 %collective-permute-start.2 = (bf16[2,3,288,720]{3,2,1,0:T(8,128)(2,1)}, bf16[2,3,288,720]{3,2,1,0:T(8,128)(2,1)}, u32[]{:S(2)}, u32[]{:S(2)}) collective-permute-start(bf16[2,3,288,720]{3,2,1,0:T(8,128)(2,1)} %copy-done.3), channel_id=1, source_target_pairs={{8,0},{16,8},{24,16},{9,1},{17,9},{25,17},{10,2},{18,10},{26,18},{... | collective-permute-start | bytes 7464968 | tf_op jit(solution)/shard_map/ppermute | solution.py:1540
  171.4 56.9 %copy-start.14 = (f32[1,2304]{1,0:T(1,128)}, f32[1,2304]{1,0:T(1,128)S(1)}, u32[]{:S(2)}) copy-start(f32[1,2304]{1,0:T(1,128)S(1)} %reshape.148.gain) | copy-start | bytes 27652
  364.1 23.7 %copy-start.27 = (bf16[2048,720]{1,0:T(8,128)(2,1)}, bf16[2048,720]{1,0:T(8,128)(2,1)S(1)}, u32[]{:S(2)}) copy-start(bf16[2048,720]{1,0:T(8,128)(2,1)S(1)} %get-tuple-element.95.hidden) | copy-start | bytes 8847364
  364.1 23.6 %slice-start.2 = ((s8[9437184]{0:T(1024)(128)(4,1)}), s8[4194304]{0:T(1024)(128)(4,1)S(1)}, s32[]{:S(2)}) async-start(s8[9437184]{0:T(1024)(128)(4,1)} %bitcast.139), calls=%async_computation.5 | async-start | bytes 8388608
  364.1 23.6 %slice-start.3 = ((s8[9437184]{0:T(1024)(128)(4,1)}), s8[4194304]{0:T(1024)(128)(4,1)S(1)}, s32[]{:S(2)}) async-start(s8[9437184]{0:T(1024)(128)(4,1)} %bitcast.139), calls=%async_computation.6 | async-start | bytes 8388608
  395.9 31.4 %copy-start.23 = (bf16[2304,720]{1,0:T(8,128)(2,1)}, bf16[2304,720]{1,0:T(8,128)(2,1)S(1)}, u32[]{:S(2)}) copy-start(bf16[2304,720]{1,0:T(8,128)(2,1)S(1)} %multiply_convert_fusion) | copy-start | bytes 9953284
  396.0 31.3 %collective-permute-start.4 = (bf16[576,720]{1,0:T(8,128)(2,1)S(1)}, bf16[576,720]{1,0:T(8,128)(2,1)S(1)}, u32[]{:S(2)}, u32[]{:S(2)}) collective-permute-start(bf16[576,720]{1,0:T(8,128)(2,1)S(1)} %get-tuple-element.104), channel_id=1, source_target_pairs={{24,16},{25,17},{26,18},{27,19},{28,20},{29,21},{30,22},{31,23}} | collective-permute-start | bytes 2488328 | tf_op jit(solution)/shard_map/ppermute | solution.py:1580
  396.9 30.4 %collective-permute-start.3 = (bf16[576,720]{1,0:T(8,128)(2,1)S(1)}, bf16[576,720]{1,0:T(8,128)(2,1)S(1)}, u32[]{:S(2)}, u32[]{:S(2)}) collective-permute-start(bf16[576,720]{1,0:T(8,128)(2,1)S(1)} %get-tuple-element.105), channel_id=1, source_target_pairs={{0,8},{1,9},{2,10},{3,11},{4,12},{5,13},{6,14},{7,15}} | collective-permute-start | bytes 2488328 | tf_op jit(solution)/shard_map/ppermute | solution.py:1579
  521.6 58.6 %collective-permute-start.8 = (bf16[576,720]{1,0:T(8,128)(2,1)}, bf16[576,720]{1,0:T(8,128)(2,1)}, u32[]{:S(2)}, u32[]{:S(2)}) collective-permute-start(bf16[576,720]{1,0:T(8,128)(2,1)} %get-tuple-element.77), channel_id=1, source_target_pairs={{0,8},{8,16},{1,9},{9,17},{2,10},{10,18},{3,11},{11,19},{4,12},{12... | collective-permute-start | bytes 2488328 | tf_op jit(solution)/shard_map/ppermute | solution.py:1579
  530.3 49.9 %collective-permute-start.9 = (bf16[576,720]{1,0:T(8,128)(2,1)}, bf16[576,720]{1,0:T(8,128)(2,1)}, u32[]{:S(2)}, u32[]{:S(2)}) collective-permute-start(bf16[576,720]{1,0:T(8,128)(2,1)} %get-tuple-element.78), channel_id=1, source_target_pairs={{16,8},{24,16},{17,9},{25,17},{18,10},{26,18},{19,11},{27,19},{20,... | collective-permute-start | bytes 2488328 | tf_op jit(solution)/shard_map/ppermute | solution.py:1580
  539.2 49.4 %collective-permute-start.5 = (bf16[4,288,576]{2,1,0:T(8,128)(2,1)S(1)}, bf16[4,288,576]{2,1,0:T(8,128)(2,1)S(1)}, u32[]{:S(2)}, u32[]{:S(2)}) collective-permute-start(bf16[4,288,576]{2,1,0:T(8,128)(2,1)S(1)} %dynamic-slice_bitcast_fusion), channel_id=1, source_target_pairs={{0,4},{4,0},{1,5},{5,1},{2,6},{6,2},{3,7},{7,3},{8,12},{12,8},{9,1... | collective-permute-start | bytes 3981320 | tf_op jit(solution)/shard_map/ppermute | solution.py:1468
  540.3 49.8 %collective-permute-start.6 = (bf16[2,576,720]{2,1,0:T(8,128)(2,1)}, bf16[2,576,720]{2,1,0:T(8,128)(2,1)S(1)}, u32[]{:S(2)}, u32[]{:S(2)}) collective-permute-start(bf16[2,576,720]{2,1,0:T(8,128)(2,1)} %get-tuple-element.74), channel_id=1, source_target_pairs={{0,8},{8,16},{16,24},{1,9},{9,17},{17,25},{2,10},{10,18},{18,26},{... | collective-permute-start | bytes 4976648 | tf_op jit(solution)/shard_map/ppermute | solution.py:1607
  544.2 47.1 %collective-permute-start.7 = (bf16[2,576,720]{2,1,0:T(8,128)(2,1)}, bf16[2,576,720]{2,1,0:T(8,128)(2,1)}, u32[]{:S(2)}, u32[]{:S(2)}) collective-permute-start(bf16[2,576,720]{2,1,0:T(8,128)(2,1)} %get-tuple-element.75), channel_id=1, source_target_pairs={{8,0},{16,8},{24,16},{9,1},{17,9},{25,17},{10,2},{18,10},{26,18},{... | collective-permute-start | bytes 4976648 | tf_op jit(solution)/shard_map/ppermute | solution.py:1609
  550.6 29.7 %copy-start.24 = (bf16[2304,720]{1,0:T(8,128)(2,1)S(1)}, bf16[2304,720]{1,0:T(8,128)(2,1)}, u32[]{:S(2)}) copy-start(bf16[2304,720]{1,0:T(8,128)(2,1)} %copy-done.23) | copy-start | bytes 9953284
  582.3 24.5 %collective-permute-start.10 = (bf16[576,720]{1,0:T(8,128)(2,1)S(1)}, bf16[576,720]{1,0:T(8,128)(2,1)S(1)}, u32[]{:S(2)}, u32[]{:S(2)}) collective-permute-start(bf16[576,720]{1,0:T(8,128)(2,1)S(1)} %get-tuple-element.81), channel_id=1, source_target_pairs={{0,8},{8,16},{16,24},{1,9},{9,17},{17,25},{2,10},{10,18},{18,26},{... | collective-permute-start | bytes 2488328 | tf_op jit(solution)/shard_map/ppermute | solution.py:1607
  587.3 19.5 %collective-permute-start.11 = (bf16[576,720]{1,0:T(8,128)(2,1)S(1)}, bf16[576,720]{1,0:T(8,128)(2,1)S(1)}, u32[]{:S(2)}, u32[]{:S(2)}) collective-permute-start(bf16[576,720]{1,0:T(8,128)(2,1)S(1)} %get-tuple-element.82), channel_id=1, source_target_pairs={{8,0},{16,8},{24,16},{9,1},{17,9},{25,17},{10,2},{18,10},{26,18},{... | collective-permute-start | bytes 2488328 | tf_op jit(solution)/shard_map/ppermute | solution.py:1609
  595.7 152.9 %collective-permute-start.12 = (bf16[2,288,720]{2,1,0:T(8,128)(2,1)}, bf16[2,288,720]{2,1,0:T(8,128)(2,1)}, u32[]{:S(2)}, u32[]{:S(2)}) collective-permute-start(bf16[2,288,720]{2,1,0:T(8,128)(2,1)} %pad_maximum_fusion), channel_id=1, source_target_pairs={{0,4},{4,0},{1,5},{5,1},{2,6},{6,2},{3,7},{7,3},{8,12},{12,8},{9,1... | collective-permute-start | bytes 2488328 | tf_op jit(solution)/shard_map/ppermute | solution.py:1468
  607.2 139.5 %collective-permute-start.13 = (bf16[288,720]{1,0:T(8,128)(2,1)S(1)}, bf16[288,720]{1,0:T(8,128)(2,1)S(1)}, u32[]{:S(2)}, u32[]{:S(2)}) collective-permute-start(bf16[288,720]{1,0:T(8,128)(2,1)S(1)} %fusion.7), channel_id=1, source_target_pairs={{0,4},{4,0},{1,5},{5,1},{2,6},{6,2},{3,7},{7,3},{8,12},{12,8},{9,1... | collective-permute-start | bytes 1244168 | tf_op jit(solution)/shard_map/ppermute | solution.py:1468
  (40 other events, 293.4 us)
Sparse Core Ops, SparseCore 0:
  162.3 72.8 all-gather.2
  521.7 113.2 reduce-scatter.1

commit v10 on v9

--- a/solution.py
+++ b/solution.py
@@ -512,7 +512,7 @@
         ],
         cost_estimate=COST,
         compiler_params=pltpu.CompilerParams(
-            collective_id=1, has_side_effects=True, vmem_limit_bytes=32 << 20
+            collective_id=1, has_side_effects=True, vmem_limit_bytes=60 << 20
         ),
     )(tokens, tokens_away, gain, qkv, turned_out, *wide, *wide_away)
 
@@ -706,7 +706,7 @@
         ],
         cost_estimate=COST,
         compiler_params=pltpu.CompilerParams(
-            collective_id=2, has_side_effects=True, vmem_limit_bytes=40 << 20
+            collective_id=2, has_side_effects=True, vmem_limit_bytes=60 << 20
         ),
     )(part, tokens, gain, *wide, first_low, first_high, second_low, second_high)
 

time: 777 us -> 765 us (0.985)
  local copies, waits for them, and re-layouts: 29.3 us -> 17.2 us
  Pallas kernels: 501 us -> 509 us
    unnamed x98 -> x68, local copies, waits for them, and re-layouts: 16.8 us -> 2.44 us
  transfers between devices with their start and end apart: 16 -> 16, of which waited for: 3 -> 4; matrix products, arithmetic and copies ran while one was open for 14% -> 15% of each run, Pallas kernels for 36% -> 37%
where the time goes in v10:
time: 765 us; the launch traced here: 759 us
  Pallas kernels  509 us (67%)
  matrix products  140 us (18%)
  starting transfers between devices  34.8 us (5%)
  other arithmetic  28 us (4%)
  local copies, waits for them, and re-layouts  17.2 us (2%)
  between operations  14.7 us (2%)
  waiting for transfers between devices  14.5 us (2%)
    pallas_call x1, Pallas kernels, first_gather(): pl.pallas_call(functools.partial(first_gather_kernel, count), out_shape=(...  140 us
    pallas_call x1, Pallas kernels, last_sum(): pl.pallas_call(functools.partial(last_sum_kernel, count), out_shape=(jax....  136 us
    pallas_call x1, Pallas kernels, second_gather(): pl.pallas_call(functools.partial(second_gather_kernel, count), out_shape=...  92.9 us
    pallas_call x1, Pallas kernels, first_sum(): pl.pallas_call(functools.partial(first_sum_kernel, count), out_shape=(jax...  92.5 us
    dot_general x5, matrix products, matmul(): return jnp.dot(left, right, preferred_element_type=F32)  61.2 us
    dot_general x5, matrix products, rows_inner(): lax.dot_general(left, right, (((0,), (0,)), ((), ())), preferred_element_...  50 us
    pallas_call x1, Pallas kernels, attention_back(): pl.pallas_call(functools.partial(attention_back_kernel, blocks), out_shap...  29.7 us
    dot_general x3, matrix products, cols_inner(): lax.dot_general(left, right, (((1,), (1,)), ((), ())), preferred_element_...  28.8 us
  transfers between devices with their start and end apart: 16, of which 4 were waited for; matrix products, arithmetic and copies ran while one was open for 15% of the time, Pallas kernels for 37%

profile of v10, /device:TPU:0, one launch (start us, length us, event | category | flops | bytes accessed | tf_op | source)
XLA Modules:
  0.0 758.6 jit_solution(11518639988016344937)
XLA Ops:
  17.4 139.8 %shard_map.221 = (bf16[2,128,2304]{2,1,0:T(8,128)(2,1)}, bf16[4,2,128,2304]{3,2,1,0:T(8,128)(2,1)}, bf16[4,2,288,1728]{3,2,1,0:T(8,128)(2,1)}, bf16[4,288,576]{2...) custom-call(bf16[128,2304]{1,0:T(8,128)(2,1)} %get-tuple-element.112.tokens, ...), custom_call_target="tpu_custom_call" | custom-call | bytes 314572800 | tf_op jit(solution)/shard_map/pallas_call | solution.py:489
  165.0 15.9 %fusion.9.projected = f32[1024,1728]{1,0:T(8,128)} fusion(bf16[1024,2304]{1,0:T(8,128)(2,1)} %bitcast.140, bf16[2304,1728]{1,0:T(8,128)(2,1)} %bitcast.106), kind=kOutput, calls=%fused_computation.60 | convolution fusion | flops 8153726976 | bytes 19759104 | tf_op jit(solution)/shard_map/dot_general | solution.py:1448
  180.9 18.7 %shard_map.222 = (bf16[1024,576]{1,0:T(8,128)(2,1)S(1)}, bf16[9,1024,64]{2,1,0:T(8,128)(2,1)S(1)}, bf16[9,1024,64]{2,1,0:T(8,128)(2,1)}, bf16[9,1024,64]{2,1,0:T(8,128)(2,1)}, f32[9,1,1024]{2,1,0:T(1,128)S(1)}) custom-call(s32[1]{0:T(128)} %dynamic_slice.71.length_ref, f32[1024,1728]{1,0:T(8,128)} %fusion.9.projected, f32[1024,128]{1,0:T(8,128)S(1)} %copy-done.1, ...), custom_call_target="tpu_custom_call" | custom-call | flops 2415919104 | bytes 20971520 | tf_op jit(solution)/shard_map/pallas_call | solution.py:107
  199.6 5.6 collective-permute-done
  208.2 5.6 convolution_convert_fusion.2
  213.8 3.9 collective-permute-done.1.second_low
  217.7 4.3 collective-permute-done.2.second_high
  222.0 92.9 %shard_map.223 = (f32[256,2304]{1,0:T(8,128)}, f32[2,128,2304]{2,1,0:T(8,128)}, bf16[2,4,2,128,2304]{4,3,2,1,0:T(8,128)(2,1)}, bf16[4,2,288,720]{3,2,1,0:T(8,128...) custom-call(bf16[4,256,2304]{2,1,0:T(8,128)(2,1)} %bitcast.122, bf16[256,2304]{1,0:T(8,128)(2,1)} %bitcast.119, ...), custom_call_target="tpu_custom_call" | custom-call | bytes 314572800 | tf_op jit(solution)/shard_map/pallas_call | solution.py:683
  315.0 12.9 %fusion.11 = f32[2048,720]{1,0:T(8,128)} fusion(bf16[2048,2304]{1,0:T(8,128)(2,1)} %bitcast.136, bf16[2304,720]{1,0:T(8,128)(2,1)} %bitcast.148), kind=kOutput, calls=%fused_computation.62 | convolution fusion | flops 6794772480 | bytes 18653184 | tf_op jit(solution)/shard_map/dot_general | solution.py:1448
  327.9 11.8 %fusion.10 = f32[2048,720]{1,0:T(8,128)} fusion(bf16[2048,2304]{1,0:T(8,128)(2,1)} %bitcast.133, bf16[2304,720]{1,0:T(8,128)(2,1)S(1)} %bitcast.124), kind=kOutput, calls=%fused_computation.61 | convolution fusion | flops 6794772480 | bytes 18653184 | tf_op jit(solution)/shard_map/dot_general | solution.py:1448
  339.7 15.7 %multiply_convert_fusion.1 = (bf16[2048,720]{1,0:T(8,128)(2,1)S(1)}, bf16[2048,720]{1,0:T(8,128)(2,1)S(1)}, bf16[2048,720]{1,0:T(8,128)(2,1)}) fusion(f32[2048,720]{1,0:T(8,128)} %fusion.11, f32[2048,720]{1,0:T(8,128)} %fusion.10, bf16[2048,2304]{1,0:T(8,128)(2,1)S(1)} %bitcast.138, bf16[2304,720]{1,0:T(8,128)(2,1)} %bitcast.146), kind=kOutput, calls=%fused_computation.4 | convolution fusion | flops 6822789120 | bytes 33398784 | tf_op jit(solution)/shard_map/dot_general | solution.py:1448
  355.4 9.5 %convolution_convert_fusion.4 = bf16[2304,720]{1,0:T(8,128)(2,1)} fusion(bf16[2048,2304]{1,0:T(8,128)(2,1)S(1)} %bitcast.139, bf16[2048,720]{1,0:T(8,128)(2,1)S(1)} %get-tuple-element.96), kind=kOutput, calls=%fused_computation.11 | convolution fusion | flops 6796431360 | bytes 15704064 | tf_op jit(solution)/shard_map/dot_general | solution.py:1452
  364.9 9.8 %convolution_convert_fusion.1 = bf16[2048,2304]{1,0:T(8,128)(2,1)} fusion(bf16[2048,720]{1,0:T(8,128)(2,1)S(1)} %get-tuple-element.96, bf16[2304,720]{1,0:T(8,128)(2,1)S(1)} %bitcast.149), kind=kOutput, calls=%fused_computation.2 | convolution fusion | flops 6799491072 | bytes 15704064 | tf_op jit(solution)/shard_map/dot_general | solution.py:1456
  374.7 10.3 %multiply_convert_fusion = bf16[2304,720]{1,0:T(8,128)(2,1)S(1)} fusion(bf16[2048,2304]{1,0:T(8,128)(2,1)} %bitcast.134, bf16[2048,720]{1,0:T(8,128)(2,1)S(1)} %get-tuple-element.95.hidden), kind=kOutput, calls=%fused_computation.3 | convolution fusion | flops 6798090240 | bytes 15704064 | tf_op jit(solution)/shard_map/dot_general | solution.py:1452
  388.3 13.4 %add_convert_fusion = bf16[2048,2304]{1,0:T(8,128)(2,1)} fusion(bf16[2048,2304]{1,0:T(8,128)(2,1)} %convolution_convert_fusion.1, bf16[2048,720]{1,0:T(8,128)(2,1)} %get-tuple-element.97, bf16[2304,720]{1,0:T(8,128)(2,1)S(1)} %bitcast.147), kind=kOutput, calls=%fused_computation | convolution fusion | flops 6808928256 | bytes 25141248 | tf_op jit(solution)/shard_map/dot_general | solution.py:1456
  401.6 12.4 %convolution_convert_fusion.3 = bf16[2304,720]{1,0:T(8,128)(2,1)} fusion(bf16[2048,2304]{1,0:T(8,128)(2,1)} %bitcast.137, bf16[2048,720]{1,0:T(8,128)(2,1)} %get-tuple-element.97), kind=kOutput, calls=%fused_computation.10 | convolution fusion | flops 6796431360 | bytes 15704064 | tf_op jit(solution)/shard_map/dot_general | solution.py:1452
  417.7 92.5 %shard_map.224 = (f32[256,2304]{1,0:T(8,128)}, bf16[4,2,128,2304]{3,2,1,0:T(8,128)(2,1)}, f32[1,2304]{1,0:T(1,128)}, bf16[2,576,720]{2,1,0:T(8,128)(2,1)}, bf16[...) custom-call(bf16[2,4,2,128,2304]{4,3,2,1,0:T(8,128)(2,1)} %bitcast.104, bf16[4,576,720]{2,1,0:T(8,128)(2,1)} %bitcast.109, ...), custom_call_target="tpu_custom_call" | custom-call | bytes 314572800 | tf_op jit(solution)/shard_map/pallas_call | solution.py:1047
  510.3 8.7 %collective-permute-start.8 = (bf16[576,720]{1,0:T(8,128)(2,1)}, bf16[576,720]{1,0:T(8,128)(2,1)}, u32[]{:S(2)}, u32[]{:S(2)}) collective-permute-start(bf16[576,720]{1,0:T(8,128)(2,1)} %get-tuple-element.77), channel_id=1, source_target_pairs={{0,8},{8,16},{1,9},{9,17},{2,10},{10,18},{3,11},{11,19},{4,12},{12... | collective-permute-start | bytes 2488328 | tf_op jit(solution)/shard_map/ppermute | solution.py:1579
  520.5 6.9 convolution_convert_fusion.5
  535.6 4.9 convolution_convert_fusion.6.grad_context
  540.5 29.7 %shard_map.225.projected_from = bf16[1024,1728]{1,0:T(8,128)(2,1)} custom-call(s32[1]{0:T(128)} %dynamic_slice.71.length_ref, bf16[1024,576]{1,0:T(8,128)(2,1)} %convolution_convert_fusion.6.grad_context, bf16[9,1024,64]{2,1,0:T(8,128)(2,1)} %copy-done.2, bf16[9,1024,64]{2,1,0:T(8,128)(2,1)} %get-tuple-element.71.k_heads, ...), custom_call_target="tpu_custom_call" | custom-call | flops 6039797760 | bytes 20971520 | tf_op jit(solution)/shard_map/pallas_call | solution.py:186
  572.2 4.8 collective-permute-start.10
  586.3 10.9 %convolution_convert_fusion = bf16[2304,1728]{1,0:T(8,128)(2,1)} fusion(bf16[1024,2304]{1,0:T(8,128)(2,1)S(1)} %bitcast.143, bf16[1024,1728]{1,0:T(8,128)(2,1)S(1)} %copy-done.8), kind=kOutput, calls=%fused_computation.1 | convolution fusion | flops 8157708288 | bytes 16220160 | tf_op jit(solution)/shard_map/dot_general | solution.py:1452
  598.3 135.8 %shard_map.226 = (f32[288,1728]{1,0:T(8,128)}, f32[288,576]{1,0:T(8,128)}, bf16[2,128,2304]{2,1,0:T(8,128)(2,1)}, f32[2,2304]{1,0:T(2,128)}) custom-call(bf16[1024,1728]{1,0:T(8,128)(2,1)} %shard_map.225.projected_from, bf16[2304,1728]{1,0:T(8,128)(2,1)} %bitcast.107, bf16[4,2,288,1728]{3,2,1,0:T(8,128)(2,1)} %bitcast.108, ...), custom_call_target="tpu_custom_call" | custom-call | bytes 314572800 | tf_op jit(solution)/shard_map/pallas_call | solution.py:1393
  (131 shorter events, 67.2 us)
Async XLA Ops:
  7.2 320.7 %all-gather.3.cloned.1.call-start = ((), (), s32[]{:S(2)}) async-start(), calls=%async_computation.2 | async-start | bytes 10616832 | tf_op jit(solution)/shard_map/all_gather | solution.py:1532
  17.4 146.4 %copy-start.30 = (s32[2]{0:T(128)S(1)}, s32[2]{0:T(128)}, u32[]{:S(2)}) copy-start(s32[2]{0:T(128)} %param.15) | copy-start | bytes 28
  17.4 147.0 %copy-start.25 = (bf16[2304]{0:T(1024)(128)(2,1)S(1)}, bf16[2304]{0:T(1024)(128)(2,1)}, u32[]{:S(2)}) copy-start(bf16[2304]{0:T(1024)(128)(2,1)} %param.21) | copy-start | bytes 13828
  157.2 589.7 %reduce-scatter.2.cloned.1.call-start = ((), (), s32[]{:S(2)}) async-start(), calls=%async_computation.1 | async-start | bytes 10616832 | tf_op jit(solution)/shard_map/reduce_scatter | solution.py:1635
  157.2 48.0 %collective-permute-start = (bf16[4,288,576]{2,1,0:T(8,128)(2,1)}, bf16[4,288,576]{2,1,0:T(8,128)(2,1)}, u32[]{:S(2)}, u32[]{:S(2)}) collective-permute-start(bf16[4,288,576]{2,1,0:T(8,128)(2,1)} %get-tuple-element.56), channel_id=1, source_target_pairs={{0,4},{4,0},{1,5},{5,1},{2,6},{6,2},{3,7},{7,3},{8,12},{12,8},{9,1... | collective-permute-start | bytes 3981320 | tf_op jit(solution)/shard_map/ppermute | solution.py:1468
  158.8 58.9 %collective-permute-start.1 = (bf16[2,3,288,720]{3,2,1,0:T(8,128)(2,1)}, bf16[2,3,288,720]{3,2,1,0:T(8,128)(2,1)S(1)}, u32[]{:S(2)}, u32[]{:S(2)}) collective-permute-start(bf16[2,3,288,720]{3,2,1,0:T(8,128)(2,1)} %get-tuple-element.58.first_low), channel_id=1, source_target_pairs={{0,8},{8,16},{16,24},{1,9},{9,17},{17,25},{2,10},{10,18},{18,26},{... | collective-permute-start | bytes 7464968 | tf_op jit(solution)/shard_map/ppermute | solution.py:1539
  162.5 59.5 %collective-permute-start.2 = (bf16[2,3,288,720]{3,2,1,0:T(8,128)(2,1)}, bf16[2,3,288,720]{3,2,1,0:T(8,128)(2,1)}, u32[]{:S(2)}, u32[]{:S(2)}) collective-permute-start(bf16[2,3,288,720]{3,2,1,0:T(8,128)(2,1)} %get-tuple-element.59.first_high), channel_id=1, source_target_pairs={{8,0},{16,8},{24,16},{9,1},{17,9},{25,17},{10,2},{18,10},{26,18},{... | collective-permute-start | bytes 7464968 | tf_op jit(solution)/shard_map/ppermute | solution.py:1540
  165.0 15.9 %copy-start = (f32[1024,128]{1,0:T(8,128)S(1)}, f32[1024,128]{1,0:T(8,128)}, u32[]{:S(2)}) copy-start(f32[1024,128]{1,0:T(8,128)} %constant.132.clone.sine) | copy-start | bytes 1572868
  165.0 15.9 %copy-start.1 = (f32[1024,128]{1,0:T(8,128)S(1)}, f32[1024,128]{1,0:T(8,128)}, u32[]{:S(2)}) copy-start(f32[1024,128]{1,0:T(8,128)} %constant.131.clone.cosine) | copy-start | bytes 1572868
  180.9 24.4 %copy-start.17 = (bf16[4,288,576]{2,1,0:T(8,128)(2,1)S(1)}, bf16[4,288,576]{2,1,0:T(8,128)(2,1)}, u32[]{:S(2)}) copy-start(bf16[4,288,576]{2,1,0:T(8,128)(2,1)} %get-tuple-element.56) | copy-start | bytes 3981316
  355.4 19.3 %copy-start.10 = (bf16[2048,720]{1,0:T(8,128)(2,1)}, bf16[2048,720]{1,0:T(8,128)(2,1)S(1)}, u32[]{:S(2)}) copy-start(bf16[2048,720]{1,0:T(8,128)(2,1)S(1)} %get-tuple-element.95.hidden) | copy-start | bytes 8847364
  385.0 31.4 %copy-start.6 = (bf16[2304,720]{1,0:T(8,128)(2,1)}, bf16[2304,720]{1,0:T(8,128)(2,1)S(1)}, u32[]{:S(2)}) copy-start(bf16[2304,720]{1,0:T(8,128)(2,1)S(1)} %multiply_convert_fusion) | copy-start | bytes 9953284
  385.1 31.2 %collective-permute-start.4 = (bf16[576,720]{1,0:T(8,128)(2,1)S(1)}, bf16[576,720]{1,0:T(8,128)(2,1)S(1)}, u32[]{:S(2)}, u32[]{:S(2)}) collective-permute-start(bf16[576,720]{1,0:T(8,128)(2,1)S(1)} %get-tuple-element.104), channel_id=1, source_target_pairs={{24,16},{25,17},{26,18},{27,19},{28,20},{29,21},{30,22},{31,23}} | collective-permute-start | bytes 2488328 | tf_op jit(solution)/shard_map/ppermute | solution.py:1580
  386.0 30.4 %collective-permute-start.3 = (bf16[576,720]{1,0:T(8,128)(2,1)S(1)}, bf16[576,720]{1,0:T(8,128)(2,1)S(1)}, u32[]{:S(2)}, u32[]{:S(2)}) collective-permute-start(bf16[576,720]{1,0:T(8,128)(2,1)S(1)} %get-tuple-element.105), channel_id=1, source_target_pairs={{0,8},{1,9},{2,10},{3,11},{4,12},{5,13},{6,14},{7,15}} | collective-permute-start | bytes 2488328 | tf_op jit(solution)/shard_map/ppermute | solution.py:1579
  510.3 59.9 %collective-permute-start.8 = (bf16[576,720]{1,0:T(8,128)(2,1)}, bf16[576,720]{1,0:T(8,128)(2,1)}, u32[]{:S(2)}, u32[]{:S(2)}) collective-permute-start(bf16[576,720]{1,0:T(8,128)(2,1)} %get-tuple-element.77), channel_id=1, source_target_pairs={{0,8},{8,16},{1,9},{9,17},{2,10},{10,18},{3,11},{11,19},{4,12},{12... | collective-permute-start | bytes 2488328 | tf_op jit(solution)/shard_map/ppermute | solution.py:1579
  518.9 51.2 %collective-permute-start.9 = (bf16[576,720]{1,0:T(8,128)(2,1)S(1)}, bf16[576,720]{1,0:T(8,128)(2,1)}, u32[]{:S(2)}, u32[]{:S(2)}) collective-permute-start(bf16[576,720]{1,0:T(8,128)(2,1)S(1)} %get-tuple-element.78), channel_id=1, source_target_pairs={{16,8},{24,16},{17,9},{25,17},{18,10},{26,18},{19,11},{27,19},{20,... | collective-permute-start | bytes 2488328 | tf_op jit(solution)/shard_map/ppermute | solution.py:1580
  528.8 50.0 %collective-permute-start.5 = (bf16[4,288,576]{2,1,0:T(8,128)(2,1)}, bf16[4,288,576]{2,1,0:T(8,128)(2,1)}, u32[]{:S(2)}, u32[]{:S(2)}) collective-permute-start(bf16[4,288,576]{2,1,0:T(8,128)(2,1)} %dynamic-slice_bitcast_fusion), channel_id=1, source_target_pairs={{0,4},{4,0},{1,5},{5,1},{2,6},{6,2},{3,7},{7,3},{8,12},{12,8},{9,1... | collective-permute-start | bytes 3981320 | tf_op jit(solution)/shard_map/ppermute | solution.py:1468
  530.3 51.5 %collective-permute-start.6 = (bf16[2,576,720]{2,1,0:T(8,128)(2,1)}, bf16[2,576,720]{2,1,0:T(8,128)(2,1)S(1)}, u32[]{:S(2)}, u32[]{:S(2)}) collective-permute-start(bf16[2,576,720]{2,1,0:T(8,128)(2,1)} %get-tuple-element.74), channel_id=1, source_target_pairs={{0,8},{8,16},{16,24},{1,9},{9,17},{17,25},{2,10},{10,18},{18,26},{... | collective-permute-start | bytes 4976648 | tf_op jit(solution)/shard_map/ppermute | solution.py:1607
  534.1 47.7 %collective-permute-start.7 = (bf16[2,576,720]{2,1,0:T(8,128)(2,1)}, bf16[2,576,720]{2,1,0:T(8,128)(2,1)S(1)}, u32[]{:S(2)}, u32[]{:S(2)}) collective-permute-start(bf16[2,576,720]{2,1,0:T(8,128)(2,1)} %get-tuple-element.75), channel_id=1, source_target_pairs={{8,0},{16,8},{24,16},{9,1},{17,9},{25,17},{10,2},{18,10},{26,18},{... | collective-permute-start | bytes 4976648 | tf_op jit(solution)/shard_map/ppermute | solution.py:1609
  540.5 29.7 %copy-start.7 = (bf16[2304,720]{1,0:T(8,128)(2,1)S(1)}, bf16[2304,720]{1,0:T(8,128)(2,1)}, u32[]{:S(2)}) copy-start(bf16[2304,720]{1,0:T(8,128)(2,1)} %copy-done.6) | copy-start | bytes 9953284
  572.2 25.0 %collective-permute-start.10 = (bf16[576,720]{1,0:T(8,128)(2,1)S(1)}, bf16[576,720]{1,0:T(8,128)(2,1)S(1)}, u32[]{:S(2)}, u32[]{:S(2)}) collective-permute-start(bf16[576,720]{1,0:T(8,128)(2,1)S(1)} %get-tuple-element.81), channel_id=1, source_target_pairs={{0,8},{8,16},{16,24},{1,9},{9,17},{17,25},{2,10},{10,18},{18,26},{... | collective-permute-start | bytes 2488328 | tf_op jit(solution)/shard_map/ppermute | solution.py:1607
  577.0 20.2 %collective-permute-start.11 = (bf16[576,720]{1,0:T(8,128)(2,1)S(1)}, bf16[576,720]{1,0:T(8,128)(2,1)S(1)}, u32[]{:S(2)}, u32[]{:S(2)}) collective-permute-start(bf16[576,720]{1,0:T(8,128)(2,1)S(1)} %get-tuple-element.82), channel_id=1, source_target_pairs={{8,0},{16,8},{24,16},{9,1},{17,9},{25,17},{10,2},{18,10},{26,18},{... | collective-permute-start | bytes 2488328 | tf_op jit(solution)/shard_map/ppermute | solution.py:1609
  584.2 157.6 %collective-permute-start.12 = (bf16[2,288,720]{2,1,0:T(8,128)(2,1)S(1)}, bf16[2,288,720]{2,1,0:T(8,128)(2,1)}, u32[]{:S(2)}, u32[]{:S(2)}) collective-permute-start(bf16[2,288,720]{2,1,0:T(8,128)(2,1)S(1)} %pad_maximum_fusion), channel_id=1, source_target_pairs={{0,4},{4,0},{1,5},{5,1},{2,6},{6,2},{3,7},{7,3},{8,12},{12,8},{9,1... | collective-permute-start | bytes 2488328 | tf_op jit(solution)/shard_map/ppermute | solution.py:1468
  597.7 141.2 %collective-permute-start.13 = (bf16[288,720]{1,0:T(8,128)(2,1)S(1)}, bf16[288,720]{1,0:T(8,128)(2,1)}, u32[]{:S(2)}, u32[]{:S(2)}) collective-permute-start(bf16[288,720]{1,0:T(8,128)(2,1)S(1)} %fusion.7), channel_id=1, source_target_pairs={{0,4},{4,0},{1,5},{5,1},{2,6},{6,2},{3,7},{7,3},{8,12},{12,8},{9,1... | collective-permute-start | bytes 1244168 | tf_op jit(solution)/shard_map/ppermute | solution.py:1468
  (25 other events, 191.6 us)
Sparse Core Ops, SparseCore 0:
  157.3 72.7 all-gather.2
  510.4 113.6 reduce-scatter.1

commit v11 on v10

--- a/solution.py
+++ b/solution.py
@@ -381,10 +381,10 @@
 
 
 def first_gather_kernel(
-    count, tokens, tokens_away, gain, qkv, turned_out,
+    count, tokens_all, gain, qkv, turned_out,
     wide_0, wide_1, wide_2, away_0, away_1, away_2,
     token_rows, normed_full, qkv_full, out_half, low_pair, high_pair,
-    landed, normed, wide_landed, qkv_stage, out_stage,
+    tokens, landed, normed, wide_landed, qkv_stage, out_stage,
     send, recv, local, qkv_local, out_local,
 ):
     z, c, t = lax.axis_index("fsdp"), lax.axis_index("cp"), lax.axis_index("tp")
@@ -407,7 +407,9 @@
     rows_y = [mail.slot() for _ in range(2)]
     rows_core = [mail.slot() for _ in range(4)]
 
-    mail.start(rows_x, tokens_away, landed, cp=1 - c)
+    mail.start(rows_x, tokens_all.at[1 - c], landed, cp=1 - c)
+    load = pltpu.make_async_copy(tokens_all.at[c], tokens, local.at[0])
+    load.start()
     heads.send(1)
 
     def rows_out(source, side, half):
@@ -422,6 +424,7 @@
 
     stage_qkv.begin()
     stage_out.begin()
+    load.wait()
     rows_out(tokens, 0, c)
     stage_qkv.turn()
     stage_out.turn()
@@ -480,11 +483,11 @@
     mail.finish()
 
 
-def first_gather(count, tokens, tokens_away, gain, qkv, turned_out, wide, wide_away):
+def first_gather(count, tokens, gain, qkv, turned_out, wide, wide_away):
     slots = 6 * count + 16
     anywhere = pl.BlockSpec(memory_space=pl.ANY)
     vmem = pl.BlockSpec(memory_space=pltpu.VMEM)
-    pair = (2,) + tokens.shape
+    pair = (2,) + tokens.shape[1:]
     wide_shape = (3,) + wide[0].shape
     return pl.pallas_call(
         functools.partial(first_gather_kernel, count),
@@ -496,10 +499,11 @@
             jax.ShapeDtypeStruct((2,) + wide_shape, BF),
             jax.ShapeDtypeStruct((2,) + wide_shape, BF),
         ),
-        in_specs=[vmem, anywhere, vmem] + [anywhere] * 8,
+        in_specs=[anywhere, vmem] + [anywhere] * 8,
         out_specs=(vmem,) + (anywhere,) * 5,
         scratch_shapes=[
-            pltpu.VMEM(tokens.shape, BF),
+            pltpu.VMEM(tokens.shape[1:], BF),
+            pltpu.VMEM(tokens.shape[1:], BF),
             pltpu.VMEM(pair, BF),
             pltpu.VMEM(wide_shape, BF),
             pltpu.VMEM((1,) + qkv.shape, BF),
@@ -514,7 +518,7 @@
         compiler_params=pltpu.CompilerParams(
             collective_id=1, has_side_effects=True, vmem_limit_bytes=60 << 20
         ),
-    )(tokens, tokens_away, gain, qkv, turned_out, *wide, *wide_away)
+    )(tokens, gain, qkv, turned_out, *wide, *wide_away)
 
 
 def in_pieces(rows, body, size=16):
@@ -843,7 +847,11 @@
     loads = [
         pltpu.make_async_copy(source, target, loads_local.at[k])
         for k, (source, target) in enumerate(
-            ((down_from, down), (middle_from, middle), (cotangent_from, cotangent))
+            (
+                (down_from, down),
+                (middle_from, middle),
+                (cotangent_from.at[:, t, c], cotangent),
+            )
         )
     ]
     mail = Mail(send, recv)
@@ -985,7 +993,7 @@
             row = pl.ds(piece * half + rows.start + place.start, place.size)
             summed = own[1, 1, piece, local_row, :].astype(F32) + second[k, place, :].astype(F32)
             grad, products = norm_back(middle[row, :], gain[...], summed)
-            grad = cotangent[row, :].astype(F32) + grad
+            grad = cotangent[piece, local_row, :].astype(F32) + grad
             grad_middle[row, :] = grad
             grad_attention[piece, local_row, :] = (BRANCH * grad).astype(BF)
             gain_rows[...] += jnp.sum(products, axis=0, keepdims=True)
@@ -1067,7 +1075,7 @@
             pltpu.VMEM((2, hidden.shape[0] // 8, hidden.shape[1]), BF),
             pltpu.VMEM((2, hidden.shape[0] // 8, width), BF),
             pltpu.VMEM((rows, width), F32),
-            pltpu.VMEM((rows, width), BF),
+            pltpu.VMEM((2, rows // 2, width), BF),
             pltpu.VMEM(down.shape, BF),
             pltpu.SemaphoreType.DMA((slots,)),
             pltpu.SemaphoreType.DMA((slots,)),
@@ -1521,7 +1529,7 @@
     own_wide = [jnp.where(c == 0, low, high) for low, high in parts]
     wide_away = [jnp.where(c == 0, high, low) for low, high in parts]
     token_rows, normed_one, full_qkv, out_half, first_low, first_high = first_gather(
-        count, pick(tokens, c), pick(tokens, 1 - c), gain_one[None], qkv, out_weight.T,
+        count, tokens, gain_one[None], qkv, out_weight.T,
         own_wide, wide_away,
     )
     token_rows = token_rows.reshape(rows, width)
@@ -1553,9 +1561,7 @@
     full_gate, full_up, full_down = (
         full.reshape(width, hidden_width) for full in (full_gate, full_up, full_down)
     )
-    t = lax.axis_index("tp")
     cotangents_all = cotangents.reshape(sets * seq, width)
-    cotangent_rows = pick(pick(cotangents, t, 1), c, 1).reshape(rows, width)
     gate_pre = matmul(normed_two, full_gate)
     up_pre = matmul(normed_two, full_up)
     hidden_exact, silu_back = jax.vjp(silu_product, gate_pre, up_pre)
@@ -1594,7 +1600,7 @@
     part = grad_normed_two.astype(BF).reshape(sets, lanes, slots, local, width)
     part, gone = lax.optimization_barrier((part, gone))
     grad_middle, grad_attention, gain_two_rows, pair_up, pair_down, feedforward = first_sum(
-        count, part, gate_blocks, up_blocks, hidden, middle, cotangent_rows, gain_two[None],
+        count, part, gate_blocks, up_blocks, hidden, middle, cotangents, gain_two[None],
         full_down,
     )
     grad_attention = grad_attention.reshape(seq, width)

time: 765 us -> 770 us (level)
  waiting for transfers between devices: 14.5 us -> 25.4 us
    ppermute x2, waiting for transfers between devices: 0.01 us -> 10.5 us  [sent(): lax.ppermute(leaving_up, 'fsdp', up_hop[:hop])]
  transfers between devices with their start and end apart: 16 -> 16, of which waited for: 4 -> 5; matrix products, arithmetic and copies ran while one was open for 15% -> 14% of each run, Pallas kernels for 37% -> 35%
where the time goes in v11:
time: 770 us; the launch traced here: 763 us
  Pallas kernels  502 us (65%)
  matrix products  144 us (19%)
  starting transfers between devices  36.8 us (5%)
  other arithmetic  26.6 us (3%)
  waiting for transfers between devices  25.4 us (3%)
  between operations  14.8 us (2%)
  local copies, waits for them, and re-layouts  13.8 us (2%)
    pallas_call x1, Pallas kernels, first_gather(): pl.pallas_call(functools.partial(first_gather_kernel, count), out_shape=(...  139 us
    pallas_call x1, Pallas kernels, last_sum(): pl.pallas_call(functools.partial(last_sum_kernel, count), out_shape=(jax....  129 us
    pallas_call x1, Pallas kernels, second_gather(): pl.pallas_call(functools.partial(second_gather_kernel, count), out_shape=...  93 us
    pallas_call x1, Pallas kernels, first_sum(): pl.pallas_call(functools.partial(first_sum_kernel, count), out_shape=(jax...  92.5 us
    dot_general x5, matrix products, matmul(): return jnp.dot(left, right, preferred_element_type=F32)  61.9 us
    dot_general x5, matrix products, rows_inner(): lax.dot_general(left, right, (((0,), (0,)), ((), ())), preferred_element_...  49.1 us
    dot_general x3, matrix products, cols_inner(): lax.dot_general(left, right, (((1,), (1,)), ((), ())), preferred_element_...  32.7 us
    pallas_call x1, Pallas kernels, attention_back(): pl.pallas_call(functools.partial(attention_back_kernel, blocks), out_shap...  29.3 us
  transfers between devices with their start and end apart: 16, of which 5 were waited for; matrix products, arithmetic and copies ran while one was open for 14% of the time, Pallas kernels for 35%

profile of v11, /device:TPU:0, one launch (start us, length us, event | category | flops | bytes accessed | tf_op | source)
XLA Modules:
  0.0 763.3 jit_solution(9716473642791149468)
XLA Ops:
  16.2 139.4 %shard_map.221 = (bf16[2,128,2304]{2,1,0:T(8,128)(2,1)}, bf16[4,2,128,2304]{3,2,1,0:T(8,128)(2,1)}, bf16[4,2,288,1728]{3,2,1,0:T(8,128)(2,1)}, bf16[4,288,576]{2...) custom-call(bf16[2,128,2304]{2,1,0:T(8,128)(2,1)} %tokens_all.1, ...), custom_call_target="tpu_custom_call" | custom-call | bytes 314572800 | tf_op jit(solution)/shard_map/pallas_call | solution.py:492
  163.4 16.0 %fusion.9.projected = f32[1024,1728]{1,0:T(8,128)} fusion(bf16[1024,2304]{1,0:T(8,128)(2,1)} %bitcast.134, bf16[2304,1728]{1,0:T(8,128)(2,1)} %bitcast.104), kind=kOutput, calls=%fused_computation.57 | convolution fusion | flops 8153726976 | bytes 19759104 | tf_op jit(solution)/shard_map/dot_general | solution.py:1456
  179.4 18.8 %shard_map.222 = (bf16[1024,576]{1,0:T(8,128)(2,1)S(1)}, bf16[9,1024,64]{2,1,0:T(8,128)(2,1)S(1)}, bf16[9,1024,64]{2,1,0:T(8,128)(2,1)}, bf16[9,1024,64]{2,1,0:T(8,128)(2,1)}, f32[9,1,1024]{2,1,0:T(1,128)S(1)}) custom-call(s32[1]{0:T(128)} %dynamic_slice.58.length_ref, f32[1024,1728]{1,0:T(8,128)} %fusion.9.projected, f32[1024,128]{1,0:T(8,128)S(1)} %copy-done, ...), custom_call_target="tpu_custom_call" | custom-call | flops 2415919104 | bytes 20971520 | tf_op jit(solution)/shard_map/pallas_call | solution.py:107
  198.2 5.5 collective-permute-done
  206.6 5.6 convolution_convert_fusion.2
  220.4 93.0 %shard_map.223 = (f32[256,2304]{1,0:T(8,128)}, f32[2,128,2304]{2,1,0:T(8,128)}, bf16[2,4,2,128,2304]{4,3,2,1,0:T(8,128)(2,1)}, bf16[4,2,288,720]{3,2,1,0:T(8,128...) custom-call(bf16[4,256,2304]{2,1,0:T(8,128)(2,1)} %bitcast.119, bf16[256,2304]{1,0:T(8,128)(2,1)} %bitcast.117, ...), custom_call_target="tpu_custom_call" | custom-call | bytes 314572800 | tf_op jit(solution)/shard_map/pallas_call | solution.py:687
  313.4 12.9 %fusion.11 = f32[2048,720]{1,0:T(8,128)} fusion(bf16[2048,2304]{1,0:T(8,128)(2,1)} %bitcast.130, bf16[2304,720]{1,0:T(8,128)(2,1)} %bitcast.142), kind=kOutput, calls=%fused_computation.59 | convolution fusion | flops 6794772480 | bytes 18653184 | tf_op jit(solution)/shard_map/dot_general | solution.py:1456
  326.3 12.0 %fusion.10 = f32[2048,720]{1,0:T(8,128)} fusion(bf16[2048,2304]{1,0:T(8,128)(2,1)} %bitcast.98, bf16[2304,720]{1,0:T(8,128)(2,1)S(1)} %bitcast.121), kind=kOutput, calls=%fused_computation.58 | convolution fusion | flops 6794772480 | bytes 18653184 | tf_op jit(solution)/shard_map/dot_general | solution.py:1456
  338.2 16.3 %multiply_convert_fusion.1 = (bf16[2048,720]{1,0:T(8,128)(2,1)S(1)}, bf16[2048,720]{1,0:T(8,128)(2,1)}, bf16[2048,720]{1,0:T(8,128)(2,1)}) fusion(f32[2048,720]{1,0:T(8,128)} %fusion.11, f32[2048,720]{1,0:T(8,128)} %fusion.10, bf16[2048,2304]{1,0:T(8,128)(2,1)S(1)} %bitcast.132, bf16[2304,720]{1,0:T(8,128)(2,1)} %bitcast.140), kind=kOutput, calls=%fused_computation.4 | convolution fusion | flops 6822789120 | bytes 33398784 | tf_op jit(solution)/shard_map/dot_general | solution.py:1456
  354.5 13.8 %convolution_convert_fusion.1 = bf16[2048,2304]{1,0:T(8,128)(2,1)} fusion(bf16[2048,720]{1,0:T(8,128)(2,1)} %get-tuple-element.96, bf16[2304,720]{1,0:T(8,128)(2,1)} %bitcast.143), kind=kOutput, calls=%fused_computation.2 | convolution fusion | flops 6799491072 | bytes 15704064 | tf_op jit(solution)/shard_map/dot_general | solution.py:1464
  368.3 11.3 %convolution_convert_fusion.4 = bf16[2304,720]{1,0:T(8,128)(2,1)} fusion(bf16[2048,2304]{1,0:T(8,128)(2,1)S(1)} %bitcast.133, bf16[2048,720]{1,0:T(8,128)(2,1)} %get-tuple-element.96), kind=kOutput, calls=%fused_computation.11 | convolution fusion | flops 6796431360 | bytes 15704064 | tf_op jit(solution)/shard_map/dot_general | solution.py:1460
  379.6 8.1 %multiply_convert_fusion = bf16[2304,720]{1,0:T(8,128)(2,1)S(1)} fusion(bf16[2048,2304]{1,0:T(8,128)(2,1)S(1)} %bitcast.102, bf16[2048,720]{1,0:T(8,128)(2,1)S(1)} %get-tuple-element.95.hidden), kind=kOutput, calls=%fused_computation.3 | convolution fusion | flops 6798090240 | bytes 15704064 | tf_op jit(solution)/shard_map/dot_general | solution.py:1460
  391.0 13.3 %add_convert_fusion = bf16[2048,2304]{1,0:T(8,128)(2,1)} fusion(bf16[2048,2304]{1,0:T(8,128)(2,1)} %convolution_convert_fusion.1, bf16[2048,720]{1,0:T(8,128)(2,1)} %get-tuple-element.97, bf16[2304,720]{1,0:T(8,128)(2,1)S(1)} %bitcast.141), kind=kOutput, calls=%fused_computation | convolution fusion | flops 6808928256 | bytes 25141248 | tf_op jit(solution)/shard_map/dot_general | solution.py:1464
  404.4 12.4 %convolution_convert_fusion.3 = bf16[2304,720]{1,0:T(8,128)(2,1)} fusion(bf16[2048,2304]{1,0:T(8,128)(2,1)} %bitcast.131, bf16[2048,720]{1,0:T(8,128)(2,1)} %get-tuple-element.97), kind=kOutput, calls=%fused_computation.10 | convolution fusion | flops 6796431360 | bytes 15704064 | tf_op jit(solution)/shard_map/dot_general | solution.py:1460
  417.3 92.5 %shard_map.224 = (f32[256,2304]{1,0:T(8,128)}, bf16[4,2,128,2304]{3,2,1,0:T(8,128)(2,1)}, f32[1,2304]{1,0:T(1,128)}, bf16[2,576,720]{2,1,0:T(8,128)(2,1)}, bf16[...) custom-call(bf16[2,4,2,128,2304]{4,3,2,1,0:T(8,128)(2,1)} %bitcast.103, bf16[4,576,720]{2,1,0:T(8,128)(2,1)} %bitcast.107, ...), custom_call_target="tpu_custom_call" | custom-call | bytes 314572800 | tf_op jit(solution)/shard_map/pallas_call | solution.py:1055
  511.1 6.4 convolution_convert_fusion.5
  520.2 9.5 %collective-permute-start.6 = (bf16[2,576,720]{2,1,0:T(8,128)(2,1)}, bf16[2,576,720]{2,1,0:T(8,128)(2,1)}, u32[]{:S(2)}, u32[]{:S(2)}) collective-permute-start(bf16[2,576,720]{2,1,0:T(8,128)(2,1)} %get-tuple-element.74), channel_id=1, source_target_pairs={{0,8},{8,16},{16,24},{1,9},{9,17},{17,25},{2,10},{10,18},{18,26},{... | collective-permute-start | bytes 4976648 | tf_op jit(solution)/shard_map/ppermute | solution.py:1613
  529.7 4.7 collective-permute-start.8
  536.1 4.9 convolution_convert_fusion.6.grad_context
  541.0 29.3 %shard_map.225.projected_from = bf16[1024,1728]{1,0:T(8,128)(2,1)} custom-call(s32[1]{0:T(128)} %dynamic_slice.58.length_ref, bf16[1024,576]{1,0:T(8,128)(2,1)} %convolution_convert_fusion.6.grad_context, bf16[9,1024,64]{2,1,0:T(8,128)(2,1)} %copy-done.2, bf16[9,1024,64]{2,1,0:T(8,128)(2,1)} %get-tuple-element.71.k_heads, ...), custom_call_target="tpu_custom_call" | custom-call | flops 6039797760 | bytes 20971520 | tf_op jit(solution)/shard_map/pallas_call | solution.py:186
  570.3 10.5 %collective-permute-done.8 = bf16[576,720]{1,0:T(8,128)(2,1)} collective-permute-done((bf16[576,720]{1,0:T(8,128)(2,1)S(1)}, bf16[576,720]{1,0:T(8,128)(2,1)}, u32[]{:S(2)}, u32[]{:S(2)}) %collective-permute-start.8) | collective-permute-done | bytes 829472 | tf_op jit(solution)/shard_map/ppermute | solution.py:1585
  582.7 6.8 collective-permute-start.10
  597.2 10.9 %convolution_convert_fusion = bf16[2304,1728]{1,0:T(8,128)(2,1)} fusion(bf16[1024,2304]{1,0:T(8,128)(2,1)S(1)} %bitcast.137, bf16[1024,1728]{1,0:T(8,128)(2,1)S(1)} %copy-done.8), kind=kOutput, calls=%fused_computation.1 | convolution fusion | flops 8157708288 | bytes 16220160 | tf_op jit(solution)/shard_map/dot_general | solution.py:1460
  610.6 129.3 %shard_map.226 = (f32[288,1728]{1,0:T(8,128)}, f32[288,576]{1,0:T(8,128)}, bf16[2,128,2304]{2,1,0:T(8,128)(2,1)}, f32[2,2304]{1,0:T(2,128)}) custom-call(bf16[1024,1728]{1,0:T(8,128)(2,1)} %shard_map.225.projected_from, bf16[2304,1728]{1,0:T(8,128)(2,1)} %bitcast.105, bf16[4,2,288,1728]{3,2,1,0:T(8,128)(2,1)} %bitcast.106, ...), custom_call_target="tpu_custom_call" | custom-call | bytes 314572800 | tf_op jit(solution)/shard_map/pallas_call | solution.py:1401
  (132 shorter events, 65.6 us)
Async XLA Ops:
  7.2 319.0 %all-gather.3.cloned.1.call-start = ((), (), s32[]{:S(2)}) async-start(), calls=%async_computation.2 | async-start | bytes 10616832 | tf_op jit(solution)/shard_map/all_gather | solution.py:1540
  16.2 146.0 %copy-start.24 = (bf16[2304]{0:T(1024)(128)(2,1)S(1)}, bf16[2304]{0:T(1024)(128)(2,1)}, u32[]{:S(2)}) copy-start(bf16[2304]{0:T(1024)(128)(2,1)} %param.21) | copy-start | bytes 13828
  16.2 146.6 %copy-start.28 = (s32[2]{0:T(128)S(1)}, s32[2]{0:T(128)}, u32[]{:S(2)}) copy-start(s32[2]{0:T(128)} %param.15) | copy-start | bytes 28
  155.6 596.0 %reduce-scatter.2.cloned.1.call-start = ((), (), s32[]{:S(2)}) async-start(), calls=%async_computation.1 | async-start | bytes 10616832 | tf_op jit(solution)/shard_map/reduce_scatter | solution.py:1641
  155.6 48.0 %collective-permute-start = (bf16[4,288,576]{2,1,0:T(8,128)(2,1)}, bf16[4,288,576]{2,1,0:T(8,128)(2,1)}, u32[]{:S(2)}, u32[]{:S(2)}) collective-permute-start(bf16[4,288,576]{2,1,0:T(8,128)(2,1)} %get-tuple-element.56), channel_id=1, source_target_pairs={{0,4},{4,0},{1,5},{5,1},{2,6},{6,2},{3,7},{7,3},{8,12},{12,8},{9,1... | collective-permute-start | bytes 3981320 | tf_op jit(solution)/shard_map/ppermute | solution.py:1476
  157.2 58.9 %collective-permute-start.1 = (bf16[2,3,288,720]{3,2,1,0:T(8,128)(2,1)}, bf16[2,3,288,720]{3,2,1,0:T(8,128)(2,1)S(1)}, u32[]{:S(2)}, u32[]{:S(2)}) collective-permute-start(bf16[2,3,288,720]{3,2,1,0:T(8,128)(2,1)} %get-tuple-element.58.first_low), channel_id=1, source_target_pairs={{0,8},{8,16},{16,24},{1,9},{9,17},{17,25},{2,10},{10,18},{18,26},{... | collective-permute-start | bytes 7464968 | tf_op jit(solution)/shard_map/ppermute | solution.py:1547
  160.8 59.5 %collective-permute-start.2 = (bf16[2,3,288,720]{3,2,1,0:T(8,128)(2,1)}, bf16[2,3,288,720]{3,2,1,0:T(8,128)(2,1)}, u32[]{:S(2)}, u32[]{:S(2)}) collective-permute-start(bf16[2,3,288,720]{3,2,1,0:T(8,128)(2,1)} %get-tuple-element.59.first_high), channel_id=1, source_target_pairs={{8,0},{16,8},{24,16},{9,1},{17,9},{25,17},{10,2},{18,10},{26,18},{... | collective-permute-start | bytes 7464968 | tf_op jit(solution)/shard_map/ppermute | solution.py:1548
  354.5 25.1 %copy-start.10 = (bf16[2048,720]{1,0:T(8,128)(2,1)}, bf16[2048,720]{1,0:T(8,128)(2,1)S(1)}, u32[]{:S(2)}) copy-start(bf16[2048,720]{1,0:T(8,128)(2,1)S(1)} %get-tuple-element.95.hidden) | copy-start | bytes 8847364
  354.5 25.1 %slice-start = ((s8[9437184]{0:T(1024)(128)(4,1)}), s8[4194304]{0:T(1024)(128)(4,1)S(1)}, s32[]{:S(2)}) async-start(s8[9437184]{0:T(1024)(128)(4,1)} %bitcast.100), calls=%async_computation.3 | async-start | bytes 8388608
  354.5 25.1 %slice-start.1 = ((s8[9437184]{0:T(1024)(128)(4,1)}), s8[1048576]{0:T(1024)(128)(4,1)S(1)}, s32[]{:S(2)}) async-start(s8[9437184]{0:T(1024)(128)(4,1)} %bitcast.100), calls=%async_computation.4 | async-start | bytes 2097152
  387.7 29.0 %copy-start.6 = (bf16[2304,720]{1,0:T(8,128)(2,1)}, bf16[2304,720]{1,0:T(8,128)(2,1)S(1)}, u32[]{:S(2)}) copy-start(bf16[2304,720]{1,0:T(8,128)(2,1)S(1)} %multiply_convert_fusion) | copy-start | bytes 9953284
  387.9 28.9 %collective-permute-start.4 = (bf16[576,720]{1,0:T(8,128)(2,1)S(1)}, bf16[576,720]{1,0:T(8,128)(2,1)S(1)}, u32[]{:S(2)}, u32[]{:S(2)}) collective-permute-start(bf16[576,720]{1,0:T(8,128)(2,1)S(1)} %get-tuple-element.104), channel_id=1, source_target_pairs={{24,16},{25,17},{26,18},{27,19},{28,20},{29,21},{30,22},{31,23}} | collective-permute-start | bytes 2488328 | tf_op jit(solution)/shard_map/ppermute | solution.py:1586
  388.8 28.0 %collective-permute-start.3 = (bf16[576,720]{1,0:T(8,128)(2,1)S(1)}, bf16[576,720]{1,0:T(8,128)(2,1)S(1)}, u32[]{:S(2)}, u32[]{:S(2)}) collective-permute-start(bf16[576,720]{1,0:T(8,128)(2,1)S(1)} %get-tuple-element.105), channel_id=1, source_target_pairs={{0,8},{1,9},{2,10},{3,11},{4,12},{5,13},{6,14},{7,15}} | collective-permute-start | bytes 2488328 | tf_op jit(solution)/shard_map/ppermute | solution.py:1585
  511.1 25.0 %copy-start.26 = (bf16[4,2,128,2304]{3,2,1,0:T(8,128)(2,1)S(1)}, bf16[4,2,128,2304]{3,2,1,0:T(8,128)(2,1)}, u32[]{:S(2)}) copy-start(bf16[4,2,128,2304]{3,2,1,0:T(8,128)(2,1)} %get-tuple-element.69) | copy-start | bytes 14155780
  517.6 73.2 %collective-permute-start.5 = (bf16[4,288,576]{2,1,0:T(8,128)(2,1)S(1)}, bf16[4,288,576]{2,1,0:T(8,128)(2,1)S(1)}, u32[]{:S(2)}, u32[]{:S(2)}) collective-permute-start(bf16[4,288,576]{2,1,0:T(8,128)(2,1)S(1)} %dynamic-slice_bitcast_fusion), channel_id=1, source_target_pairs={{0,4},{4,0},{1,5},{5,1},{2,6},{6,2},{3,7},{7,3},{8,12},{12,8},{9,1... | collective-permute-start | bytes 3981320 | tf_op jit(solution)/shard_map/ppermute | solution.py:1476
  518.9 73.4 %collective-permute-start.7 = (bf16[2,576,720]{2,1,0:T(8,128)(2,1)}, bf16[2,576,720]{2,1,0:T(8,128)(2,1)}, u32[]{:S(2)}, u32[]{:S(2)}) collective-permute-start(bf16[2,576,720]{2,1,0:T(8,128)(2,1)} %get-tuple-element.75), channel_id=1, source_target_pairs={{8,0},{16,8},{24,16},{9,1},{17,9},{25,17},{10,2},{18,10},{26,18},{... | collective-permute-start | bytes 4976648 | tf_op jit(solution)/shard_map/ppermute | solution.py:1615
  520.2 72.1 %collective-permute-start.6 = (bf16[2,576,720]{2,1,0:T(8,128)(2,1)}, bf16[2,576,720]{2,1,0:T(8,128)(2,1)}, u32[]{:S(2)}, u32[]{:S(2)}) collective-permute-start(bf16[2,576,720]{2,1,0:T(8,128)(2,1)} %get-tuple-element.74), channel_id=1, source_target_pairs={{0,8},{8,16},{16,24},{1,9},{9,17},{17,25},{2,10},{10,18},{18,26},{... | collective-permute-start | bytes 4976648 | tf_op jit(solution)/shard_map/ppermute | solution.py:1613
  529.7 51.2 %collective-permute-start.8 = (bf16[576,720]{1,0:T(8,128)(2,1)S(1)}, bf16[576,720]{1,0:T(8,128)(2,1)}, u32[]{:S(2)}, u32[]{:S(2)}) collective-permute-start(bf16[576,720]{1,0:T(8,128)(2,1)S(1)} %get-tuple-element.77), channel_id=1, source_target_pairs={{0,8},{8,16},{1,9},{9,17},{2,10},{10,18},{3,11},{11,19},{4,12},{12... | collective-permute-start | bytes 2488328 | tf_op jit(solution)/shard_map/ppermute | solution.py:1585
  534.3 46.5 %collective-permute-start.9 = (bf16[576,720]{1,0:T(8,128)(2,1)S(1)}, bf16[576,720]{1,0:T(8,128)(2,1)}, u32[]{:S(2)}, u32[]{:S(2)}) collective-permute-start(bf16[576,720]{1,0:T(8,128)(2,1)S(1)} %get-tuple-element.78), channel_id=1, source_target_pairs={{16,8},{24,16},{17,9},{25,17},{18,10},{26,18},{19,11},{27,19},{20,... | collective-permute-start | bytes 2488328 | tf_op jit(solution)/shard_map/ppermute | solution.py:1586
  541.0 39.9 %copy-start.7 = (bf16[2304,720]{1,0:T(8,128)(2,1)S(1)}, bf16[2304,720]{1,0:T(8,128)(2,1)}, u32[]{:S(2)}) copy-start(bf16[2304,720]{1,0:T(8,128)(2,1)} %copy-done.6) | copy-start | bytes 9953284
  582.7 25.4 %collective-permute-start.10 = (bf16[576,720]{1,0:T(8,128)(2,1)S(1)}, bf16[576,720]{1,0:T(8,128)(2,1)S(1)}, u32[]{:S(2)}, u32[]{:S(2)}) collective-permute-start(bf16[576,720]{1,0:T(8,128)(2,1)S(1)} %get-tuple-element.81), channel_id=1, source_target_pairs={{0,8},{8,16},{16,24},{1,9},{9,17},{17,25},{2,10},{10,18},{18,26},{... | collective-permute-start | bytes 2488328 | tf_op jit(solution)/shard_map/ppermute | solution.py:1613
  589.5 19.7 %collective-permute-start.11 = (bf16[576,720]{1,0:T(8,128)(2,1)S(1)}, bf16[576,720]{1,0:T(8,128)(2,1)S(1)}, u32[]{:S(2)}, u32[]{:S(2)}) collective-permute-start(bf16[576,720]{1,0:T(8,128)(2,1)S(1)} %get-tuple-element.82), channel_id=1, source_target_pairs={{8,0},{16,8},{24,16},{9,1},{17,9},{25,17},{10,2},{18,10},{26,18},{... | collective-permute-start | bytes 2488328 | tf_op jit(solution)/shard_map/ppermute | solution.py:1615
  597.0 149.5 %collective-permute-start.12 = (bf16[2,288,720]{2,1,0:T(8,128)(2,1)}, bf16[2,288,720]{2,1,0:T(8,128)(2,1)}, u32[]{:S(2)}, u32[]{:S(2)}) collective-permute-start(bf16[2,288,720]{2,1,0:T(8,128)(2,1)} %pad_maximum_fusion), channel_id=1, source_target_pairs={{0,4},{4,0},{1,5},{5,1},{2,6},{6,2},{3,7},{7,3},{8,12},{12,8},{9,1... | collective-permute-start | bytes 2488328 | tf_op jit(solution)/shard_map/ppermute | solution.py:1476
  609.6 135.0 %collective-permute-start.13 = (bf16[288,720]{1,0:T(8,128)(2,1)S(1)}, bf16[288,720]{1,0:T(8,128)(2,1)S(1)}, u32[]{:S(2)}, u32[]{:S(2)}) collective-permute-start(bf16[288,720]{1,0:T(8,128)(2,1)S(1)} %fusion.7), channel_id=1, source_target_pairs={{0,4},{4,0},{1,5},{5,1},{2,6},{6,2},{3,7},{7,3},{8,12},{12,8},{9,1... | collective-permute-start | bytes 1244168 | tf_op jit(solution)/shard_map/ppermute | solution.py:1476
  (26 other events, 251.7 us)
Sparse Core Ops, SparseCore 0:
  155.7 72.7 all-gather.2
  509.9 99.0 reduce-scatter.1
